TPU v7x, 32 devices: a whole 2x2x4 slice. The times are simulated.
32 devices in a mesh: ctx: 8 (over y, x, core), fsdp: 4 (over z).
Axes of the slice: x: 2, y: 2, z: 4, core: 2. Of those that a mesh axis runs over, the one named last changes fastest.
Arguments:
- hidden_in: bfloat16 [4, 1024, 2048], P('fsdp', 'ctx'), may hold values from -18 to 18
- out_grad: bfloat16 [4, 1024, 2048], P('fsdp', 'ctx'), may hold values from -6 to 6
- positions: int32 [4, 1024], P('fsdp', 'ctx'), may hold values from 0 to 1023, as said below
- block_order: int32 [16], replicated, may hold values from 0 to 15, as said below
- attn_gain: float32 [2048], replicated, may hold values from 0.25 to 1.75
- ffn_gain: float32 [2048], replicated, may hold values from 0.25 to 1.75
- qkv_weight: bfloat16 [2048, 3072], P('fsdp'), may hold values from -1 to 1
- out_weight: bfloat16 [2048, 2048], P('fsdp'), may hold values from -0.5 to 0.5
- ffn_weight: bfloat16 [2048, 3, 8192], P(None, None, 'fsdp'), may hold values from -0.125 to 0.125
Outputs:
- hidden_out: bfloat16 [4, 1024, 2048], P('fsdp', 'ctx')
- input_grad: float32 [4, 1024, 2048], P('fsdp', 'ctx')
- qkv_weight_grad: float32 [2048, 3072], P(('ctx', 'fsdp'))
- out_weight_grad: float32 [2048, 2048], P(('ctx', 'fsdp'))
- ffn_weight_grad: float32 [2048, 3, 8192], P('ctx', None, 'fsdp')
- attn_gain_grad: float32 [2048], P(('ctx', 'fsdp'))
- ffn_gain_grad: float32 [2048], P(('ctx', 'fsdp'))
Inputs may be any that keep to these rules, and one draw needn't show every extreme that they name: `block_order`: the two slots 2c and 2c + 1 hold two blocks whose numbers add up to 15, and every block number appears once. In initial token order, a sequence's positions rise by one from token to token and restart at 0 at its first token and at the start of each packed document; the first sequence is a single document; they are listed in storage order.
All inputs are finite; a program needn't handle non-finite values.
Results may differ from a plain program's by a relative error of at most 0.03.
Values may be sent and summed in bfloat16 or wider, within the bound.
No kernel may reach another device: no remote copies, remote signals or barrier semaphores. Data moves between devices by JAX's collectives and lax.ppermute only.
A program may use at most 576 MiB of HBM per device.

v0:
```python
import math

import jax
import jax.numpy as jnp
from jax import lax
from jax.experimental import pallas as pl
from jax.experimental.pallas import tpu as pltpu
from jax.sharding import PartitionSpec as P


H = 32
KV = 8
HD = 64

NORM_EPS = 1e-05
ROPE_BASE = 500000.0
FFN_TILE = 512


BF = jnp.bfloat16
F32 = jnp.float32


def mm(a, b, dims):
    return lax.dot_general(a, b, (dims, ((), ())), preferred_element_type=F32)


def nn(a, b):
    return mm(a, b, ((1,), (0,)))


def nt(a, b):
    return mm(a, b, ((1,), (1,)))


def tn(a, b):
    return mm(a, b, ((0,), (0,)))


def swap(value, axis, offset):
    count = lax.axis_size(axis)
    return lax.ppermute(value, axis, [(i, i ^ offset) for i in range(count)])


def rotate(values, token_places):
    head_dim = values.shape[-1]
    half_dim = head_dim // 2
    frequency = jnp.power(ROPE_BASE, -(jnp.arange(half_dim, dtype=F32) * 2.0 / head_dim))
    angles = token_places.astype(F32)[:, None] * frequency[None, :]
    cosine = jnp.concatenate([jnp.cos(angles), jnp.cos(angles)], axis=-1)[:, None, :]
    sine_part = jnp.concatenate([jnp.sin(angles), jnp.sin(angles)], axis=-1)[:, None, :]
    turned = jnp.concatenate([-values[..., half_dim:], values[..., :half_dim]], axis=-1)
    return values * cosine + turned * sine_part


def norm_scale(values):
    return lax.rsqrt(jnp.mean(values * values, axis=-1, keepdims=True) + NORM_EPS)


def lookup(entries, row_ids):
    matches = row_ids[:, None] == jnp.arange(entries.shape[0], dtype=jnp.int32)[None, :]
    return jnp.sum(jnp.where(matches, entries[None, :], 0), axis=1)


def anchors_of(block_order, owner, row_count):
    block_len = row_count // 2
    row_ids = owner * row_count + jnp.arange(row_count, dtype=jnp.int32)
    return lookup(block_order, row_ids // block_len) * block_len + row_ids % block_len


def after(value, *earlier):
    return lax.optimization_barrier((value, earlier))[0]


def ids():
    return lax.axis_index("ctx"), lax.axis_index("fsdp")


def gather_pieces(weight):
    rows, columns = weight.shape
    share = columns // lax.axis_size("ctx")
    half = rows // 2
    mine = lax.dynamic_slice(weight, (0, lax.axis_index("ctx") * share), (rows, share))
    planes = {}
    planes[3] = swap(mine, "fsdp", 3)
    planes[1] = swap(mine, "fsdp", 1)
    planes[2] = swap(planes[3], "fsdp", 1)
    pieces = []
    for away in (1, 3, 2):
        first = planes[away]
        along_x, along_y = swap(first, "ctx", 2), swap(first, "ctx", 4)
        top, low = swap(along_y[:half], "ctx", 2), swap(along_x[half:], "ctx", 4)
        parts = [(0, 0, first), (2, 0, along_x), (4, 0, along_y), (6, 0, top), (6, half, low)]
        for offset, start, part in parts:
            pieces.append((away, offset, start, part))
            pieces.append((away, offset + 1, start, swap(part, "ctx", 1)))
    return pieces, (planes[1], (pieces[-4][3], pieces[-2][3]))


def pieces_kernel(places, rows_in, share, back, ids_ref, x_ref, own_ref, *refs):
    count = len(places)
    piece_refs, refs = refs[:count], refs[count:]
    if back:
        y_ref, refs = refs[0], refs[1:]
    else:
        (cos_ref, sin_ref, q_ref, pair_ref, y_ref), refs = refs[:5], refs[5:]
    own_buf, bufs, sems = refs[0], refs[1:-1], refs[-1]
    me, plane = ids_ref[0], ids_ref[1]
    copies = [pltpu.make_async_copy(own_ref, own_buf, sems.at[count])]
    for i in range(count):
        copies.append(pltpu.make_async_copy(piece_refs[i], bufs[i], sems.at[i]))
    for copy in copies:
        copy.start()

    def tokens(start, size):
        return x_ref[:, pl.ds(pl.multiple_of(start, 128), size)]

    copies[0].wait()
    if back:
        y_ref[...] = jnp.zeros_like(y_ref)
        y_ref[:, pl.ds(pl.multiple_of(plane * rows_in, 128), rows_in)] = nt(
            x_ref[...], own_buf[...]
        )
    else:
        y_ref[...] = nn(tokens(plane * rows_in, rows_in), own_buf[...])
    for i, (away, offset, start, height) in enumerate(places):
        copies[i + 1].wait()
        inner = (plane ^ away) * rows_in + start
        outer = (me ^ offset) * share
        if back:
            at = pl.ds(pl.multiple_of(inner, 128), height)
            y_ref[:, at] += nt(tokens(outer, share), bufs[i][...])
        else:
            at = pl.ds(pl.multiple_of(outer, 128), share)
            y_ref[:, at] += nn(tokens(inner, height), bufs[i][...])
    if not back:
        cosine, sine = cos_ref[...], sin_ref[...]
        queries, keys = H * HD, KV * HD
        for start in range(0, queries + keys, 128):
            tile = turn(y_ref[:, start : start + 128], cosine, sine)
            if start < queries:
                q_ref[:, start : start + 128] = (tile * (1.0 / math.sqrt(HD))).astype(BF)
            else:
                pair_ref[:, start - queries : start - queries + 128] = tile.astype(BF)
        pair_ref[:, keys:] = y_ref[:, queries + keys :].astype(BF)


def pieces_call(x, own, pieces, extra, out_shape, scratch, back):
    me, plane = ids()
    rows_in, columns = own.shape
    share = columns // lax.axis_size("ctx")
    places = tuple((away, offset, start, part.shape[0]) for away, offset, start, part in pieces)
    arrays = [part for _, _, _, part in pieces]
    hbm, vmem = pl.BlockSpec(memory_space=pl.ANY), pl.BlockSpec(memory_space=pltpu.VMEM)
    return pl.pallas_call(
        lambda *refs: pieces_kernel(places, rows_in, share, back, *refs),
        out_shape=out_shape,
        in_specs=[pl.BlockSpec(memory_space=pltpu.SMEM), vmem, hbm]
        + [hbm] * len(arrays)
        + [vmem] * len(extra),
        out_specs=jax.tree.map(lambda _: vmem, out_shape),
        scratch_shapes=scratch
        + [pltpu.VMEM(own.shape, own.dtype)]
        + [pltpu.VMEM(part.shape, part.dtype) for part in arrays]
        + [pltpu.SemaphoreType.DMA((len(arrays) + 1,))],
        compiler_params=pltpu.CompilerParams(vmem_limit_bytes=32 << 20),
        cost_estimate=pl.CostEstimate(
            flops=2 * x.shape[0] * rows_in * lax.axis_size("fsdp") * columns,
            bytes_accessed=2 * rows_in * lax.axis_size("fsdp") * columns,
            transcendentals=0,
        ),
        name="pieces_back" if back else "pieces_forward",
    )(jnp.stack([me, plane]), x, own, *arrays, *extra)


def pieces_forward(x, own, pieces, cosine, sine):
    rows, columns = x.shape[0], own.shape[1]
    out_shape = (
        jax.ShapeDtypeStruct((rows, H * HD), BF),
        jax.ShapeDtypeStruct((rows, 2 * KV * HD), BF),
    )
    scratch = [pltpu.VMEM((rows, columns), F32)]
    return pieces_call(x, own, pieces, [cosine, sine], out_shape, scratch, False)


def pieces_back(x, own, pieces):
    out_shape = jax.ShapeDtypeStruct((x.shape[0], own.shape[0] * lax.axis_size("fsdp")), F32)
    return pieces_call(x, own, pieces, [], out_shape, [], True)


def gather_blocks(weight, before_fsdp, before_ctx):
    rows, columns = weight.shape
    share = columns // lax.axis_size("ctx")
    mine = lax.dynamic_slice(weight, (0, lax.axis_index("ctx") * share), (rows, share))
    planes = lax.all_gather(after(mine, before_fsdp), "fsdp")
    return lax.all_gather(after(planes, before_ctx), "ctx")


def whole_of(blocks):
    ctx_count, fsdp_count, rows, share = blocks.shape
    return blocks.transpose(1, 2, 0, 3).reshape(fsdp_count * rows, ctx_count * share)


def out_forward_kernel(x_ref, w_ref, hidden_ref, gain_ref, residual_ref, normed_ref):
    step = pl.program_id(0)

    @pl.when(step == 0)
    def _():
        residual_ref[...] = hidden_ref[...].astype(F32)

    rows = w_ref.shape[2]
    for plane in range(w_ref.shape[1]):
        residual_ref[:, plane * rows : (plane + 1) * rows] += nt(x_ref[...], w_ref[0, plane])

    @pl.when(step == pl.num_programs(0) - 1)
    def _():
        residual = residual_ref[...]
        normed_ref[...] = (residual * norm_scale(residual) * gain_ref[...]).astype(BF)


def out_forward(attn_rows, blocks, hidden, gain):
    rows, width = hidden.shape
    ctx_count, fsdp_count, height, share = blocks.shape
    if share % 128:
        residual = hidden.astype(F32) + nt(attn_rows, whole_of(blocks))
        return residual, (residual * norm_scale(residual) * gain).astype(BF)
    return pl.pallas_call(
        out_forward_kernel,
        grid=(ctx_count,),
        out_shape=(
            jax.ShapeDtypeStruct((rows, width), F32),
            jax.ShapeDtypeStruct((rows, width), BF),
        ),
        in_specs=[
            pl.BlockSpec((rows, share), lambda c: (0, c)),
            pl.BlockSpec((1, fsdp_count, height, share), lambda c: (c, 0, 0, 0)),
            pl.BlockSpec((rows, width), lambda c: (0, 0)),
            pl.BlockSpec((1, width), lambda c: (0, 0)),
        ],
        out_specs=(
            pl.BlockSpec((rows, width), lambda c: (0, 0)),
            pl.BlockSpec((rows, width), lambda c: (0, 0)),
        ),
        compiler_params=pltpu.CompilerParams(vmem_limit_bytes=24 << 20),
        cost_estimate=pl.CostEstimate(
            flops=2 * rows * width * ctx_count * share,
            bytes_accessed=2 * width * ctx_count * share,
            transcendentals=0,
        ),
        name="out_forward",
    )(attn_rows, blocks, hidden, gain[None])


def out_back_kernel(x_ref, w_ref, y_ref):
    rows = w_ref.shape[2]
    total = nn(x_ref[:, :rows], w_ref[0, 0])
    for plane in range(1, w_ref.shape[1]):
        total += nn(x_ref[:, plane * rows : (plane + 1) * rows], w_ref[0, plane])
    y_ref[...] = total.astype(BF)


def out_back(x, blocks):
    rows, width = x.shape
    ctx_count, fsdp_count, height, share = blocks.shape
    if share % 128:
        return nn(x, whole_of(blocks)).astype(BF)
    return pl.pallas_call(
        out_back_kernel,
        grid=(ctx_count,),
        out_shape=jax.ShapeDtypeStruct((rows, ctx_count * share), BF),
        in_specs=[
            pl.BlockSpec((rows, width), lambda c: (0, 0)),
            pl.BlockSpec((1, fsdp_count, height, share), lambda c: (c, 0, 0, 0)),
        ],
        out_specs=pl.BlockSpec((rows, share), lambda c: (0, c)),
        compiler_params=pltpu.CompilerParams(vmem_limit_bytes=24 << 20),
        cost_estimate=pl.CostEstimate(
            flops=2 * rows * width * ctx_count * share,
            bytes_accessed=2 * width * ctx_count * share,
            transcendentals=0,
        ),
        name="out_back",
    )(x, blocks)


def gather_rows(values, label=None):
    count = lax.axis_size("fsdp")
    planes = {0: values}
    if count == 4 and label:
        planes[3] = swap(values, "fsdp", 3)
        planes[1] = swap(values, "fsdp", 1)
        planes[2] = swap(planes[3], "fsdp", 1)
    else:
        for away in range(1, count):
            planes[away] = swap(values, "fsdp", away)
    half = count // 2
    return tuple(
        jnp.concatenate([planes[away] for away in group], axis=0)
        for group in (range(half), range(half, count))
    )


def sum_rows(halves):
    count = lax.axis_size("fsdp")
    half = count // 2
    rows = halves[0].shape[0] // half
    parts = [
        halves[away // half][away % half * rows : (away % half + 1) * rows] for away in range(count)
    ]
    if count == 4:
        passed = swap(parts[2].astype(BF), "fsdp", 1).astype(F32)
        one = swap(parts[1].astype(BF), "fsdp", 1).astype(F32)
        third = swap((parts[3] + passed).astype(BF), "fsdp", 3).astype(F32)
        return parts[0] + one + third
    total = parts[0]
    for away in range(1, count):
        total = total + swap(parts[away].astype(BF), "fsdp", away).astype(F32)
    return total


def by_offset(values):
    count, plane = lax.axis_size("fsdp"), lax.axis_index("fsdp")
    rows = values.shape[0] // count
    return jnp.concatenate(
        [
            lax.dynamic_slice(values, ((plane ^ away) * rows, 0), (rows, values.shape[1]))
            for away in range(count)
        ],
        axis=0,
    )


def columns_to_owner(values):
    return lax.all_to_all(values, "fsdp", split_axis=1, concat_axis=0, tiled=True)


def rows_to_owner(values):
    count = lax.axis_size("fsdp")
    rows, columns = values.shape
    out = lax.all_to_all(values, "fsdp", split_axis=0, concat_axis=0, tiled=True)
    return out.reshape(count, rows // count, columns)


def joined(parts):
    return jnp.concatenate([parts[i] for i in range(parts.shape[0])], axis=1)


def sum_over_ctx(part_for):
    pairs = lax.axis_size("ctx") // 2
    sent = jnp.stack([part_for(2 * pair + 1).astype(BF) for pair in range(pairs)])
    got = swap(sent, "ctx", 1)
    sums = [part_for(2 * pair).astype(F32) + got[pair].astype(F32) for pair in range(pairs)]
    total = sums[0]
    for pair in range(1, pairs):
        total = total + swap(sums[pair].astype(BF), "ctx", 2 * pair).astype(F32)
    return total


def ctx_rows_sum(values):
    height = values.shape[0] // lax.axis_size("ctx")
    me = lax.axis_index("ctx")

    def part(offset):
        return lax.dynamic_slice(
            values, ((me ^ offset) * height, 0), (height, values.shape[1])
        )

    return sum_over_ctx(part)


def key_offsets():
    count = lax.axis_size("ctx")
    return list(range(0, count, 2)) + list(range(1, count, 2))


def gather_keys(piece):
    same = [piece] + [swap(piece, "ctx", far) for far in range(2, lax.axis_size("ctx"), 2)]
    mine = jnp.concatenate(same, axis=0)
    other = swap(mine, "ctx", 1)
    return jnp.concatenate([mine, other], axis=0)


def sum_pairs(parts, cosine, sine):
    _, count, width = parts.shape
    pairs = lax.axis_size("ctx") // 2
    parts = parts.reshape(2, 2, pairs, count // (2 * pairs), width)
    got = swap(parts[:, 1], "ctx", 1)
    sums = parts[:, 0].astype(F32) + got.astype(F32)
    far = [swap(sums[:, pair].astype(BF), "ctx", 2 * pair) for pair in range(1, pairs)]
    return pair_turn(sums[:, 0], far, cosine, sine)


def half_mask(shape):
    return lax.broadcasted_iota(jnp.int32, shape, len(shape) - 1) % 128 < HD


def turn(values, cosine, sine):
    lanes = lax.broadcasted_iota(jnp.int32, values.shape, 1) % HD
    turned = jnp.where(
        lanes < HD // 2, pltpu.roll(values, 128 - HD // 2, 1), pltpu.roll(values, HD // 2, 1)
    )
    return values * cosine + turned * sine


def doubled(tile, odd):
    wide = tile.astype(F32)
    other = pltpu.roll(wide, HD, 1)
    return jnp.where(half_mask(tile.shape) == (odd == 0), wide, other).astype(BF)


def split_heads(tile_pair):
    zero = jnp.zeros((), tile_pair.dtype)
    parts = []
    for j in range(2):
        tile = tile_pair[:, j * 128 : (j + 1) * 128]
        mask = half_mask(tile.shape)
        parts += [jnp.where(mask, tile, zero), jnp.where(mask, zero, tile)]
    return jnp.concatenate(parts, axis=0)


def merge_heads(stacked):
    rows = stacked.shape[0] // 4
    tiles = []
    for j in range(2):
        even = stacked[2 * j * rows : (2 * j + 1) * rows]
        odd = stacked[(2 * j + 1) * rows : (2 * j + 2) * rows]
        tiles.append(jnp.where(half_mask(even.shape), even, odd))
    return jnp.concatenate(tiles, axis=1)


def attend_kernel(q_ref, k_ref, v_ref, key_ref, own_ref, rows_ref, attended_ref, log_ref):
    odd = pl.program_id(0) % 2
    rows = q_ref.shape[0]
    queries = split_heads(q_ref[...])
    keys, values = doubled(k_ref[...], odd), doubled(v_ref[...], odd)
    allowed = key_ref[:, :1] <= own_ref[...]
    bias = jnp.where(allowed, 0.0, -1e30).astype(F32)
    bias = jnp.concatenate([bias] * 4, axis=1)
    scores = nt(keys, queries) + bias
    top = jnp.max(scores, axis=0, keepdims=True)
    weights = jnp.exp(scores - top)
    total = jnp.sum(weights, axis=0, keepdims=True)
    summed = tn(weights.astype(BF), values)
    log_ref[0] = top + jnp.log(total)
    attended = merge_heads(summed / jnp.transpose(jnp.broadcast_to(total, (128, 4 * rows))))
    attended_ref[...] = attended
    rows_ref[...] = attended.astype(BF)


def attend(queries, keys_values, key_anchor, own_anchor):
    rows, width = queries.shape
    count, both = keys_values.shape
    tiles = both // 256
    return pl.pallas_call(
        attend_kernel,
        grid=(KV,),
        out_shape=(
            jax.ShapeDtypeStruct((rows, width), BF),
            jax.ShapeDtypeStruct((rows, width), F32),
            jax.ShapeDtypeStruct((KV, 1, 4 * rows), F32),
        ),
        in_specs=[
            pl.BlockSpec((rows, 256), lambda g: (0, g)),
            pl.BlockSpec((count, 128), lambda g: (0, g // 2)),
            pl.BlockSpec((count, 128), lambda g: (0, tiles + g // 2)),
            pl.BlockSpec((count, 128), lambda g: (0, 0)),
            pl.BlockSpec((1, rows), lambda g: (0, 0)),
        ],
        out_specs=(
            pl.BlockSpec((rows, 256), lambda g: (0, g)),
            pl.BlockSpec((rows, 256), lambda g: (0, g)),
            pl.BlockSpec((1, 1, 4 * rows), lambda g: (g, 0, 0)),
        ),
        compiler_params=pltpu.CompilerParams(vmem_limit_bytes=48 << 20),
        cost_estimate=pl.CostEstimate(
            flops=4 * rows * width * count,
            bytes_accessed=2 * count * both,
            transcendentals=rows * H * count,
        ),
        name="attend",
    )(queries, keys_values, keys_values, key_anchor, own_anchor)


def attend_back_kernel(
    chunk, q_ref, grad_ref, attended_ref, k_ref, v_ref, key_ref, own_ref, log_ref, cos_ref, sin_ref,
    dq_ref, pair_ref,
):
    odd = pl.program_id(0) % 2
    rows = q_ref.shape[0]
    count = k_ref.shape[0]
    queries, grads = split_heads(q_ref[...]), split_heads(grad_ref[...])
    product = grads.astype(F32) * split_heads(attended_ref[...])
    delta = jnp.sum(jnp.transpose(product), axis=0, keepdims=True)
    log_total = log_ref[0]
    total = jnp.zeros((4 * rows, 128), F32)
    keep = half_mask((chunk, 128)) == (odd == 0)
    for start in range(0, count, chunk):
        at = slice(start, start + chunk)
        keys, values = doubled(k_ref[at, :], odd), doubled(v_ref[at, :], odd)
        allowed = key_ref[at, :1] <= own_ref[...]
        bias = jnp.where(allowed, 0.0, -1e30).astype(F32)
        bias = jnp.concatenate([bias] * 4, axis=1)
        probs = jnp.exp(nt(keys, queries) + bias - log_total)
        value_grad = nn(probs.astype(BF), grads)
        score_grad = (probs * (nt(values, grads) - delta)).astype(BF)
        key_grad = nn(score_grad, queries)
        total += tn(score_grad, keys)
        for part, value in enumerate((key_grad, value_grad)):
            value = (value + pltpu.roll(value, HD, 1)).astype(BF)
            pair_ref[part, at, :] = jnp.where(keep, value, pair_ref[part, at, :])
    merged = merge_heads(total) * (1.0 / math.sqrt(HD))
    cosine, sine = cos_ref[...], sin_ref[...]
    for j in range(2):
        tile = slice(j * 128, (j + 1) * 128)
        dq_ref[:, tile] = turn(merged[:, tile], cosine, -sine).astype(BF)


def attend_back(queries, grads, attended, keys_values, key_anchor, own_anchor, logs, cosine, sine):
    rows, width = queries.shape
    count, both = keys_values.shape
    tiles = both // 256
    wide = pl.BlockSpec((rows, 256), lambda g: (0, g))
    small = pl.BlockSpec((rows, 128), lambda g: (0, 0))
    return pl.pallas_call(
        lambda *refs: attend_back_kernel(256, *refs),
        grid=(KV,),
        out_shape=(
            jax.ShapeDtypeStruct((rows, width), BF),
            jax.ShapeDtypeStruct((2, count, both // 2), BF),
        ),
        in_specs=[
            wide,
            wide,
            wide,
            pl.BlockSpec((count, 128), lambda g: (0, g // 2)),
            pl.BlockSpec((count, 128), lambda g: (0, tiles + g // 2)),
            pl.BlockSpec((count, 128), lambda g: (0, 0)),
            pl.BlockSpec((1, rows), lambda g: (0, 0)),
            pl.BlockSpec((1, 1, 4 * rows), lambda g: (g, 0, 0)),
            small,
            small,
        ],
        out_specs=(
            wide,
            pl.BlockSpec((2, count, 128), lambda g: (0, 0, g // 2)),
        ),
        compiler_params=pltpu.CompilerParams(vmem_limit_bytes=48 << 20),
        cost_estimate=pl.CostEstimate(
            flops=10 * rows * width * count,
            bytes_accessed=4 * count * both,
            transcendentals=rows * H * count,
        ),
        name="attend_back",
    )(queries, grads, attended, keys_values, keys_values, key_anchor, own_anchor, logs, cosine, sine)


def pair_turn_kernel(own_ref, *refs):
    got, (cos_ref, sin_ref, y_ref) = refs[:-3], refs[-3:]
    total = own_ref[...]
    for ref in got:
        total = total + ref[...].astype(F32)
    cosine, sine = cos_ref[...], sin_ref[...]
    width = total.shape[2]
    for start in range(0, width, 128):
        tile = slice(start, start + 128)
        y_ref[:, tile] = turn(total[0, :, tile], cosine, -sine).astype(BF)
    y_ref[:, width:] = total[1].astype(BF)


def pair_turn(own, got, cosine, sine):
    _, rows, width = own.shape
    return pl.pallas_call(
        pair_turn_kernel,
        out_shape=jax.ShapeDtypeStruct((rows, 2 * width), BF),
        name="pair_turn",
    )(own, *got, cosine, sine)


def ffn_kernel(x_ref, act_ref, w_ref, out_ref, sum_ref):
    step = pl.program_id(0)
    gate_w, up_w = w_ref[0], w_ref[1]
    x = x_ref[...]
    gate, up = nn(x, gate_w), nn(x, up_w)
    act_grad = act_ref[...]
    sig = jax.nn.sigmoid(gate)
    silu = gate * sig
    gate_grad = (act_grad * up * sig * (1.0 + gate * (1.0 - sig))).astype(BF)
    up_grad = (act_grad * silu).astype(BF)
    out_ref[0], out_ref[1], out_ref[2] = gate_grad, up_grad, (silu * up).astype(BF)
    part = nt(gate_grad, gate_w) + nt(up_grad, up_w)

    @pl.when(step == 0)
    def _():
        sum_ref[...] = part

    @pl.when(step > 0)
    def _():
        sum_ref[...] += part


def ffn_middle(rows_in, act_grad, weights):
    rows, width = rows_in.shape
    hidden = weights.shape[2]
    tile = FFN_TILE
    return pl.pallas_call(
        ffn_kernel,
        grid=(hidden // tile,),
        out_shape=(
            jax.ShapeDtypeStruct((3, rows, hidden), BF),
            jax.ShapeDtypeStruct((rows, width), F32),
        ),
        in_specs=[
            pl.BlockSpec((rows, width), lambda j: (0, 0)),
            pl.BlockSpec((rows, tile), lambda j: (0, j)),
            pl.BlockSpec((2, width, tile), lambda j: (0, 0, j)),
        ],
        out_specs=(
            pl.BlockSpec((3, rows, tile), lambda j: (0, 0, j)),
            pl.BlockSpec((rows, width), lambda j: (0, 0)),
        ),
        compiler_params=pltpu.CompilerParams(vmem_limit_bytes=40 << 20),
        cost_estimate=pl.CostEstimate(
            flops=8 * rows * width * hidden,
            bytes_accessed=4 * width * hidden,
            transcendentals=rows * hidden,
        ),
        name="ffn_middle",
    )(rows_in, act_grad, weights)


def products_kernel(in_a, in_b, grad_a, grad_b, right_a, right_b, out_ref):
    def emit(left_a, left_b):
        out_ref[0] = (tn(left_a[...], right_a[0]) + tn(left_b[...], right_b[0])).astype(BF)

    @pl.when(pl.program_id(0) < 2)
    def _():
        emit(in_a, in_b)

    @pl.when(pl.program_id(0) == 2)
    def _():
        emit(grad_a, grad_b)


def ffn_products(rows_in, rows_out, parts):
    rows, width = rows_in[0].shape
    hidden = parts[0].shape[2]
    tile = FFN_TILE
    last = width // tile - 1
    left = pl.BlockSpec((rows, tile), lambda k, i: (0, jnp.where(k < 2, i, last)))
    grad = pl.BlockSpec((rows, tile), lambda k, i: (0, jnp.where(k == 2, i, 0)))
    right = pl.BlockSpec((1, rows, hidden), lambda k, i: (k, 0, 0))
    return pl.pallas_call(
        products_kernel,
        grid=(3, width // tile),
        out_shape=jax.ShapeDtypeStruct((3, width, hidden), BF),
        in_specs=[left, left, grad, grad, right, right],
        out_specs=pl.BlockSpec((1, tile, hidden), lambda k, i: (k, i, 0)),
        compiler_params=pltpu.CompilerParams(vmem_limit_bytes=32 << 20),
        cost_estimate=pl.CostEstimate(
            flops=12 * rows * width * hidden,
            bytes_accessed=6 * width * hidden,
            transcendentals=0,
        ),
        name="ffn_products",
    )(*rows_in, *rows_out, *parts)


def simple_kernel(x_ref, w_ref, y_ref):
    y_ref[...] = nn(x_ref[...], w_ref[0])


def down_back(x, weights):
    rows, width = x.shape
    hidden = weights.shape[2]
    tile = FFN_TILE
    return pl.pallas_call(
        simple_kernel,
        grid=(hidden // tile,),
        out_shape=jax.ShapeDtypeStruct((rows, hidden), F32),
        in_specs=[
            pl.BlockSpec((rows, width), lambda j: (0, 0)),
            pl.BlockSpec((1, width, tile), lambda j: (2, 0, j)),
        ],
        out_specs=pl.BlockSpec((rows, tile), lambda j: (0, j)),
        compiler_params=pltpu.CompilerParams(vmem_limit_bytes=24 << 20),
        cost_estimate=pl.CostEstimate(
            flops=2 * rows * width * hidden,
            bytes_accessed=2 * width * hidden,
            transcendentals=0,
        ),
        name="down_back",
    )(x, weights)


def share_kernel(count, pairs, ids_ref, *refs):
    lefts, rights = refs[:count], refs[count : 2 * count]
    rest = refs[2 * count :]
    step = pl.program_id(0)
    terms, (sent_ref, kept_ref) = rest[:-2], rest[-2:]
    parts = [tn(left[...], right[...]) for left, right in zip(lefts, rights)]
    if terms:
        tall = [jnp.broadcast_to(term[...], (64, term.shape[1])) for term in terms]
        parts.append(jnp.transpose(jnp.concatenate(tall, axis=0)))
    block = jnp.concatenate(parts, axis=1).astype(BF)

    @pl.when(step < pairs)
    def _():
        sent_ref[0] = block

    @pl.when(step >= pairs)
    def _():
        kept_ref[0] = block


def share_products(lefts, rights, terms):
    ctx_count = lax.axis_size("ctx")
    pairs = ctx_count // 2
    rows, width = lefts[0].shape
    height = width // ctx_count
    columns = sum(right.shape[1] for right in rights) + 64 * len(terms)

    def place(i, ids_ref):
        offset = jnp.where(i < pairs, 2 * i + 1, 2 * (i - pairs))
        return (0, ids_ref[0] ^ offset)

    shape = jax.ShapeDtypeStruct((pairs, height, columns), BF)
    return pl.pallas_call(
        lambda *refs: share_kernel(len(lefts), pairs, *refs),
        grid_spec=pltpu.PrefetchScalarGridSpec(
            num_scalar_prefetch=1,
            grid=(ctx_count,),
            in_specs=[pl.BlockSpec((rows, height), place) for _ in lefts]
            + [pl.BlockSpec(right.shape, lambda i, ids_ref: (0, 0)) for right in rights]
            + [pl.BlockSpec((1, height), place) for _ in terms],
            out_specs=(
                pl.BlockSpec(
                    (1, height, columns), lambda i, ids_ref: (jnp.minimum(i, pairs - 1), 0, 0)
                ),
                pl.BlockSpec(
                    (1, height, columns), lambda i, ids_ref: (jnp.maximum(i - pairs, 0), 0, 0)
                ),
            ),
        ),
        out_shape=(shape, shape),
        compiler_params=pltpu.CompilerParams(vmem_limit_bytes=24 << 20),
        cost_estimate=pl.CostEstimate(
            flops=2 * rows * width * columns,
            bytes_accessed=2 * (rows + columns) * width,
            transcendentals=0,
        ),
        name="share_terms" if terms else "share_products",
    )(jnp.stack(ids()), *lefts, *rights, *[term[None] for term in terms])


def share_sum(lefts, rights, terms):
    pairs = lax.axis_size("ctx") // 2
    if (lefts[0].shape[1] // (2 * pairs)) % 128:
        values = [tn(left, right) for left, right in zip(lefts, rights)]
        values += [jnp.broadcast_to(term[:, None], (term.shape[0], 64)) for term in terms]
        return ctx_rows_sum(jnp.concatenate(values, axis=1)).astype(BF)
    sent, kept = share_products(lefts, rights, terms)
    got = swap(sent, "ctx", 1)
    total = kept[0].astype(F32) + got[0].astype(F32)
    for pair in range(1, pairs):
        part = (kept[pair].astype(F32) + got[pair].astype(F32)).astype(BF)
        total = total + swap(part, "ctx", 2 * pair).astype(F32)
    return total.astype(BF)


def layer(
    hidden_in,
    out_grad,
    positions,
    block_order,
    attn_gain,
    ffn_gain,
    qkv_weight,
    out_weight,
    ffn_weight,
):
    ctx_count = lax.axis_size("ctx")
    me, _ = ids()
    rows = hidden_in.shape[1]
    queries_width, kv_width = H * HD, KV * HD
    ffn_parts = ffn_weight.transpose(1, 0, 2)

    frequency = jnp.power(ROPE_BASE, -(jnp.arange(HD // 2, dtype=F32) * 2.0 / HD))
    angles = positions[0].astype(F32)[:, None] * frequency[None, :]
    cosine = jnp.tile(jnp.cos(angles), (1, 4))
    sine = jnp.tile(jnp.concatenate([-jnp.sin(angles), jnp.sin(angles)], axis=1), (1, 2))
    own_anchor = anchors_of(block_order, me, rows)[None]
    key_anchor = jnp.concatenate(
        [anchors_of(block_order, me ^ offset, rows) for offset in key_offsets()]
    )
    key_anchor = jnp.broadcast_to(key_anchor[:, None], (rows * ctx_count, 128))

    inputs = hidden_in[0].astype(F32)
    grad_in = out_grad[0]
    scale_one = norm_scale(inputs)
    normed_one = (inputs * scale_one * attn_gain).astype(BF)

    fast = ctx_count == 8 and (qkv_weight.shape[1] // ctx_count) % 128 == 0
    if fast:
        qkv_pieces, marks = gather_pieces(qkv_weight)
        out_blocks = gather_blocks(out_weight, *marks)
        queries, pair = pieces_forward(normed_one, qkv_weight, qkv_pieces, cosine, sine)
    else:
        out_blocks = gather_blocks(out_weight, normed_one, normed_one)
        qkv_full = whole_of(gather_blocks(qkv_weight, normed_one, normed_one))
        projected = nn(normed_one, qkv_full)
        turned = rotate(
            projected[:, : queries_width + kv_width].reshape(rows, H + KV, HD), positions[0]
        ).reshape(rows, queries_width + kv_width)
        queries = (turned[:, :queries_width] * (1.0 / math.sqrt(HD))).astype(BF)
        pair = jnp.concatenate(
            [turned[:, queries_width:], projected[:, queries_width + kv_width :]], axis=1
        ).astype(BF)
    keys_values = gather_keys(pair)
    rows_out = gather_rows(after(grad_in, pair))
    act_grad = []
    for half in rows_out:
        act_grad.append(down_back(half, ffn_parts))

    attn_rows, attended, logs = attend(queries, keys_values, key_anchor, own_anchor)
    residual, normed_two = out_forward(attn_rows, out_blocks, hidden_in[0], ffn_gain)
    scale_two = norm_scale(residual)
    rows_in = gather_rows(normed_two, "normed")

    attn_share = by_offset(columns_to_owner(after(attn_rows, rows_in[1])))
    middle = []
    for half, act in zip(rows_in, act_grad):
        middle.append(ffn_middle(half, act, ffn_parts))
    parts, partial = [m[0] for m in middle], [m[1] for m in middle]
    sum_grad = sum_rows(partial)
    rows_one = lax.all_gather(after(normed_one, rows_in), "fsdp", tiled=True)
    products = ffn_products(rows_in, rows_out, parts).transpose(1, 0, 2)
    ffn_weight_grad = lax.psum_scatter(products, "ctx", scatter_dimension=0, tiled=True)
    ffn_weight_grad = ffn_weight_grad.astype(F32)
    out_partial = [nt(part[2], ffn_parts[2]) for part in parts]

    unit_two = residual * scale_two
    ffn_gain_term = jnp.sum(sum_grad * unit_two, axis=0)
    scaled_two = ffn_gain * sum_grad
    residual_grad = grad_in.astype(F32) + scale_two * (
        scaled_two - unit_two * jnp.mean(scaled_two * unit_two, axis=-1, keepdims=True)
    )
    residual_bf = residual_grad.astype(BF)
    residual_planes = jnp.concatenate(gather_rows(residual_bf), axis=0)
    attn_grad = out_back(residual_bf, out_blocks)
    query_part, pair_grads = attend_back(
        queries, attn_grad, attended, keys_values, key_anchor, own_anchor, logs, cosine, sine
    )
    query_owned = columns_to_owner(query_part)
    pair_part = sum_pairs(pair_grads, cosine, sine)
    pair_owned = columns_to_owner(pair_part)
    first_sums = share_sum(
        [residual_planes, after(rows_one, pair_part)], [attn_share, query_owned], []
    )
    first_sums = rows_to_owner(first_sums).astype(F32)

    projected_grad = jnp.concatenate([query_part, pair_part], axis=1)
    if fast:
        normed_one_grad = pieces_back(projected_grad, qkv_weight, qkv_pieces)
    else:
        normed_one_grad = nt(projected_grad, qkv_full)
    unit_one = inputs * scale_one
    attn_gain_term = jnp.sum(normed_one_grad * unit_one, axis=0)
    scaled_one = attn_gain * normed_one_grad
    input_grad = residual_grad + scale_one * (
        scaled_one - unit_one * jnp.mean(scaled_one * unit_one, axis=-1, keepdims=True)
    )

    last_sums = share_sum([rows_one], [pair_owned], [attn_gain_term, ffn_gain_term])
    last_sums = rows_to_owner(last_sums).astype(F32)

    out_sum = sum_rows([after(half, pair_part) for half in out_partial])
    output = (residual + out_sum).astype(BF)

    out_columns, pair_columns = attn_share.shape[1], pair_owned.shape[1]
    out_weight_grad = joined(first_sums[:, :, :out_columns])
    qkv_grad = jnp.concatenate(
        [joined(first_sums[:, :, out_columns:]), joined(last_sums[:, :, :pair_columns])], axis=1
    )
    gain_grads = jnp.sum(last_sums[:, :, pair_columns:], axis=0)
    return (
        output[None],
        input_grad[None],
        qkv_grad,
        out_weight_grad,
        ffn_weight_grad,
        gain_grads[:, 0],
        gain_grads[:, 64],
    )


def solution(mesh):
    step = sharded(mesh)
    return step


def sharded(mesh):
    return jax.shard_map(
        layer,
        mesh=mesh,
        in_specs=(
            P("fsdp", "ctx", None),
            P("fsdp", "ctx", None),
            P("fsdp", "ctx"),
            P(),
            P(),
            P(),
            P("fsdp", None),
            P("fsdp", None),
            P(None, None, "fsdp"),
        ),
        out_specs=(
            P("fsdp", "ctx", None),
            P("fsdp", "ctx", None),
            P(("ctx", "fsdp"), None),
            P(("ctx", "fsdp"), None),
            P("ctx", None, "fsdp"),
            P(("ctx", "fsdp")),
            P(("ctx", "fsdp")),
        ),
        check_vma=False,
    )
```

profile of v0, /device:TPU:0, one launch (start us, length us, event | category | flops | bytes accessed | tf_op | source)
XLA Modules:
  0.0 626.5 jit_solution(1771020760305620644)
XLA Ops:
  12.3 8.5 %collective-permute-done.refs_3_ = bf16[512,384]{1,0:T(8,128)(2,1)} collective-permute-done((bf16[512,384]{1,0:T(8,128)(2,1)S(1)}, bf16[512,384]{1,0:T(8,128)(2,1)}, u32[]{:S(2)}, u32[]{:S(2)}) %collective-permute-start) | collective-permute-done | bytes 393248 | tf_op jit(solution)/shard_map/ppermute | solution.py:42
  24.7 11.2 %collective-permute-done.10.refs_13_ = bf16[512,384]{1,0:T(8,128)(2,1)} collective-permute-done((bf16[512,384]{1,0:T(8,128)(2,1)S(1)}, bf16[512,384]{1,0:T(8,128)(2,1)}, u32[]{:S(2)}, u32[]{:S(2)}) %collective-permute-start.10) | collective-permute-done | bytes 393248 | tf_op jit(solution)/shard_map/ppermute | solution.py:42
  35.9 21.1 %collective-permute-start.20 = (bf16[512,384]{1,0:T(8,128)(2,1)}, bf16[512,384]{1,0:T(8,128)(2,1)S(1)}, u32[]{:S(2)}, u32[]{:S(2)}) collective-permute-start(bf16[512,384]{1,0:T(8,128)(2,1)} %collective-permute-done.10.refs_13_), channel_id=1, source_target_pairs={{0,1},{1,0},{2,3},{3,2},{4,5},{5,4},{6,7},{7,6},{8,9},{9,8},{10,11... | collective-permute-start | bytes 1179656 | tf_op jit(solution)/shard_map/ppermute | solution.py:42
  57.0 7.4 %collective-permute-done.20.refs_23_ = bf16[512,384]{1,0:T(8,128)(2,1)S(1)} collective-permute-done((bf16[512,384]{1,0:T(8,128)(2,1)}, bf16[512,384]{1,0:T(8,128)(2,1)S(1)}, u32[]{:S(2)}, u32[]{:S(2)}) %collective-permute-start.20) | collective-permute-done | bytes 393248 | tf_op jit(solution)/shard_map/ppermute | solution.py:42
  146.8 14.6 %pieces_forward.1 = (bf16[128,2048]{1,0:T(8,128)(2,1)S(1)}, bf16[128,1024]{1,0:T(8,128)(2,1)S(1)}) custom-call(s32[2]{0:T(128)S(1)} %pad_add_fusion.refs_0_, bf16[128,2048]{1,0:T(8,128)(2,1)S(1)} %fusion.6.refs_1_, bf16[512,3072]{1,0:T(8,128)(2,1)S(1)} %copy-done.5, bf16[512,384]{1,0:T(8,128)(2,1)} %collective-permute-done.refs_3_, ...), custom_call_target="tpu_custom_call" | custom-call | flops 1610612736 | bytes 12582912 | tf_op jit(solution)/shard_map/pieces_forward/pallas_call | solution.py:155
  181.5 13.6 %attend.1 = (bf16[128,2048]{1,0:T(8,128)(2,1)S(1)}, f32[128,2048]{1,0:T(8,128)S(1)}, f32[8,1,512]{2,1,0:T(1,128)S(1)}) custom-call(bf16[128,2048]{1,0:T(8,128)(2,1)S(1)} %get-tuple-element.32.q_ref.refs_0_, bf16[1024,1024]{1,0:T(8,128)(2,1)S(1)} %constant_dynamic-update-slice_fusion.k_ref.v_ref.refs_3_.refs_4_, ...), custom_call_target="tpu_custom_call" | custom-call | flops 1073741824 | bytes 2097152 | tf_op jit(solution)/shard_map/attend/pallas_call | solution.py:454
  218.1 8.9 %collective-permute-done.37 = bf16[128,2048]{1,0:T(8,128)(2,1)S(1)} collective-permute-done((bf16[128,2048]{1,0:T(8,128)(2,1)S(1)}, bf16[128,2048]{1,0:T(8,128)(2,1)S(1)}, u32[]{:S(2)}, u32[]{:S(2)}) %collective-permute-start.37) | collective-permute-done | bytes 524320 | tf_op jit(solution)/shard_map/ppermute | solution.py:42
  227.0 22.5 %collective-permute-start.38 = (bf16[128,2048]{1,0:T(8,128)(2,1)S(1)}, bf16[128,2048]{1,0:T(8,128)(2,1)S(1)}, u32[]{:S(2)}, u32[]{:S(2)}) collective-permute-start(bf16[128,2048]{1,0:T(8,128)(2,1)S(1)} %collective-permute-done.37), channel_id=1, source_target_pairs={{0,1},{1,0},{2,3},{3,2},{4,5},{5,4},{6,7},{7,6},{8,9},{9,8},{10,11... | collective-permute-start | bytes 1572872 | tf_op jit(solution)/shard_map/ppermute | solution.py:42
  251.8 9.9 %collective-permute-done.38 = bf16[128,2048]{1,0:T(8,128)(2,1)S(1)} collective-permute-done((bf16[128,2048]{1,0:T(8,128)(2,1)S(1)}, bf16[128,2048]{1,0:T(8,128)(2,1)S(1)}, u32[]{:S(2)}, u32[]{:S(2)}) %collective-permute-start.38) | collective-permute-done | bytes 524320 | tf_op jit(solution)/shard_map/ppermute | solution.py:42
  262.9 8.7 %copy-done.2 = bf16[2048,3,2048]{2,0,1:T(8,128)(2,1)S(1)} copy-done((bf16[2048,3,2048]{2,0,1:T(8,128)(2,1)S(1)}, bf16[2048,3,2048]{2,0,1:T(8,128)(2,1)}, u32[]{:S(2)}) %copy-start.2) | copy-done | bytes 25165848
  280.7 13.2 %ffn_middle.2 = (bf16[3,256,2048]{2,1,0:T(8,128)(2,1)S(1)}, f32[256,2048]{1,0:T(8,128)S(1)}) custom-call(bf16[256,2048]{1,0:T(8,128)(2,1)S(1)} %copy-done.82, f32[256,2048]{1,0:T(8,128)S(1)} %down_back.2.act_ref, bf16[3,2048,2048]{2,1,0:T(8,128)(2,1)} %bitcast.148), custom_call_target="tpu_custom_call" | custom-call | flops 8589934592 | bytes 16777216 | tf_op jit(solution)/shard_map/ffn_middle/pallas_call | solution.py:605
  295.3 14.3 %ffn_middle.3 = (bf16[3,256,2048]{2,1,0:T(8,128)(2,1)S(1)}, f32[256,2048]{1,0:T(8,128)S(1)}) custom-call(bf16[256,2048]{1,0:T(8,128)(2,1)S(1)} %copy-done.84, f32[256,2048]{1,0:T(8,128)S(1)} %down_back.3.act_ref, bf16[3,2048,2048]{2,1,0:T(8,128)(2,1)} %bitcast.149), custom_call_target="tpu_custom_call" | custom-call | flops 8589934592 | bytes 16777216 | tf_op jit(solution)/shard_map/ffn_middle/pallas_call | solution.py:605
  309.6 18.0 %ffn_products.1 = bf16[3,2048,2048]{2,1,0:T(8,128)(2,1)} custom-call(bf16[256,2048]{1,0:T(8,128)(2,1)S(1)} %copy-done.82, bf16[256,2048]{1,0:T(8,128)(2,1)S(1)} %copy-done.84, bf16[256,2048]{1,0:T(8,128)(2,1)S(1)} %copy-done.26, bf16[256,2048]{1,0:T(8,128)(2,1)S(1)} %copy-done.29, bf16[3,256,2048]{2,1,0:T(8,128)(2,1)S(1)} %get-tuple-element.40.right_a, ...), custom_call_target="tpu_custom_call" | custom-call | flops 12884901888 | bytes 25165824 | tf_op jit(solution)/shard_map/ffn_products/pallas_call | solution.py:652
  332.7 11.2 %collective-permute-done.41 = bf16[128,2048]{1,0:T(8,128)(2,1)S(1)} collective-permute-done((bf16[128,2048]{1,0:T(8,128)(2,1)S(1)}, bf16[128,2048]{1,0:T(8,128)(2,1)S(1)}, u32[]{:S(2)}, u32[]{:S(2)}) %collective-permute-start.41) | collective-permute-done | bytes 524320 | tf_op jit(solution)/shard_map/ppermute | solution.py:42
  345.3 10.5 %collective-permute-done.36 = bf16[128,2048]{1,0:T(8,128)(2,1)S(1)} collective-permute-done((bf16[128,2048]{1,0:T(8,128)(2,1)S(1)}, bf16[128,2048]{1,0:T(8,128)(2,1)S(1)}, u32[]{:S(2)}, u32[]{:S(2)}) %collective-permute-start.36) | collective-permute-done | bytes 524320 | tf_op jit(solution)/shard_map/ppermute | solution.py:42
  355.8 9.2 %collective-permute-done.42 = bf16[128,2048]{1,0:T(8,128)(2,1)S(1)} collective-permute-done((bf16[128,2048]{1,0:T(8,128)(2,1)S(1)}, bf16[128,2048]{1,0:T(8,128)(2,1)S(1)}, u32[]{:S(2)}, u32[]{:S(2)}) %collective-permute-start.42) | collective-permute-done | bytes 524320 | tf_op jit(solution)/shard_map/ppermute | solution.py:42
  374.6 19.8 %attend_back.1 = (bf16[128,2048]{1,0:T(8,128)(2,1)S(1)}, bf16[2,1024,512]{2,1,0:T(8,128)(2,1)S(1)}) custom-call(bf16[128,2048]{1,0:T(8,128)(2,1)S(1)} %copy-done.92, bf16[128,2048]{1,0:T(8,128)(2,1)S(1)} %out_back.1.refs_1_, f32[128,2048]{1,0:T(8,128)S(1)} %copy-done.98, bf16[1024,1024]{1,0:T(8,128)(2,1)} %copy-done.86, bf16[1024,1024]{1,0:T(8,128)(2,1)} %copy-done.86, ...), custom_call_target="tpu_custom_call" | custom-call | flops 2684354560 | bytes 4194304 | tf_op jit(solution)/shard_map/attend_back/pallas_call | solution.py:524
  402.4 15.1 %all-to-all-done = bf16[128,4,512]{2,0,1:T(8,128)(2,1)} async-done(((bf16[128,4,512]{2,0,1:T(8,128)(2,1)}), bf16[128,4,512]{2,0,1:T(8,128)(2,1)}, u32[]{:S(2)}, u32[]{:S(2)}) %all-to-all-start) | async-done | bytes 524320 | tf_op jit(solution)/shard_map/all_to_all | solution.py:334
  438.2 33.8 %collective-permute-done.51 = bf16[128,2048]{1,0:T(8,128)(2,1)} collective-permute-done((bf16[128,2048]{1,0:T(8,128)(2,1)S(1)}, bf16[128,2048]{1,0:T(8,128)(2,1)}, u32[]{:S(2)}, u32[]{:S(2)}) %collective-permute-start.51) | collective-permute-done | bytes 524320 | tf_op jit(solution)/shard_map/ppermute | solution.py:42
  481.4 6.6 %share_products.1 = (bf16[4,256,1024]{2,1,0:T(8,128)(2,1)}, bf16[4,256,1024]{2,1,0:T(8,128)(2,1)S(1)}) custom-call(s32[2]{0:T(128)S(1)} %copy-done.88, bf16[512,2048]{1,0:T(8,128)(2,1)S(1)} %copy-done.33, bf16[512,2048]{1,0:T(8,128)(2,1)S(1)} %copy-done.89, bf16[512,512]{1,0:T(8,128)(2,1)S(1)} %copy-done.80, bf16[512,512]{1,0:T(8,128)(2,1)S(1)} %bitcast.160), custom_call_target="tpu_custom_call" | custom-call | flops 2147483648 | bytes 6291456 | tf_op jit(solution)/shard_map/share_products/pallas_call | solution.py:727
  489.3 7.5 %fusion.1 = f32[256,2048]{1,0:T(8,128)} fusion(bf16[3,2048,2048]{2,1,0:T(8,128)(2,1)} %bitcast.150, bf16[3,256,2048]{2,1,0:T(8,128)(2,1)} %copy-done.96), kind=kOutput, calls=%fused_computation.2 | convolution fusion | flops 2147483648 | bytes 11534336 | tf_op jit(solution)/shard_map/dot_general | solution.py:25
  523.1 12.7 %pieces_back.1 = f32[128,2048]{1,0:T(8,128)S(1)} custom-call(s32[2]{0:T(128)S(1)} %copy-done.88, bf16[128,3072]{1,0:T(8,128)(2,1)S(1)} %pad_maximum_fusion.2.refs_1_, bf16[512,3072]{1,0:T(8,128)(2,1)S(1)} %copy-done.6, bf16[512,384]{1,0:T(8,128)(2,1)} %collective-permute-done.refs_3_, bf16[512,384]{1,0:T(8,128)(2,1)} %collective-permute-done.1.refs_4_, ...), custom_call_target="tpu_custom_call" | custom-call | flops 1610612736 | bytes 12582912 | tf_op jit(solution)/shard_map/pieces_back/pallas_call | solution.py:155
  578.2 10.2 %collective-permute-done.55 = bf16[256,1024]{1,0:T(8,128)(2,1)} collective-permute-done((bf16[256,1024]{1,0:T(8,128)(2,1)}, bf16[256,1024]{1,0:T(8,128)(2,1)}, u32[]{:S(2)}, u32[]{:S(2)}) %collective-permute-start.55) | collective-permute-done | bytes 524320 | tf_op jit(solution)/shard_map/ppermute | solution.py:42
  591.3 6.5 %all-to-all-done.4 = bf16[4,64,384]{2,1,0:T(8,128)(2,1)S(1)} async-done(((bf16[4,64,384]{2,1,0:T(8,128)(2,1)}), bf16[4,64,384]{2,1,0:T(8,128)(2,1)S(1)}, u32[]{:S(2)}, u32[]{:S(2)}) %all-to-all-start.4) | async-done | bytes 196640 | tf_op jit(solution)/shard_map/all_to_all | solution.py:340
  (451 shorter events, 296.0 us)
Async XLA Ops:
  7.2 75.7 %all-gather.8.cloned.1.call-start = ((), (), s32[]{:S(2)}) async-start(), calls=%async_computation.8 | async-start | bytes 1310720 | tf_op jit(solution)/shard_map/all_gather | solution.py:195
  20.8 178.8 %all-gather.10.cloned.1.call-start = ((), (), s32[]{:S(2)}) async-start(), calls=%async_computation.9 | async-start | bytes 9437184 | tf_op jit(solution)/shard_map/all_gather | solution.py:196
  35.9 28.5 %collective-permute-start.20 = (bf16[512,384]{1,0:T(8,128)(2,1)}, bf16[512,384]{1,0:T(8,128)(2,1)S(1)}, u32[]{:S(2)}, u32[]{:S(2)}) collective-permute-start(bf16[512,384]{1,0:T(8,128)(2,1)} %collective-permute-done.10.refs_13_), channel_id=1, source_target_pairs={{0,1},{1,0},{2,3},{3,2},{4,5},{5,4},{6,7},{7,6},{8,9},{9,8},{10,11... | collective-permute-start | bytes 1179656 | tf_op jit(solution)/shard_map/ppermute | solution.py:42
  82.9 395.2 %all-gather.6.cloned.1.call-start = ((), (), s32[]{:S(2)}) async-start(), calls=%async_computation.6 | async-start | bytes 2621440 | tf_op jit(solution)/shard_map/all_gather | solution.py:835
  86.2 31.2 %collective-permute-start.12 = (bf16[512,384]{1,0:T(8,128)(2,1)}, bf16[512,384]{1,0:T(8,128)(2,1)S(1)}, u32[]{:S(2)}, u32[]{:S(2)}) collective-permute-start(bf16[512,384]{1,0:T(8,128)(2,1)} %collective-permute-done.10.refs_13_), channel_id=1, source_target_pairs={{0,8},{4,12},{8,0},{12,4},{16,24},{20,28},{24,16},{28,20},{1,9},{5... | collective-permute-start | bytes 1179656 | tf_op jit(solution)/shard_map/ppermute | solution.py:42
  93.3 27.5 %collective-permute-start.11 = (bf16[512,384]{1,0:T(8,128)(2,1)}, bf16[512,384]{1,0:T(8,128)(2,1)}, u32[]{:S(2)}, u32[]{:S(2)}) collective-permute-start(bf16[512,384]{1,0:T(8,128)(2,1)} %collective-permute-done.10.refs_13_), channel_id=1, source_target_pairs={{0,4},{4,0},{8,12},{12,8},{16,20},{20,16},{24,28},{28,24},{1,5},{5... | collective-permute-start | bytes 1179656 | tf_op jit(solution)/shard_map/ppermute | solution.py:42
  176.9 39.0 %collective-permute-start.39 = (bf16[128,2048]{1,0:T(8,128)(2,1)}, bf16[128,2048]{1,0:T(8,128)(2,1)}, u32[]{:S(2)}, u32[]{:S(2)}) collective-permute-start(bf16[128,2048]{1,0:T(8,128)(2,1)} %bitcast.10), channel_id=1, source_target_pairs={{0,2},{1,3},{2,0},{3,1},{4,6},{5,7},{6,4},{7,5},{8,10},{9,11},{10,... | collective-permute-start | bytes 1572872 | tf_op jit(solution)/shard_map/ppermute | solution.py:42
  180.4 36.5 %collective-permute-start.40 = (bf16[128,2048]{1,0:T(8,128)(2,1)}, bf16[128,2048]{1,0:T(8,128)(2,1)}, u32[]{:S(2)}, u32[]{:S(2)}) collective-permute-start(bf16[128,2048]{1,0:T(8,128)(2,1)} %bitcast.10), channel_id=1, source_target_pairs={{0,3},{1,2},{2,1},{3,0},{4,7},{5,6},{6,5},{7,4},{8,11},{9,10},{10,... | collective-permute-start | bytes 1572872 | tf_op jit(solution)/shard_map/ppermute | solution.py:42
  180.4 69.0 %collective-permute-start.35 = (bf16[128,2048]{1,0:T(8,128)(2,1)}, bf16[128,2048]{1,0:T(8,128)(2,1)}, u32[]{:S(2)}, u32[]{:S(2)}) collective-permute-start(bf16[128,2048]{1,0:T(8,128)(2,1)} %bitcast.10), channel_id=1, source_target_pairs={{0,1},{1,0},{2,3},{3,2},{4,5},{5,4},{6,7},{7,6},{8,9},{9,8},{10,11... | collective-permute-start | bytes 1572872 | tf_op jit(solution)/shard_map/ppermute | solution.py:42
  216.9 33.7 %collective-permute-start.34 = (bf16[128,2048]{1,0:T(8,128)(2,1)S(1)}, bf16[128,2048]{1,0:T(8,128)(2,1)S(1)}, u32[]{:S(2)}, u32[]{:S(2)}) collective-permute-start(bf16[128,2048]{1,0:T(8,128)(2,1)S(1)} %get-tuple-element.38), channel_id=1, source_target_pairs={{0,1},{1,0},{2,3},{3,2},{4,5},{5,4},{6,7},{7,6},{8,9},{9,8},{10,11... | collective-permute-start | bytes 1572872 | tf_op jit(solution)/shard_map/ppermute | solution.py:42
  227.0 34.7 %collective-permute-start.38 = (bf16[128,2048]{1,0:T(8,128)(2,1)S(1)}, bf16[128,2048]{1,0:T(8,128)(2,1)S(1)}, u32[]{:S(2)}, u32[]{:S(2)}) collective-permute-start(bf16[128,2048]{1,0:T(8,128)(2,1)S(1)} %collective-permute-done.37), channel_id=1, source_target_pairs={{0,1},{1,0},{2,3},{3,2},{4,5},{5,4},{6,7},{7,6},{8,9},{9,8},{10,11... | collective-permute-start | bytes 1572872 | tf_op jit(solution)/shard_map/ppermute | solution.py:42
  262.8 351.3 %reduce-scatter.2.cloned.1.call-start = ((), (), s32[]{:S(2)}) async-start(), calls=%async_computation.7 | async-start | bytes 28311552 | tf_op jit(solution)/shard_map/reduce_scatter | solution.py:837
  396.7 31.7 %collective-permute-start.43 = (bf16[2,4,128,512]{3,2,0,1:T(8,128)(2,1)}, bf16[2,4,128,512]{3,2,0,1:T(8,128)(2,1)}, u32[]{:S(2)}, u32[]{:S(2)}) collective-permute-start(bf16[2,4,128,512]{3,2,0,1:T(8,128)(2,1)} %bitcast.144), channel_id=1, source_target_pairs={{0,4},{4,0},{8,12},{12,8},{16,20},{20,16},{24,28},{28,24},{1,5},{5... | collective-permute-start | bytes 3145736 | tf_op jit(solution)/shard_map/ppermute | solution.py:42
  421.1 50.9 %collective-permute-start.51 = (bf16[128,2048]{1,0:T(8,128)(2,1)S(1)}, bf16[128,2048]{1,0:T(8,128)(2,1)}, u32[]{:S(2)}, u32[]{:S(2)}) collective-permute-start(bf16[128,2048]{1,0:T(8,128)(2,1)S(1)} %get-tuple-element.71.x_ref), channel_id=1, source_target_pairs={{0,2},{1,3},{2,0},{3,1},{4,6},{5,7},{6,4},{7,5},{8,10},{9,11},{10,... | collective-permute-start | bytes 1572872 | tf_op jit(solution)/shard_map/ppermute | solution.py:42
  421.1 50.9 %collective-permute-start.50 = (bf16[128,2048]{1,0:T(8,128)(2,1)S(1)}, bf16[128,2048]{1,0:T(8,128)(2,1)}, u32[]{:S(2)}, u32[]{:S(2)}) collective-permute-start(bf16[128,2048]{1,0:T(8,128)(2,1)S(1)} %get-tuple-element.71.x_ref), channel_id=1, source_target_pairs={{0,1},{1,0},{2,3},{3,2},{4,5},{5,4},{6,7},{7,6},{8,9},{9,8},{10,11... | collective-permute-start | bytes 1572872 | tf_op jit(solution)/shard_map/ppermute | solution.py:42
  424.9 53.2 %all-to-all-start.1 = ((bf16[128,4,512]{2,0,1:T(8,128)(2,1)}), bf16[128,4,512]{2,0,1:T(8,128)(2,1)S(1)}, u32[]{:S(2)}, u32[]{:S(2)}) async-start(bf16[128,4,512]{2,0,1:T(8,128)(2,1)} %bitcast.166), calls=%async_computation.1 | async-start | bytes 1048576 | tf_op jit(solution)/shard_map/all_to_all | solution.py:334
  430.4 45.4 %collective-permute-start.44 = (bf16[2,128,512]{2,1,0:T(8,128)(2,1)S(1)}, bf16[2,128,512]{2,1,0:T(8,128)(2,1)}, u32[]{:S(2)}, u32[]{:S(2)}) collective-permute-start(bf16[2,128,512]{2,1,0:T(8,128)(2,1)S(1)} %get-tuple-element.89), channel_id=1, source_target_pairs={{0,8},{4,12},{8,0},{12,4},{16,24},{20,28},{24,16},{28,20},{1,9},{5... | collective-permute-start | bytes 786440 | tf_op jit(solution)/shard_map/ppermute | solution.py:42
  431.9 43.9 %collective-permute-start.45 = (bf16[2,128,512]{2,1,0:T(8,128)(2,1)S(1)}, bf16[2,128,512]{2,1,0:T(8,128)(2,1)}, u32[]{:S(2)}, u32[]{:S(2)}) collective-permute-start(bf16[2,128,512]{2,1,0:T(8,128)(2,1)S(1)} %get-tuple-element.88), channel_id=1, source_target_pairs={{0,16},{4,20},{8,24},{12,28},{16,0},{20,4},{24,8},{28,12},{1,17},{... | collective-permute-start | bytes 786440 | tf_op jit(solution)/shard_map/ppermute | solution.py:42
  436.5 39.4 %collective-permute-start.46 = (bf16[2,128,512]{2,1,0:T(8,128)(2,1)S(1)}, bf16[2,128,512]{2,1,0:T(8,128)(2,1)}, u32[]{:S(2)}, u32[]{:S(2)}) collective-permute-start(bf16[2,128,512]{2,1,0:T(8,128)(2,1)S(1)} %get-tuple-element.87), channel_id=1, source_target_pairs={{0,24},{4,28},{8,16},{12,20},{16,8},{20,12},{24,0},{28,4},{1,25},{... | collective-permute-start | bytes 786440 | tf_op jit(solution)/shard_map/ppermute | solution.py:42
  489.3 68.0 %collective-permute-start.53 = (bf16[4,256,1024]{2,1,0:T(8,128)(2,1)}, bf16[4,256,1024]{2,1,0:T(8,128)(2,1)}, u32[]{:S(2)}, u32[]{:S(2)}) collective-permute-start(bf16[4,256,1024]{2,1,0:T(8,128)(2,1)} %get-tuple-element.54), channel_id=1, source_target_pairs={{0,4},{4,0},{8,12},{12,8},{16,20},{20,16},{24,28},{28,24},{1,5},{5... | collective-permute-start | bytes 6291464 | tf_op jit(solution)/shard_map/ppermute | solution.py:42
  497.6 39.7 %all-to-all-start.3 = ((bf16[128,4,256]{2,0,1:T(8,128)(2,1)}), bf16[128,4,256]{2,0,1:T(8,128)(2,1)}, u32[]{:S(2)}, u32[]{:S(2)}) async-start(bf16[128,4,256]{2,0,1:T(8,128)(2,1)} %bitcast.147), calls=%async_computation.3 | async-start | bytes 524288 | tf_op jit(solution)/shard_map/all_to_all | solution.py:334
  567.4 37.1 %collective-permute-start.47 = (bf16[128,2048]{1,0:T(8,128)(2,1)}, bf16[128,2048]{1,0:T(8,128)(2,1)}, u32[]{:S(2)}, u32[]{:S(2)}) collective-permute-start(bf16[128,2048]{1,0:T(8,128)(2,1)} %slice.358), channel_id=1, source_target_pairs={{0,1},{1,0},{2,3},{3,2},{4,5},{5,4},{6,7},{7,6},{8,9},{9,8},{10,11... | collective-permute-start | bytes 1572872 | tf_op jit(solution)/shard_map/ppermute | solution.py:42
  569.1 35.4 %collective-permute-start.49 = (bf16[128,2048]{1,0:T(8,128)(2,1)}, bf16[128,2048]{1,0:T(8,128)(2,1)}, u32[]{:S(2)}, u32[]{:S(2)}) collective-permute-start(bf16[128,2048]{1,0:T(8,128)(2,1)} %add_convert_fusion.4), channel_id=1, source_target_pairs={{0,3},{1,2},{2,1},{3,0},{4,7},{5,6},{6,5},{7,4},{8,11},{9,10},{10,... | collective-permute-start | bytes 1572872 | tf_op jit(solution)/shard_map/ppermute | solution.py:42
  572.3 25.6 %all-to-all-start.4 = ((bf16[4,64,384]{2,1,0:T(8,128)(2,1)}), bf16[4,64,384]{2,1,0:T(8,128)(2,1)S(1)}, u32[]{:S(2)}, u32[]{:S(2)}) async-start(bf16[4,64,384]{2,1,0:T(8,128)(2,1)} %bitcast.46), calls=%async_computation.4 | async-start | bytes 393216 | tf_op jit(solution)/shard_map/all_to_all | solution.py:340
  (155 other events, 2394.4 us)
Sparse Core Ops, SparseCore 0:
  20.9 36.5 all-gather.7
  83.0 69.4 all-gather.9
  262.9 44.1 all-gather.5
  327.7 159.6 reduce-scatter.1
where the time goes:
time: 632 us; the launch traced here: 626 us
  waiting for transfers between devices  217 us (34%)
  Pallas kernels  134 us (21%)
  starting transfers between devices  125 us (20%)
  local copies, waits for them, and re-layouts  88 us (14%)
  other arithmetic  33.5 us (5%)
  between operations  15.3 us (2%)
  matrix products  13.6 us (2%)
    ppermute x61, waiting for transfers between devices, swap(): return lax.ppermute(value, axis, [(i, i ^ offset) for i in range(count)])  189 us
    ppermute x61, starting transfers between devices, swap(): return lax.ppermute(value, axis, [(i, i ^ offset) for i in range(count)])  105 us
    unnamed x234, local copies, waits for them, and re-layouts  67.2 us
    pallas_call x2, Pallas kernels, ffn_middle(): pl.pallas_call(ffn_kernel, grid=(hidden // tile,), out_shape=(jax.ShapeDt...  27.5 us
    pallas_call x2, Pallas kernels, pieces_call(): pl.pallas_call(lambda *refs: pieces_kernel(places, rows_in, share, back,...  27.3 us
    pallas_call x1, Pallas kernels, attend_back(): pl.pallas_call(lambda *refs: attend_back_kernel(256, *refs), grid=(KV,),...  19.8 us
    pallas_call x1, Pallas kernels, ffn_products(): pl.pallas_call(products_kernel, grid=(3, width // tile), out_shape=jax.Sh...  18 us
    all_to_all x3, waiting for transfers between devices, columns_to_owner(): lax.all_to_all(values, 'fsdp', split_axis=1, concat_axis=0, tiled=True)  15.1 us
  transfers between devices with their start and end apart: 70, of which 37 were waited for; matrix products, arithmetic and copies ran while one was open for 10% of the time, Pallas kernels for 21%

commit v1 on v0

--- a/solution.py
+++ b/solution.py
@@ -76,7 +76,7 @@
     return lax.axis_index("ctx"), lax.axis_index("fsdp")
 
 
-def gather_pieces(weight):
+def gather_pieces(weight, early, ones):
     rows, columns = weight.shape
     share = columns // lax.axis_size("ctx")
     half = rows // 2
@@ -84,7 +84,8 @@
     planes = {}
     planes[3] = swap(mine, "fsdp", 3)
     planes[1] = swap(mine, "fsdp", 1)
-    planes[2] = swap(planes[3], "fsdp", 1)
+    planes[2] = swap(after(planes[3], early), "fsdp", 1)
+    rows_one = gather_rows(ones)
     pieces = []
     for away in (1, 3, 2):
         first = planes[away]
@@ -94,114 +95,121 @@
         for offset, start, part in parts:
             pieces.append((away, offset, start, part))
             pieces.append((away, offset + 1, start, swap(part, "ctx", 1)))
-    return pieces, (planes[1], (pieces[-4][3], pieces[-2][3]))
-
-
-def pieces_kernel(places, rows_in, share, back, ids_ref, x_ref, own_ref, *refs):
+    return pieces, (planes[1], (pieces[-4][3], pieces[-2][3])), rows_one
+
+
+def pieces_kernel(places, rows_in, share, ids_ref, x_ref, own_ref, *refs):
     count = len(places)
     piece_refs, refs = refs[:count], refs[count:]
-    if back:
-        y_ref, refs = refs[0], refs[1:]
-    else:
-        (cos_ref, sin_ref, q_ref, pair_ref, y_ref), refs = refs[:5], refs[5:]
-    own_buf, bufs, sems = refs[0], refs[1:-1], refs[-1]
+    cos_ref, sin_ref, q_ref, pair_ref, full_ref, y_ref, buf, in_sems, out_sems = refs
     me, plane = ids_ref[0], ids_ref[1]
-    copies = [pltpu.make_async_copy(own_ref, own_buf, sems.at[count])]
-    for i in range(count):
-        copies.append(pltpu.make_async_copy(piece_refs[i], bufs[i], sems.at[i]))
-    for copy in copies:
-        copy.start()
-
-    def tokens(start, size):
-        return x_ref[:, pl.ds(pl.multiple_of(start, 128), size)]
-
-    copies[0].wait()
-    if back:
-        y_ref[...] = jnp.zeros_like(y_ref)
-        y_ref[:, pl.ds(pl.multiple_of(plane * rows_in, 128), rows_in)] = nt(
-            x_ref[...], own_buf[...]
+
+    def block(away):
+        return pl.ds(pl.multiple_of((plane ^ away) * rows_in, 128), rows_in)
+
+    own_copy = pltpu.make_async_copy(own_ref, buf.at[block(0)], in_sems.at[count])
+    own_copy.start()
+    copies = []
+    for i, (away, offset, start, height) in enumerate(places):
+        at = pl.ds(pl.multiple_of((plane ^ away) * rows_in + start, 128), height)
+        columns = pl.ds(pl.multiple_of((me ^ offset) * share, 128), share)
+        copies.append(pltpu.make_async_copy(piece_refs[i], buf.at[at, columns], in_sems.at[i]))
+        copies[-1].start()
+    outs = []
+    order = [0] + list(dict.fromkeys(away for away, _, _, _ in places))
+    for away in order:
+        if away:
+            for copy, place in zip(copies, places):
+                if place[0] == away:
+                    copy.wait()
+        else:
+            own_copy.wait()
+        outs.append(
+            pltpu.make_async_copy(buf.at[block(away)], full_ref.at[block(away)], out_sems.at[away])
         )
-    else:
-        y_ref[...] = nn(tokens(plane * rows_in, rows_in), own_buf[...])
-    for i, (away, offset, start, height) in enumerate(places):
-        copies[i + 1].wait()
-        inner = (plane ^ away) * rows_in + start
-        outer = (me ^ offset) * share
-        if back:
-            at = pl.ds(pl.multiple_of(inner, 128), height)
-            y_ref[:, at] += nt(tokens(outer, share), bufs[i][...])
+        outs[-1].start()
+        part = nn(x_ref[:, block(away)], buf[block(away)])
+        y_ref[...] = part if away == 0 else y_ref[...] + part
+    cosine, sine = cos_ref[...], sin_ref[...]
+    queries, keys = H * HD, KV * HD
+    for start in range(0, queries + keys, 128):
+        tile = turn(y_ref[:, start : start + 128], cosine, sine)
+        if start < queries:
+            q_ref[:, start : start + 128] = (tile * (1.0 / math.sqrt(HD))).astype(BF)
         else:
-            at = pl.ds(pl.multiple_of(outer, 128), share)
-            y_ref[:, at] += nn(tokens(inner, height), bufs[i][...])
-    if not back:
-        cosine, sine = cos_ref[...], sin_ref[...]
-        queries, keys = H * HD, KV * HD
-        for start in range(0, queries + keys, 128):
-            tile = turn(y_ref[:, start : start + 128], cosine, sine)
-            if start < queries:
-                q_ref[:, start : start + 128] = (tile * (1.0 / math.sqrt(HD))).astype(BF)
-            else:
-                pair_ref[:, start - queries : start - queries + 128] = tile.astype(BF)
-        pair_ref[:, keys:] = y_ref[:, queries + keys :].astype(BF)
-
-
-def pieces_call(x, own, pieces, extra, out_shape, scratch, back):
+            pair_ref[:, start - queries : start - queries + 128] = tile.astype(BF)
+    pair_ref[:, keys:] = y_ref[:, queries + keys :].astype(BF)
+    for copy in outs:
+        copy.wait()
+
+
+def pieces_forward(x, own, pieces, cosine, sine):
     me, plane = ids()
     rows_in, columns = own.shape
+    rows, width = x.shape
     share = columns // lax.axis_size("ctx")
     places = tuple((away, offset, start, part.shape[0]) for away, offset, start, part in pieces)
     arrays = [part for _, _, _, part in pieces]
-    hbm, vmem = pl.BlockSpec(memory_space=pl.ANY), pl.BlockSpec(memory_space=pltpu.VMEM)
+    hbm, vmem = pl.BlockSpec(memory_space=pltpu.HBM), pl.BlockSpec(memory_space=pltpu.VMEM)
     return pl.pallas_call(
-        lambda *refs: pieces_kernel(places, rows_in, share, back, *refs),
-        out_shape=out_shape,
+        lambda *refs: pieces_kernel(places, rows_in, share, *refs),
+        out_shape=(
+            jax.ShapeDtypeStruct((rows, H * HD), BF),
+            jax.ShapeDtypeStruct((rows, 2 * KV * HD), BF),
+            jax.ShapeDtypeStruct((width, columns), BF),
+        ),
         in_specs=[pl.BlockSpec(memory_space=pltpu.SMEM), vmem, hbm]
         + [hbm] * len(arrays)
-        + [vmem] * len(extra),
-        out_specs=jax.tree.map(lambda _: vmem, out_shape),
-        scratch_shapes=scratch
-        + [pltpu.VMEM(own.shape, own.dtype)]
-        + [pltpu.VMEM(part.shape, part.dtype) for part in arrays]
-        + [pltpu.SemaphoreType.DMA((len(arrays) + 1,))],
+        + [vmem, vmem],
+        out_specs=(vmem, vmem, hbm),
+        scratch_shapes=[
+            pltpu.VMEM((rows, columns), F32),
+            pltpu.VMEM((width, columns), BF),
+            pltpu.SemaphoreType.DMA((len(arrays) + 1,)),
+            pltpu.SemaphoreType.DMA((width // rows_in,)),
+        ],
         compiler_params=pltpu.CompilerParams(vmem_limit_bytes=32 << 20),
         cost_estimate=pl.CostEstimate(
-            flops=2 * x.shape[0] * rows_in * lax.axis_size("fsdp") * columns,
-            bytes_accessed=2 * rows_in * lax.axis_size("fsdp") * columns,
-            transcendentals=0,
-        ),
-        name="pieces_back" if back else "pieces_forward",
-    )(jnp.stack([me, plane]), x, own, *arrays, *extra)
-
-
-def pieces_forward(x, own, pieces, cosine, sine):
-    rows, columns = x.shape[0], own.shape[1]
-    out_shape = (
-        jax.ShapeDtypeStruct((rows, H * HD), BF),
-        jax.ShapeDtypeStruct((rows, 2 * KV * HD), BF),
-    )
-    scratch = [pltpu.VMEM((rows, columns), F32)]
-    return pieces_call(x, own, pieces, [cosine, sine], out_shape, scratch, False)
-
-
-def pieces_back(x, own, pieces):
-    out_shape = jax.ShapeDtypeStruct((x.shape[0], own.shape[0] * lax.axis_size("fsdp")), F32)
-    return pieces_call(x, own, pieces, [], out_shape, [], True)
+            flops=2 * rows * width * columns, bytes_accessed=4 * width * columns, transcendentals=0
+        ),
+        name="pieces_forward",
+    )(jnp.stack([me, plane]), x, own, *arrays, cosine, sine)
 
 
 def gather_blocks(weight, before_fsdp, before_ctx):
     rows, columns = weight.shape
+    me, plane = ids()
     share = columns // lax.axis_size("ctx")
-    mine = lax.dynamic_slice(weight, (0, lax.axis_index("ctx") * share), (rows, share))
+    mine = lax.dynamic_slice(weight, (0, me * share), (rows, share))
     planes = lax.all_gather(after(mine, before_fsdp), "fsdp")
-    return lax.all_gather(after(planes, before_ctx), "ctx")
-
-
-def whole_of(blocks):
-    ctx_count, fsdp_count, rows, share = blocks.shape
-    return blocks.transpose(1, 2, 0, 3).reshape(fsdp_count * rows, ctx_count * share)
-
-
-def out_forward_kernel(x_ref, w_ref, hidden_ref, gain_ref, residual_ref, normed_ref):
+    others = jnp.stack(
+        [
+            lax.dynamic_index_in_dim(planes, plane ^ away, 0, keepdims=False)
+            for away in range(1, planes.shape[0])
+        ]
+    )
+    return lax.all_gather(after(others, before_ctx), "ctx")
+
+
+def whole_of(own, blocks):
+    ctx_count, others, rows, share = blocks.shape
+    plane = lax.axis_index("fsdp")
+    columns = ctx_count * share
+    full = jnp.zeros(((others + 1) * rows, columns), own.dtype)
+    full = lax.dynamic_update_slice(full, own, (plane * rows, 0))
+    for away in range(1, others + 1):
+        part = blocks[:, away - 1].transpose(1, 0, 2).reshape(rows, columns)
+        full = lax.dynamic_update_slice(full, part, ((plane ^ away) * rows, 0))
+    return full
+
+
+def in_hbm(value):
+    return pltpu.with_memory_space_constraint(value, pltpu.HBM)
+
+
+def out_forward_kernel(
+    ids_ref, x_ref, own_ref, w_ref, hidden_ref, gain_ref, residual_ref, normed_ref
+):
     step = pl.program_id(0)
 
     @pl.when(step == 0)
@@ -209,8 +217,10 @@
         residual_ref[...] = hidden_ref[...].astype(F32)
 
     rows = w_ref.shape[2]
-    for plane in range(w_ref.shape[1]):
-        residual_ref[:, plane * rows : (plane + 1) * rows] += nt(x_ref[...], w_ref[0, plane])
+    plane = ids_ref[1]
+    for away in range(w_ref.shape[1] + 1):
+        at = pl.ds(pl.multiple_of((plane ^ away) * rows, 128), rows)
+        residual_ref[:, at] += nt(x_ref[...], w_ref[0, away - 1] if away else own_ref[...])
 
     @pl.when(step == pl.num_programs(0) - 1)
     def _():
@@ -218,28 +228,34 @@
         normed_ref[...] = (residual * norm_scale(residual) * gain_ref[...]).astype(BF)
 
 
-def out_forward(attn_rows, blocks, hidden, gain):
+def out_specs_of(blocks):
+    _, others, height, share = blocks.shape
+    return [
+        pl.BlockSpec((height, share), lambda c, ids_ref: (0, c)),
+        pl.BlockSpec((1, others, height, share), lambda c, ids_ref: (c, 0, 0, 0)),
+    ]
+
+
+def out_forward(attn_rows, own, blocks, hidden, gain):
     rows, width = hidden.shape
-    ctx_count, fsdp_count, height, share = blocks.shape
+    ctx_count, _, _, share = blocks.shape
     if share % 128:
-        residual = hidden.astype(F32) + nt(attn_rows, whole_of(blocks))
+        residual = hidden.astype(F32) + nt(attn_rows, whole_of(own, blocks))
         return residual, (residual * norm_scale(residual) * gain).astype(BF)
+    whole = pl.BlockSpec((rows, width), lambda c, ids_ref: (0, 0))
     return pl.pallas_call(
         out_forward_kernel,
-        grid=(ctx_count,),
+        grid_spec=pltpu.PrefetchScalarGridSpec(
+            num_scalar_prefetch=1,
+            grid=(ctx_count,),
+            in_specs=[pl.BlockSpec((rows, share), lambda c, ids_ref: (0, c))]
+            + out_specs_of(blocks)
+            + [whole, pl.BlockSpec((1, width), lambda c, ids_ref: (0, 0))],
+            out_specs=(whole, whole),
+        ),
         out_shape=(
             jax.ShapeDtypeStruct((rows, width), F32),
             jax.ShapeDtypeStruct((rows, width), BF),
-        ),
-        in_specs=[
-            pl.BlockSpec((rows, share), lambda c: (0, c)),
-            pl.BlockSpec((1, fsdp_count, height, share), lambda c: (c, 0, 0, 0)),
-            pl.BlockSpec((rows, width), lambda c: (0, 0)),
-            pl.BlockSpec((1, width), lambda c: (0, 0)),
-        ],
-        out_specs=(
-            pl.BlockSpec((rows, width), lambda c: (0, 0)),
-            pl.BlockSpec((rows, width), lambda c: (0, 0)),
         ),
         compiler_params=pltpu.CompilerParams(vmem_limit_bytes=24 << 20),
         cost_estimate=pl.CostEstimate(
@@ -248,31 +264,35 @@
             transcendentals=0,
         ),
         name="out_forward",
-    )(attn_rows, blocks, hidden, gain[None])
-
-
-def out_back_kernel(x_ref, w_ref, y_ref):
+    )(jnp.stack(ids()), attn_rows, in_hbm(own), in_hbm(blocks), hidden, gain[None])
+
+
+def out_back_kernel(ids_ref, x_ref, own_ref, w_ref, y_ref):
     rows = w_ref.shape[2]
-    total = nn(x_ref[:, :rows], w_ref[0, 0])
-    for plane in range(1, w_ref.shape[1]):
-        total += nn(x_ref[:, plane * rows : (plane + 1) * rows], w_ref[0, plane])
+    plane = ids_ref[1]
+    total = None
+    for away in range(w_ref.shape[1] + 1):
+        at = pl.ds(pl.multiple_of((plane ^ away) * rows, 128), rows)
+        part = nn(x_ref[:, at], w_ref[0, away - 1] if away else own_ref[...])
+        total = part if total is None else total + part
     y_ref[...] = total.astype(BF)
 
 
-def out_back(x, blocks):
+def out_back(x, own, blocks):
     rows, width = x.shape
-    ctx_count, fsdp_count, height, share = blocks.shape
+    ctx_count, _, _, share = blocks.shape
     if share % 128:
-        return nn(x, whole_of(blocks)).astype(BF)
+        return nn(x, whole_of(own, blocks)).astype(BF)
     return pl.pallas_call(
         out_back_kernel,
-        grid=(ctx_count,),
+        grid_spec=pltpu.PrefetchScalarGridSpec(
+            num_scalar_prefetch=1,
+            grid=(ctx_count,),
+            in_specs=[pl.BlockSpec((rows, width), lambda c, ids_ref: (0, 0))]
+            + out_specs_of(blocks),
+            out_specs=pl.BlockSpec((rows, share), lambda c, ids_ref: (0, c)),
+        ),
         out_shape=jax.ShapeDtypeStruct((rows, ctx_count * share), BF),
-        in_specs=[
-            pl.BlockSpec((rows, width), lambda c: (0, 0)),
-            pl.BlockSpec((1, fsdp_count, height, share), lambda c: (c, 0, 0, 0)),
-        ],
-        out_specs=pl.BlockSpec((rows, share), lambda c: (0, c)),
         compiler_params=pltpu.CompilerParams(vmem_limit_bytes=24 << 20),
         cost_estimate=pl.CostEstimate(
             flops=2 * rows * width * ctx_count * share,
@@ -280,7 +300,7 @@
             transcendentals=0,
         ),
         name="out_back",
-    )(x, blocks)
+    )(jnp.stack(ids()), x, in_hbm(own), in_hbm(blocks))
 
 
 def gather_rows(values, label=None):
@@ -293,11 +313,17 @@
     else:
         for away in range(1, count):
             planes[away] = swap(values, "fsdp", away)
-    half = count // 2
-    return tuple(
-        jnp.concatenate([planes[away] for away in group], axis=0)
-        for group in (range(half), range(half, count))
-    )
+    return halves_of([planes[away] for away in range(count)])
+
+
+def fetch_rows(values):
+    count = lax.axis_size("fsdp")
+    return [values] + [swap(values, "fsdp", away) for away in range(1, count)]
+
+
+def halves_of(planes):
+    half = len(planes) // 2
+    return (jnp.concatenate(planes[:half], axis=0), jnp.concatenate(planes[half:], axis=0))
 
 
 def sum_rows(halves):
@@ -692,6 +718,34 @@
     )(x, weights)
 
 
+def down_kernel(a_ref, b_ref, w_ref, y_ref):
+    rows = a_ref.shape[1]
+    for half, ref in enumerate((a_ref, b_ref)):
+        y_ref[half * rows : (half + 1) * rows] = nt(ref[0], w_ref[0])
+
+
+def down_forward(parts, weights):
+    _, rows, hidden = parts[0].shape
+    width = weights.shape[1]
+    tile = FFN_TILE
+    left = pl.BlockSpec((1, rows, hidden), lambda j: (2, 0, 0))
+    total = pl.pallas_call(
+        down_kernel,
+        grid=(width // tile,),
+        out_shape=jax.ShapeDtypeStruct((2 * rows, width), F32),
+        in_specs=[left, left, pl.BlockSpec((1, tile, hidden), lambda j: (2, j, 0))],
+        out_specs=pl.BlockSpec((2 * rows, tile), lambda j: (0, j)),
+        compiler_params=pltpu.CompilerParams(vmem_limit_bytes=24 << 20),
+        cost_estimate=pl.CostEstimate(
+            flops=4 * rows * width * hidden,
+            bytes_accessed=2 * width * hidden,
+            transcendentals=0,
+        ),
+        name="down_forward",
+    )(*parts, weights)
+    return total[:rows], total[rows:]
+
+
 def share_kernel(count, pairs, ids_ref, *refs):
     lefts, rights = refs[:count], refs[count : 2 * count]
     rest = refs[2 * count :]
@@ -782,7 +836,7 @@
     me, _ = ids()
     rows = hidden_in.shape[1]
     queries_width, kv_width = H * HD, KV * HD
-    ffn_parts = ffn_weight.transpose(1, 0, 2)
+    ffn_parts = in_hbm(ffn_weight.transpose(1, 0, 2))
 
     frequency = jnp.power(ROPE_BASE, -(jnp.arange(HD // 2, dtype=F32) * 2.0 / HD))
     angles = positions[0].astype(F32)[:, None] * frequency[None, :]
@@ -801,12 +855,16 @@
 
     fast = ctx_count == 8 and (qkv_weight.shape[1] // ctx_count) % 128 == 0
     if fast:
-        qkv_pieces, marks = gather_pieces(qkv_weight)
+        early = (cosine, sine, own_anchor, key_anchor)
+        qkv_pieces, marks, rows_one = gather_pieces(qkv_weight, early, normed_one)
         out_blocks = gather_blocks(out_weight, *marks)
-        queries, pair = pieces_forward(normed_one, qkv_weight, qkv_pieces, cosine, sine)
+        queries, pair, qkv_full = pieces_forward(
+            normed_one, qkv_weight, qkv_pieces, cosine, sine
+        )
     else:
         out_blocks = gather_blocks(out_weight, normed_one, normed_one)
-        qkv_full = whole_of(gather_blocks(qkv_weight, normed_one, normed_one))
+        rows_one = gather_rows(normed_one)
+        qkv_full = whole_of(qkv_weight, gather_blocks(qkv_weight, normed_one, normed_one))
         projected = nn(normed_one, qkv_full)
         turned = rotate(
             projected[:, : queries_width + kv_width].reshape(rows, H + KV, HD), positions[0]
@@ -815,16 +873,19 @@
         pair = jnp.concatenate(
             [turned[:, queries_width:], projected[:, queries_width + kv_width :]], axis=1
         ).astype(BF)
+    rows_one = by_offset(jnp.concatenate(rows_one, axis=0))
     keys_values = gather_keys(pair)
-    rows_out = gather_rows(after(grad_in, pair))
+    rows_out = fetch_rows(after(grad_in, pair))
+    attn_rows, attended, logs = attend(queries, keys_values, key_anchor, own_anchor)
+    residual, normed_two = out_forward(
+        attn_rows, out_weight, out_blocks, hidden_in[0], ffn_gain
+    )
+    scale_two = norm_scale(residual)
+    rows_in = gather_rows(normed_two, "normed")
+    rows_out = halves_of(after(rows_out, normed_two))
     act_grad = []
     for half in rows_out:
         act_grad.append(down_back(half, ffn_parts))
-
-    attn_rows, attended, logs = attend(queries, keys_values, key_anchor, own_anchor)
-    residual, normed_two = out_forward(attn_rows, out_blocks, hidden_in[0], ffn_gain)
-    scale_two = norm_scale(residual)
-    rows_in = gather_rows(normed_two, "normed")
 
     attn_share = by_offset(columns_to_owner(after(attn_rows, rows_in[1])))
     middle = []
@@ -832,11 +893,10 @@
         middle.append(ffn_middle(half, act, ffn_parts))
     parts, partial = [m[0] for m in middle], [m[1] for m in middle]
     sum_grad = sum_rows(partial)
-    rows_one = lax.all_gather(after(normed_one, rows_in), "fsdp", tiled=True)
     products = ffn_products(rows_in, rows_out, parts).transpose(1, 0, 2)
     ffn_weight_grad = lax.psum_scatter(products, "ctx", scatter_dimension=0, tiled=True)
     ffn_weight_grad = ffn_weight_grad.astype(F32)
-    out_partial = [nt(part[2], ffn_parts[2]) for part in parts]
+    out_partial = down_forward(parts, ffn_parts)
 
     unit_two = residual * scale_two
     ffn_gain_term = jnp.sum(sum_grad * unit_two, axis=0)
@@ -845,24 +905,22 @@
         scaled_two - unit_two * jnp.mean(scaled_two * unit_two, axis=-1, keepdims=True)
     )
     residual_bf = residual_grad.astype(BF)
-    residual_planes = jnp.concatenate(gather_rows(residual_bf), axis=0)
-    attn_grad = out_back(residual_bf, out_blocks)
+    residual_planes = fetch_rows(residual_bf)
+    attn_grad = out_back(residual_bf, out_weight, out_blocks)
     query_part, pair_grads = attend_back(
         queries, attn_grad, attended, keys_values, key_anchor, own_anchor, logs, cosine, sine
     )
     query_owned = columns_to_owner(query_part)
     pair_part = sum_pairs(pair_grads, cosine, sine)
     pair_owned = columns_to_owner(pair_part)
+    residual_planes = jnp.concatenate(after(residual_planes, pair_part), axis=0)
     first_sums = share_sum(
         [residual_planes, after(rows_one, pair_part)], [attn_share, query_owned], []
     )
     first_sums = rows_to_owner(first_sums).astype(F32)
 
     projected_grad = jnp.concatenate([query_part, pair_part], axis=1)
-    if fast:
-        normed_one_grad = pieces_back(projected_grad, qkv_weight, qkv_pieces)
-    else:
-        normed_one_grad = nt(projected_grad, qkv_full)
+    normed_one_grad = nt(projected_grad, qkv_full)
     unit_one = inputs * scale_one
     attn_gain_term = jnp.sum(normed_one_grad * unit_one, axis=0)
     scaled_one = attn_gain * normed_one_grad

time: 632 us -> 584 us (0.924)
  starting transfers between devices: 125 us -> 90 us
  local copies, waits for them, and re-layouts: 88 us -> 66.9 us
  waiting for transfers between devices: 217 us -> 229 us
    ppermute x61 -> x64, starting transfers between devices: 105 us -> 59.2 us  [swap(): return lax.ppermute(value, axis, [(i, i ^ offset) for i in range(count)])]
    unnamed x234 -> x170, local copies, waits for them, and re-layouts: 67.2 us -> 42.4 us
    all_to_all x3, waiting for transfers between devices: 15.1 us -> 26.3 us  [columns_to_owner(): lax.all_to_all(values, 'fsdp', split_axis=1, concat_axis=0, tiled=True)]
    all_to_all x3, starting transfers between devices: 12.5 us -> 23.5 us  [columns_to_owner(): lax.all_to_all(values, 'fsdp', split_axis=1, concat_axis=0, tiled=True)]
    dot_general x2 -> x1, matrix products: 13.6 us -> 9.88 us  [mm(): return lax.dot_general(a, b, (dims, ((), ())), preferred_element_type=F32)]
    ppermute x61 -> x64, waiting for transfers between devices: 189 us -> 191 us  [swap(): return lax.ppermute(value, axis, [(i, i ^ offset) for i in range(count)])]
  transfers between devices with their start and end apart: 70 -> 72, of which waited for: 37 -> 31; matrix products, arithmetic and copies ran while one was open for 10% -> 12% of each run, Pallas kernels for 21% -> 17%
where the time goes in v1:
time: 584 us; the launch traced here: 581 us
  waiting for transfers between devices  229 us (39%)
  Pallas kernels  133 us (23%)
  starting transfers between devices  90 us (15%)
  local copies, waits for them, and re-layouts  66.9 us (11%)
  other arithmetic  37.7 us (6%)
  between operations  14.9 us (3%)
  matrix products  9.88 us (2%)
    ppermute x64, waiting for transfers between devices, swap(): return lax.ppermute(value, axis, [(i, i ^ offset) for i in range(count)])  191 us
    ppermute x64, starting transfers between devices, swap(): return lax.ppermute(value, axis, [(i, i ^ offset) for i in range(count)])  59.2 us
    unnamed x170, local copies, waits for them, and re-layouts  42.4 us
    pallas_call x2, Pallas kernels, ffn_middle(): pl.pallas_call(ffn_kernel, grid=(hidden // tile,), out_shape=(jax.ShapeDt...  27.4 us
    all_to_all x3, waiting for transfers between devices, columns_to_owner(): lax.all_to_all(values, 'fsdp', split_axis=1, concat_axis=0, tiled=True)  26.3 us
    all_to_all x3, starting transfers between devices, columns_to_owner(): lax.all_to_all(values, 'fsdp', split_axis=1, concat_axis=0, tiled=True)  23.5 us
    pallas_call x1, Pallas kernels, attend_back(): pl.pallas_call(lambda *refs: attend_back_kernel(256, *refs), grid=(KV,),...  19.6 us
    pallas_call x1, Pallas kernels, ffn_products(): pl.pallas_call(products_kernel, grid=(3, width // tile), out_shape=jax.Sh...  17.9 us
  transfers between devices with their start and end apart: 72, of which 31 were waited for; matrix products, arithmetic and copies ran while one was open for 12% of the time, Pallas kernels for 17%

profile of v1, /device:TPU:0, one launch (start us, length us, event | category | flops | bytes accessed | tf_op | source)
XLA Modules:
  0.0 581.3 jit_solution(15033504178796778085)
XLA Ops:
  16.8 14.3 %collective-permute-done.refs_3_ = bf16[512,384]{1,0:T(8,128)(2,1)} collective-permute-done((bf16[512,384]{1,0:T(8,128)(2,1)S(1)}, bf16[512,384]{1,0:T(8,128)(2,1)}, u32[]{:S(2)}, u32[]{:S(2)}) %collective-permute-start) | collective-permute-done | bytes 393248 | tf_op jit(solution)/shard_map/ppermute | solution.py:42
  34.0 18.2 %collective-permute-done.20.refs_23_ = bf16[512,384]{1,0:T(8,128)(2,1)} collective-permute-done((bf16[512,384]{1,0:T(8,128)(2,1)S(1)}, bf16[512,384]{1,0:T(8,128)(2,1)}, u32[]{:S(2)}, u32[]{:S(2)}) %collective-permute-start.20) | collective-permute-done | bytes 393248 | tf_op jit(solution)/shard_map/ppermute | solution.py:42
  55.3 7.1 %collective-permute-done.24.refs_27_ = bf16[512,384]{1,0:T(8,128)(2,1)S(1)} collective-permute-done((bf16[512,384]{1,0:T(8,128)(2,1)}, bf16[512,384]{1,0:T(8,128)(2,1)S(1)}, u32[]{:S(2)}, u32[]{:S(2)}) %collective-permute-start.24) | collective-permute-done | bytes 393248 | tf_op jit(solution)/shard_map/ppermute | solution.py:42
  76.1 10.5 %collective-permute-done.14.refs_17_ = bf16[512,384]{1,0:T(8,128)(2,1)S(1)} collective-permute-done((bf16[512,384]{1,0:T(8,128)(2,1)S(1)}, bf16[512,384]{1,0:T(8,128)(2,1)S(1)}, u32[]{:S(2)}, u32[]{:S(2)}) %collective-permute-start.14) | collective-permute-done | bytes 393248 | tf_op jit(solution)/shard_map/ppermute | solution.py:42
  90.4 7.8 %collective-permute-done.4.refs_7_ = bf16[512,384]{1,0:T(8,128)(2,1)S(1)} collective-permute-done((bf16[512,384]{1,0:T(8,128)(2,1)}, bf16[512,384]{1,0:T(8,128)(2,1)S(1)}, u32[]{:S(2)}, u32[]{:S(2)}) %collective-permute-start.4) | collective-permute-done | bytes 393248 | tf_op jit(solution)/shard_map/ppermute | solution.py:42
  142.1 7.1 %pieces_forward.1 = (bf16[128,2048]{1,0:T(8,128)(2,1)S(1)}, bf16[128,1024]{1,0:T(8,128)(2,1)S(1)}, bf16[2048,3072]{1,0:T(8,128)(2,1)}) custom-call(s32[2]{0:T(128)S(1)} %pad_add_fusion.refs_0_.ids_ref, bf16[128,2048]{1,0:T(8,128)(2,1)S(1)} %fusion.4.refs_1_, bf16[512,3072]{1,0:T(8,128)(2,1)S(1)} %copy-done.2, bf16[512,384]{1,0:T(8,128)(2,1)} %collective-permute-done.refs_3_, ...), custom_call_target="tpu_custom_call" | custom-call | flops 1610612736 | bytes 25165824 | tf_op jit(solution)/shard_map/pieces_forward/pallas_call | solution.py:154
  169.9 13.6 %attend.1 = (bf16[128,2048]{1,0:T(8,128)(2,1)S(1)}, f32[128,2048]{1,0:T(8,128)S(1)}, f32[8,1,512]{2,1,0:T(1,128)S(1)}) custom-call(bf16[128,2048]{1,0:T(8,128)(2,1)S(1)} %get-tuple-element.42.q_ref.refs_0_, bf16[1024,1024]{1,0:T(8,128)(2,1)S(1)} %constant_dynamic-update-slice_fusion.1.k_ref.v_ref.refs_3_.refs_4_, ...), custom_call_target="tpu_custom_call" | custom-call | flops 1073741824 | bytes 2097152 | tf_op jit(solution)/shard_map/attend/pallas_call | solution.py:480
  185.8 8.5 %out_forward.1 = (f32[128,2048]{1,0:T(8,128)S(1)}, bf16[128,2048]{1,0:T(8,128)(2,1)S(1)}) custom-call(s32[2]{0:T(128)S(1)} %pad_add_fusion.refs_0_.ids_ref, bf16[128,2048]{1,0:T(8,128)(2,1)S(1)} %get-tuple-element.70.x_ref, bf16[512,2048]{1,0:T(8,128)(2,1)} %own_ref.3, bf16[8,3,512,256]{3,2,1,0:T(8,128)(2,1)} %bitcast.154, bf16[128,2048]{1,0:T(8,128)(2,1)S(1)} %bitcast.139, ...), custom_call_target="tpu_custom_call" | custom-call | flops 1073741824 | bytes 8388608 | tf_op jit(solution)/shard_map/out_forward/pallas_call | solution.py:246
  194.9 26.2 %collective-permute-done.36 = bf16[128,2048]{1,0:T(8,128)(2,1)} collective-permute-done((bf16[128,2048]{1,0:T(8,128)(2,1)S(1)}, bf16[128,2048]{1,0:T(8,128)(2,1)}, u32[]{:S(2)}, u32[]{:S(2)}) %collective-permute-start.36) | collective-permute-done | bytes 524320 | tf_op jit(solution)/shard_map/ppermute | solution.py:42
  235.8 13.1 %ffn_middle.2 = (bf16[3,256,2048]{2,1,0:T(8,128)(2,1)S(1)}, f32[256,2048]{1,0:T(8,128)S(1)}) custom-call(bf16[256,2048]{1,0:T(8,128)(2,1)S(1)} %constant_dynamic-update-slice_fusion.6.x_ref.in_a, f32[256,2048]{1,0:T(8,128)S(1)} %down_back.2.act_ref, bf16[3,2048,2048]{2,1,0:T(8,128)(2,1)} %bitcast.150), custom_call_target="tpu_custom_call" | custom-call | flops 8589934592 | bytes 16777216 | tf_op jit(solution)/shard_map/ffn_middle/pallas_call | solution.py:631
  250.4 14.3 %ffn_middle.3 = (bf16[3,256,2048]{2,1,0:T(8,128)(2,1)S(1)}, f32[256,2048]{1,0:T(8,128)S(1)}) custom-call(bf16[256,2048]{1,0:T(8,128)(2,1)S(1)} %constant_dynamic-update-slice_fusion.10.x_ref.in_b, f32[256,2048]{1,0:T(8,128)S(1)} %down_back.3.act_ref, bf16[3,2048,2048]{2,1,0:T(8,128)(2,1)} %bitcast.151), custom_call_target="tpu_custom_call" | custom-call | flops 8589934592 | bytes 16777216 | tf_op jit(solution)/shard_map/ffn_middle/pallas_call | solution.py:631
  264.7 17.9 %ffn_products.1 = bf16[3,2048,2048]{2,1,0:T(8,128)(2,1)} custom-call(bf16[256,2048]{1,0:T(8,128)(2,1)S(1)} %constant_dynamic-update-slice_fusion.6.x_ref.in_a, bf16[256,2048]{1,0:T(8,128)(2,1)S(1)} %constant_dynamic-update-slice_fusion.10.x_ref.in_b, bf16[256,2048]{1,0:T(8,128)(2,1)S(1)} %constant_dynamic-update-slice_fusion.8.x_ref.grad_a, ...), custom_call_target="tpu_custom_call" | custom-call | flops 12884901888 | bytes 25165824 | tf_op jit(solution)/shard_map/ffn_products/pallas_call | solution.py:678
  287.9 11.0 %collective-permute-done.41 = bf16[128,2048]{1,0:T(8,128)(2,1)S(1)} collective-permute-done((bf16[128,2048]{1,0:T(8,128)(2,1)S(1)}, bf16[128,2048]{1,0:T(8,128)(2,1)S(1)}, u32[]{:S(2)}, u32[]{:S(2)}) %collective-permute-start.41) | collective-permute-done | bytes 524320 | tf_op jit(solution)/shard_map/ppermute | solution.py:42
  304.5 27.1 %collective-permute-done.40 = bf16[128,2048]{1,0:T(8,128)(2,1)S(1)} collective-permute-done((bf16[128,2048]{1,0:T(8,128)(2,1)S(1)}, bf16[128,2048]{1,0:T(8,128)(2,1)S(1)}, u32[]{:S(2)}, u32[]{:S(2)}) %collective-permute-start.40) | collective-permute-done | bytes 524320 | tf_op jit(solution)/shard_map/ppermute | solution.py:42
  333.6 7.7 %out_back.1.refs_1_ = bf16[128,2048]{1,0:T(8,128)(2,1)S(1)} custom-call(s32[2]{0:T(128)S(1)} %pad_add_fusion.refs_0_.ids_ref, bf16[128,2048]{1,0:T(8,128)(2,1)S(1)} %get-tuple-element.65.x_ref, bf16[512,2048]{1,0:T(8,128)(2,1)} %own_ref.3, bf16[8,3,512,256]{3,2,1,0:T(8,128)(2,1)} %bitcast.155), custom_call_target="tpu_custom_call" | custom-call | flops 1073741824 | bytes 8388608 | tf_op jit(solution)/shard_map/out_back/pallas_call | solution.py:286
  341.4 19.6 %attend_back.1 = (bf16[128,2048]{1,0:T(8,128)(2,1)S(1)}, bf16[2,1024,512]{2,1,0:T(8,128)(2,1)S(1)}) custom-call(bf16[128,2048]{1,0:T(8,128)(2,1)S(1)} %copy-done.60, bf16[128,2048]{1,0:T(8,128)(2,1)S(1)} %out_back.1.refs_1_, f32[128,2048]{1,0:T(8,128)S(1)} %copy-done.62, bf16[1024,1024]{1,0:T(8,128)(2,1)} %copy-done.58, bf16[1024,1024]{1,0:T(8,128)(2,1)} %copy-done.58, ...), custom_call_target="tpu_custom_call" | custom-call | flops 2684354560 | bytes 4194304 | tf_op jit(solution)/shard_map/attend_back/pallas_call | solution.py:550
  370.0 16.3 %all-to-all-start = ((bf16[128,4,512]{2,0,1:T(8,128)(2,1)}), bf16[128,4,512]{2,0,1:T(8,128)(2,1)S(1)}, u32[]{:S(2)}, u32[]{:S(2)}) async-start(bf16[128,4,512]{2,0,1:T(8,128)(2,1)} %bitcast.163), calls=%async_computation | async-start | bytes 1048576 | tf_op jit(solution)/shard_map/all_to_all | solution.py:360
  400.2 24.5 %all-to-all-done = bf16[128,4,512]{2,0,1:T(8,128)(2,1)S(1)} async-done(((bf16[128,4,512]{2,0,1:T(8,128)(2,1)}), bf16[128,4,512]{2,0,1:T(8,128)(2,1)S(1)}, u32[]{:S(2)}, u32[]{:S(2)}) %all-to-all-start) | async-done | bytes 524320 | tf_op jit(solution)/shard_map/all_to_all | solution.py:360
  437.5 9.0 %collective-permute-done.45.refs_1_ = bf16[2,128,512]{2,1,0:T(8,128)(2,1)S(1)} collective-permute-done((bf16[2,128,512]{2,1,0:T(8,128)(2,1)S(1)}, bf16[2,128,512]{2,1,0:T(8,128)(2,1)S(1)}, u32[]{:S(2)}, u32[]{:S(2)}) %collective-permute-start.45) | collective-permute-done | bytes 262176 | tf_op jit(solution)/shard_map/ppermute | solution.py:42
  463.8 6.6 %share_products.1 = (bf16[4,256,1024]{2,1,0:T(8,128)(2,1)}, bf16[4,256,1024]{2,1,0:T(8,128)(2,1)S(1)}) custom-call(s32[2]{0:T(128)S(1)} %pad_add_fusion.refs_0_.ids_ref, bf16[512,2048]{1,0:T(8,128)(2,1)S(1)} %copy-done.13, bf16[512,2048]{1,0:T(8,128)(2,1)S(1)} %copy-done.11, bf16[512,512]{1,0:T(8,128)(2,1)S(1)} %copy-done.26, bf16[512,512]{1,0:T(8,128)(2,1)S(1)} %bitcast.143), custom_call_target="tpu_custom_call" | custom-call | flops 2147483648 | bytes 6291456 | tf_op jit(solution)/shard_map/share_products/pallas_call | solution.py:781
  470.4 8.1 %down_forward.1 = f32[512,2048]{1,0:T(8,128)S(1)} custom-call(bf16[3,256,2048]{2,1,0:T(8,128)(2,1)S(1)} %copy-done.6, bf16[3,256,2048]{2,1,0:T(8,128)(2,1)S(1)} %copy-done.8, bf16[3,2048,2048]{2,1,0:T(8,128)(2,1)} %bitcast.152), custom_call_target="tpu_custom_call" | custom-call | flops 4294967296 | bytes 8388608 | tf_op jit(solution)/shard_map/down_forward/pallas_call | solution.py:732
  484.9 9.9 %fusion.10 = (f32[2048]{0:T(1024)S(1)}, f32[128]{0:T(128)S(1)}, f32[128,2048]{1,0:T(8,128)}) fusion(f32[128]{0:T(128)S(1)} %add_rsqrt_fusion.1, bf16[1,128,2048]{2,1,0:T(8,128)(2,1)S(1)} %copy-done.1, f32[2048]{0:T(1024)S(1)} %copy-done.75, bf16[2048,3072]{1,0:T(8,128)(2,1)} %get-tuple-element.64, bf16[128,1024]{1,0:T(8,128)(2,1)S(1)} %copy-done.67, ...), kind=kOutput, calls=%fused_computation.16 | convolution fusion | flops 1614018432 | bytes 14959616 | tf_op jit(solution)/shard_map/dot_general | solution.py:25
  529.3 10.2 %collective-permute-done.59 = bf16[256,1024]{1,0:T(8,128)(2,1)} collective-permute-done((bf16[256,1024]{1,0:T(8,128)(2,1)}, bf16[256,1024]{1,0:T(8,128)(2,1)}, u32[]{:S(2)}, u32[]{:S(2)}) %collective-permute-start.59) | collective-permute-done | bytes 524320 | tf_op jit(solution)/shard_map/ppermute | solution.py:42
  561.4 6.6 %all-to-all-done.2 = bf16[4,64,1024]{2,1,0:T(8,128)(2,1)S(1)} async-done(((bf16[4,64,1024]{2,1,0:T(8,128)(2,1)}), bf16[4,64,1024]{2,1,0:T(8,128)(2,1)S(1)}, u32[]{:S(2)}, u32[]{:S(2)}) %all-to-all-start.2) | async-done | bytes 524320 | tf_op jit(solution)/shard_map/all_to_all | solution.py:366
  (393 shorter events, 251.1 us)
Async XLA Ops:
  7.2 58.4 %all-gather.5.cloned.1.call-start = ((), (), s32[]{:S(2)}) async-start(), calls=%async_computation.7 | async-start | bytes 1310720 | tf_op jit(solution)/shard_map/all_gather | solution.py:184
  31.2 154.6 %all-gather.7.cloned.1.call-start = ((), (), s32[]{:S(2)}) async-start(), calls=%async_computation.8 | async-start | bytes 7077888 | tf_op jit(solution)/shard_map/all_gather | solution.py:191
  71.9 497.4 %reduce-scatter.2.cloned.1.call-start = ((), (), s32[]{:S(2)}) async-start(), calls=%async_computation.6 | async-start | bytes 28311552 | tf_op jit(solution)/shard_map/reduce_scatter | solution.py:897
  74.6 27.2 %collective-permute-start.2 = (bf16[512,384]{1,0:T(8,128)(2,1)}, bf16[512,384]{1,0:T(8,128)(2,1)S(1)}, u32[]{:S(2)}, u32[]{:S(2)}) collective-permute-start(bf16[512,384]{1,0:T(8,128)(2,1)} %collective-permute-done.refs_3_), channel_id=1, source_target_pairs={{0,8},{4,12},{8,0},{12,4},{16,24},{20,28},{24,16},{28,20},{1,9},{5... | collective-permute-start | bytes 1179656 | tf_op jit(solution)/shard_map/ppermute | solution.py:42
  165.2 29.7 %collective-permute-start.37 = (bf16[128,2048]{1,0:T(8,128)(2,1)S(1)}, bf16[128,2048]{1,0:T(8,128)(2,1)}, u32[]{:S(2)}, u32[]{:S(2)}) collective-permute-start(bf16[128,2048]{1,0:T(8,128)(2,1)S(1)} %bitcast.157), channel_id=1, source_target_pairs={{0,3},{1,2},{2,1},{3,0},{4,7},{5,6},{6,5},{7,4},{8,11},{9,10},{10,... | collective-permute-start | bytes 1572872 | tf_op jit(solution)/shard_map/ppermute | solution.py:42
  165.3 55.8 %collective-permute-start.36 = (bf16[128,2048]{1,0:T(8,128)(2,1)S(1)}, bf16[128,2048]{1,0:T(8,128)(2,1)}, u32[]{:S(2)}, u32[]{:S(2)}) collective-permute-start(bf16[128,2048]{1,0:T(8,128)(2,1)S(1)} %bitcast.158), channel_id=1, source_target_pairs={{0,2},{1,3},{2,0},{3,1},{4,6},{5,7},{6,4},{7,5},{8,10},{9,11},{10,... | collective-permute-start | bytes 1572872 | tf_op jit(solution)/shard_map/ppermute | solution.py:42
  165.4 55.7 %collective-permute-start.35 = (bf16[128,2048]{1,0:T(8,128)(2,1)S(1)}, bf16[128,2048]{1,0:T(8,128)(2,1)}, u32[]{:S(2)}, u32[]{:S(2)}) collective-permute-start(bf16[128,2048]{1,0:T(8,128)(2,1)S(1)} %bitcast.159), channel_id=1, source_target_pairs={{0,1},{1,0},{2,3},{3,2},{4,5},{5,4},{6,7},{7,6},{8,9},{9,8},{10,11... | collective-permute-start | bytes 1572872 | tf_op jit(solution)/shard_map/ppermute | solution.py:42
  194.3 41.4 %collective-permute-start.38 = (bf16[128,2048]{1,0:T(8,128)(2,1)S(1)}, bf16[128,2048]{1,0:T(8,128)(2,1)S(1)}, u32[]{:S(2)}, u32[]{:S(2)}) collective-permute-start(bf16[128,2048]{1,0:T(8,128)(2,1)S(1)} %get-tuple-element.48), channel_id=1, source_target_pairs={{0,3},{1,2},{2,1},{3,0},{4,7},{5,6},{6,5},{7,4},{8,11},{9,10},{10,... | collective-permute-start | bytes 1572872 | tf_op jit(solution)/shard_map/ppermute | solution.py:42
  194.4 41.4 %collective-permute-start.34 = (bf16[128,2048]{1,0:T(8,128)(2,1)S(1)}, bf16[128,2048]{1,0:T(8,128)(2,1)S(1)}, u32[]{:S(2)}, u32[]{:S(2)}) collective-permute-start(bf16[128,2048]{1,0:T(8,128)(2,1)S(1)} %get-tuple-element.48), channel_id=1, source_target_pairs={{0,1},{1,0},{2,3},{3,2},{4,5},{5,4},{6,7},{7,6},{8,9},{9,8},{10,11... | collective-permute-start | bytes 1572872 | tf_op jit(solution)/shard_map/ppermute | solution.py:42
  287.9 43.8 %collective-permute-start.40 = (bf16[128,2048]{1,0:T(8,128)(2,1)S(1)}, bf16[128,2048]{1,0:T(8,128)(2,1)S(1)}, u32[]{:S(2)}, u32[]{:S(2)}) collective-permute-start(bf16[128,2048]{1,0:T(8,128)(2,1)S(1)} %slice.345), channel_id=1, source_target_pairs={{0,1},{1,0},{2,3},{3,2},{4,5},{5,4},{6,7},{7,6},{8,9},{9,8},{10,11... | collective-permute-start | bytes 1572872 | tf_op jit(solution)/shard_map/ppermute | solution.py:42
  299.0 32.6 %collective-permute-start.42 = (bf16[128,2048]{1,0:T(8,128)(2,1)S(1)}, bf16[128,2048]{1,0:T(8,128)(2,1)S(1)}, u32[]{:S(2)}, u32[]{:S(2)}) collective-permute-start(bf16[128,2048]{1,0:T(8,128)(2,1)S(1)} %add_convert_fusion.5), channel_id=1, source_target_pairs={{0,3},{1,2},{2,1},{3,0},{4,7},{5,6},{6,5},{7,4},{8,11},{9,10},{10,... | collective-permute-start | bytes 1572872 | tf_op jit(solution)/shard_map/ppermute | solution.py:42
  300.0 63.3 %collective-permute-start.55 = (bf16[128,2048]{1,0:T(8,128)(2,1)S(1)}, bf16[128,2048]{1,0:T(8,128)(2,1)}, u32[]{:S(2)}, u32[]{:S(2)}) collective-permute-start(bf16[128,2048]{1,0:T(8,128)(2,1)S(1)} %fusion.4.refs_1_), channel_id=1, source_target_pairs={{0,3},{1,2},{2,1},{3,0},{4,7},{5,6},{6,5},{7,4},{8,11},{9,10},{10,... | collective-permute-start | bytes 1572872 | tf_op jit(solution)/shard_map/ppermute | solution.py:42
  302.9 63.3 %collective-permute-start.54 = (bf16[128,2048]{1,0:T(8,128)(2,1)S(1)}, bf16[128,2048]{1,0:T(8,128)(2,1)}, u32[]{:S(2)}, u32[]{:S(2)}) collective-permute-start(bf16[128,2048]{1,0:T(8,128)(2,1)S(1)} %fusion.4.refs_1_), channel_id=1, source_target_pairs={{0,2},{1,3},{2,0},{3,1},{4,6},{5,7},{6,4},{7,5},{8,10},{9,11},{10,... | collective-permute-start | bytes 1572872 | tf_op jit(solution)/shard_map/ppermute | solution.py:42
  302.9 63.3 %collective-permute-start.53 = (bf16[128,2048]{1,0:T(8,128)(2,1)S(1)}, bf16[128,2048]{1,0:T(8,128)(2,1)}, u32[]{:S(2)}, u32[]{:S(2)}) collective-permute-start(bf16[128,2048]{1,0:T(8,128)(2,1)S(1)} %fusion.4.refs_1_), channel_id=1, source_target_pairs={{0,1},{1,0},{2,3},{3,2},{4,5},{5,4},{6,7},{7,6},{8,9},{9,8},{10,11... | collective-permute-start | bytes 1572872 | tf_op jit(solution)/shard_map/ppermute | solution.py:42
  363.3 31.3 %collective-permute-start.43 = (bf16[2,4,128,512]{3,2,0,1:T(8,128)(2,1)}, bf16[2,4,128,512]{3,2,0,1:T(8,128)(2,1)}, u32[]{:S(2)}, u32[]{:S(2)}) collective-permute-start(bf16[2,4,128,512]{3,2,0,1:T(8,128)(2,1)} %bitcast.135), channel_id=1, source_target_pairs={{0,4},{4,0},{8,12},{12,8},{16,20},{20,16},{24,28},{28,24},{1,5},{5... | collective-permute-start | bytes 3145736 | tf_op jit(solution)/shard_map/ppermute | solution.py:42
  370.0 54.7 %all-to-all-start = ((bf16[128,4,512]{2,0,1:T(8,128)(2,1)}), bf16[128,4,512]{2,0,1:T(8,128)(2,1)S(1)}, u32[]{:S(2)}, u32[]{:S(2)}) async-start(bf16[128,4,512]{2,0,1:T(8,128)(2,1)} %bitcast.163), calls=%async_computation | async-start | bytes 1048576 | tf_op jit(solution)/shard_map/all_to_all | solution.py:360
  389.3 60.2 %collective-permute-start.52 = (bf16[128,2048]{1,0:T(8,128)(2,1)S(1)}, bf16[128,2048]{1,0:T(8,128)(2,1)}, u32[]{:S(2)}, u32[]{:S(2)}) collective-permute-start(bf16[128,2048]{1,0:T(8,128)(2,1)S(1)} %get-tuple-element.65.x_ref), channel_id=1, source_target_pairs={{0,3},{1,2},{2,1},{3,0},{4,7},{5,6},{6,5},{7,4},{8,11},{9,10},{10,... | collective-permute-start | bytes 1572872 | tf_op jit(solution)/shard_map/ppermute | solution.py:42
  393.1 59.8 %collective-permute-start.51 = (bf16[128,2048]{1,0:T(8,128)(2,1)S(1)}, bf16[128,2048]{1,0:T(8,128)(2,1)}, u32[]{:S(2)}, u32[]{:S(2)}) collective-permute-start(bf16[128,2048]{1,0:T(8,128)(2,1)S(1)} %get-tuple-element.65.x_ref), channel_id=1, source_target_pairs={{0,2},{1,3},{2,0},{3,1},{4,6},{5,7},{6,4},{7,5},{8,10},{9,11},{10,... | collective-permute-start | bytes 1572872 | tf_op jit(solution)/shard_map/ppermute | solution.py:42
  393.1 59.8 %collective-permute-start.50 = (bf16[128,2048]{1,0:T(8,128)(2,1)S(1)}, bf16[128,2048]{1,0:T(8,128)(2,1)}, u32[]{:S(2)}, u32[]{:S(2)}) collective-permute-start(bf16[128,2048]{1,0:T(8,128)(2,1)S(1)} %get-tuple-element.65.x_ref), channel_id=1, source_target_pairs={{0,1},{1,0},{2,3},{3,2},{4,5},{5,4},{6,7},{7,6},{8,9},{9,8},{10,11... | collective-permute-start | bytes 1572872 | tf_op jit(solution)/shard_map/ppermute | solution.py:42
  398.5 34.5 %collective-permute-start.46 = (bf16[2,128,512]{2,1,0:T(8,128)(2,1)}, bf16[2,128,512]{2,1,0:T(8,128)(2,1)}, u32[]{:S(2)}, u32[]{:S(2)}) collective-permute-start(bf16[2,128,512]{2,1,0:T(8,128)(2,1)} %get-tuple-element.111), channel_id=1, source_target_pairs={{0,24},{4,28},{8,16},{12,20},{16,8},{20,12},{24,0},{28,4},{1,25},{... | collective-permute-start | bytes 786440 | tf_op jit(solution)/shard_map/ppermute | solution.py:42
  425.5 32.2 %all-to-all-start.1 = ((bf16[128,4,512]{2,0,1:T(8,128)(2,1)}), bf16[128,4,512]{2,0,1:T(8,128)(2,1)S(1)}, u32[]{:S(2)}, u32[]{:S(2)}) async-start(bf16[128,4,512]{2,0,1:T(8,128)(2,1)} %bitcast.161), calls=%async_computation.1 | async-start | bytes 1048576 | tf_op jit(solution)/shard_map/all_to_all | solution.py:360
  470.4 38.5 %collective-permute-start.56 = (bf16[4,256,1024]{2,1,0:T(8,128)(2,1)}, bf16[4,256,1024]{2,1,0:T(8,128)(2,1)}, u32[]{:S(2)}, u32[]{:S(2)}) collective-permute-start(bf16[4,256,1024]{2,1,0:T(8,128)(2,1)} %get-tuple-element.72), channel_id=1, source_target_pairs={{0,4},{4,0},{8,12},{12,8},{16,20},{20,16},{24,28},{28,24},{1,5},{5... | collective-permute-start | bytes 6291464 | tf_op jit(solution)/shard_map/ppermute | solution.py:42
  521.0 37.4 %collective-permute-start.47 = (bf16[128,2048]{1,0:T(8,128)(2,1)}, bf16[128,2048]{1,0:T(8,128)(2,1)}, u32[]{:S(2)}, u32[]{:S(2)}) collective-permute-start(bf16[128,2048]{1,0:T(8,128)(2,1)} %slice.343), channel_id=1, source_target_pairs={{0,1},{1,0},{2,3},{3,2},{4,5},{5,4},{6,7},{7,6},{8,9},{9,8},{10,11... | collective-permute-start | bytes 1572872 | tf_op jit(solution)/shard_map/ppermute | solution.py:42
  522.7 35.6 %collective-permute-start.49 = (bf16[128,2048]{1,0:T(8,128)(2,1)}, bf16[128,2048]{1,0:T(8,128)(2,1)}, u32[]{:S(2)}, u32[]{:S(2)}) collective-permute-start(bf16[128,2048]{1,0:T(8,128)(2,1)} %add_convert_fusion.4), channel_id=1, source_target_pairs={{0,3},{1,2},{2,1},{3,0},{4,7},{5,6},{6,5},{7,4},{8,11},{9,10},{10,... | collective-permute-start | bytes 1572872 | tf_op jit(solution)/shard_map/ppermute | solution.py:42
  (125 other events, 1625.3 us)
Sparse Core Ops, SparseCore 0:
  31.3 29.2 all-gather.4
  72.0 52.9 all-gather.6
  282.7 165.5 reduce-scatter.1

commit v2 on v1

--- a/solution.py
+++ b/solution.py
@@ -76,7 +76,7 @@
     return lax.axis_index("ctx"), lax.axis_index("fsdp")
 
 
-def gather_pieces(weight, early, ones):
+def gather_pieces(weight, early):
     rows, columns = weight.shape
     share = columns // lax.axis_size("ctx")
     half = rows // 2
@@ -85,7 +85,6 @@
     planes[3] = swap(mine, "fsdp", 3)
     planes[1] = swap(mine, "fsdp", 1)
     planes[2] = swap(after(planes[3], early), "fsdp", 1)
-    rows_one = gather_rows(ones)
     pieces = []
     for away in (1, 3, 2):
         first = planes[away]
@@ -95,7 +94,7 @@
         for offset, start, part in parts:
             pieces.append((away, offset, start, part))
             pieces.append((away, offset + 1, start, swap(part, "ctx", 1)))
-    return pieces, (planes[1], (pieces[-4][3], pieces[-2][3])), rows_one
+    return pieces, (planes[2], (pieces[-4][3], pieces[-2][3]))
 
 
 def pieces_kernel(places, rows_in, share, ids_ref, x_ref, own_ref, *refs):
@@ -173,7 +172,7 @@
             flops=2 * rows * width * columns, bytes_accessed=4 * width * columns, transcendentals=0
         ),
         name="pieces_forward",
-    )(jnp.stack([me, plane]), x, own, *arrays, cosine, sine)
+    )(jnp.stack([me, plane]), x, in_hbm(own), *[in_hbm(part) for part in arrays], cosine, sine)
 
 
 def gather_blocks(weight, before_fsdp, before_ctx):
@@ -207,100 +206,144 @@
     return pltpu.with_memory_space_constraint(value, pltpu.HBM)
 
 
-def out_forward_kernel(
-    ids_ref, x_ref, own_ref, w_ref, hidden_ref, gain_ref, residual_ref, normed_ref
+def out_kernel(back, ids_ref, x_ref, own_ref, blocks_ref, *refs):
+    hidden_ref, gain_ref = (None, None) if back else refs[:2]
+    outs = refs if back else refs[2:]
+    own_buf, buf, sems = outs[-3:]
+    ctx_count, others, rows, share = buf.shape
+    plane = ids_ref[1]
+    copies = [pltpu.make_async_copy(own_ref, own_buf, sems.at[ctx_count])]
+    for c in range(ctx_count):
+        copies.append(pltpu.make_async_copy(blocks_ref.at[c], buf.at[c], sems.at[c]))
+    for copy in copies:
+        copy.start()
+
+    def features(away):
+        return pl.ds(pl.multiple_of((plane ^ away) * rows, 128), rows)
+
+    copies[0].wait()
+    if back:
+        y_ref = outs[0]
+        own_part = nn(x_ref[:, features(0)], own_buf[...])
+        for c in range(ctx_count):
+            copies[c + 1].wait()
+            at = slice(c * share, (c + 1) * share)
+            total = own_part[:, at]
+            for away in range(1, others + 1):
+                total += nn(x_ref[:, features(away)], buf[c, away - 1])
+            y_ref[:, at] = total.astype(BF)
+        return
+    residual_ref, normed_ref = outs[:2]
+    residual_ref[...] = hidden_ref[...].astype(F32)
+    residual_ref[:, features(0)] += nt(x_ref[...], own_buf[...])
+    for c in range(ctx_count):
+        copies[c + 1].wait()
+        x = x_ref[:, c * share : (c + 1) * share]
+        for away in range(1, others + 1):
+            residual_ref[:, features(away)] += nt(x, buf[c, away - 1])
+    residual = residual_ref[...]
+    normed_ref[...] = (residual * norm_scale(residual) * gain_ref[...]).astype(BF)
+
+
+def out_call(back, x, own, blocks, extra, out_shape):
+    vmem, hbm = pl.BlockSpec(memory_space=pltpu.VMEM), pl.BlockSpec(memory_space=pltpu.HBM)
+    return pl.pallas_call(
+        lambda *refs: out_kernel(back, *refs),
+        out_shape=out_shape,
+        in_specs=[pl.BlockSpec(memory_space=pltpu.SMEM), vmem, hbm, hbm] + [vmem] * len(extra),
+        out_specs=jax.tree.map(lambda _: vmem, out_shape),
+        scratch_shapes=[
+            pltpu.VMEM(own.shape, own.dtype),
+            pltpu.VMEM(blocks.shape, blocks.dtype),
+            pltpu.SemaphoreType.DMA((blocks.shape[0] + 1,)),
+        ],
+        compiler_params=pltpu.CompilerParams(vmem_limit_bytes=24 << 20),
+        cost_estimate=pl.CostEstimate(
+            flops=2 * x.shape[0] * own.size * (blocks.shape[1] + 1),
+            bytes_accessed=2 * own.size * (blocks.shape[1] + 1),
+            transcendentals=0,
+        ),
+        name="out_back" if back else "out_forward",
+    )(jnp.stack(ids()), x, in_hbm(own), in_hbm(blocks), *extra)
+
+
+def out_forward(attn_rows, own, blocks, hidden, gain):
+    if blocks.shape[3] % 128:
+        residual = hidden.astype(F32) + nt(attn_rows, whole_of(own, blocks))
+        return residual, (residual * norm_scale(residual) * gain).astype(BF)
+    out_shape = (
+        jax.ShapeDtypeStruct(hidden.shape, F32),
+        jax.ShapeDtypeStruct(hidden.shape, BF),
+    )
+    return out_call(False, attn_rows, own, blocks, [hidden, gain[None]], out_shape)
+
+
+def out_back(x, own, blocks):
+    if blocks.shape[3] % 128:
+        return nn(x, whole_of(own, blocks)).astype(BF)
+    out_shape = jax.ShapeDtypeStruct((x.shape[0], own.shape[1]), BF)
+    return out_call(True, x, own, blocks, [], out_shape)
+
+
+def one_back_kernel(
+    query_ref, pair_ref, w_ref, hidden_ref, gain_ref, residual_ref, y_ref, term_ref
 ):
     step = pl.program_id(0)
-
-    @pl.when(step == 0)
-    def _():
-        residual_ref[...] = hidden_ref[...].astype(F32)
-
-    rows = w_ref.shape[2]
-    plane = ids_ref[1]
-    for away in range(w_ref.shape[1] + 1):
-        at = pl.ds(pl.multiple_of((plane ^ away) * rows, 128), rows)
-        residual_ref[:, at] += nt(x_ref[...], w_ref[0, away - 1] if away else own_ref[...])
+    rows = w_ref.shape[0]
+    split = query_ref.shape[1]
+    y_ref[:, pl.ds(pl.multiple_of(step * rows, 128), rows)] = nt(
+        query_ref[...], w_ref[:, :split]
+    ) + nt(pair_ref[...], w_ref[:, split:])
 
     @pl.when(step == pl.num_programs(0) - 1)
     def _():
-        residual = residual_ref[...]
-        normed_ref[...] = (residual * norm_scale(residual) * gain_ref[...]).astype(BF)
-
-
-def out_specs_of(blocks):
-    _, others, height, share = blocks.shape
-    return [
-        pl.BlockSpec((height, share), lambda c, ids_ref: (0, c)),
-        pl.BlockSpec((1, others, height, share), lambda c, ids_ref: (c, 0, 0, 0)),
-    ]
-
-
-def out_forward(attn_rows, own, blocks, hidden, gain):
+        grad = y_ref[...]
+        inputs = hidden_ref[...].astype(F32)
+        scale = norm_scale(inputs)
+        unit = inputs * scale
+        term_ref[...] = jnp.sum(grad * unit, axis=0, keepdims=True)
+        scaled = gain_ref[...] * grad
+        y_ref[...] = residual_ref[...] + scale * (
+            scaled - unit * jnp.mean(scaled * unit, axis=-1, keepdims=True)
+        )
+
+
+def one_back(query_part, pair_part, weight, hidden, gain, residual_grad):
     rows, width = hidden.shape
-    ctx_count, _, _, share = blocks.shape
-    if share % 128:
-        residual = hidden.astype(F32) + nt(attn_rows, whole_of(own, blocks))
-        return residual, (residual * norm_scale(residual) * gain).astype(BF)
-    whole = pl.BlockSpec((rows, width), lambda c, ids_ref: (0, 0))
+    columns = weight.shape[1]
+    tile = FFN_TILE
+
+    def whole(array):
+        return pl.BlockSpec(array.shape, lambda j: (0, 0))
+
+    gain = gain[None]
     return pl.pallas_call(
-        out_forward_kernel,
-        grid_spec=pltpu.PrefetchScalarGridSpec(
-            num_scalar_prefetch=1,
-            grid=(ctx_count,),
-            in_specs=[pl.BlockSpec((rows, share), lambda c, ids_ref: (0, c))]
-            + out_specs_of(blocks)
-            + [whole, pl.BlockSpec((1, width), lambda c, ids_ref: (0, 0))],
-            out_specs=(whole, whole),
-        ),
+        one_back_kernel,
+        grid=(width // tile,),
         out_shape=(
             jax.ShapeDtypeStruct((rows, width), F32),
-            jax.ShapeDtypeStruct((rows, width), BF),
+            jax.ShapeDtypeStruct((1, width), F32),
+        ),
+        in_specs=[
+            whole(query_part),
+            whole(pair_part),
+            pl.BlockSpec((tile, columns), lambda j: (j, 0)),
+            whole(hidden),
+            whole(gain),
+            whole(residual_grad),
+        ],
+        out_specs=(
+            pl.BlockSpec((rows, width), lambda j: (0, 0)),
+            pl.BlockSpec((1, width), lambda j: (0, 0)),
         ),
         compiler_params=pltpu.CompilerParams(vmem_limit_bytes=24 << 20),
         cost_estimate=pl.CostEstimate(
-            flops=2 * rows * width * ctx_count * share,
-            bytes_accessed=2 * width * ctx_count * share,
+            flops=2 * rows * width * columns,
+            bytes_accessed=2 * width * columns,
             transcendentals=0,
         ),
-        name="out_forward",
-    )(jnp.stack(ids()), attn_rows, in_hbm(own), in_hbm(blocks), hidden, gain[None])
-
-
-def out_back_kernel(ids_ref, x_ref, own_ref, w_ref, y_ref):
-    rows = w_ref.shape[2]
-    plane = ids_ref[1]
-    total = None
-    for away in range(w_ref.shape[1] + 1):
-        at = pl.ds(pl.multiple_of((plane ^ away) * rows, 128), rows)
-        part = nn(x_ref[:, at], w_ref[0, away - 1] if away else own_ref[...])
-        total = part if total is None else total + part
-    y_ref[...] = total.astype(BF)
-
-
-def out_back(x, own, blocks):
-    rows, width = x.shape
-    ctx_count, _, _, share = blocks.shape
-    if share % 128:
-        return nn(x, whole_of(own, blocks)).astype(BF)
-    return pl.pallas_call(
-        out_back_kernel,
-        grid_spec=pltpu.PrefetchScalarGridSpec(
-            num_scalar_prefetch=1,
-            grid=(ctx_count,),
-            in_specs=[pl.BlockSpec((rows, width), lambda c, ids_ref: (0, 0))]
-            + out_specs_of(blocks),
-            out_specs=pl.BlockSpec((rows, share), lambda c, ids_ref: (0, c)),
-        ),
-        out_shape=jax.ShapeDtypeStruct((rows, ctx_count * share), BF),
-        compiler_params=pltpu.CompilerParams(vmem_limit_bytes=24 << 20),
-        cost_estimate=pl.CostEstimate(
-            flops=2 * rows * width * ctx_count * share,
-            bytes_accessed=2 * width * ctx_count * share,
-            transcendentals=0,
-        ),
-        name="out_back",
-    )(jnp.stack(ids()), x, in_hbm(own), in_hbm(blocks))
+        name="one_back",
+    )(query_part, pair_part, in_hbm(weight), hidden, gain, residual_grad)
 
 
 def gather_rows(values, label=None):
@@ -344,31 +387,22 @@
     return total
 
 
-def by_offset(values):
-    count, plane = lax.axis_size("fsdp"), lax.axis_index("fsdp")
-    rows = values.shape[0] // count
-    return jnp.concatenate(
-        [
-            lax.dynamic_slice(values, ((plane ^ away) * rows, 0), (rows, values.shape[1]))
-            for away in range(count)
-        ],
-        axis=0,
-    )
+def by_feature(values):
+    rows, width = values.shape
+    ctx_count, fsdp_count = lax.axis_size("ctx"), lax.axis_size("fsdp")
+    blocks = values.reshape(rows, ctx_count, fsdp_count, width // (ctx_count * fsdp_count))
+    return blocks.transpose(0, 2, 1, 3).reshape(rows, width)
+
+
+def gather_planes(values):
+    count = lax.axis_size("fsdp")
+    rows, columns = values.shape
+    copies = jnp.broadcast_to(values[None], (count, rows, columns)).reshape(count * rows, columns)
+    return lax.all_to_all(copies, "fsdp", split_axis=0, concat_axis=0, tiled=True)
 
 
 def columns_to_owner(values):
     return lax.all_to_all(values, "fsdp", split_axis=1, concat_axis=0, tiled=True)
-
-
-def rows_to_owner(values):
-    count = lax.axis_size("fsdp")
-    rows, columns = values.shape
-    out = lax.all_to_all(values, "fsdp", split_axis=0, concat_axis=0, tiled=True)
-    return out.reshape(count, rows // count, columns)
-
-
-def joined(parts):
-    return jnp.concatenate([parts[i] for i in range(parts.shape[0])], axis=1)
 
 
 def sum_over_ctx(part_for):
@@ -406,12 +440,11 @@
     return jnp.concatenate([mine, other], axis=0)
 
 
-def sum_pairs(parts, cosine, sine):
-    _, count, width = parts.shape
+def sum_pairs(kept, sent, cosine, sine):
+    _, count, width = kept.shape
     pairs = lax.axis_size("ctx") // 2
-    parts = parts.reshape(2, 2, pairs, count // (2 * pairs), width)
-    got = swap(parts[:, 1], "ctx", 1)
-    sums = parts[:, 0].astype(F32) + got.astype(F32)
+    got = swap(sent, "ctx", 1)
+    sums = (kept.astype(F32) + got.astype(F32)).reshape(2, pairs, count // pairs, width)
     far = [swap(sums[:, pair].astype(BF), "ctx", 2 * pair) for pair in range(1, pairs)]
     return pair_turn(sums[:, 0], far, cosine, sine)
 
@@ -509,7 +542,7 @@
 
 def attend_back_kernel(
     chunk, q_ref, grad_ref, attended_ref, k_ref, v_ref, key_ref, own_ref, log_ref, cos_ref, sin_ref,
-    dq_ref, pair_ref,
+    dq_ref, kept_ref, sent_ref,
 ):
     odd = pl.program_id(0) % 2
     rows = q_ref.shape[0]
@@ -531,9 +564,13 @@
         score_grad = (probs * (nt(values, grads) - delta)).astype(BF)
         key_grad = nn(score_grad, queries)
         total += tn(score_grad, keys)
+        far = start >= count // 2
+        out_ref, at = (sent_ref if far else kept_ref), slice(
+            start - far * (count // 2), start - far * (count // 2) + chunk
+        )
         for part, value in enumerate((key_grad, value_grad)):
             value = (value + pltpu.roll(value, HD, 1)).astype(BF)
-            pair_ref[part, at, :] = jnp.where(keep, value, pair_ref[part, at, :])
+            out_ref[part, at, :] = jnp.where(keep, value, out_ref[part, at, :])
     merged = merge_heads(total) * (1.0 / math.sqrt(HD))
     cosine, sine = cos_ref[...], sin_ref[...]
     for j in range(2):
@@ -552,7 +589,8 @@
         grid=(KV,),
         out_shape=(
             jax.ShapeDtypeStruct((rows, width), BF),
-            jax.ShapeDtypeStruct((2, count, both // 2), BF),
+            jax.ShapeDtypeStruct((2, count // 2, both // 2), BF),
+            jax.ShapeDtypeStruct((2, count // 2, both // 2), BF),
         ),
         in_specs=[
             wide,
@@ -568,7 +606,8 @@
         ],
         out_specs=(
             wide,
-            pl.BlockSpec((2, count, 128), lambda g: (0, 0, g // 2)),
+            pl.BlockSpec((2, count // 2, 128), lambda g: (0, 0, g // 2)),
+            pl.BlockSpec((2, count // 2, 128), lambda g: (0, 0, g // 2)),
         ),
         compiler_params=pltpu.CompilerParams(vmem_limit_bytes=48 << 20),
         cost_estimate=pl.CostEstimate(
@@ -746,24 +785,26 @@
     return total[:rows], total[rows:]
 
 
-def share_kernel(count, pairs, ids_ref, *refs):
+def share_kernel(count, ids_ref, *refs):
     lefts, rights = refs[:count], refs[count : 2 * count]
-    rest = refs[2 * count :]
-    step = pl.program_id(0)
-    terms, (sent_ref, kept_ref) = rest[:-2], rest[-2:]
-    parts = [tn(left[...], right[...]) for left, right in zip(lefts, rights)]
+    terms, (kept_ref, sent_ref) = refs[2 * count : -2], refs[-2:]
+    half = kept_ref.shape[1]
+    own = ids_ref[0] % 2 == 0
+    column = 0
+    for left, right in zip(lefts, rights):
+        width = right.shape[1]
+        part = tn(left[...], right[...]).astype(BF)
+        at = slice(column, column + width)
+        kept_ref[0, :, at] = jnp.where(own, part[:half], part[half:])
+        sent_ref[0, :, at] = jnp.where(own, part[half:], part[:half])
+        column += width
     if terms:
-        tall = [jnp.broadcast_to(term[...], (64, term.shape[1])) for term in terms]
-        parts.append(jnp.transpose(jnp.concatenate(tall, axis=0)))
-    block = jnp.concatenate(parts, axis=1).astype(BF)
-
-    @pl.when(step < pairs)
-    def _():
-        sent_ref[0] = block
-
-    @pl.when(step >= pairs)
-    def _():
-        kept_ref[0] = block
+        tall = jnp.concatenate(
+            [jnp.broadcast_to(term[...], (64, term.shape[1])) for term in terms], axis=0
+        )
+        part = jnp.transpose(tall).astype(BF)
+        kept_ref[0, :, column:] = jnp.where(own, part[:half], part[half:])
+        sent_ref[0, :, column:] = jnp.where(own, part[half:], part[:half])
 
 
 def share_products(lefts, rights, terms):
@@ -773,27 +814,20 @@
     height = width // ctx_count
     columns = sum(right.shape[1] for right in rights) + 64 * len(terms)
 
-    def place(i, ids_ref):
-        offset = jnp.where(i < pairs, 2 * i + 1, 2 * (i - pairs))
-        return (0, ids_ref[0] ^ offset)
+    def place(j, ids_ref):
+        return (0, (ids_ref[0] // 2) ^ j)
 
     shape = jax.ShapeDtypeStruct((pairs, height, columns), BF)
+    out = pl.BlockSpec((1, height, columns), lambda j, ids_ref: (j, 0, 0))
     return pl.pallas_call(
-        lambda *refs: share_kernel(len(lefts), pairs, *refs),
+        lambda *refs: share_kernel(len(lefts), *refs),
         grid_spec=pltpu.PrefetchScalarGridSpec(
             num_scalar_prefetch=1,
-            grid=(ctx_count,),
-            in_specs=[pl.BlockSpec((rows, height), place) for _ in lefts]
-            + [pl.BlockSpec(right.shape, lambda i, ids_ref: (0, 0)) for right in rights]
-            + [pl.BlockSpec((1, height), place) for _ in terms],
-            out_specs=(
-                pl.BlockSpec(
-                    (1, height, columns), lambda i, ids_ref: (jnp.minimum(i, pairs - 1), 0, 0)
-                ),
-                pl.BlockSpec(
-                    (1, height, columns), lambda i, ids_ref: (jnp.maximum(i - pairs, 0), 0, 0)
-                ),
-            ),
+            grid=(pairs,),
+            in_specs=[pl.BlockSpec((rows, 2 * height), place) for _ in lefts]
+            + [pl.BlockSpec(right.shape, lambda j, ids_ref: (0, 0)) for right in rights]
+            + [pl.BlockSpec((1, 2 * height), place) for _ in terms],
+            out_specs=(out, out),
         ),
         out_shape=(shape, shape),
         compiler_params=pltpu.CompilerParams(vmem_limit_bytes=24 << 20),
@@ -808,17 +842,30 @@
 
 def share_sum(lefts, rights, terms):
     pairs = lax.axis_size("ctx") // 2
-    if (lefts[0].shape[1] // (2 * pairs)) % 128:
+    if (lefts[0].shape[1] // pairs) % 128:
         values = [tn(left, right) for left, right in zip(lefts, rights)]
         values += [jnp.broadcast_to(term[:, None], (term.shape[0], 64)) for term in terms]
-        return ctx_rows_sum(jnp.concatenate(values, axis=1)).astype(BF)
-    sent, kept = share_products(lefts, rights, terms)
+        return ctx_rows_sum(jnp.concatenate(values, axis=1))
+    kept, sent = share_products(lefts, rights, terms)
     got = swap(sent, "ctx", 1)
     total = kept[0].astype(F32) + got[0].astype(F32)
     for pair in range(1, pairs):
         part = (kept[pair].astype(F32) + got[pair].astype(F32)).astype(BF)
         total = total + swap(part, "ctx", 2 * pair).astype(F32)
-    return total.astype(BF)
+    return total
+
+
+def own_features(terms):
+    ctx_count, fsdp_count = lax.axis_size("ctx"), lax.axis_size("fsdp")
+    total = jnp.stack(terms)
+    away = 1
+    while away < fsdp_count:
+        total = total + swap(total, "fsdp", away)
+        away *= 2
+    blocks = total.reshape(len(terms), ctx_count, fsdp_count, -1)
+    own = lax.dynamic_index_in_dim(blocks, lax.axis_index("fsdp"), 2, keepdims=False)
+    own = own.reshape(len(terms), -1)
+    return [own[i] for i in range(len(terms))]
 
 
 def layer(
@@ -856,14 +903,14 @@
     fast = ctx_count == 8 and (qkv_weight.shape[1] // ctx_count) % 128 == 0
     if fast:
         early = (cosine, sine, own_anchor, key_anchor)
-        qkv_pieces, marks, rows_one = gather_pieces(qkv_weight, early, normed_one)
+        qkv_pieces, marks = gather_pieces(qkv_weight, early)
         out_blocks = gather_blocks(out_weight, *marks)
         queries, pair, qkv_full = pieces_forward(
             normed_one, qkv_weight, qkv_pieces, cosine, sine
         )
     else:
-        out_blocks = gather_blocks(out_weight, normed_one, normed_one)
-        rows_one = gather_rows(normed_one)
+        marks = (normed_one, normed_one)
+        out_blocks = gather_blocks(out_weight, *marks)
         qkv_full = whole_of(qkv_weight, gather_blocks(qkv_weight, normed_one, normed_one))
         projected = nn(normed_one, qkv_full)
         turned = rotate(
@@ -873,7 +920,7 @@
         pair = jnp.concatenate(
             [turned[:, queries_width:], projected[:, queries_width + kv_width :]], axis=1
         ).astype(BF)
-    rows_one = by_offset(jnp.concatenate(rows_one, axis=0))
+    own_one = columns_to_owner(by_feature(after(normed_one, marks[0])))
     keys_values = gather_keys(pair)
     rows_out = fetch_rows(after(grad_in, pair))
     attn_rows, attended, logs = attend(queries, keys_values, key_anchor, own_anchor)
@@ -887,11 +934,11 @@
     for half in rows_out:
         act_grad.append(down_back(half, ffn_parts))
 
-    attn_share = by_offset(columns_to_owner(after(attn_rows, rows_in[1])))
+    all_attn = gather_planes(after(attn_rows, rows_in[1]))
     middle = []
     for half, act in zip(rows_in, act_grad):
-        middle.append(ffn_middle(half, act, ffn_parts))
-    parts, partial = [m[0] for m in middle], [m[1] for m in middle]
+        middle.append(ffn_middle(half, in_hbm(act), ffn_parts))
+    parts, partial = [in_hbm(m[0]) for m in middle], [m[1] for m in middle]
     sum_grad = sum_rows(partial)
     products = ffn_products(rows_in, rows_out, parts).transpose(1, 0, 2)
     ffn_weight_grad = lax.psum_scatter(products, "ctx", scatter_dimension=0, tiled=True)
@@ -905,49 +952,37 @@
         scaled_two - unit_two * jnp.mean(scaled_two * unit_two, axis=-1, keepdims=True)
     )
     residual_bf = residual_grad.astype(BF)
-    residual_planes = fetch_rows(residual_bf)
+    own_residual = columns_to_owner(by_feature(residual_bf))
     attn_grad = out_back(residual_bf, out_weight, out_blocks)
-    query_part, pair_grads = attend_back(
+    query_part, kept, sent = attend_back(
         queries, attn_grad, attended, keys_values, key_anchor, own_anchor, logs, cosine, sine
     )
-    query_owned = columns_to_owner(query_part)
-    pair_part = sum_pairs(pair_grads, cosine, sine)
-    pair_owned = columns_to_owner(pair_part)
-    residual_planes = jnp.concatenate(after(residual_planes, pair_part), axis=0)
-    first_sums = share_sum(
-        [residual_planes, after(rows_one, pair_part)], [attn_share, query_owned], []
+    all_query = gather_planes(query_part)
+    pair_part = sum_pairs(kept, sent, cosine, sine)
+    all_pair = gather_planes(pair_part)
+    first_sums = share_sum([own_residual, own_one], [after(all_attn, pair_part), all_query], [])
+    input_grad, attn_gain_term = one_back(
+        query_part, pair_part, qkv_full, hidden_in[0], attn_gain, residual_grad
     )
-    first_sums = rows_to_owner(first_sums).astype(F32)
-
-    projected_grad = jnp.concatenate([query_part, pair_part], axis=1)
-    normed_one_grad = nt(projected_grad, qkv_full)
-    unit_one = inputs * scale_one
-    attn_gain_term = jnp.sum(normed_one_grad * unit_one, axis=0)
-    scaled_one = attn_gain * normed_one_grad
-    input_grad = residual_grad + scale_one * (
-        scaled_one - unit_one * jnp.mean(scaled_one * unit_one, axis=-1, keepdims=True)
-    )
-
-    last_sums = share_sum([rows_one], [pair_owned], [attn_gain_term, ffn_gain_term])
-    last_sums = rows_to_owner(last_sums).astype(F32)
+    terms = own_features([attn_gain_term[0], ffn_gain_term])
+    last_sums = share_sum([own_one], [all_pair], terms)
 
     out_sum = sum_rows([after(half, pair_part) for half in out_partial])
     output = (residual + out_sum).astype(BF)
 
-    out_columns, pair_columns = attn_share.shape[1], pair_owned.shape[1]
-    out_weight_grad = joined(first_sums[:, :, :out_columns])
+    pairs_width = 2 * kv_width
+    out_weight_grad = first_sums[:, :queries_width]
     qkv_grad = jnp.concatenate(
-        [joined(first_sums[:, :, out_columns:]), joined(last_sums[:, :, :pair_columns])], axis=1
+        [first_sums[:, queries_width:], last_sums[:, :pairs_width]], axis=1
     )
-    gain_grads = jnp.sum(last_sums[:, :, pair_columns:], axis=0)
     return (
         output[None],
         input_grad[None],
         qkv_grad,
         out_weight_grad,
         ffn_weight_grad,
-        gain_grads[:, 0],
-        gain_grads[:, 64],
+        last_sums[:, pairs_width],
+        last_sums[:, pairs_width + 64],
     )
 
 

time: 584 us -> 572 us (0.979)
  the two profiles are of different devices: /device:TPU:0 before, /device:TPU:16 now
where the time goes in v2:
time: 572 us; the launch traced here: 566 us
  waiting for transfers between devices  243 us (42%)
  Pallas kernels  142 us (25%)
  starting transfers between devices  84 us (15%)
  local copies, waits for them, and re-layouts  58.3 us (10%)
  other arithmetic  24.1 us (4%)
  between operations  14.9 us (3%)
    ppermute x60, waiting for transfers between devices, swap(): return lax.ppermute(value, axis, [(i, i ^ offset) for i in range(count)])  208 us
    ppermute x60, starting transfers between devices, swap(): return lax.ppermute(value, axis, [(i, i ^ offset) for i in range(count)])  53.8 us
    pallas_call x2, Pallas kernels, ffn_middle(): pl.pallas_call(ffn_kernel, grid=(hidden // tile,), out_shape=(jax.ShapeDt...  26.8 us
    unnamed x124, local copies, waits for them, and re-layouts  23.3 us
    pallas_call x1, Pallas kernels, ffn_products(): pl.pallas_call(products_kernel, grid=(3, width // tile), out_shape=jax.Sh...  21.9 us
    pallas_call x1, Pallas kernels, attend_back(): pl.pallas_call(lambda *refs: attend_back_kernel(256, *refs), grid=(KV,),...  20.2 us
    all_to_all x3, starting transfers between devices, gather_planes(): lax.all_to_all(copies, 'fsdp', split_axis=0, concat_axis=0, tiled=True)  19.9 us
    all_gather x1, waiting for transfers between devices, gather_blocks(): planes = lax.all_gather(after(mine, before_fsdp), 'fsdp')  15.1 us
  transfers between devices with their start and end apart: 68, of which 38 were waited for; matrix products, arithmetic and copies ran while one was open for 10% of the time, Pallas kernels for 19%

profile of v2, /device:TPU:16, one launch (start us, length us, event | category | flops | bytes accessed | tf_op | source)
XLA Modules:
  0.0 566.2 jit_solution(12766102499209462616)
XLA Ops:
  10.6 17.1 %collective-permute-done.10.refs_13_ = bf16[512,384]{1,0:T(8,128)(2,1)} collective-permute-done((bf16[512,384]{1,0:T(8,128)(2,1)S(1)}, bf16[512,384]{1,0:T(8,128)(2,1)}, u32[]{:S(2)}, u32[]{:S(2)}) %collective-permute-start.10) | collective-permute-done | bytes 393248 | tf_op jit(solution)/shard_map/ppermute | solution.py:42
  29.8 8.4 %collective-permute-done.20.refs_23_ = bf16[512,384]{1,0:T(8,128)(2,1)S(1)} collective-permute-done((bf16[512,384]{1,0:T(8,128)(2,1)}, bf16[512,384]{1,0:T(8,128)(2,1)S(1)}, u32[]{:S(2)}, u32[]{:S(2)}) %collective-permute-start.20) | collective-permute-done | bytes 393248 | tf_op jit(solution)/shard_map/ppermute | solution.py:42
  50.7 15.1 %all-gather.5.cloned.1.call-done = bf16[2048,256]{1,0:T(8,128)(2,1)} async-done(((bf16[512,256]{1,0:T(8,128)(2,1)}), bf16[2048,256]{1,0:T(8,128)(2,1)}) %all-gather.5.cloned.1.call-update) | async-done | bytes 1048592 | tf_op jit(solution)/shard_map/all_gather | solution.py:183
  71.6 6.9 %collective-permute-done.refs_3_ = bf16[512,384]{1,0:T(8,128)(2,1)S(1)} collective-permute-done((bf16[512,384]{1,0:T(8,128)(2,1)S(1)}, bf16[512,384]{1,0:T(8,128)(2,1)S(1)}, u32[]{:S(2)}, u32[]{:S(2)}) %collective-permute-start) | collective-permute-done | bytes 393248 | tf_op jit(solution)/shard_map/ppermute | solution.py:42
  88.5 7.7 %collective-permute-done.4.refs_7_ = bf16[512,384]{1,0:T(8,128)(2,1)S(1)} collective-permute-done((bf16[512,384]{1,0:T(8,128)(2,1)S(1)}, bf16[512,384]{1,0:T(8,128)(2,1)S(1)}, u32[]{:S(2)}, u32[]{:S(2)}) %collective-permute-start.4) | collective-permute-done | bytes 393248 | tf_op jit(solution)/shard_map/ppermute | solution.py:42
  150.4 13.6 %attend.1 = (bf16[128,2048]{1,0:T(8,128)(2,1)S(1)}, f32[128,2048]{1,0:T(8,128)S(1)}, f32[8,1,512]{2,1,0:T(1,128)S(1)}) custom-call(bf16[128,2048]{1,0:T(8,128)(2,1)S(1)} %get-tuple-element.42.q_ref.refs_0_, bf16[1024,1024]{1,0:T(8,128)(2,1)S(1)} %constant_dynamic-update-slice_fusion.1.k_ref.v_ref.refs_3_.refs_4_, ...), custom_call_target="tpu_custom_call" | custom-call | flops 1073741824 | bytes 2097152 | tf_op jit(solution)/shard_map/attend/pallas_call | solution.py:513
  184.1 20.5 %collective-permute-done.36 = bf16[128,2048]{1,0:T(8,128)(2,1)} collective-permute-done((bf16[128,2048]{1,0:T(8,128)(2,1)}, bf16[128,2048]{1,0:T(8,128)(2,1)}, u32[]{:S(2)}, u32[]{:S(2)}) %collective-permute-start.36) | collective-permute-done | bytes 524320 | tf_op jit(solution)/shard_map/ppermute | solution.py:42
  225.9 13.2 %ffn_middle.2 = (bf16[3,256,2048]{2,1,0:T(8,128)(2,1)S(1)}, f32[256,2048]{1,0:T(8,128)S(1)}) custom-call(bf16[256,2048]{1,0:T(8,128)(2,1)S(1)} %constant_dynamic-update-slice_fusion.6.x_ref.in_a, f32[256,2048]{1,0:T(8,128)} %copy-done.11, bf16[3,2048,2048]{2,1,0:T(8,128)(2,1)} %bitcast.93), custom_call_target="tpu_custom_call" | custom-call | flops 8589934592 | bytes 16777216 | tf_op jit(solution)/shard_map/ffn_middle/pallas_call | solution.py:670
  242.2 13.7 %ffn_middle.3 = (bf16[3,256,2048]{2,1,0:T(8,128)(2,1)S(1)}, f32[256,2048]{1,0:T(8,128)S(1)}) custom-call(bf16[256,2048]{1,0:T(8,128)(2,1)S(1)} %constant_dynamic-update-slice_fusion.10.x_ref.in_b, f32[256,2048]{1,0:T(8,128)} %copy-done.10, bf16[3,2048,2048]{2,1,0:T(8,128)(2,1)} %bitcast.94), custom_call_target="tpu_custom_call" | custom-call | flops 8589934592 | bytes 16777216 | tf_op jit(solution)/shard_map/ffn_middle/pallas_call | solution.py:670
  257.4 21.9 %ffn_products.1 = bf16[3,2048,2048]{2,1,0:T(8,128)(2,1)} custom-call(bf16[256,2048]{1,0:T(8,128)(2,1)S(1)} %constant_dynamic-update-slice_fusion.6.x_ref.in_a, bf16[256,2048]{1,0:T(8,128)(2,1)S(1)} %constant_dynamic-update-slice_fusion.10.x_ref.in_b, bf16[256,2048]{1,0:T(8,128)(2,1)S(1)} %constant_dynamic-update-slice_fusion.8.x_ref.grad_a, ...), custom_call_target="tpu_custom_call" | custom-call | flops 12884901888 | bytes 25165824 | tf_op jit(solution)/shard_map/ffn_products/pallas_call | solution.py:717
  285.0 10.7 %collective-permute-done.41 = bf16[128,2048]{1,0:T(8,128)(2,1)S(1)} collective-permute-done((bf16[128,2048]{1,0:T(8,128)(2,1)S(1)}, bf16[128,2048]{1,0:T(8,128)(2,1)S(1)}, u32[]{:S(2)}, u32[]{:S(2)}) %collective-permute-start.41) | collective-permute-done | bytes 524320 | tf_op jit(solution)/shard_map/ppermute | solution.py:42
  307.0 19.1 %collective-permute-done.42 = bf16[128,2048]{1,0:T(8,128)(2,1)S(1)} collective-permute-done((bf16[128,2048]{1,0:T(8,128)(2,1)}, bf16[128,2048]{1,0:T(8,128)(2,1)S(1)}, u32[]{:S(2)}, u32[]{:S(2)}) %collective-permute-start.42) | collective-permute-done | bytes 524320 | tf_op jit(solution)/shard_map/ppermute | solution.py:42
  337.1 7.0 %all-to-all-done = bf16[128,4,512]{0,2,1:T(8,128)(2,1)} async-done(((bf16[128,4,512]{0,2,1:T(8,128)(2,1)}), bf16[128,4,512]{0,2,1:T(8,128)(2,1)}, u32[]{:S(2)}, u32[]{:S(2)}) %all-to-all-start) | async-done | bytes 524320 | tf_op jit(solution)/shard_map/all_to_all | solution.py:405
  346.8 7.8 %all-to-all-start.2 = ((bf16[4,128,2048]{2,1,0:T(8,128)(2,1)}), bf16[4,128,2048]{2,1,0:T(8,128)(2,1)}, u32[]{:S(2)}, u32[]{:S(2)}) async-start(bf16[4,128,2048]{2,1,0:T(8,128)(2,1)} %broadcast_in_dim.122), calls=%async_computation.2 | async-start | bytes 4194304 | tf_op jit(solution)/shard_map/all_to_all | solution.py:401
  360.1 20.2 %attend_back.1 = (bf16[128,2048]{1,0:T(8,128)(2,1)S(1)}, bf16[2,512,512]{2,1,0:T(8,128)(2,1)S(1)}, bf16[2,512,512]{2,1,0:T(8,128)(2,1)}) custom-call(bf16[128,2048]{1,0:T(8,128)(2,1)S(1)} %copy-done.28, bf16[128,2048]{1,0:T(8,128)(2,1)S(1)} %out_back.1.refs_1_, f32[128,2048]{1,0:T(8,128)S(1)} %copy-done.30, bf16[1024,1024]{1,0:T(8,128)(2,1)} %copy-done.26, ...), custom_call_target="tpu_custom_call" | custom-call | flops 2684354560 | bytes 4194304 | tf_op jit(solution)/shard_map/attend_back/pallas_call | solution.py:587
  381.3 12.3 %all-to-all-done.2 = bf16[4,128,2048]{2,1,0:T(8,128)(2,1)} async-done(((bf16[4,128,2048]{2,1,0:T(8,128)(2,1)}), bf16[4,128,2048]{2,1,0:T(8,128)(2,1)}, u32[]{:S(2)}, u32[]{:S(2)}) %all-to-all-start.2) | async-done | bytes 2097184 | tf_op jit(solution)/shard_map/all_to_all | solution.py:401
  395.2 8.0 %all-to-all-start.3 = ((bf16[4,128,2048]{2,1,0:T(8,128)(2,1)}), bf16[4,128,2048]{2,1,0:T(8,128)(2,1)}, u32[]{:S(2)}, u32[]{:S(2)}) async-start(bf16[4,128,2048]{2,1,0:T(8,128)(2,1)} %broadcast_in_dim.123), calls=%async_computation.3 | async-start | bytes 4194304 | tf_op jit(solution)/shard_map/all_to_all | solution.py:401
  410.9 7.9 %down_forward.1 = f32[512,2048]{1,0:T(8,128)S(1)} custom-call(bf16[3,256,2048]{2,1,0:T(8,128)(2,1)} %copy-done.6, bf16[3,256,2048]{2,1,0:T(8,128)(2,1)} %copy-done.7, bf16[3,2048,2048]{2,1,0:T(8,128)(2,1)} %bitcast.95), custom_call_target="tpu_custom_call" | custom-call | flops 4294967296 | bytes 8388608 | tf_op jit(solution)/shard_map/down_forward/pallas_call | solution.py:771
  436.7 9.6 %one_back.1 = (f32[128,2048]{1,0:T(8,128)}, f32[1,2048]{1,0:T(1,128)S(1)}) custom-call(bf16[128,2048]{1,0:T(8,128)(2,1)S(1)} %get-tuple-element.64.query_ref, bf16[128,1024]{1,0:T(8,128)(2,1)S(1)} %copy-done.8, bf16[2048,3072]{1,0:T(8,128)(2,1)} %copy-done.2, bf16[128,2048]{1,0:T(8,128)(2,1)S(1)} %bitcast.84, f32[1,2048]{1,0:T(1,128)S(1)} %bitcast.90, ...), custom_call_target="tpu_custom_call" | custom-call | flops 1610612736 | bytes 12582912 | tf_op jit(solution)/shard_map/one_back/pallas_call | solution.py:320
  465.0 6.9 %share_products.1 = (bf16[4,64,4096]{2,1,0:T(8,128)(2,1)S(1)}, bf16[4,64,4096]{2,1,0:T(8,128)(2,1)}) custom-call(s32[2]{0:T(128)S(1)} %pad_add_fusion.refs_0_, bf16[512,512]{1,0:T(8,128)(2,1)S(1)} %bitcast.88, bf16[512,512]{1,0:T(8,128)(2,1)S(1)} %bitcast.86, bf16[512,2048]{1,0:T(8,128)(2,1)} %bitcast.30.refs_3_, bf16[512,2048]{1,0:T(8,128)(2,1)} %bitcast.31.refs_4_), custom_call_target="tpu_custom_call" | custom-call | flops 2147483648 | bytes 4718592 | tf_op jit(solution)/shard_map/share_products/pallas_call | solution.py:822
  473.3 19.1 %collective-permute-done.48 = bf16[128,2048]{1,0:T(8,128)(2,1)} collective-permute-done((bf16[128,2048]{1,0:T(8,128)(2,1)}, bf16[128,2048]{1,0:T(8,128)(2,1)}, u32[]{:S(2)}, u32[]{:S(2)}) %collective-permute-start.48) | collective-permute-done | bytes 524320 | tf_op jit(solution)/shard_map/ppermute | solution.py:42
  501.4 15.0 %collective-permute-done.49 = bf16[128,2048]{1,0:T(8,128)(2,1)S(1)} collective-permute-done((bf16[128,2048]{1,0:T(8,128)(2,1)}, bf16[128,2048]{1,0:T(8,128)(2,1)S(1)}, u32[]{:S(2)}, u32[]{:S(2)}) %collective-permute-start.49) | collective-permute-done | bytes 524320 | tf_op jit(solution)/shard_map/ppermute | solution.py:42
  530.1 9.7 %collective-permute-done.51 = bf16[64,4096]{1,0:T(8,128)(2,1)S(1)} collective-permute-done((bf16[64,4096]{1,0:T(8,128)(2,1)S(1)}, bf16[64,4096]{1,0:T(8,128)(2,1)S(1)}, u32[]{:S(2)}, u32[]{:S(2)}) %collective-permute-start.51) | collective-permute-done | bytes 524320 | tf_op jit(solution)/shard_map/ppermute | solution.py:42
  539.8 9.9 %collective-permute-done.53 = bf16[64,4096]{1,0:T(8,128)(2,1)S(1)} collective-permute-done((bf16[64,4096]{1,0:T(8,128)(2,1)S(1)}, bf16[64,4096]{1,0:T(8,128)(2,1)S(1)}, u32[]{:S(2)}, u32[]{:S(2)}) %collective-permute-start.53) | collective-permute-done | bytes 524320 | tf_op jit(solution)/shard_map/ppermute | solution.py:42
  (340 shorter events, 250.1 us)
Async XLA Ops:
  7.2 58.7 %all-gather.5.cloned.1.call-start = ((), (), s32[]{:S(2)}) async-start(), calls=%async_computation.7 | async-start | bytes 1310720 | tf_op jit(solution)/shard_map/all_gather | solution.py:183
  38.2 128.1 %all-gather.7.cloned.1.call-start = ((), (), s32[]{:S(2)}) async-start(), calls=%async_computation.8 | async-start | bytes 7077888 | tf_op jit(solution)/shard_map/all_gather | solution.py:190
  68.0 486.0 %reduce-scatter.2.cloned.1.call-start = ((), (), s32[]{:S(2)}) async-start(), calls=%async_computation.6 | async-start | bytes 28311552 | tf_op jit(solution)/shard_map/reduce_scatter | solution.py:944
  88.4 25.1 %collective-permute-start.15 = (bf16[512,384]{1,0:T(8,128)(2,1)S(1)}, bf16[512,384]{1,0:T(8,128)(2,1)S(1)}, u32[]{:S(2)}, u32[]{:S(2)}) collective-permute-start(bf16[512,384]{1,0:T(8,128)(2,1)S(1)} %collective-permute-done.14.refs_17_), channel_id=1, source_target_pairs={{0,4},{4,0},{8,12},{12,8},{16,20},{20,16},{24,28},{28,24},{1,5},{5... | collective-permute-start | bytes 1179656 | tf_op jit(solution)/shard_map/ppermute | solution.py:42
  146.4 37.7 %collective-permute-start.37 = (bf16[128,2048]{1,0:T(8,128)(2,1)}, bf16[128,2048]{1,0:T(8,128)(2,1)}, u32[]{:S(2)}, u32[]{:S(2)}) collective-permute-start(bf16[128,2048]{1,0:T(8,128)(2,1)} %bitcast.10), channel_id=1, source_target_pairs={{0,3},{1,2},{2,1},{3,0},{4,7},{5,6},{6,5},{7,4},{8,11},{9,10},{10,... | collective-permute-start | bytes 1572872 | tf_op jit(solution)/shard_map/ppermute | solution.py:42
  147.0 57.6 %collective-permute-start.36 = (bf16[128,2048]{1,0:T(8,128)(2,1)}, bf16[128,2048]{1,0:T(8,128)(2,1)}, u32[]{:S(2)}, u32[]{:S(2)}) collective-permute-start(bf16[128,2048]{1,0:T(8,128)(2,1)} %bitcast.10), channel_id=1, source_target_pairs={{0,2},{1,3},{2,0},{3,1},{4,6},{5,7},{6,4},{7,5},{8,10},{9,11},{10,... | collective-permute-start | bytes 1572872 | tf_op jit(solution)/shard_map/ppermute | solution.py:42
  149.5 55.2 %collective-permute-start.35 = (bf16[128,2048]{1,0:T(8,128)(2,1)}, bf16[128,2048]{1,0:T(8,128)(2,1)}, u32[]{:S(2)}, u32[]{:S(2)}) collective-permute-start(bf16[128,2048]{1,0:T(8,128)(2,1)} %bitcast.10), channel_id=1, source_target_pairs={{0,1},{1,0},{2,3},{3,2},{4,5},{5,4},{6,7},{7,6},{8,9},{9,8},{10,11... | collective-permute-start | bytes 1572872 | tf_op jit(solution)/shard_map/ppermute | solution.py:42
  172.8 49.6 %collective-permute-start.38 = (bf16[128,2048]{1,0:T(8,128)(2,1)S(1)}, bf16[128,2048]{1,0:T(8,128)(2,1)S(1)}, u32[]{:S(2)}, u32[]{:S(2)}) collective-permute-start(bf16[128,2048]{1,0:T(8,128)(2,1)S(1)} %get-tuple-element.48), channel_id=1, source_target_pairs={{0,3},{1,2},{2,1},{3,0},{4,7},{5,6},{6,5},{7,4},{8,11},{9,10},{10,... | collective-permute-start | bytes 1572872 | tf_op jit(solution)/shard_map/ppermute | solution.py:42
  174.3 51.5 %collective-permute-start.34 = (bf16[128,2048]{1,0:T(8,128)(2,1)S(1)}, bf16[128,2048]{1,0:T(8,128)(2,1)S(1)}, u32[]{:S(2)}, u32[]{:S(2)}) collective-permute-start(bf16[128,2048]{1,0:T(8,128)(2,1)S(1)} %get-tuple-element.48), channel_id=1, source_target_pairs={{0,1},{1,0},{2,3},{3,2},{4,5},{5,4},{6,7},{7,6},{8,9},{9,8},{10,11... | collective-permute-start | bytes 1572872 | tf_op jit(solution)/shard_map/ppermute | solution.py:42
  283.0 23.9 %collective-permute-start.40 = (bf16[128,2048]{1,0:T(8,128)(2,1)}, bf16[128,2048]{1,0:T(8,128)(2,1)S(1)}, u32[]{:S(2)}, u32[]{:S(2)}) collective-permute-start(bf16[128,2048]{1,0:T(8,128)(2,1)} %slice.257), channel_id=1, source_target_pairs={{0,1},{1,0},{2,3},{3,2},{4,5},{5,4},{6,7},{7,6},{8,9},{9,8},{10,11... | collective-permute-start | bytes 1572872 | tf_op jit(solution)/shard_map/ppermute | solution.py:42
  296.6 29.4 %collective-permute-start.42 = (bf16[128,2048]{1,0:T(8,128)(2,1)}, bf16[128,2048]{1,0:T(8,128)(2,1)S(1)}, u32[]{:S(2)}, u32[]{:S(2)}) collective-permute-start(bf16[128,2048]{1,0:T(8,128)(2,1)} %add_convert_fusion.5), channel_id=1, source_target_pairs={{0,3},{1,2},{2,1},{3,0},{4,7},{5,6},{6,5},{7,4},{8,11},{9,10},{10,... | collective-permute-start | bytes 1572872 | tf_op jit(solution)/shard_map/ppermute | solution.py:42
  300.2 32.8 %all-to-all-start.1 = ((bf16[128,4,512]{0,2,1:T(8,128)(2,1)}), bf16[128,4,512]{0,2,1:T(8,128)(2,1)}, u32[]{:S(2)}, u32[]{:S(2)}) async-start(bf16[128,4,512]{0,2,1:T(8,128)(2,1)} %bitcast.27), calls=%async_computation.1 | async-start | bytes 1048576 | tf_op jit(solution)/shard_map/all_to_all | solution.py:405
  346.8 46.8 %all-to-all-start.2 = ((bf16[4,128,2048]{2,1,0:T(8,128)(2,1)}), bf16[4,128,2048]{2,1,0:T(8,128)(2,1)}, u32[]{:S(2)}, u32[]{:S(2)}) async-start(bf16[4,128,2048]{2,1,0:T(8,128)(2,1)} %broadcast_in_dim.122), calls=%async_computation.2 | async-start | bytes 4194304 | tf_op jit(solution)/shard_map/all_to_all | solution.py:401
  381.3 23.9 %collective-permute-start.43 = (bf16[2,512,512]{2,1,0:T(8,128)(2,1)}, bf16[2,512,512]{2,1,0:T(8,128)(2,1)}, u32[]{:S(2)}, u32[]{:S(2)}) collective-permute-start(bf16[2,512,512]{2,1,0:T(8,128)(2,1)} %get-tuple-element.61), channel_id=1, source_target_pairs={{0,4},{4,0},{8,12},{12,8},{16,20},{20,16},{24,28},{28,24},{1,5},{5... | collective-permute-start | bytes 3145736 | tf_op jit(solution)/shard_map/ppermute | solution.py:42
  395.2 63.3 %all-to-all-start.3 = ((bf16[4,128,2048]{2,1,0:T(8,128)(2,1)}), bf16[4,128,2048]{2,1,0:T(8,128)(2,1)}, u32[]{:S(2)}, u32[]{:S(2)}) async-start(bf16[4,128,2048]{2,1,0:T(8,128)(2,1)} %broadcast_in_dim.123), calls=%async_computation.3 | async-start | bytes 4194304 | tf_op jit(solution)/shard_map/all_to_all | solution.py:401
  410.3 23.2 %collective-permute-start.44 = (bf16[2,128,512]{2,1,0:T(8,128)(2,1)S(1)}, bf16[2,128,512]{2,1,0:T(8,128)(2,1)}, u32[]{:S(2)}, u32[]{:S(2)}) collective-permute-start(bf16[2,128,512]{2,1,0:T(8,128)(2,1)S(1)} %get-tuple-element.101), channel_id=1, source_target_pairs={{0,8},{4,12},{8,0},{12,4},{16,24},{20,28},{24,16},{28,20},{1,9},{5... | collective-permute-start | bytes 786440 | tf_op jit(solution)/shard_map/ppermute | solution.py:42
  456.5 45.0 %collective-permute-start.47 = (bf16[128,2048]{1,0:T(8,128)(2,1)}, bf16[128,2048]{1,0:T(8,128)(2,1)}, u32[]{:S(2)}, u32[]{:S(2)}) collective-permute-start(bf16[128,2048]{1,0:T(8,128)(2,1)} %slice.255), channel_id=1, source_target_pairs={{0,1},{1,0},{2,3},{3,2},{4,5},{5,4},{6,7},{7,6},{8,9},{9,8},{10,11... | collective-permute-start | bytes 1572872 | tf_op jit(solution)/shard_map/ppermute | solution.py:42
  457.0 35.4 %collective-permute-start.48 = (bf16[128,2048]{1,0:T(8,128)(2,1)}, bf16[128,2048]{1,0:T(8,128)(2,1)}, u32[]{:S(2)}, u32[]{:S(2)}) collective-permute-start(bf16[128,2048]{1,0:T(8,128)(2,1)} %slice.254), channel_id=1, source_target_pairs={{0,1},{1,0},{2,3},{3,2},{4,5},{5,4},{6,7},{7,6},{8,9},{9,8},{10,11... | collective-permute-start | bytes 1572872 | tf_op jit(solution)/shard_map/ppermute | solution.py:42
  459.7 39.5 %all-to-all-start.4 = ((bf16[4,128,1024]{2,1,0:T(8,128)(2,1)}), bf16[4,128,1024]{2,1,0:T(8,128)(2,1)S(1)}, u32[]{:S(2)}, u32[]{:S(2)}) async-start(bf16[4,128,1024]{2,1,0:T(8,128)(2,1)} %broadcast_in_dim.124), calls=%async_computation.4 | async-start | bytes 2097152 | tf_op jit(solution)/shard_map/all_to_all | solution.py:401
  463.9 35.0 %collective-permute-start.55 = (f32[2,2048]{1,0:T(2,128)S(1)}, f32[2,2048]{1,0:T(2,128)S(1)}, u32[]{:S(2)}, u32[]{:S(2)}) collective-permute-start(f32[2,2048]{1,0:T(2,128)S(1)} %fusion.25), channel_id=1, source_target_pairs={{0,2},{1,3},{2,0},{3,1},{4,6},{5,7},{6,4},{7,5},{8,10},{9,11},{10,... | collective-permute-start | bytes 49160 | tf_op jit(solution)/shard_map/ppermute | solution.py:42
  473.3 48.9 %collective-permute-start.50 = (bf16[4,64,4096]{2,1,0:T(8,128)(2,1)}, bf16[4,64,4096]{2,1,0:T(8,128)(2,1)}, u32[]{:S(2)}, u32[]{:S(2)}) collective-permute-start(bf16[4,64,4096]{2,1,0:T(8,128)(2,1)} %get-tuple-element.71), channel_id=1, source_target_pairs={{0,4},{4,0},{8,12},{12,8},{16,20},{20,16},{24,28},{28,24},{1,5},{5... | collective-permute-start | bytes 6291464 | tf_op jit(solution)/shard_map/ppermute | solution.py:42
  494.4 22.1 %collective-permute-start.49 = (bf16[128,2048]{1,0:T(8,128)(2,1)}, bf16[128,2048]{1,0:T(8,128)(2,1)S(1)}, u32[]{:S(2)}, u32[]{:S(2)}) collective-permute-start(bf16[128,2048]{1,0:T(8,128)(2,1)} %add_convert_fusion.4), channel_id=1, source_target_pairs={{0,3},{1,2},{2,1},{3,0},{4,7},{5,6},{6,5},{7,4},{8,11},{9,10},{10,... | collective-permute-start | bytes 1572872 | tf_op jit(solution)/shard_map/ppermute | solution.py:42
  525.3 24.3 %collective-permute-start.53 = (bf16[64,4096]{1,0:T(8,128)(2,1)S(1)}, bf16[64,4096]{1,0:T(8,128)(2,1)S(1)}, u32[]{:S(2)}, u32[]{:S(2)}) collective-permute-start(bf16[64,4096]{1,0:T(8,128)(2,1)S(1)} %get-tuple-element.90), channel_id=1, source_target_pairs={{0,24},{4,28},{8,16},{12,20},{16,8},{20,12},{24,0},{28,4},{1,25},{... | collective-permute-start | bytes 1572872 | tf_op jit(solution)/shard_map/ppermute | solution.py:42
  526.2 24.6 %collective-permute-start.52 = (bf16[64,4096]{1,0:T(8,128)(2,1)S(1)}, bf16[64,4096]{1,0:T(8,128)(2,1)S(1)}, u32[]{:S(2)}, u32[]{:S(2)}) collective-permute-start(bf16[64,4096]{1,0:T(8,128)(2,1)S(1)} %get-tuple-element.91), channel_id=1, source_target_pairs={{0,16},{4,20},{8,24},{12,28},{16,0},{20,4},{24,8},{28,12},{1,17},{... | collective-permute-start | bytes 1572872 | tf_op jit(solution)/shard_map/ppermute | solution.py:42
  (102 other events, 1883.1 us)
Sparse Core Ops, SparseCore 0:
  38.4 27.4 all-gather.4
  68.3 56.9 all-gather.6
  279.5 166.3 reduce-scatter.1

commit v3 on v2

--- a/solution.py
+++ b/solution.py
@@ -155,7 +155,7 @@
         out_shape=(
             jax.ShapeDtypeStruct((rows, H * HD), BF),
             jax.ShapeDtypeStruct((rows, 2 * KV * HD), BF),
-            jax.ShapeDtypeStruct((width, columns), BF),
+            pltpu.HBM((width, columns), BF),
         ),
         in_specs=[pl.BlockSpec(memory_space=pltpu.SMEM), vmem, hbm]
         + [hbm] * len(arrays)
@@ -346,17 +346,13 @@
     )(query_part, pair_part, in_hbm(weight), hidden, gain, residual_grad)
 
 
-def gather_rows(values, label=None):
-    count = lax.axis_size("fsdp")
-    planes = {0: values}
-    if count == 4 and label:
-        planes[3] = swap(values, "fsdp", 3)
-        planes[1] = swap(values, "fsdp", 1)
-        planes[2] = swap(planes[3], "fsdp", 1)
-    else:
-        for away in range(1, count):
-            planes[away] = swap(values, "fsdp", away)
-    return halves_of([planes[away] for away in range(count)])
+def pass_rows(values):
+    if lax.axis_size("fsdp") != 4:
+        return fetch_rows(values)
+    third = swap(values, "fsdp", 3)
+    first = swap(values, "fsdp", 1)
+    second = swap(third, "fsdp", 1)
+    return [values, first, second, third]
 
 
 def fetch_rows(values):
@@ -392,6 +388,17 @@
     ctx_count, fsdp_count = lax.axis_size("ctx"), lax.axis_size("fsdp")
     blocks = values.reshape(rows, ctx_count, fsdp_count, width // (ctx_count * fsdp_count))
     return blocks.transpose(0, 2, 1, 3).reshape(rows, width)
+
+
+def by_offset(planes):
+    count, plane = len(planes), lax.axis_index("fsdp")
+    joined = planes
+    bit = 1
+    while bit < count:
+        odd = (plane & bit) != 0
+        joined = [jnp.where(odd, joined[i ^ bit], joined[i]) for i in range(count)]
+        bit *= 2
+    return jnp.concatenate(joined, axis=0)
 
 
 def gather_planes(values):
@@ -671,7 +678,7 @@
         ffn_kernel,
         grid=(hidden // tile,),
         out_shape=(
-            jax.ShapeDtypeStruct((3, rows, hidden), BF),
+            pltpu.HBM((3, rows, hidden), BF),
             jax.ShapeDtypeStruct((rows, width), F32),
         ),
         in_specs=[
@@ -717,7 +724,7 @@
     return pl.pallas_call(
         products_kernel,
         grid=(3, width // tile),
-        out_shape=jax.ShapeDtypeStruct((3, width, hidden), BF),
+        out_shape=pltpu.HBM((3, width, hidden), BF),
         in_specs=[left, left, grad, grad, right, right],
         out_specs=pl.BlockSpec((1, tile, hidden), lambda k, i: (k, i, 0)),
         compiler_params=pltpu.CompilerParams(vmem_limit_bytes=32 << 20),
@@ -741,7 +748,7 @@
     return pl.pallas_call(
         simple_kernel,
         grid=(hidden // tile,),
-        out_shape=jax.ShapeDtypeStruct((rows, hidden), F32),
+        out_shape=pltpu.HBM((rows, hidden), F32),
         in_specs=[
             pl.BlockSpec((rows, width), lambda j: (0, 0)),
             pl.BlockSpec((1, width, tile), lambda j: (2, 0, j)),
@@ -840,18 +847,25 @@
     )(jnp.stack(ids()), *lefts, *rights, *[term[None] for term in terms])
 
 
-def share_sum(lefts, rights, terms):
+def share_start(lefts, rights, terms):
     pairs = lax.axis_size("ctx") // 2
     if (lefts[0].shape[1] // pairs) % 128:
         values = [tn(left, right) for left, right in zip(lefts, rights)]
         values += [jnp.broadcast_to(term[:, None], (term.shape[0], 64)) for term in terms]
-        return ctx_rows_sum(jnp.concatenate(values, axis=1))
+        return [ctx_rows_sum(jnp.concatenate(values, axis=1))]
     kept, sent = share_products(lefts, rights, terms)
     got = swap(sent, "ctx", 1)
-    total = kept[0].astype(F32) + got[0].astype(F32)
+    parts = [kept[0], got[0]]
     for pair in range(1, pairs):
         part = (kept[pair].astype(F32) + got[pair].astype(F32)).astype(BF)
-        total = total + swap(part, "ctx", 2 * pair).astype(F32)
+        parts.append(swap(part, "ctx", 2 * pair))
+    return parts
+
+
+def share_finish(parts):
+    total = parts[0].astype(F32)
+    for part in parts[1:]:
+        total = total + part.astype(F32)
     return total
 
 
@@ -920,15 +934,15 @@
         pair = jnp.concatenate(
             [turned[:, queries_width:], projected[:, queries_width + kv_width :]], axis=1
         ).astype(BF)
-    own_one = columns_to_owner(by_feature(after(normed_one, marks[0])))
+    own_one = columns_to_owner(by_feature(after(normed_one, pair)))
     keys_values = gather_keys(pair)
-    rows_out = fetch_rows(after(grad_in, pair))
+    rows_out = fetch_rows(after(grad_in, marks[0]))
     attn_rows, attended, logs = attend(queries, keys_values, key_anchor, own_anchor)
     residual, normed_two = out_forward(
         attn_rows, out_weight, out_blocks, hidden_in[0], ffn_gain
     )
     scale_two = norm_scale(residual)
-    rows_in = gather_rows(normed_two, "normed")
+    rows_in = halves_of(pass_rows(normed_two))
     rows_out = halves_of(after(rows_out, normed_two))
     act_grad = []
     for half in rows_out:
@@ -957,15 +971,17 @@
     query_part, kept, sent = attend_back(
         queries, attn_grad, attended, keys_values, key_anchor, own_anchor, logs, cosine, sine
     )
-    all_query = gather_planes(query_part)
+    query_planes = pass_rows(query_part)
     pair_part = sum_pairs(kept, sent, cosine, sine)
     all_pair = gather_planes(pair_part)
-    first_sums = share_sum([own_residual, own_one], [after(all_attn, pair_part), all_query], [])
+    all_query = by_offset(after(query_planes, pair_part))
+    first_sums = share_start([own_residual, own_one], [after(all_attn, pair_part), all_query], [])
     input_grad, attn_gain_term = one_back(
         query_part, pair_part, qkv_full, hidden_in[0], attn_gain, residual_grad
     )
     terms = own_features([attn_gain_term[0], ffn_gain_term])
-    last_sums = share_sum([own_one], [all_pair], terms)
+    last_sums = share_finish(share_start([own_one], [all_pair], terms))
+    first_sums = share_finish(after(first_sums, last_sums))
 
     out_sum = sum_rows([after(half, pair_part) for half in out_partial])
     output = (residual + out_sum).astype(BF)

time: 572 us -> 596 us (1.042)
  the two profiles are of different devices: /device:TPU:16 before, /device:TPU:0 now
where the time goes in v3:
time: 596 us; the launch traced here: 587 us
  waiting for transfers between devices  236 us (40%)
  Pallas kernels  148 us (25%)
  starting transfers between devices  112 us (19%)
  local copies, waits for them, and re-layouts  47.4 us (8%)
  other arithmetic  29.4 us (5%)
  between operations  14.9 us (2%)
    ppermute x63, waiting for transfers between devices, swap(): return lax.ppermute(value, axis, [(i, i ^ offset) for i in range(count)])  217 us
    ppermute x63, starting transfers between devices, swap(): return lax.ppermute(value, axis, [(i, i ^ offset) for i in range(count)])  92.5 us
    pallas_call x2, Pallas kernels, ffn_middle(): pl.pallas_call(ffn_kernel, grid=(hidden // tile,), out_shape=(pltpu.HBM((...  28.3 us
    pallas_call x1, Pallas kernels, ffn_products(): pl.pallas_call(products_kernel, grid=(3, width // tile), out_shape=pltpu....  21.9 us
    pallas_call x1, Pallas kernels, attend_back(): pl.pallas_call(lambda *refs: attend_back_kernel(256, *refs), grid=(KV,),...  20.3 us
    all_gather x1, waiting for transfers between devices, gather_blocks(): planes = lax.all_gather(after(mine, before_fsdp), 'fsdp')  15.4 us
    pallas_call x1, Pallas kernels, attend(): pl.pallas_call(attend_kernel, grid=(KV,), out_shape=(jax.ShapeDtypeStruct...  14 us
    pallas_call x2, Pallas kernels, down_back(): pl.pallas_call(simple_kernel, grid=(hidden // tile,), out_shape=pltpu.HBM...  13.2 us
  transfers between devices with their start and end apart: 70, of which 35 were waited for; matrix products, arithmetic and copies ran while one was open for 10% of the time, Pallas kernels for 19%

profile of v3, /device:TPU:0, one launch (start us, length us, event | category | flops | bytes accessed | tf_op | source)
XLA Modules:
  0.0 587.3 jit_solution(9183196223921625720)
XLA Ops:
  15.2 7.5 %collective-permute-done.10.refs_13_ = bf16[512,384]{1,0:T(8,128)(2,1)} collective-permute-done((bf16[512,384]{1,0:T(8,128)(2,1)S(1)}, bf16[512,384]{1,0:T(8,128)(2,1)}, u32[]{:S(2)}, u32[]{:S(2)}) %collective-permute-start.10) | collective-permute-done | bytes 393248 | tf_op jit(solution)/shard_map/ppermute | solution.py:42
  22.9 8.1 %collective-permute-start.20 = (bf16[512,384]{1,0:T(8,128)(2,1)}, bf16[512,384]{1,0:T(8,128)(2,1)S(1)}, u32[]{:S(2)}, u32[]{:S(2)}) collective-permute-start(bf16[512,384]{1,0:T(8,128)(2,1)} %collective-permute-done.10.refs_13_), channel_id=1, source_target_pairs={{0,1},{1,0},{2,3},{3,2},{4,5},{5,4},{6,7},{7,6},{8,9},{9,8},{10,11... | collective-permute-start | bytes 1179656 | tf_op jit(solution)/shard_map/ppermute | solution.py:42
  32.7 7.0 %collective-permute-done.20.refs_23_ = bf16[512,384]{1,0:T(8,128)(2,1)S(1)} collective-permute-done((bf16[512,384]{1,0:T(8,128)(2,1)}, bf16[512,384]{1,0:T(8,128)(2,1)S(1)}, u32[]{:S(2)}, u32[]{:S(2)}) %collective-permute-start.20) | collective-permute-done | bytes 393248 | tf_op jit(solution)/shard_map/ppermute | solution.py:42
  42.9 6.6 %collective-permute-done.24.refs_27_ = bf16[512,384]{1,0:T(8,128)(2,1)S(1)} collective-permute-done((bf16[512,384]{1,0:T(8,128)(2,1)S(1)}, bf16[512,384]{1,0:T(8,128)(2,1)S(1)}, u32[]{:S(2)}, u32[]{:S(2)}) %collective-permute-start.24) | collective-permute-done | bytes 393248 | tf_op jit(solution)/shard_map/ppermute | solution.py:42
  52.7 15.4 %all-gather.5.cloned.1.call-done = bf16[2048,256]{1,0:T(8,128)(2,1)} async-done(((bf16[512,256]{1,0:T(8,128)(2,1)}), bf16[2048,256]{1,0:T(8,128)(2,1)}) %all-gather.5.cloned.1.call-update) | async-done | bytes 1048592 | tf_op jit(solution)/shard_map/all_gather | solution.py:183
  122.0 9.5 %pieces_forward.1 = (bf16[128,2048]{1,0:T(8,128)(2,1)S(1)}, bf16[128,1024]{1,0:T(8,128)(2,1)S(1)}, bf16[2048,3072]{1,0:T(8,128)(2,1)}) custom-call(s32[2]{0:T(128)S(1)} %pad_add_fusion.refs_0_, bf16[128,2048]{1,0:T(8,128)(2,1)S(1)} %fusion.2.refs_1_, bf16[512,3072]{1,0:T(8,128)(2,1)} %refs_2_.3, bf16[512,384]{1,0:T(8,128)(2,1)} %copy-done.43, ...), custom_call_target="tpu_custom_call" | custom-call | flops 1610612736 | bytes 25165824 | tf_op jit(solution)/shard_map/pieces_forward/pallas_call | solution.py:153
  152.9 14.0 %attend.1 = (bf16[128,2048]{1,0:T(8,128)(2,1)S(1)}, f32[128,2048]{1,0:T(8,128)S(1)}, f32[8,1,512]{2,1,0:T(1,128)S(1)}) custom-call(bf16[128,2048]{1,0:T(8,128)(2,1)S(1)} %get-tuple-element.51.q_ref.refs_0_, bf16[1024,1024]{1,0:T(8,128)(2,1)S(1)} %constant_dynamic-update-slice_fusion.1.k_ref.v_ref.refs_3_.refs_4_, ...), custom_call_target="tpu_custom_call" | custom-call | flops 1073741824 | bytes 2097152 | tf_op jit(solution)/shard_map/attend/pallas_call | solution.py:520
  176.5 30.7 %collective-permute-done.36 = bf16[128,2048]{1,0:T(8,128)(2,1)} collective-permute-done((bf16[128,2048]{1,0:T(8,128)(2,1)S(1)}, bf16[128,2048]{1,0:T(8,128)(2,1)}, u32[]{:S(2)}, u32[]{:S(2)}) %collective-permute-start.36) | collective-permute-done | bytes 524320 | tf_op jit(solution)/shard_map/ppermute | solution.py:42
  210.6 6.6 %down_back.3.act_ref = f32[256,2048]{1,0:T(8,128)} custom-call(bf16[256,2048]{1,0:T(8,128)(2,1)S(1)} %constant_dynamic-update-slice_fusion.12.x_ref.grad_b, bf16[3,2048,2048]{2,1,0:T(8,128)(2,1)} %bitcast.88), custom_call_target="tpu_custom_call" | custom-call | flops 2147483648 | bytes 8388608 | tf_op jit(solution)/shard_map/down_back/pallas_call | solution.py:748
  217.1 6.7 %down_back.2.act_ref = f32[256,2048]{1,0:T(8,128)} custom-call(bf16[256,2048]{1,0:T(8,128)(2,1)S(1)} %constant_dynamic-update-slice_fusion.8.x_ref.grad_a, bf16[3,2048,2048]{2,1,0:T(8,128)(2,1)} %bitcast.89), custom_call_target="tpu_custom_call" | custom-call | flops 2147483648 | bytes 8388608 | tf_op jit(solution)/shard_map/down_back/pallas_call | solution.py:748
  224.0 14.1 %ffn_middle.2 = (bf16[3,256,2048]{2,1,0:T(8,128)(2,1)}, f32[256,2048]{1,0:T(8,128)S(1)}) custom-call(bf16[256,2048]{1,0:T(8,128)(2,1)S(1)} %constant_dynamic-update-slice_fusion.6.x_ref.in_a, f32[256,2048]{1,0:T(8,128)} %down_back.2.act_ref, bf16[3,2048,2048]{2,1,0:T(8,128)(2,1)} %bitcast.90), custom_call_target="tpu_custom_call" | custom-call | flops 8589934592 | bytes 16777216 | tf_op jit(solution)/shard_map/ffn_middle/pallas_call | solution.py:677
  239.5 14.2 %ffn_middle.3 = (bf16[3,256,2048]{2,1,0:T(8,128)(2,1)}, f32[256,2048]{1,0:T(8,128)S(1)}) custom-call(bf16[256,2048]{1,0:T(8,128)(2,1)S(1)} %constant_dynamic-update-slice_fusion.10.x_ref.in_b, f32[256,2048]{1,0:T(8,128)} %down_back.3.act_ref, bf16[3,2048,2048]{2,1,0:T(8,128)(2,1)} %bitcast.91), custom_call_target="tpu_custom_call" | custom-call | flops 8589934592 | bytes 16777216 | tf_op jit(solution)/shard_map/ffn_middle/pallas_call | solution.py:677
  253.7 21.9 %ffn_products.1 = bf16[3,2048,2048]{2,1,0:T(8,128)(2,1)} custom-call(bf16[256,2048]{1,0:T(8,128)(2,1)S(1)} %constant_dynamic-update-slice_fusion.6.x_ref.in_a, bf16[256,2048]{1,0:T(8,128)(2,1)S(1)} %constant_dynamic-update-slice_fusion.10.x_ref.in_b, bf16[256,2048]{1,0:T(8,128)(2,1)S(1)} %constant_dynamic-update-slice_fusion.8.x_ref.grad_a, ...), custom_call_target="tpu_custom_call" | custom-call | flops 12884901888 | bytes 25165824 | tf_op jit(solution)/shard_map/ffn_products/pallas_call | solution.py:724
  281.3 10.7 %collective-permute-done.41 = bf16[128,2048]{1,0:T(8,128)(2,1)S(1)} collective-permute-done((bf16[128,2048]{1,0:T(8,128)(2,1)S(1)}, bf16[128,2048]{1,0:T(8,128)(2,1)S(1)}, u32[]{:S(2)}, u32[]{:S(2)}) %collective-permute-start.41) | collective-permute-done | bytes 524320 | tf_op jit(solution)/shard_map/ppermute | solution.py:42
  302.8 14.1 %collective-permute-done.42 = bf16[128,2048]{1,0:T(8,128)(2,1)S(1)} collective-permute-done((bf16[128,2048]{1,0:T(8,128)(2,1)}, bf16[128,2048]{1,0:T(8,128)(2,1)S(1)}, u32[]{:S(2)}, u32[]{:S(2)}) %collective-permute-start.42) | collective-permute-done | bytes 524320 | tf_op jit(solution)/shard_map/ppermute | solution.py:42
  326.6 6.6 %all-to-all-start = ((bf16[128,4,512]{0,2,1:T(8,128)(2,1)}), bf16[128,4,512]{0,2,1:T(8,128)(2,1)}, u32[]{:S(2)}, u32[]{:S(2)}) async-start(bf16[128,4,512]{0,2,1:T(8,128)(2,1)} %bitcast.102), calls=%async_computation | async-start | bytes 1048576 | tf_op jit(solution)/shard_map/all_to_all | solution.py:412
  339.1 20.3 %attend_back.1 = (bf16[128,2048]{1,0:T(8,128)(2,1)S(1)}, bf16[2,512,512]{2,1,0:T(8,128)(2,1)S(1)}, bf16[2,512,512]{2,1,0:T(8,128)(2,1)}) custom-call(bf16[128,2048]{1,0:T(8,128)(2,1)S(1)} %copy-done.26, bf16[128,2048]{1,0:T(8,128)(2,1)S(1)} %out_back.1.refs_1_, f32[128,2048]{1,0:T(8,128)S(1)} %copy-done.28, bf16[1024,1024]{1,0:T(8,128)(2,1)} %copy-done.24, ...), custom_call_target="tpu_custom_call" | custom-call | flops 2684354560 | bytes 4194304 | tf_op jit(solution)/shard_map/attend_back/pallas_call | solution.py:594
  374.1 8.0 %down_forward.1 = f32[512,2048]{1,0:T(8,128)S(1)} custom-call(bf16[3,256,2048]{2,1,0:T(8,128)(2,1)} %get-tuple-element.61.a_ref.right_a, bf16[3,256,2048]{2,1,0:T(8,128)(2,1)} %get-tuple-element.64.b_ref.right_b, bf16[3,2048,2048]{2,1,0:T(8,128)(2,1)} %bitcast.92), custom_call_target="tpu_custom_call" | custom-call | flops 4294967296 | bytes 8388608 | tf_op jit(solution)/shard_map/down_forward/pallas_call | solution.py:778
  382.2 36.6 %collective-permute-done.51 = bf16[128,2048]{1,0:T(8,128)(2,1)} collective-permute-done((bf16[128,2048]{1,0:T(8,128)(2,1)S(1)}, bf16[128,2048]{1,0:T(8,128)(2,1)}, u32[]{:S(2)}, u32[]{:S(2)}) %collective-permute-start.51) | collective-permute-done | bytes 524320 | tf_op jit(solution)/shard_map/ppermute | solution.py:42
  418.8 21.3 %collective-permute-start.52 = (bf16[128,2048]{1,0:T(8,128)(2,1)}, bf16[128,2048]{1,0:T(8,128)(2,1)}, u32[]{:S(2)}, u32[]{:S(2)}) collective-permute-start(bf16[128,2048]{1,0:T(8,128)(2,1)} %collective-permute-done.51), channel_id=1, source_target_pairs={{0,1},{1,0},{2,3},{3,2},{4,5},{5,4},{6,7},{7,6},{8,9},{9,8},{10,11... | collective-permute-start | bytes 1572872 | tf_op jit(solution)/shard_map/ppermute | solution.py:42
  461.3 9.3 %one_back.1 = (f32[128,2048]{1,0:T(8,128)}, f32[1,2048]{1,0:T(1,128)S(1)}) custom-call(bf16[128,2048]{1,0:T(8,128)(2,1)S(1)} %copy-done.8, bf16[128,1024]{1,0:T(8,128)(2,1)S(1)} %copy-done.3, bf16[2048,3072]{1,0:T(8,128)(2,1)} %get-tuple-element.74.w_ref, bf16[128,2048]{1,0:T(8,128)(2,1)S(1)} %bitcast.81, f32[1,2048]{1,0:T(1,128)S(1)} %bitcast.87, ...), custom_call_target="tpu_custom_call" | custom-call | flops 1610612736 | bytes 12582912 | tf_op jit(solution)/shard_map/one_back/pallas_call | solution.py:320
  491.0 25.6 %collective-permute-done.58 = f32[2,2048]{1,0:T(2,128)S(1)} collective-permute-done((f32[2,2048]{1,0:T(2,128)S(1)}, f32[2,2048]{1,0:T(2,128)S(1)}, u32[]{:S(2)}, u32[]{:S(2)}) %collective-permute-start.58) | collective-permute-done | bytes 16416 | tf_op jit(solution)/shard_map/ppermute | solution.py:42
  552.6 11.1 %collective-permute-done.56 = bf16[64,4096]{1,0:T(8,128)(2,1)S(1)} collective-permute-done((bf16[64,4096]{1,0:T(8,128)(2,1)S(1)}, bf16[64,4096]{1,0:T(8,128)(2,1)S(1)}, u32[]{:S(2)}, u32[]{:S(2)}) %collective-permute-start.56) | collective-permute-done | bytes 524320 | tf_op jit(solution)/shard_map/ppermute | solution.py:42
  563.7 9.2 %collective-permute-done.55 = bf16[64,4096]{1,0:T(8,128)(2,1)S(1)} collective-permute-done((bf16[64,4096]{1,0:T(8,128)(2,1)S(1)}, bf16[64,4096]{1,0:T(8,128)(2,1)S(1)}, u32[]{:S(2)}, u32[]{:S(2)}) %collective-permute-start.55) | collective-permute-done | bytes 524320 | tf_op jit(solution)/shard_map/ppermute | solution.py:42
  (348 shorter events, 237.2 us)
Async XLA Ops:
  7.2 60.9 %all-gather.5.cloned.1.call-start = ((), (), s32[]{:S(2)}) async-start(), calls=%async_computation.6 | async-start | bytes 1310720 | tf_op jit(solution)/shard_map/all_gather | solution.py:183
  39.7 129.5 %all-gather.7.cloned.1.call-start = ((), (), s32[]{:S(2)}) async-start(), calls=%async_computation.7 | async-start | bytes 7077888 | tf_op jit(solution)/shard_map/all_gather | solution.py:190
  70.3 504.8 %reduce-scatter.2.cloned.1.call-start = ((), (), s32[]{:S(2)}) async-start(), calls=%async_computation.5 | async-start | bytes 28311552 | tf_op jit(solution)/shard_map/reduce_scatter | solution.py:958
  93.1 23.6 %collective-permute-start.15 = (bf16[512,384]{1,0:T(8,128)(2,1)S(1)}, bf16[512,384]{1,0:T(8,128)(2,1)S(1)}, u32[]{:S(2)}, u32[]{:S(2)}) collective-permute-start(bf16[512,384]{1,0:T(8,128)(2,1)S(1)} %collective-permute-done.14.refs_17_), channel_id=1, source_target_pairs={{0,4},{4,0},{8,12},{12,8},{16,20},{20,16},{24,28},{28,24},{1,5},{5... | collective-permute-start | bytes 1179656 | tf_op jit(solution)/shard_map/ppermute | solution.py:42
  148.2 28.3 %collective-permute-start.37 = (bf16[128,2048]{1,0:T(8,128)(2,1)S(1)}, bf16[128,2048]{1,0:T(8,128)(2,1)}, u32[]{:S(2)}, u32[]{:S(2)}) collective-permute-start(bf16[128,2048]{1,0:T(8,128)(2,1)S(1)} %bitcast.98), channel_id=1, source_target_pairs={{0,3},{1,2},{2,1},{3,0},{4,7},{5,6},{6,5},{7,4},{8,11},{9,10},{10,... | collective-permute-start | bytes 1572872 | tf_op jit(solution)/shard_map/ppermute | solution.py:42
  149.0 58.3 %collective-permute-start.36 = (bf16[128,2048]{1,0:T(8,128)(2,1)S(1)}, bf16[128,2048]{1,0:T(8,128)(2,1)}, u32[]{:S(2)}, u32[]{:S(2)}) collective-permute-start(bf16[128,2048]{1,0:T(8,128)(2,1)S(1)} %bitcast.99), channel_id=1, source_target_pairs={{0,2},{1,3},{2,0},{3,1},{4,6},{5,7},{6,4},{7,5},{8,10},{9,11},{10,... | collective-permute-start | bytes 1572872 | tf_op jit(solution)/shard_map/ppermute | solution.py:42
  149.4 57.9 %collective-permute-start.35 = (bf16[128,2048]{1,0:T(8,128)(2,1)S(1)}, bf16[128,2048]{1,0:T(8,128)(2,1)}, u32[]{:S(2)}, u32[]{:S(2)}) collective-permute-start(bf16[128,2048]{1,0:T(8,128)(2,1)S(1)} %bitcast.100), channel_id=1, source_target_pairs={{0,1},{1,0},{2,3},{3,2},{4,5},{5,4},{6,7},{7,6},{8,9},{9,8},{10,11... | collective-permute-start | bytes 1572872 | tf_op jit(solution)/shard_map/ppermute | solution.py:42
  175.7 48.1 %collective-permute-start.38 = (bf16[128,2048]{1,0:T(8,128)(2,1)S(1)}, bf16[128,2048]{1,0:T(8,128)(2,1)S(1)}, u32[]{:S(2)}, u32[]{:S(2)}) collective-permute-start(bf16[128,2048]{1,0:T(8,128)(2,1)S(1)} %get-tuple-element.57), channel_id=1, source_target_pairs={{0,3},{1,2},{2,1},{3,0},{4,7},{5,6},{6,5},{7,4},{8,11},{9,10},{10,... | collective-permute-start | bytes 1572872 | tf_op jit(solution)/shard_map/ppermute | solution.py:42
  176.5 47.4 %collective-permute-start.34 = (bf16[128,2048]{1,0:T(8,128)(2,1)S(1)}, bf16[128,2048]{1,0:T(8,128)(2,1)S(1)}, u32[]{:S(2)}, u32[]{:S(2)}) collective-permute-start(bf16[128,2048]{1,0:T(8,128)(2,1)S(1)} %get-tuple-element.57), channel_id=1, source_target_pairs={{0,1},{1,0},{2,3},{3,2},{4,5},{5,4},{6,7},{7,6},{8,9},{9,8},{10,11... | collective-permute-start | bytes 1572872 | tf_op jit(solution)/shard_map/ppermute | solution.py:42
  281.3 21.6 %collective-permute-start.40 = (bf16[128,2048]{1,0:T(8,128)(2,1)}, bf16[128,2048]{1,0:T(8,128)(2,1)S(1)}, u32[]{:S(2)}, u32[]{:S(2)}) collective-permute-start(bf16[128,2048]{1,0:T(8,128)(2,1)} %slice.257), channel_id=1, source_target_pairs={{0,1},{1,0},{2,3},{3,2},{4,5},{5,4},{6,7},{7,6},{8,9},{9,8},{10,11... | collective-permute-start | bytes 1572872 | tf_op jit(solution)/shard_map/ppermute | solution.py:42
  292.9 24.1 %collective-permute-start.42 = (bf16[128,2048]{1,0:T(8,128)(2,1)}, bf16[128,2048]{1,0:T(8,128)(2,1)S(1)}, u32[]{:S(2)}, u32[]{:S(2)}) collective-permute-start(bf16[128,2048]{1,0:T(8,128)(2,1)} %add_convert_fusion.5), channel_id=1, source_target_pairs={{0,3},{1,2},{2,1},{3,0},{4,7},{5,6},{6,5},{7,4},{8,11},{9,10},{10,... | collective-permute-start | bytes 1572872 | tf_op jit(solution)/shard_map/ppermute | solution.py:42
  298.3 28.2 %all-to-all-start.1 = ((bf16[128,4,512]{0,2,1:T(8,128)(2,1)}), bf16[128,4,512]{0,2,1:T(8,128)(2,1)}, u32[]{:S(2)}, u32[]{:S(2)}) async-start(bf16[128,4,512]{0,2,1:T(8,128)(2,1)} %bitcast.27), calls=%async_computation.1 | async-start | bytes 1048576 | tf_op jit(solution)/shard_map/all_to_all | solution.py:412
  326.6 34.7 %all-to-all-start = ((bf16[128,4,512]{0,2,1:T(8,128)(2,1)}), bf16[128,4,512]{0,2,1:T(8,128)(2,1)}, u32[]{:S(2)}, u32[]{:S(2)}) async-start(bf16[128,4,512]{0,2,1:T(8,128)(2,1)} %bitcast.102), calls=%async_computation | async-start | bytes 1048576 | tf_op jit(solution)/shard_map/all_to_all | solution.py:412
  361.2 78.9 %collective-permute-start.43 = (bf16[2,512,512]{2,1,0:T(8,128)(2,1)}, bf16[2,512,512]{2,1,0:T(8,128)(2,1)}, u32[]{:S(2)}, u32[]{:S(2)}) collective-permute-start(bf16[2,512,512]{2,1,0:T(8,128)(2,1)} %get-tuple-element.70), channel_id=1, source_target_pairs={{0,4},{4,0},{8,12},{12,8},{16,20},{20,16},{24,28},{28,24},{1,5},{5... | collective-permute-start | bytes 3145736 | tf_op jit(solution)/shard_map/ppermute | solution.py:42
  362.8 117.3 %all-to-all-start.2 = ((bf16[4,128,2048]{2,1,0:T(8,128)(2,1)}), bf16[4,128,2048]{2,1,0:T(8,128)(2,1)}, u32[]{:S(2)}, u32[]{:S(2)}) async-start(bf16[4,128,2048]{2,1,0:T(8,128)(2,1)} %broadcast_in_dim.116), calls=%async_computation.2 | async-start | bytes 4194304 | tf_op jit(solution)/shard_map/all_to_all | solution.py:408
  368.1 50.7 %collective-permute-start.51 = (bf16[128,2048]{1,0:T(8,128)(2,1)S(1)}, bf16[128,2048]{1,0:T(8,128)(2,1)}, u32[]{:S(2)}, u32[]{:S(2)}) collective-permute-start(bf16[128,2048]{1,0:T(8,128)(2,1)S(1)} %copy-done.8), channel_id=1, source_target_pairs={{0,3},{1,2},{2,1},{3,0},{4,7},{5,6},{6,5},{7,4},{8,11},{9,10},{10,... | collective-permute-start | bytes 1572872 | tf_op jit(solution)/shard_map/ppermute | solution.py:42
  382.1 78.3 %collective-permute-start.50 = (bf16[128,2048]{1,0:T(8,128)(2,1)S(1)}, bf16[128,2048]{1,0:T(8,128)(2,1)}, u32[]{:S(2)}, u32[]{:S(2)}) collective-permute-start(bf16[128,2048]{1,0:T(8,128)(2,1)S(1)} %copy-done.8), channel_id=1, source_target_pairs={{0,1},{1,0},{2,3},{3,2},{4,5},{5,4},{6,7},{7,6},{8,9},{9,8},{10,11... | collective-permute-start | bytes 1572872 | tf_op jit(solution)/shard_map/ppermute | solution.py:42
  418.8 41.6 %collective-permute-start.52 = (bf16[128,2048]{1,0:T(8,128)(2,1)}, bf16[128,2048]{1,0:T(8,128)(2,1)}, u32[]{:S(2)}, u32[]{:S(2)}) collective-permute-start(bf16[128,2048]{1,0:T(8,128)(2,1)} %collective-permute-done.51), channel_id=1, source_target_pairs={{0,1},{1,0},{2,3},{3,2},{4,5},{5,4},{6,7},{7,6},{8,9},{9,8},{10,11... | collective-permute-start | bytes 1572872 | tf_op jit(solution)/shard_map/ppermute | solution.py:42
  475.1 61.6 %collective-permute-start.47 = (bf16[128,2048]{1,0:T(8,128)(2,1)}, bf16[128,2048]{1,0:T(8,128)(2,1)}, u32[]{:S(2)}, u32[]{:S(2)}) collective-permute-start(bf16[128,2048]{1,0:T(8,128)(2,1)} %slice.255), channel_id=1, source_target_pairs={{0,1},{1,0},{2,3},{3,2},{4,5},{5,4},{6,7},{7,6},{8,9},{9,8},{10,11... | collective-permute-start | bytes 1572872 | tf_op jit(solution)/shard_map/ppermute | solution.py:42
  476.9 40.0 %collective-permute-start.48 = (bf16[128,2048]{1,0:T(8,128)(2,1)}, bf16[128,2048]{1,0:T(8,128)(2,1)}, u32[]{:S(2)}, u32[]{:S(2)}) collective-permute-start(bf16[128,2048]{1,0:T(8,128)(2,1)} %slice.254), channel_id=1, source_target_pairs={{0,1},{1,0},{2,3},{3,2},{4,5},{5,4},{6,7},{7,6},{8,9},{9,8},{10,11... | collective-permute-start | bytes 1572872 | tf_op jit(solution)/shard_map/ppermute | solution.py:42
  481.3 47.2 %all-to-all-start.3 = ((bf16[4,128,1024]{2,1,0:T(8,128)(2,1)}), bf16[4,128,1024]{2,1,0:T(8,128)(2,1)S(1)}, u32[]{:S(2)}, u32[]{:S(2)}) async-start(bf16[4,128,1024]{2,1,0:T(8,128)(2,1)} %broadcast_in_dim.117), calls=%async_computation.3 | async-start | bytes 2097152 | tf_op jit(solution)/shard_map/all_to_all | solution.py:408
  484.8 31.8 %collective-permute-start.58 = (f32[2,2048]{1,0:T(2,128)S(1)}, f32[2,2048]{1,0:T(2,128)S(1)}, u32[]{:S(2)}, u32[]{:S(2)}) collective-permute-start(f32[2,2048]{1,0:T(2,128)S(1)} %fusion.23), channel_id=1, source_target_pairs={{0,2},{1,3},{2,0},{3,1},{4,6},{5,7},{6,4},{7,5},{8,10},{9,11},{10,... | collective-permute-start | bytes 49160 | tf_op jit(solution)/shard_map/ppermute | solution.py:42
  549.5 23.5 %collective-permute-start.55 = (bf16[64,4096]{1,0:T(8,128)(2,1)S(1)}, bf16[64,4096]{1,0:T(8,128)(2,1)S(1)}, u32[]{:S(2)}, u32[]{:S(2)}) collective-permute-start(bf16[64,4096]{1,0:T(8,128)(2,1)S(1)} %get-tuple-element.108), channel_id=1, source_target_pairs={{0,16},{4,20},{8,24},{12,28},{16,0},{20,4},{24,8},{28,12},{1,17},{... | collective-permute-start | bytes 1572872 | tf_op jit(solution)/shard_map/ppermute | solution.py:42
  550.1 22.9 %collective-permute-start.54 = (bf16[64,4096]{1,0:T(8,128)(2,1)S(1)}, bf16[64,4096]{1,0:T(8,128)(2,1)S(1)}, u32[]{:S(2)}, u32[]{:S(2)}) collective-permute-start(bf16[64,4096]{1,0:T(8,128)(2,1)S(1)} %get-tuple-element.109), channel_id=1, source_target_pairs={{0,8},{4,12},{8,0},{12,4},{16,24},{20,28},{24,16},{28,20},{1,9},{5... | collective-permute-start | bytes 1572872 | tf_op jit(solution)/shard_map/ppermute | solution.py:42
  (105 other events, 1921.5 us)
Sparse Core Ops, SparseCore 0:
  39.9 28.1 all-gather.4
  70.5 57.1 all-gather.6
  275.8 155.7 reduce-scatter.1

commit v4 on v3

--- a/solution.py
+++ b/solution.py
@@ -15,6 +15,7 @@
 NORM_EPS = 1e-05
 ROPE_BASE = 500000.0
 FFN_TILE = 512
+KEY_CHUNK = 256
 
 
 BF = jnp.bfloat16
@@ -286,7 +287,7 @@
 
 
 def one_back_kernel(
-    query_ref, pair_ref, w_ref, hidden_ref, gain_ref, residual_ref, y_ref, term_ref
+    query_ref, pair_ref, w_ref, hidden_ref, gain_ref, residual_ref, y_ref
 ):
     step = pl.program_id(0)
     rows = w_ref.shape[0]
@@ -301,7 +302,6 @@
         inputs = hidden_ref[...].astype(F32)
         scale = norm_scale(inputs)
         unit = inputs * scale
-        term_ref[...] = jnp.sum(grad * unit, axis=0, keepdims=True)
         scaled = gain_ref[...] * grad
         y_ref[...] = residual_ref[...] + scale * (
             scaled - unit * jnp.mean(scaled * unit, axis=-1, keepdims=True)
@@ -320,10 +320,7 @@
     return pl.pallas_call(
         one_back_kernel,
         grid=(width // tile,),
-        out_shape=(
-            jax.ShapeDtypeStruct((rows, width), F32),
-            jax.ShapeDtypeStruct((1, width), F32),
-        ),
+        out_shape=jax.ShapeDtypeStruct((rows, width), F32),
         in_specs=[
             whole(query_part),
             whole(pair_part),
@@ -332,10 +329,7 @@
             whole(gain),
             whole(residual_grad),
         ],
-        out_specs=(
-            pl.BlockSpec((rows, width), lambda j: (0, 0)),
-            pl.BlockSpec((1, width), lambda j: (0, 0)),
-        ),
+        out_specs=pl.BlockSpec((rows, width), lambda j: (0, 0)),
         compiler_params=pltpu.CompilerParams(vmem_limit_bytes=24 << 20),
         cost_estimate=pl.CostEstimate(
             flops=2 * rows * width * columns,
@@ -358,11 +352,6 @@
 def fetch_rows(values):
     count = lax.axis_size("fsdp")
     return [values] + [swap(values, "fsdp", away) for away in range(1, count)]
-
-
-def halves_of(planes):
-    half = len(planes) // 2
-    return (jnp.concatenate(planes[:half], axis=0), jnp.concatenate(planes[half:], axis=0))
 
 
 def sum_rows(halves):
@@ -443,8 +432,7 @@
 def gather_keys(piece):
     same = [piece] + [swap(piece, "ctx", far) for far in range(2, lax.axis_size("ctx"), 2)]
     mine = jnp.concatenate(same, axis=0)
-    other = swap(mine, "ctx", 1)
-    return jnp.concatenate([mine, other], axis=0)
+    return mine, swap(mine, "ctx", 1)
 
 
 def sum_pairs(kept, sent, cosine, sine):
@@ -494,87 +482,110 @@
     return jnp.concatenate(tiles, axis=1)
 
 
-def attend_kernel(q_ref, k_ref, v_ref, key_ref, own_ref, rows_ref, attended_ref, log_ref):
+def key_chunks(refs, chunk):
+    first = 0
+    for k_ref, v_ref in refs:
+        for start in range(0, k_ref.shape[0], chunk):
+            at = slice(start, start + chunk)
+            yield first + start, k_ref.at[at, :], v_ref.at[at, :]
+        first += k_ref.shape[0]
+
+
+def masked_scores(keys, queries, key_ref, own_ref, start):
+    allowed = key_ref[start : start + keys.shape[0], :1] <= own_ref[...]
+    bias = jnp.where(allowed, 0.0, -1e30).astype(F32)
+    return nt(keys, queries) + jnp.concatenate([bias] * 4, axis=1)
+
+
+def attend_kernel(
+    chunk, q_ref, ka_ref, va_ref, kb_ref, vb_ref, key_ref, own_ref, rows_ref, attended_ref, log_ref
+):
     odd = pl.program_id(0) % 2
     rows = q_ref.shape[0]
     queries = split_heads(q_ref[...])
-    keys, values = doubled(k_ref[...], odd), doubled(v_ref[...], odd)
-    allowed = key_ref[:, :1] <= own_ref[...]
-    bias = jnp.where(allowed, 0.0, -1e30).astype(F32)
-    bias = jnp.concatenate([bias] * 4, axis=1)
-    scores = nt(keys, queries) + bias
-    top = jnp.max(scores, axis=0, keepdims=True)
-    weights = jnp.exp(scores - top)
-    total = jnp.sum(weights, axis=0, keepdims=True)
-    summed = tn(weights.astype(BF), values)
+    parts = list(key_chunks(((ka_ref, va_ref), (kb_ref, vb_ref)), chunk))
+    scores = [
+        masked_scores(doubled(k_ref[...], odd), queries, key_ref, own_ref, start)
+        for start, k_ref, _ in parts
+    ]
+    top = jnp.max(scores[0], axis=0, keepdims=True)
+    for score in scores[1:]:
+        top = jnp.maximum(top, jnp.max(score, axis=0, keepdims=True))
+    total = jnp.zeros_like(top)
+    summed = jnp.zeros((4 * rows, 128), F32)
+    for score, (_, _, v_ref) in zip(scores, parts):
+        weights = jnp.exp(score - top)
+        total += jnp.sum(weights, axis=0, keepdims=True)
+        summed += tn(weights.astype(BF), doubled(v_ref[...], odd))
     log_ref[0] = top + jnp.log(total)
     attended = merge_heads(summed / jnp.transpose(jnp.broadcast_to(total, (128, 4 * rows))))
     attended_ref[...] = attended
     rows_ref[...] = attended.astype(BF)
 
 
+def key_specs(parts):
+    tiles = parts[0].shape[1] // 256
+    specs, arrays = [], []
+    for part in parts:
+        specs.append(pl.BlockSpec((part.shape[0], 128), lambda g: (0, g // 2)))
+        specs.append(pl.BlockSpec((part.shape[0], 128), lambda g: (0, tiles + g // 2)))
+        arrays += [part, part]
+    return specs, arrays
+
+
 def attend(queries, keys_values, key_anchor, own_anchor):
     rows, width = queries.shape
-    count, both = keys_values.shape
-    tiles = both // 256
+    count = key_anchor.shape[0]
+    specs, arrays = key_specs(keys_values)
+    wide = pl.BlockSpec((rows, 256), lambda g: (0, g))
     return pl.pallas_call(
-        attend_kernel,
+        lambda *refs: attend_kernel(KEY_CHUNK, *refs),
         grid=(KV,),
         out_shape=(
             jax.ShapeDtypeStruct((rows, width), BF),
             jax.ShapeDtypeStruct((rows, width), F32),
             jax.ShapeDtypeStruct((KV, 1, 4 * rows), F32),
         ),
-        in_specs=[
-            pl.BlockSpec((rows, 256), lambda g: (0, g)),
-            pl.BlockSpec((count, 128), lambda g: (0, g // 2)),
-            pl.BlockSpec((count, 128), lambda g: (0, tiles + g // 2)),
+        in_specs=[wide]
+        + specs
+        + [
             pl.BlockSpec((count, 128), lambda g: (0, 0)),
             pl.BlockSpec((1, rows), lambda g: (0, 0)),
         ],
-        out_specs=(
-            pl.BlockSpec((rows, 256), lambda g: (0, g)),
-            pl.BlockSpec((rows, 256), lambda g: (0, g)),
-            pl.BlockSpec((1, 1, 4 * rows), lambda g: (g, 0, 0)),
-        ),
+        out_specs=(wide, wide, pl.BlockSpec((1, 1, 4 * rows), lambda g: (g, 0, 0))),
         compiler_params=pltpu.CompilerParams(vmem_limit_bytes=48 << 20),
         cost_estimate=pl.CostEstimate(
             flops=4 * rows * width * count,
-            bytes_accessed=2 * count * both,
+            bytes_accessed=4 * count * KV * HD,
             transcendentals=rows * H * count,
         ),
         name="attend",
-    )(queries, keys_values, keys_values, key_anchor, own_anchor)
+    )(queries, *arrays, key_anchor, own_anchor)
 
 
 def attend_back_kernel(
-    chunk, q_ref, grad_ref, attended_ref, k_ref, v_ref, key_ref, own_ref, log_ref, cos_ref, sin_ref,
-    dq_ref, kept_ref, sent_ref,
+    chunk, q_ref, grad_ref, attended_ref, ka_ref, va_ref, kb_ref, vb_ref, key_ref, own_ref, log_ref,
+    cos_ref, sin_ref, dq_ref, kept_ref, sent_ref,
 ):
     odd = pl.program_id(0) % 2
     rows = q_ref.shape[0]
-    count = k_ref.shape[0]
+    half = ka_ref.shape[0]
     queries, grads = split_heads(q_ref[...]), split_heads(grad_ref[...])
     product = grads.astype(F32) * split_heads(attended_ref[...])
     delta = jnp.sum(jnp.transpose(product), axis=0, keepdims=True)
     log_total = log_ref[0]
     total = jnp.zeros((4 * rows, 128), F32)
     keep = half_mask((chunk, 128)) == (odd == 0)
-    for start in range(0, count, chunk):
-        at = slice(start, start + chunk)
-        keys, values = doubled(k_ref[at, :], odd), doubled(v_ref[at, :], odd)
-        allowed = key_ref[at, :1] <= own_ref[...]
-        bias = jnp.where(allowed, 0.0, -1e30).astype(F32)
-        bias = jnp.concatenate([bias] * 4, axis=1)
-        probs = jnp.exp(nt(keys, queries) + bias - log_total)
+    for start, k_ref, v_ref in key_chunks(((ka_ref, va_ref), (kb_ref, vb_ref)), chunk):
+        keys, values = doubled(k_ref[...], odd), doubled(v_ref[...], odd)
+        scores = masked_scores(keys, queries, key_ref, own_ref, start)
+        probs = jnp.exp(scores - log_total)
         value_grad = nn(probs.astype(BF), grads)
         score_grad = (probs * (nt(values, grads) - delta)).astype(BF)
         key_grad = nn(score_grad, queries)
         total += tn(score_grad, keys)
-        far = start >= count // 2
-        out_ref, at = (sent_ref if far else kept_ref), slice(
-            start - far * (count // 2), start - far * (count // 2) + chunk
-        )
+        out_ref = kept_ref if start < half else sent_ref
+        at = slice(start % half, start % half + chunk)
         for part, value in enumerate((key_grad, value_grad)):
             value = (value + pltpu.roll(value, HD, 1)).astype(BF)
             out_ref[part, at, :] = jnp.where(keep, value, out_ref[part, at, :])
@@ -587,43 +598,37 @@
 
 def attend_back(queries, grads, attended, keys_values, key_anchor, own_anchor, logs, cosine, sine):
     rows, width = queries.shape
-    count, both = keys_values.shape
-    tiles = both // 256
+    count = key_anchor.shape[0]
+    specs, arrays = key_specs(keys_values)
     wide = pl.BlockSpec((rows, 256), lambda g: (0, g))
     small = pl.BlockSpec((rows, 128), lambda g: (0, 0))
+    pair = pl.BlockSpec((2, count // 2, 128), lambda g: (0, 0, g // 2))
     return pl.pallas_call(
-        lambda *refs: attend_back_kernel(256, *refs),
+        lambda *refs: attend_back_kernel(KEY_CHUNK, *refs),
         grid=(KV,),
         out_shape=(
             jax.ShapeDtypeStruct((rows, width), BF),
-            jax.ShapeDtypeStruct((2, count // 2, both // 2), BF),
-            jax.ShapeDtypeStruct((2, count // 2, both // 2), BF),
-        ),
-        in_specs=[
-            wide,
-            wide,
-            wide,
-            pl.BlockSpec((count, 128), lambda g: (0, g // 2)),
-            pl.BlockSpec((count, 128), lambda g: (0, tiles + g // 2)),
+            jax.ShapeDtypeStruct((2, count // 2, KV * HD), BF),
+            jax.ShapeDtypeStruct((2, count // 2, KV * HD), BF),
+        ),
+        in_specs=[wide, wide, wide]
+        + specs
+        + [
             pl.BlockSpec((count, 128), lambda g: (0, 0)),
             pl.BlockSpec((1, rows), lambda g: (0, 0)),
             pl.BlockSpec((1, 1, 4 * rows), lambda g: (g, 0, 0)),
             small,
             small,
         ],
-        out_specs=(
-            wide,
-            pl.BlockSpec((2, count // 2, 128), lambda g: (0, 0, g // 2)),
-            pl.BlockSpec((2, count // 2, 128), lambda g: (0, 0, g // 2)),
-        ),
+        out_specs=(wide, pair, pair),
         compiler_params=pltpu.CompilerParams(vmem_limit_bytes=48 << 20),
         cost_estimate=pl.CostEstimate(
             flops=10 * rows * width * count,
-            bytes_accessed=4 * count * both,
+            bytes_accessed=8 * count * KV * HD,
             transcendentals=rows * H * count,
         ),
         name="attend_back",
-    )(queries, grads, attended, keys_values, keys_values, key_anchor, own_anchor, logs, cosine, sine)
+    )(queries, grads, attended, *arrays, key_anchor, own_anchor, logs, cosine, sine)
 
 
 def pair_turn_kernel(own_ref, *refs):
@@ -648,10 +653,20 @@
     )(own, *got, cosine, sine)
 
 
-def ffn_kernel(x_ref, act_ref, w_ref, out_ref, sum_ref):
+def join_rows(x_buf, refs):
+    @pl.when((pl.program_id(0) == 0))
+    def _():
+        rows = refs[0].shape[0]
+        for i, ref in enumerate(refs):
+            x_buf[i * rows : (i + 1) * rows] = ref[...]
+
+
+def ffn_kernel(count, *refs):
+    rows_refs, (act_ref, w_ref, out_ref, sum_ref, x_buf) = refs[:count], refs[count:]
+    join_rows(x_buf, rows_refs)
     step = pl.program_id(0)
     gate_w, up_w = w_ref[0], w_ref[1]
-    x = x_ref[...]
+    x = x_buf[...]
     gate, up = nn(x, gate_w), nn(x, up_w)
     act_grad = act_ref[...]
     sig = jax.nn.sigmoid(gate)
@@ -670,26 +685,28 @@
         sum_ref[...] += part
 
 
-def ffn_middle(rows_in, act_grad, weights):
-    rows, width = rows_in.shape
+def ffn_middle(blocks, act_grad, half, weights):
+    width = blocks[0].shape[1]
+    rows = blocks[0].shape[0] * len(blocks)
     hidden = weights.shape[2]
     tile = FFN_TILE
     return pl.pallas_call(
-        ffn_kernel,
+        lambda *refs: ffn_kernel(len(blocks), *refs),
         grid=(hidden // tile,),
         out_shape=(
             pltpu.HBM((3, rows, hidden), BF),
             jax.ShapeDtypeStruct((rows, width), F32),
         ),
-        in_specs=[
-            pl.BlockSpec((rows, width), lambda j: (0, 0)),
-            pl.BlockSpec((rows, tile), lambda j: (0, j)),
+        in_specs=[pl.BlockSpec(block.shape, lambda j: (0, 0)) for block in blocks]
+        + [
+            pl.BlockSpec((rows, tile), lambda j: (half, j)),
             pl.BlockSpec((2, width, tile), lambda j: (0, 0, j)),
         ],
         out_specs=(
             pl.BlockSpec((3, rows, tile), lambda j: (0, 0, j)),
             pl.BlockSpec((rows, width), lambda j: (0, 0)),
         ),
+        scratch_shapes=[pltpu.VMEM((rows, width), BF)],
         compiler_params=pltpu.CompilerParams(vmem_limit_bytes=40 << 20),
         cost_estimate=pl.CostEstimate(
             flops=8 * rows * width * hidden,
@@ -697,39 +714,46 @@
             transcendentals=rows * hidden,
         ),
         name="ffn_middle",
-    )(rows_in, act_grad, weights)
-
-
-def products_kernel(in_a, in_b, grad_a, grad_b, right_a, right_b, out_ref):
-    def emit(left_a, left_b):
-        out_ref[0] = (tn(left_a[...], right_a[0]) + tn(left_b[...], right_b[0])).astype(BF)
+    )(*blocks, act_grad, weights)
+
+
+def products_kernel(count, *refs):
+    in_refs, grad_refs = refs[:count], refs[count : 2 * count]
+    right_a, right_b, out_ref = refs[2 * count :]
+    half = count // 2
+
+    def emit(lefts):
+        left_a = jnp.concatenate([ref[...] for ref in lefts[:half]], axis=0)
+        left_b = jnp.concatenate([ref[...] for ref in lefts[half:]], axis=0)
+        out_ref[0] = (tn(left_a, right_a[0]) + tn(left_b, right_b[0])).astype(BF)
 
     @pl.when(pl.program_id(0) < 2)
     def _():
-        emit(in_a, in_b)
+        emit(in_refs)
 
     @pl.when(pl.program_id(0) == 2)
     def _():
-        emit(grad_a, grad_b)
+        emit(grad_refs)
 
 
 def ffn_products(rows_in, rows_out, parts):
+    count = len(rows_in)
     rows, width = rows_in[0].shape
     hidden = parts[0].shape[2]
     tile = FFN_TILE
     last = width // tile - 1
     left = pl.BlockSpec((rows, tile), lambda k, i: (0, jnp.where(k < 2, i, last)))
     grad = pl.BlockSpec((rows, tile), lambda k, i: (0, jnp.where(k == 2, i, 0)))
-    right = pl.BlockSpec((1, rows, hidden), lambda k, i: (k, 0, 0))
+    right = pl.BlockSpec((1, rows * count // 2, hidden), lambda k, i: (k, 0, 0))
     return pl.pallas_call(
-        products_kernel,
+        lambda *refs: products_kernel(count, *refs),
         grid=(3, width // tile),
         out_shape=pltpu.HBM((3, width, hidden), BF),
-        in_specs=[left, left, grad, grad, right, right],
+        in_specs=[left] * count + [grad] * count + [right, right],
         out_specs=pl.BlockSpec((1, tile, hidden), lambda k, i: (k, i, 0)),
         compiler_params=pltpu.CompilerParams(vmem_limit_bytes=32 << 20),
         cost_estimate=pl.CostEstimate(
-            flops=12 * rows * width * hidden,
+            flops=6 * count * rows * width * hidden,
             bytes_accessed=6 * width * hidden,
             transcendentals=0,
         ),
@@ -737,23 +761,25 @@
     )(*rows_in, *rows_out, *parts)
 
 
-def simple_kernel(x_ref, w_ref, y_ref):
-    y_ref[...] = nn(x_ref[...], w_ref[0])
-
-
-def down_back(x, weights):
-    rows, width = x.shape
+def down_back_kernel(count, *refs):
+    rows_refs, (w_ref, y_ref, x_buf) = refs[:count], refs[count:]
+    join_rows(x_buf, rows_refs)
+    y_ref[...] = nn(x_buf[...], w_ref[0])
+
+
+def down_back(blocks, weights):
+    width = blocks[0].shape[1]
+    rows = blocks[0].shape[0] * len(blocks)
     hidden = weights.shape[2]
     tile = FFN_TILE
     return pl.pallas_call(
-        simple_kernel,
+        lambda *refs: down_back_kernel(len(blocks), *refs),
         grid=(hidden // tile,),
         out_shape=pltpu.HBM((rows, hidden), F32),
-        in_specs=[
-            pl.BlockSpec((rows, width), lambda j: (0, 0)),
-            pl.BlockSpec((1, width, tile), lambda j: (2, 0, j)),
-        ],
+        in_specs=[pl.BlockSpec(block.shape, lambda j: (0, 0)) for block in blocks]
+        + [pl.BlockSpec((1, width, tile), lambda j: (2, 0, j))],
         out_specs=pl.BlockSpec((rows, tile), lambda j: (0, j)),
+        scratch_shapes=[pltpu.VMEM((rows, width), BF)],
         compiler_params=pltpu.CompilerParams(vmem_limit_bytes=24 << 20),
         cost_estimate=pl.CostEstimate(
             flops=2 * rows * width * hidden,
@@ -761,7 +787,7 @@
             transcendentals=0,
         ),
         name="down_back",
-    )(x, weights)
+    )(*blocks, weights)
 
 
 def down_kernel(a_ref, b_ref, w_ref, y_ref):
@@ -807,7 +833,7 @@
         column += width
     if terms:
         tall = jnp.concatenate(
-            [jnp.broadcast_to(term[...], (64, term.shape[1])) for term in terms], axis=0
+            [jnp.broadcast_to(term[...], (128, term.shape[1])) for term in terms], axis=0
         )
         part = jnp.transpose(tall).astype(BF)
         kept_ref[0, :, column:] = jnp.where(own, part[:half], part[half:])
@@ -819,7 +845,7 @@
     pairs = ctx_count // 2
     rows, width = lefts[0].shape
     height = width // ctx_count
-    columns = sum(right.shape[1] for right in rights) + 64 * len(terms)
+    columns = sum(right.shape[1] for right in rights) + 128 * len(terms)
 
     def place(j, ids_ref):
         return (0, (ids_ref[0] // 2) ^ j)
@@ -851,15 +877,15 @@
     pairs = lax.axis_size("ctx") // 2
     if (lefts[0].shape[1] // pairs) % 128:
         values = [tn(left, right) for left, right in zip(lefts, rights)]
-        values += [jnp.broadcast_to(term[:, None], (term.shape[0], 64)) for term in terms]
-        return [ctx_rows_sum(jnp.concatenate(values, axis=1))]
+        values += [jnp.broadcast_to(term[:, None], (term.shape[0], 128)) for term in terms]
+        return [ctx_rows_sum(jnp.concatenate(values, axis=1))], values[0]
     kept, sent = share_products(lefts, rights, terms)
     got = swap(sent, "ctx", 1)
     parts = [kept[0], got[0]]
     for pair in range(1, pairs):
         part = (kept[pair].astype(F32) + got[pair].astype(F32)).astype(BF)
         parts.append(swap(part, "ctx", 2 * pair))
-    return parts
+    return parts, sent
 
 
 def share_finish(parts):
@@ -867,6 +893,23 @@
     for part in parts[1:]:
         total = total + part.astype(F32)
     return total
+
+
+def own_rows_of(values, height):
+    index = lax.axis_index("ctx") * lax.axis_size("fsdp") + lax.axis_index("fsdp")
+    return lax.dynamic_slice_in_dim(values, index * height, height, 0)
+
+
+def feature_rows(values):
+    count, plane = lax.axis_size("fsdp"), lax.axis_index("fsdp")
+    values = by_feature(values)
+    rows, width = values.shape
+    width //= count
+    out = []
+    for away in range(count):
+        part = lax.dynamic_slice(values, (0, (plane ^ away) * width), (rows, width))
+        out.append(swap(part, "fsdp", away) if away else part)
+    return out
 
 
 def own_features(terms):
@@ -893,7 +936,7 @@
     out_weight,
     ffn_weight,
 ):
-    ctx_count = lax.axis_size("ctx")
+    ctx_count, fsdp_count = lax.axis_size("ctx"), lax.axis_size("fsdp")
     me, _ = ids()
     rows = hidden_in.shape[1]
     queries_width, kv_width = H * HD, KV * HD
@@ -942,17 +985,17 @@
         attn_rows, out_weight, out_blocks, hidden_in[0], ffn_gain
     )
     scale_two = norm_scale(residual)
-    rows_in = halves_of(pass_rows(normed_two))
-    rows_out = halves_of(after(rows_out, normed_two))
-    act_grad = []
-    for half in rows_out:
-        act_grad.append(down_back(half, ffn_parts))
-
-    all_attn = gather_planes(after(attn_rows, rows_in[1]))
+    rows_in = pass_rows(normed_two)
+    rows_out = after(rows_out, normed_two)
+    act_grad = down_back(rows_out, ffn_parts)
+
+    all_attn = lax.all_gather(after(attn_rows, rows_in[2]), "fsdp", tiled=True)
     middle = []
-    for half, act in zip(rows_in, act_grad):
-        middle.append(ffn_middle(half, in_hbm(act), ffn_parts))
-    parts, partial = [in_hbm(m[0]) for m in middle], [m[1] for m in middle]
+    half = fsdp_count // 2
+    for index in range(2):
+        blocks = rows_in[index * half : (index + 1) * half]
+        middle.append(ffn_middle(blocks, act_grad, index, ffn_parts))
+    parts, partial = [m[0] for m in middle], [m[1] for m in middle]
     sum_grad = sum_rows(partial)
     products = ffn_products(rows_in, rows_out, parts).transpose(1, 0, 2)
     ffn_weight_grad = lax.psum_scatter(products, "ctx", scatter_dimension=0, tiled=True)
@@ -966,39 +1009,43 @@
         scaled_two - unit_two * jnp.mean(scaled_two * unit_two, axis=-1, keepdims=True)
     )
     residual_bf = residual_grad.astype(BF)
-    own_residual = columns_to_owner(by_feature(residual_bf))
+    out_sum = sum_rows([after(part, residual_bf) for part in out_partial])
+    output = (residual + out_sum).astype(BF)
+    (ffn_term,) = own_features([ffn_gain_term])
     attn_grad = out_back(residual_bf, out_weight, out_blocks)
     query_part, kept, sent = attend_back(
         queries, attn_grad, attended, keys_values, key_anchor, own_anchor, logs, cosine, sine
     )
     query_planes = pass_rows(query_part)
     pair_part = sum_pairs(kept, sent, cosine, sine)
+    own_residual = by_offset(feature_rows(after(residual_bf, sent)))
     all_pair = gather_planes(pair_part)
-    all_query = by_offset(after(query_planes, pair_part))
-    first_sums = share_start([own_residual, own_one], [after(all_attn, pair_part), all_query], [])
-    input_grad, attn_gain_term = one_back(
+    input_grad = one_back(
         query_part, pair_part, qkv_full, hidden_in[0], attn_gain, residual_grad
     )
-    terms = own_features([attn_gain_term[0], ffn_gain_term])
-    last_sums = share_finish(share_start([own_one], [all_pair], terms))
+    last_sums, last_sent = share_start([own_one], [all_pair], [ffn_term])
+    all_query = by_offset(after(query_planes, last_sent))
+    first_sums, _ = share_start(
+        [own_residual, own_one], [after(all_attn, last_sent), all_query], []
+    )
+    last_sums = share_finish(last_sums)
     first_sums = share_finish(after(first_sums, last_sums))
-
-    out_sum = sum_rows([after(half, pair_part) for half in out_partial])
-    output = (residual + out_sum).astype(BF)
 
     pairs_width = 2 * kv_width
     out_weight_grad = first_sums[:, :queries_width]
     qkv_grad = jnp.concatenate(
         [first_sums[:, queries_width:], last_sums[:, :pairs_width]], axis=1
     )
+    features = own_rows_of(attn_gain, qkv_grad.shape[0])
+    gain_grad = jnp.sum(own_rows_of(qkv_full, qkv_grad.shape[0]).astype(F32) * qkv_grad, axis=1)
     return (
         output[None],
         input_grad[None],
         qkv_grad,
         out_weight_grad,
         ffn_weight_grad,
+        gain_grad / features,
         last_sums[:, pairs_width],
-        last_sums[:, pairs_width + 64],
     )
 
 

time: 596 us -> 619 us (1.039); the launches traced: 587 us -> 617 us
  waiting for transfers between devices: 236 us -> 264 us
  Pallas kernels: 148 us -> 138 us
  local copies, waits for them, and re-layouts: 47.4 us -> 57 us
    ppermute x63 -> x66, waiting for transfers between devices: 217 us -> 248 us  [swap(): return lax.ppermute(value, axis, [(i, i ^ offset) for i in range(count)])]
    ppermute x63 -> x66, starting transfers between devices: 92.5 us -> 110 us  [swap(): return lax.ppermute(value, axis, [(i, i ^ offset) for i in range(count)])]
    unnamed x124 -> x145, local copies, waits for them, and re-layouts: 12.2 us -> 28.5 us
    pallas_call x8 -> x7, Pallas kernels: 107 us -> 98.6 us  [the longest x2 29 us: ffn_middle(): pl.pallas_call(lambda *refs: ffn_kernel(len(blocks), *refs), grid=(hidden...]
    all_to_all x2 -> x1, starting transfers between devices: 10.7 us -> 3.51 us  [columns_to_owner(): lax.all_to_all(values, 'fsdp', split_axis=1, concat_axis=0, tiled=True)]
  transfers between devices with their start and end apart: 70 -> 72, of which waited for: 35 -> 42; matrix products, arithmetic and copies ran while one was open for 10% -> 9% of each run, Pallas kernels for 19% -> 21%
where the time goes in v4:
time: 619 us; the launch traced here: 617 us
  waiting for transfers between devices  264 us (43%)
  Pallas kernels  138 us (22%)
  starting transfers between devices  117 us (19%)
  local copies, waits for them, and re-layouts  57 us (9%)
  other arithmetic  26.5 us (4%)
  between operations  14.6 us (2%)
    ppermute x66, waiting for transfers between devices, swap(): return lax.ppermute(value, axis, [(i, i ^ offset) for i in range(count)])  248 us
    ppermute x66, starting transfers between devices, swap(): return lax.ppermute(value, axis, [(i, i ^ offset) for i in range(count)])  110 us
    pallas_call x2, Pallas kernels, ffn_middle(): pl.pallas_call(lambda *refs: ffn_kernel(len(blocks), *refs), grid=(hidden...  29 us
    unnamed x145, local copies, waits for them, and re-layouts  28.5 us
    pallas_call x1, Pallas kernels, attend_back(): pl.pallas_call(lambda *refs: attend_back_kernel(KEY_CHUNK, *refs), grid=(...  20.6 us
    pallas_call x1, Pallas kernels, ffn_products(): pl.pallas_call(lambda *refs: products_kernel(count, *refs), grid=(3, widt...  18.7 us
    all_gather x1, waiting for transfers between devices, gather_blocks(): planes = lax.all_gather(after(mine, before_fsdp), 'fsdp')  15.4 us
    pallas_call x2, Pallas kernels, out_call(): pl.pallas_call(lambda *refs: out_kernel(back, *refs), out_shape=out_shape...  13.3 us
  transfers between devices with their start and end apart: 72, of which 42 were waited for; matrix products, arithmetic and copies ran while one was open for 9% of the time, Pallas kernels for 21%

profile of v4, /device:TPU:0, one launch (start us, length us, event | category | flops | bytes accessed | tf_op | source)
XLA Modules:
  0.0 617.0 jit_solution(10197657594670722747)
XLA Ops:
  15.2 7.5 %collective-permute-done.10.refs_13_ = bf16[512,384]{1,0:T(8,128)(2,1)} collective-permute-done((bf16[512,384]{1,0:T(8,128)(2,1)S(1)}, bf16[512,384]{1,0:T(8,128)(2,1)}, u32[]{:S(2)}, u32[]{:S(2)}) %collective-permute-start.10) | collective-permute-done | bytes 393248 | tf_op jit(solution)/shard_map/ppermute | solution.py:43
  22.9 8.1 %collective-permute-start.20 = (bf16[512,384]{1,0:T(8,128)(2,1)}, bf16[512,384]{1,0:T(8,128)(2,1)S(1)}, u32[]{:S(2)}, u32[]{:S(2)}) collective-permute-start(bf16[512,384]{1,0:T(8,128)(2,1)} %collective-permute-done.10.refs_13_), channel_id=1, source_target_pairs={{0,1},{1,0},{2,3},{3,2},{4,5},{5,4},{6,7},{7,6},{8,9},{9,8},{10,11... | collective-permute-start | bytes 1179656 | tf_op jit(solution)/shard_map/ppermute | solution.py:43
  52.7 15.4 %all-gather.8.cloned.1.call-done = bf16[2048,256]{1,0:T(8,128)(2,1)} async-done(((bf16[512,256]{1,0:T(8,128)(2,1)}), bf16[2048,256]{1,0:T(8,128)(2,1)}) %all-gather.8.cloned.1.call-update) | async-done | bytes 1048592 | tf_op jit(solution)/shard_map/all_gather | solution.py:184
  122.0 9.5 %pieces_forward.1 = (bf16[128,2048]{1,0:T(8,128)(2,1)S(1)}, bf16[128,1024]{1,0:T(8,128)(2,1)S(1)}, bf16[2048,3072]{1,0:T(8,128)(2,1)}) custom-call(s32[2]{0:T(128)S(1)} %pad_add_fusion.refs_0_, bf16[128,2048]{1,0:T(8,128)(2,1)S(1)} %fusion.2.refs_1_, bf16[512,3072]{1,0:T(8,128)(2,1)} %refs_2_.3, bf16[512,384]{1,0:T(8,128)(2,1)} %copy-done.54, ...), custom_call_target="tpu_custom_call" | custom-call | flops 1610612736 | bytes 25165824 | tf_op jit(solution)/shard_map/pieces_forward/pallas_call | solution.py:154
  150.7 12.6 %attend.1 = (bf16[128,2048]{1,0:T(8,128)(2,1)}, f32[128,2048]{1,0:T(8,128)S(1)}, f32[8,1,512]{2,1,0:T(1,128)S(1)}) custom-call(bf16[128,2048]{1,0:T(8,128)(2,1)S(1)} %get-tuple-element.50.refs_0_, bf16[512,1024]{1,0:T(8,128)(2,1)S(1)} %constant_dynamic-update-slice_fusion.1.refs_1_.refs_2_.refs_3_.refs_4_, ...), custom_call_target="tpu_custom_call" | custom-call | flops 1073741824 | bytes 2097152 | tf_op jit(solution)/shard_map/attend/pallas_call | solution.py:541
  166.3 7.8 %out_forward.1 = (f32[128,2048]{1,0:T(8,128)S(1)}, bf16[128,2048]{1,0:T(8,128)(2,1)}) custom-call(s32[2]{0:T(128)S(1)} %pad_add_fusion.refs_0_, bf16[128,2048]{1,0:T(8,128)(2,1)} %get-tuple-element.76.refs_1_, bf16[512,2048]{1,0:T(8,128)(2,1)} %refs_2_.5, bf16[8,3,512,256]{3,2,1,0:T(8,128)(2,1)} %bitcast.83, bf16[128,2048]{1,0:T(8,128)(2,1)S(1)} %bitcast.66, ...), custom_call_target="tpu_custom_call" | custom-call | flops 1073741824 | bytes 8388608 | tf_op jit(solution)/shard_map/out_forward/pallas_call | solution.py:251
  179.4 11.8 %collective-permute-done.38.refs_1_.refs_3_ = bf16[128,2048]{1,0:T(8,128)(2,1)S(1)} collective-permute-done((bf16[128,2048]{1,0:T(8,128)(2,1)}, bf16[128,2048]{1,0:T(8,128)(2,1)S(1)}, u32[]{:S(2)}, u32[]{:S(2)}) %collective-permute-start.38) | collective-permute-done | bytes 524320 | tf_op jit(solution)/shard_map/ppermute | solution.py:43
  191.2 31.4 %collective-permute-start.39 = (bf16[128,2048]{1,0:T(8,128)(2,1)S(1)}, bf16[128,2048]{1,0:T(8,128)(2,1)S(1)}, u32[]{:S(2)}, u32[]{:S(2)}) collective-permute-start(bf16[128,2048]{1,0:T(8,128)(2,1)S(1)} %collective-permute-done.38.refs_1_.refs_3_), channel_id=1, source_target_pairs={{0,1},{1,0},{2,3},{3,2},{4,5},{5,4},{6,7},{7,6},{8,9},{9,8},{10,11... | collective-permute-start | bytes 1572872 | tf_op jit(solution)/shard_map/ppermute | solution.py:43
  223.4 20.4 %collective-permute-done.36.refs_2_.refs_6_ = bf16[128,2048]{1,0:T(8,128)(2,1)S(1)} collective-permute-done((bf16[128,2048]{1,0:T(8,128)(2,1)S(1)}, bf16[128,2048]{1,0:T(8,128)(2,1)S(1)}, u32[]{:S(2)}, u32[]{:S(2)}) %collective-permute-start.36) | collective-permute-done | bytes 524320 | tf_op jit(solution)/shard_map/ppermute | solution.py:43
  249.8 8.7 %down_back.1.refs_2_ = f32[512,2048]{1,0:T(8,128)} custom-call(bf16[128,2048]{1,0:T(8,128)(2,1)S(1)} %bitcast.71, bf16[128,2048]{1,0:T(8,128)(2,1)S(1)} %copy-done.22, bf16[128,2048]{1,0:T(8,128)(2,1)S(1)} %copy-done.19, bf16[128,2048]{1,0:T(8,128)(2,1)S(1)} %collective-permute-done.37.refs_3_.refs_7_, bf16[3,2048,2048]{2,1,0:T(8,128)(2,1)} %bitcast.78), custom_call_target="tpu_custom_call" | custom-call | flops 4294967296 | bytes 8388608 | tf_op jit(solution)/shard_map/down_back/pallas_call | solution.py:775
  260.6 14.3 %ffn_middle.2 = (bf16[3,256,2048]{2,1,0:T(8,128)(2,1)}, f32[256,2048]{1,0:T(8,128)S(1)}) custom-call(bf16[128,2048]{1,0:T(8,128)(2,1)} %get-tuple-element.56.refs_0_, bf16[128,2048]{1,0:T(8,128)(2,1)} %collective-permute-done.34.refs_1_, f32[512,2048]{1,0:T(8,128)S(1)} %copy-done.1, bf16[3,2048,2048]{2,1,0:T(8,128)(2,1)} %bitcast.79), custom_call_target="tpu_custom_call" | custom-call | flops 8589934592 | bytes 16777216 | tf_op jit(solution)/shard_map/ffn_middle/pallas_call | solution.py:693
  275.0 14.6 %ffn_middle.3 = (bf16[3,256,2048]{2,1,0:T(8,128)(2,1)}, f32[256,2048]{1,0:T(8,128)S(1)}) custom-call(bf16[128,2048]{1,0:T(8,128)(2,1)S(1)} %copy-done.39, bf16[128,2048]{1,0:T(8,128)(2,1)S(1)} %copy-done.37, f32[512,2048]{1,0:T(8,128)S(1)} %copy-done.2, bf16[3,2048,2048]{2,1,0:T(8,128)(2,1)} %bitcast.80), custom_call_target="tpu_custom_call" | custom-call | flops 8589934592 | bytes 16777216 | tf_op jit(solution)/shard_map/ffn_middle/pallas_call | solution.py:693
  292.4 18.7 %ffn_products.1 = bf16[3,2048,2048]{2,1,0:T(8,128)(2,1)} custom-call(bf16[128,2048]{1,0:T(8,128)(2,1)} %get-tuple-element.56.refs_0_, bf16[128,2048]{1,0:T(8,128)(2,1)} %collective-permute-done.34.refs_1_, bf16[128,2048]{1,0:T(8,128)(2,1)S(1)} %copy-done.39, bf16[128,2048]{1,0:T(8,128)(2,1)S(1)} %copy-done.37, bf16[128,2048]{1,0:T(8,128)(2,1)S(1)} %bitcast.72, ...), custom_call_target="tpu_custom_call" | custom-call | flops 12884901888 | bytes 25165824 | tf_op jit(solution)/shard_map/ffn_products/pallas_call | solution.py:748
  316.2 11.3 %collective-permute-done.41 = bf16[128,2048]{1,0:T(8,128)(2,1)S(1)} collective-permute-done((bf16[128,2048]{1,0:T(8,128)(2,1)S(1)}, bf16[128,2048]{1,0:T(8,128)(2,1)S(1)}, u32[]{:S(2)}, u32[]{:S(2)}) %collective-permute-start.41) | collective-permute-done | bytes 524320 | tf_op jit(solution)/shard_map/ppermute | solution.py:43
  337.4 10.4 %collective-permute-done.42 = bf16[128,2048]{1,0:T(8,128)(2,1)S(1)} collective-permute-done((bf16[128,2048]{1,0:T(8,128)(2,1)S(1)}, bf16[128,2048]{1,0:T(8,128)(2,1)S(1)}, u32[]{:S(2)}, u32[]{:S(2)}) %collective-permute-start.42) | collective-permute-done | bytes 524320 | tf_op jit(solution)/shard_map/ppermute | solution.py:43
  355.3 20.6 %attend_back.1 = (bf16[128,2048]{1,0:T(8,128)(2,1)S(1)}, bf16[2,512,512]{2,1,0:T(8,128)(2,1)S(1)}, bf16[2,512,512]{2,1,0:T(8,128)(2,1)}) custom-call(bf16[128,2048]{1,0:T(8,128)(2,1)S(1)} %copy-done.35, bf16[128,2048]{1,0:T(8,128)(2,1)S(1)} %out_back.1.refs_1_, f32[128,2048]{1,0:T(8,128)S(1)} %copy-done.41, bf16[512,1024]{1,0:T(8,128)(2,1)} %copy-done.30, ...), custom_call_target="tpu_custom_call" | custom-call | flops 2684354560 | bytes 4194304 | tf_op jit(solution)/shard_map/attend_back/pallas_call | solution.py:606
  387.5 7.3 %down_forward.1 = f32[512,2048]{1,0:T(8,128)S(1)} custom-call(bf16[3,256,2048]{2,1,0:T(8,128)(2,1)S(1)} %copy-done.7, bf16[3,256,2048]{2,1,0:T(8,128)(2,1)S(1)} %copy-done.9, bf16[3,2048,2048]{2,1,0:T(8,128)(2,1)} %bitcast.81), custom_call_target="tpu_custom_call" | custom-call | flops 4294967296 | bytes 8388608 | tf_op jit(solution)/shard_map/down_forward/pallas_call | solution.py:804
  411.4 7.7 %collective-permute-done.49.refs_2_ = bf16[2,128,512]{2,1,0:T(8,128)(2,1)} collective-permute-done((bf16[2,128,512]{2,1,0:T(8,128)(2,1)}, bf16[2,128,512]{2,1,0:T(8,128)(2,1)}, u32[]{:S(2)}, u32[]{:S(2)}) %collective-permute-start.49) | collective-permute-done | bytes 262176 | tf_op jit(solution)/shard_map/ppermute | solution.py:43
  455.1 36.8 %collective-permute-done.53 = f32[1,2048]{1,0:T(1,128)S(1)} collective-permute-done((f32[1,2048]{1,0:T(1,128)S(1)}, f32[1,2048]{1,0:T(1,128)S(1)}, u32[]{:S(2)}, u32[]{:S(2)}) %collective-permute-start.53) | collective-permute-done | bytes 8224 | tf_op jit(solution)/shard_map/ppermute | solution.py:43
  498.7 15.7 %collective-permute-done.54 = f32[1,2048]{1,0:T(1,128)S(1)} collective-permute-done((f32[1,2048]{1,0:T(1,128)S(1)}, f32[1,2048]{1,0:T(1,128)S(1)}, u32[]{:S(2)}, u32[]{:S(2)}) %collective-permute-start.54) | collective-permute-done | bytes 8224 | tf_op jit(solution)/shard_map/ppermute | solution.py:43
  536.3 9.1 %collective-permute-done.57 = bf16[128,2048]{1,0:T(8,128)(2,1)} collective-permute-done((bf16[128,2048]{1,0:T(8,128)(2,1)}, bf16[128,2048]{1,0:T(8,128)(2,1)}, u32[]{:S(2)}, u32[]{:S(2)}) %collective-permute-start.57) | collective-permute-done | bytes 524320 | tf_op jit(solution)/shard_map/ppermute | solution.py:43
  552.9 8.9 %one_back.1 = f32[128,2048]{1,0:T(8,128)} custom-call(bf16[128,2048]{1,0:T(8,128)(2,1)S(1)} %get-tuple-element.82.query_ref, bf16[128,1024]{1,0:T(8,128)(2,1)S(1)} %copy-done.10, bf16[2048,3072]{1,0:T(8,128)(2,1)} %get-tuple-element.73.w_ref, bf16[128,2048]{1,0:T(8,128)(2,1)S(1)} %bitcast.67, f32[1,2048]{1,0:T(1,128)S(1)} %bitcast.77, f32[128,2048]{1,0:T(8,128)S(1)} %copy-done.3), custom_call_target="tpu_custom_call" | custom-call | flops 1610612736 | bytes 12582912 | tf_op jit(solution)/shard_map/one_back/pallas_call | solution.py:320
  579.4 12.2 %collective-permute-done.61 = bf16[64,4096]{1,0:T(8,128)(2,1)S(1)} collective-permute-done((bf16[64,4096]{1,0:T(8,128)(2,1)S(1)}, bf16[64,4096]{1,0:T(8,128)(2,1)S(1)}, u32[]{:S(2)}, u32[]{:S(2)}) %collective-permute-start.61) | collective-permute-done | bytes 524320 | tf_op jit(solution)/shard_map/ppermute | solution.py:43
  591.6 9.4 %collective-permute-done.60 = bf16[64,4096]{1,0:T(8,128)(2,1)S(1)} collective-permute-done((bf16[64,4096]{1,0:T(8,128)(2,1)S(1)}, bf16[64,4096]{1,0:T(8,128)(2,1)S(1)}, u32[]{:S(2)}, u32[]{:S(2)}) %collective-permute-start.60) | collective-permute-done | bytes 524320 | tf_op jit(solution)/shard_map/ppermute | solution.py:43
  (368 shorter events, 271.9 us)
Async XLA Ops:
  7.2 60.9 %all-gather.8.cloned.1.call-start = ((), (), s32[]{:S(2)}) async-start(), calls=%async_computation.5 | async-start | bytes 1310720 | tf_op jit(solution)/shard_map/all_gather | solution.py:184
  39.7 126.6 %all-gather.10.cloned.1.call-start = ((), (), s32[]{:S(2)}) async-start(), calls=%async_computation.6 | async-start | bytes 7077888 | tf_op jit(solution)/shard_map/all_gather | solution.py:191
  70.3 475.1 %all-gather.6.cloned.1.call-start = ((), (), s32[]{:S(2)}) async-start(), calls=%async_computation.3 | async-start | bytes 2621440 | tf_op jit(solution)/shard_map/all_gather | solution.py:992
  93.1 23.6 %collective-permute-start.15 = (bf16[512,384]{1,0:T(8,128)(2,1)S(1)}, bf16[512,384]{1,0:T(8,128)(2,1)S(1)}, u32[]{:S(2)}, u32[]{:S(2)}) collective-permute-start(bf16[512,384]{1,0:T(8,128)(2,1)S(1)} %collective-permute-done.14.refs_17_), channel_id=1, source_target_pairs={{0,4},{4,0},{8,12},{12,8},{16,20},{20,16},{24,28},{28,24},{1,5},{5... | collective-permute-start | bytes 1179656 | tf_op jit(solution)/shard_map/ppermute | solution.py:43
  175.0 48.5 %collective-permute-start.37 = (bf16[128,2048]{1,0:T(8,128)(2,1)S(1)}, bf16[128,2048]{1,0:T(8,128)(2,1)S(1)}, u32[]{:S(2)}, u32[]{:S(2)}) collective-permute-start(bf16[128,2048]{1,0:T(8,128)(2,1)S(1)} %bitcast.68), channel_id=1, source_target_pairs={{0,3},{1,2},{2,1},{3,0},{4,7},{5,6},{6,5},{7,4},{8,11},{9,10},{10,... | collective-permute-start | bytes 1572872 | tf_op jit(solution)/shard_map/ppermute | solution.py:43
  178.0 65.8 %collective-permute-start.36 = (bf16[128,2048]{1,0:T(8,128)(2,1)S(1)}, bf16[128,2048]{1,0:T(8,128)(2,1)S(1)}, u32[]{:S(2)}, u32[]{:S(2)}) collective-permute-start(bf16[128,2048]{1,0:T(8,128)(2,1)S(1)} %bitcast.69), channel_id=1, source_target_pairs={{0,2},{1,3},{2,0},{3,1},{4,6},{5,7},{6,4},{7,5},{8,10},{9,11},{10,... | collective-permute-start | bytes 1572872 | tf_op jit(solution)/shard_map/ppermute | solution.py:43
  178.0 66.6 %collective-permute-start.35 = (bf16[128,2048]{1,0:T(8,128)(2,1)S(1)}, bf16[128,2048]{1,0:T(8,128)(2,1)S(1)}, u32[]{:S(2)}, u32[]{:S(2)}) collective-permute-start(bf16[128,2048]{1,0:T(8,128)(2,1)S(1)} %bitcast.70), channel_id=1, source_target_pairs={{0,1},{1,0},{2,3},{3,2},{4,5},{5,4},{6,7},{7,6},{8,9},{9,8},{10,11... | collective-permute-start | bytes 1572872 | tf_op jit(solution)/shard_map/ppermute | solution.py:43
  191.2 55.4 %collective-permute-start.39 = (bf16[128,2048]{1,0:T(8,128)(2,1)S(1)}, bf16[128,2048]{1,0:T(8,128)(2,1)S(1)}, u32[]{:S(2)}, u32[]{:S(2)}) collective-permute-start(bf16[128,2048]{1,0:T(8,128)(2,1)S(1)} %collective-permute-done.38.refs_1_.refs_3_), channel_id=1, source_target_pairs={{0,1},{1,0},{2,3},{3,2},{4,5},{5,4},{6,7},{7,6},{8,9},{9,8},{10,11... | collective-permute-start | bytes 1572872 | tf_op jit(solution)/shard_map/ppermute | solution.py:43
  223.4 35.0 %collective-permute-start.34 = (bf16[128,2048]{1,0:T(8,128)(2,1)}, bf16[128,2048]{1,0:T(8,128)(2,1)}, u32[]{:S(2)}, u32[]{:S(2)}) collective-permute-start(bf16[128,2048]{1,0:T(8,128)(2,1)} %get-tuple-element.56.refs_0_), channel_id=1, source_target_pairs={{0,1},{1,0},{2,3},{3,2},{4,5},{5,4},{6,7},{7,6},{8,9},{9,8},{10,11... | collective-permute-start | bytes 1572872 | tf_op jit(solution)/shard_map/ppermute | solution.py:43
  247.5 357.6 %reduce-scatter.2.cloned.1.call-start = ((), (), s32[]{:S(2)}) async-start(), calls=%async_computation.4 | async-start | bytes 28311552 | tf_op jit(solution)/shard_map/reduce_scatter | solution.py:1001
  314.1 23.3 %collective-permute-start.40 = (bf16[128,2048]{1,0:T(8,128)(2,1)S(1)}, bf16[128,2048]{1,0:T(8,128)(2,1)S(1)}, u32[]{:S(2)}, u32[]{:S(2)}) collective-permute-start(bf16[128,2048]{1,0:T(8,128)(2,1)S(1)} %slice.235), channel_id=1, source_target_pairs={{0,1},{1,0},{2,3},{3,2},{4,5},{5,4},{6,7},{7,6},{8,9},{9,8},{10,11... | collective-permute-start | bytes 1572872 | tf_op jit(solution)/shard_map/ppermute | solution.py:43
  379.8 52.7 %all-to-all-start = ((bf16[128,4,512]{0,2,1:T(8,128)(2,1)}), bf16[128,4,512]{0,2,1:T(8,128)(2,1)S(1)}, u32[]{:S(2)}, u32[]{:S(2)}) async-start(bf16[128,4,512]{0,2,1:T(8,128)(2,1)} %bitcast.88), calls=%async_computation | async-start | bytes 1048576 | tf_op jit(solution)/shard_map/all_to_all | solution.py:401
  397.5 50.6 %collective-permute-start.44 = (bf16[128,2048]{1,0:T(8,128)(2,1)}, bf16[128,2048]{1,0:T(8,128)(2,1)}, u32[]{:S(2)}, u32[]{:S(2)}) collective-permute-start(bf16[128,2048]{1,0:T(8,128)(2,1)} %slice.232), channel_id=1, source_target_pairs={{0,1},{1,0},{2,3},{3,2},{4,5},{5,4},{6,7},{7,6},{8,9},{9,8},{10,11... | collective-permute-start | bytes 1572872 | tf_op jit(solution)/shard_map/ppermute | solution.py:43
  406.1 24.1 %collective-permute-start.47 = (bf16[2,128,512]{2,1,0:T(8,128)(2,1)}, bf16[2,128,512]{2,1,0:T(8,128)(2,1)}, u32[]{:S(2)}, u32[]{:S(2)}) collective-permute-start(bf16[2,128,512]{2,1,0:T(8,128)(2,1)} %get-tuple-element.121), channel_id=1, source_target_pairs={{0,8},{4,12},{8,0},{12,4},{16,24},{20,28},{24,16},{28,20},{1,9},{5... | collective-permute-start | bytes 786440 | tf_op jit(solution)/shard_map/ppermute | solution.py:43
  434.7 92.9 %all-to-all-start.1 = ((bf16[4,128,1024]{2,1,0:T(8,128)(2,1)}), bf16[4,128,1024]{2,1,0:T(8,128)(2,1)S(1)}, u32[]{:S(2)}, u32[]{:S(2)}) async-start(bf16[4,128,1024]{2,1,0:T(8,128)(2,1)} %broadcast_in_dim.110), calls=%async_computation.1 | async-start | bytes 2097152 | tf_op jit(solution)/shard_map/all_to_all | solution.py:397
  442.0 72.4 %collective-permute-start.50 = (bf16[128,512]{1,0:T(8,128)(2,1)}, bf16[128,512]{1,0:T(8,128)(2,1)}, u32[]{:S(2)}, u32[]{:S(2)}) collective-permute-start(bf16[128,512]{1,0:T(8,128)(2,1)} %copy.69), channel_id=1, source_target_pairs={{0,3},{1,2},{2,1},{3,0},{4,7},{5,6},{6,5},{7,4},{8,11},{9,10},{10,... | collective-permute-start | bytes 393224 | tf_op jit(solution)/shard_map/ppermute | solution.py:43
  445.8 77.9 %collective-permute-start.56 = (bf16[128,2048]{1,0:T(8,128)(2,1)S(1)}, bf16[128,2048]{1,0:T(8,128)(2,1)}, u32[]{:S(2)}, u32[]{:S(2)}) collective-permute-start(bf16[128,2048]{1,0:T(8,128)(2,1)S(1)} %get-tuple-element.82.query_ref), channel_id=1, source_target_pairs={{0,3},{1,2},{2,1},{3,0},{4,7},{5,6},{6,5},{7,4},{8,11},{9,10},{10,... | collective-permute-start | bytes 1572872 | tf_op jit(solution)/shard_map/ppermute | solution.py:43
  447.9 77.4 %collective-permute-start.43 = (bf16[128,2048]{1,0:T(8,128)(2,1)}, bf16[128,2048]{1,0:T(8,128)(2,1)}, u32[]{:S(2)}, u32[]{:S(2)}) collective-permute-start(bf16[128,2048]{1,0:T(8,128)(2,1)} %slice.233), channel_id=1, source_target_pairs={{0,1},{1,0},{2,3},{3,2},{4,5},{5,4},{6,7},{7,6},{8,9},{9,8},{10,11... | collective-permute-start | bytes 1572872 | tf_op jit(solution)/shard_map/ppermute | solution.py:43
  450.6 74.7 %collective-permute-start.45 = (bf16[128,2048]{1,0:T(8,128)(2,1)}, bf16[128,2048]{1,0:T(8,128)(2,1)}, u32[]{:S(2)}, u32[]{:S(2)}) collective-permute-start(bf16[128,2048]{1,0:T(8,128)(2,1)} %add_convert_fusion.4), channel_id=1, source_target_pairs={{0,3},{1,2},{2,1},{3,0},{4,7},{5,6},{6,5},{7,4},{8,11},{9,10},{10,... | collective-permute-start | bytes 1572872 | tf_op jit(solution)/shard_map/ppermute | solution.py:43
  454.2 37.7 %collective-permute-start.53 = (f32[1,2048]{1,0:T(1,128)S(1)}, f32[1,2048]{1,0:T(1,128)S(1)}, u32[]{:S(2)}, u32[]{:S(2)}) collective-permute-start(f32[1,2048]{1,0:T(1,128)S(1)} %bitcast.96), channel_id=1, source_target_pairs={{0,1},{1,0},{2,3},{3,2},{4,5},{5,4},{6,7},{7,6},{8,9},{9,8},{10,11... | collective-permute-start | bytes 24584 | tf_op jit(solution)/shard_map/ppermute | solution.py:43
  491.9 22.5 %collective-permute-start.54 = (f32[1,2048]{1,0:T(1,128)S(1)}, f32[1,2048]{1,0:T(1,128)S(1)}, u32[]{:S(2)}, u32[]{:S(2)}) collective-permute-start(f32[1,2048]{1,0:T(1,128)S(1)} %add.410), channel_id=1, source_target_pairs={{0,2},{1,3},{2,0},{3,1},{4,6},{5,7},{6,4},{7,5},{8,10},{9,11},{10,... | collective-permute-start | bytes 24584 | tf_op jit(solution)/shard_map/ppermute | solution.py:43
  531.7 30.1 %collective-permute-start.62 = (bf16[4,64,1152]{2,1,0:T(8,128)(2,1)}, bf16[4,64,1152]{2,1,0:T(8,128)(2,1)}, u32[]{:S(2)}, u32[]{:S(2)}) collective-permute-start(bf16[4,64,1152]{2,1,0:T(8,128)(2,1)} %get-tuple-element.77), channel_id=1, source_target_pairs={{0,4},{4,0},{8,12},{12,8},{16,20},{20,16},{24,28},{28,24},{1,5},{5... | collective-permute-start | bytes 1769480 | tf_op jit(solution)/shard_map/ppermute | solution.py:43
  578.0 23.0 %collective-permute-start.60 = (bf16[64,4096]{1,0:T(8,128)(2,1)S(1)}, bf16[64,4096]{1,0:T(8,128)(2,1)S(1)}, u32[]{:S(2)}, u32[]{:S(2)}) collective-permute-start(bf16[64,4096]{1,0:T(8,128)(2,1)S(1)} %get-tuple-element.106), channel_id=1, source_target_pairs={{0,16},{4,20},{8,24},{12,28},{16,0},{20,4},{24,8},{28,12},{1,17},{... | collective-permute-start | bytes 1572872 | tf_op jit(solution)/shard_map/ppermute | solution.py:43
  578.6 22.6 %collective-permute-start.59 = (bf16[64,4096]{1,0:T(8,128)(2,1)S(1)}, bf16[64,4096]{1,0:T(8,128)(2,1)S(1)}, u32[]{:S(2)}, u32[]{:S(2)}) collective-permute-start(bf16[64,4096]{1,0:T(8,128)(2,1)S(1)} %get-tuple-element.107), channel_id=1, source_target_pairs={{0,8},{4,12},{8,0},{12,4},{16,24},{20,28},{24,16},{28,20},{1,9},{5... | collective-permute-start | bytes 1572872 | tf_op jit(solution)/shard_map/ppermute | solution.py:43
  (118 other events, 1943.7 us)
Sparse Core Ops, SparseCore 0:
  39.9 28.1 all-gather.7
  70.5 57.1 all-gather.9
  247.6 45.1 all-gather.5
  311.2 166.8 reduce-scatter.1

commit v5 on v4

--- a/solution.py
+++ b/solution.py
@@ -354,14 +354,14 @@
     return [values] + [swap(values, "fsdp", away) for away in range(1, count)]
 
 
-def sum_rows(halves):
+def sum_rows(halves, forward):
     count = lax.axis_size("fsdp")
     half = count // 2
     rows = halves[0].shape[0] // half
     parts = [
         halves[away // half][away % half * rows : (away % half + 1) * rows] for away in range(count)
     ]
-    if count == 4:
+    if count == 4 and forward:
         passed = swap(parts[2].astype(BF), "fsdp", 1).astype(F32)
         one = swap(parts[1].astype(BF), "fsdp", 1).astype(F32)
         third = swap((parts[3] + passed).astype(BF), "fsdp", 3).astype(F32)
@@ -379,26 +379,11 @@
     return blocks.transpose(0, 2, 1, 3).reshape(rows, width)
 
 
-def by_offset(planes):
-    count, plane = len(planes), lax.axis_index("fsdp")
-    joined = planes
-    bit = 1
-    while bit < count:
-        odd = (plane & bit) != 0
-        joined = [jnp.where(odd, joined[i ^ bit], joined[i]) for i in range(count)]
-        bit *= 2
-    return jnp.concatenate(joined, axis=0)
-
-
 def gather_planes(values):
     count = lax.axis_size("fsdp")
     rows, columns = values.shape
     copies = jnp.broadcast_to(values[None], (count, rows, columns)).reshape(count * rows, columns)
     return lax.all_to_all(copies, "fsdp", split_axis=0, concat_axis=0, tiled=True)
-
-
-def columns_to_owner(values):
-    return lax.all_to_all(values, "fsdp", split_axis=1, concat_axis=0, tiled=True)
 
 
 def sum_over_ctx(part_for):
@@ -441,7 +426,7 @@
     got = swap(sent, "ctx", 1)
     sums = (kept.astype(F32) + got.astype(F32)).reshape(2, pairs, count // pairs, width)
     far = [swap(sums[:, pair].astype(BF), "ctx", 2 * pair) for pair in range(1, pairs)]
-    return pair_turn(sums[:, 0], far, cosine, sine)
+    return pair_turn(sums[:, 0], far, cosine, sine), far[0]
 
 
 def half_mask(shape):
@@ -818,74 +803,114 @@
     return total[:rows], total[rows:]
 
 
-def share_kernel(count, ids_ref, *refs):
-    lefts, rights = refs[:count], refs[count : 2 * count]
-    terms, (kept_ref, sent_ref) = refs[2 * count : -2], refs[-2:]
+def share_kernel(count, sizes, ids_ref, *refs):
+    products = len(sizes)
+    lefts = [refs[i * count : (i + 1) * count] for i in range(products)]
+    rest = refs[products * count :]
+    rights = []
+    for size in sizes:
+        rights.append(rest[:size])
+        rest = rest[size:]
+    bufs = rest[len(rest) - products :]
+    terms, (kept_ref, sent_ref) = rest[: -products - 2], rest[-products - 2 : -products]
     half = kept_ref.shape[1]
     own = ids_ref[0] % 2 == 0
-    column = 0
-    for left, right in zip(lefts, rights):
-        width = right.shape[1]
-        part = tn(left[...], right[...]).astype(BF)
-        at = slice(column, column + width)
+
+    @pl.when(pl.program_id(0) == 0)
+    def _():
+        for parts, buf in zip(rights, bufs):
+            rows = buf.shape[0] // count
+            for away in range(count):
+                if len(parts) > 1:
+                    block = parts[away][...]
+                else:
+                    start = (ids_ref[1] ^ away) * rows
+                    block = parts[0][pl.ds(pl.multiple_of(start, 16), rows), :]
+                buf[away * rows : (away + 1) * rows] = block
+
+    def emit(part, column):
+        at = slice(column, column + part.shape[1])
         kept_ref[0, :, at] = jnp.where(own, part[:half], part[half:])
         sent_ref[0, :, at] = jnp.where(own, part[half:], part[:half])
-        column += width
-    if terms:
-        tall = jnp.concatenate(
-            [jnp.broadcast_to(term[...], (128, term.shape[1])) for term in terms], axis=0
-        )
-        part = jnp.transpose(tall).astype(BF)
-        kept_ref[0, :, column:] = jnp.where(own, part[:half], part[half:])
-        sent_ref[0, :, column:] = jnp.where(own, part[half:], part[:half])
+
+    column = 0
+    for left, buf in zip(lefts, bufs):
+        joined = jnp.concatenate([ref[...] for ref in left], axis=0)
+        emit(tn(joined, buf[...]).astype(BF), column)
+        column += buf.shape[1]
+    for term in terms:
+        tall = jnp.broadcast_to(term[...], (128, term.shape[1]))
+        emit(jnp.transpose(tall).astype(BF), column)
+        column += 128
 
 
 def share_products(lefts, rights, terms):
     ctx_count = lax.axis_size("ctx")
     pairs = ctx_count // 2
-    rows, width = lefts[0].shape
+    count = len(lefts[0])
+    rows, width = lefts[0][0].shape
     height = width // ctx_count
-    columns = sum(right.shape[1] for right in rights) + 128 * len(terms)
+    groups = [right if isinstance(right, list) else [right] for right in rights]
+    widths = [group[0].shape[1] for group in groups]
+    columns = sum(widths) + 128 * len(terms)
 
     def place(j, ids_ref):
         return (0, (ids_ref[0] // 2) ^ j)
 
+    def whole(array):
+        return pl.BlockSpec(array.shape, lambda j, ids_ref: (0, 0))
+
     shape = jax.ShapeDtypeStruct((pairs, height, columns), BF)
     out = pl.BlockSpec((1, height, columns), lambda j, ids_ref: (j, 0, 0))
+    flat_lefts = [block for left in lefts for block in left]
+    flat_rights = [block for group in groups for block in group]
     return pl.pallas_call(
-        lambda *refs: share_kernel(len(lefts), *refs),
+        lambda *refs: share_kernel(count, [len(group) for group in groups], *refs),
         grid_spec=pltpu.PrefetchScalarGridSpec(
             num_scalar_prefetch=1,
             grid=(pairs,),
-            in_specs=[pl.BlockSpec((rows, 2 * height), place) for _ in lefts]
-            + [pl.BlockSpec(right.shape, lambda j, ids_ref: (0, 0)) for right in rights]
+            in_specs=[pl.BlockSpec((rows, 2 * height), place) for _ in flat_lefts]
+            + [whole(block) for block in flat_rights]
             + [pl.BlockSpec((1, 2 * height), place) for _ in terms],
             out_specs=(out, out),
+            scratch_shapes=[pltpu.VMEM((count * rows, size), BF) for size in widths],
         ),
         out_shape=(shape, shape),
-        compiler_params=pltpu.CompilerParams(vmem_limit_bytes=24 << 20),
+        compiler_params=pltpu.CompilerParams(vmem_limit_bytes=32 << 20),
         cost_estimate=pl.CostEstimate(
-            flops=2 * rows * width * columns,
-            bytes_accessed=2 * (rows + columns) * width,
+            flops=2 * count * rows * width * columns,
+            bytes_accessed=2 * (count * rows + columns) * width,
             transcendentals=0,
         ),
         name="share_terms" if terms else "share_products",
-    )(jnp.stack(ids()), *lefts, *rights, *[term[None] for term in terms])
+    )(jnp.stack(ids()), *flat_lefts, *flat_rights, *[term[None] for term in terms])
+
+
+def in_fsdp_order(value):
+    if not isinstance(value, list):
+        return value
+    plane = lax.axis_index("fsdp")
+    stacked = jnp.stack(value)
+    parts = [
+        lax.dynamic_index_in_dim(stacked, plane ^ away, 0, keepdims=False)
+        for away in range(len(value))
+    ]
+    return jnp.concatenate(parts, axis=0)
 
 
 def share_start(lefts, rights, terms):
     pairs = lax.axis_size("ctx") // 2
-    if (lefts[0].shape[1] // pairs) % 128:
-        values = [tn(left, right) for left, right in zip(lefts, rights)]
+    if (lefts[0][0].shape[1] // pairs) % 128:
+        values = [tn(in_fsdp_order(a), in_fsdp_order(b)) for a, b in zip(lefts, rights)]
         values += [jnp.broadcast_to(term[:, None], (term.shape[0], 128)) for term in terms]
-        return [ctx_rows_sum(jnp.concatenate(values, axis=1))], values[0]
+        return [ctx_rows_sum(jnp.concatenate(values, axis=1))]
     kept, sent = share_products(lefts, rights, terms)
     got = swap(sent, "ctx", 1)
     parts = [kept[0], got[0]]
     for pair in range(1, pairs):
         part = (kept[pair].astype(F32) + got[pair].astype(F32)).astype(BF)
         parts.append(swap(part, "ctx", 2 * pair))
-    return parts, sent
+    return parts
 
 
 def share_finish(parts):
@@ -977,9 +1002,9 @@
         pair = jnp.concatenate(
             [turned[:, queries_width:], projected[:, queries_width + kv_width :]], axis=1
         ).astype(BF)
-    own_one = columns_to_owner(by_feature(after(normed_one, pair)))
+    own_one = feature_rows(after(normed_one, marks[1]))
     keys_values = gather_keys(pair)
-    rows_out = fetch_rows(after(grad_in, marks[0]))
+    rows_out = fetch_rows(after(grad_in, pair))
     attn_rows, attended, logs = attend(queries, keys_values, key_anchor, own_anchor)
     residual, normed_two = out_forward(
         attn_rows, out_weight, out_blocks, hidden_in[0], ffn_gain
@@ -989,14 +1014,14 @@
     rows_out = after(rows_out, normed_two)
     act_grad = down_back(rows_out, ffn_parts)
 
-    all_attn = lax.all_gather(after(attn_rows, rows_in[2]), "fsdp", tiled=True)
+    all_attn = pass_rows(after(attn_rows, rows_in[2]))
     middle = []
     half = fsdp_count // 2
     for index in range(2):
         blocks = rows_in[index * half : (index + 1) * half]
-        middle.append(ffn_middle(blocks, act_grad, index, ffn_parts))
+        middle.append(ffn_middle(blocks, in_hbm(act_grad), index, ffn_parts))
     parts, partial = [m[0] for m in middle], [m[1] for m in middle]
-    sum_grad = sum_rows(partial)
+    sum_grad = sum_rows(partial, True)
     products = ffn_products(rows_in, rows_out, parts).transpose(1, 0, 2)
     ffn_weight_grad = lax.psum_scatter(products, "ctx", scatter_dimension=0, tiled=True)
     ffn_weight_grad = ffn_weight_grad.astype(F32)
@@ -1009,7 +1034,7 @@
         scaled_two - unit_two * jnp.mean(scaled_two * unit_two, axis=-1, keepdims=True)
     )
     residual_bf = residual_grad.astype(BF)
-    out_sum = sum_rows([after(part, residual_bf) for part in out_partial])
+    out_sum = sum_rows([after(part, residual_bf) for part in out_partial], False)
     output = (residual + out_sum).astype(BF)
     (ffn_term,) = own_features([ffn_gain_term])
     attn_grad = out_back(residual_bf, out_weight, out_blocks)
@@ -1017,17 +1042,16 @@
         queries, attn_grad, attended, keys_values, key_anchor, own_anchor, logs, cosine, sine
     )
     query_planes = pass_rows(query_part)
-    pair_part = sum_pairs(kept, sent, cosine, sine)
-    own_residual = by_offset(feature_rows(after(residual_bf, sent)))
+    pair_part, far = sum_pairs(kept, sent, cosine, sine)
+    own_residual = feature_rows(after(residual_bf, far))
     all_pair = gather_planes(pair_part)
     input_grad = one_back(
         query_part, pair_part, qkv_full, hidden_in[0], attn_gain, residual_grad
     )
-    last_sums, last_sent = share_start([own_one], [all_pair], [ffn_term])
-    all_query = by_offset(after(query_planes, last_sent))
-    first_sums, _ = share_start(
-        [own_residual, own_one], [after(all_attn, last_sent), all_query], []
+    first_sums = share_start(
+        [own_residual, own_one], [after(all_attn, input_grad), after(query_planes, input_grad)], []
     )
+    last_sums = share_start([own_one], [all_pair], [ffn_term])
     last_sums = share_finish(last_sums)
     first_sums = share_finish(after(first_sums, last_sums))
 

time: 619 us -> 565 us (0.913)
  starting transfers between devices: 117 us -> 84.1 us
  waiting for transfers between devices: 264 us -> 251 us
  local copies, waits for them, and re-layouts: 57 us -> 47.6 us
  other arithmetic: 26.5 us -> 19 us
    ppermute x66 -> x72, starting transfers between devices: 110 us -> 79.6 us  [swap(): return lax.ppermute(value, axis, [(i, i ^ offset) for i in range(count)])]
    ppermute x66 -> x72, waiting for transfers between devices: 248 us -> 236 us  [swap(): return lax.ppermute(value, axis, [(i, i ^ offset) for i in range(count)])]
    unnamed x145 -> x111, local copies, waits for them, and re-layouts: 28.5 us -> 22.8 us
  transfers between devices with their start and end apart: 72 -> 76, of which waited for: 42 -> 35; matrix products, arithmetic and copies ran while one was open for 9% -> 8% of each run, Pallas kernels for 21% -> 19%
where the time goes in v5:
time: 565 us; the launch traced here: 559 us
  waiting for transfers between devices  251 us (44%)
  Pallas kernels  142 us (25%)
  starting transfers between devices  84.1 us (15%)
  local copies, waits for them, and re-layouts  47.6 us (8%)
  other arithmetic  19 us (3%)
  between operations  14.7 us (3%)
    ppermute x72, waiting for transfers between devices, swap(): return lax.ppermute(value, axis, [(i, i ^ offset) for i in range(count)])  236 us
    ppermute x72, starting transfers between devices, swap(): return lax.ppermute(value, axis, [(i, i ^ offset) for i in range(count)])  79.6 us
    pallas_call x2, Pallas kernels, ffn_middle(): pl.pallas_call(lambda *refs: ffn_kernel(len(blocks), *refs), grid=(hidden...  28 us
    unnamed x111, local copies, waits for them, and re-layouts  22.8 us
    pallas_call x1, Pallas kernels, attend_back(): pl.pallas_call(lambda *refs: attend_back_kernel(KEY_CHUNK, *refs), grid=(...  20.3 us
    pallas_call x1, Pallas kernels, ffn_products(): pl.pallas_call(lambda *refs: products_kernel(count, *refs), grid=(3, widt...  19.3 us
    all_gather x1, waiting for transfers between devices, gather_blocks(): planes = lax.all_gather(after(mine, before_fsdp), 'fsdp')  15.2 us
    pallas_call x2, Pallas kernels, out_call(): pl.pallas_call(lambda *refs: out_kernel(back, *refs), out_shape=out_shape...  13.2 us
  transfers between devices with their start and end apart: 76, of which 35 were waited for; matrix products, arithmetic and copies ran while one was open for 8% of the time, Pallas kernels for 19%

profile of v5, /device:TPU:0, one launch (start us, length us, event | category | flops | bytes accessed | tf_op | source)
XLA Modules:
  0.0 558.5 jit_solution(999882653783369126)
XLA Ops:
  15.9 7.6 %collective-permute-done.10.refs_13_ = bf16[512,384]{1,0:T(8,128)(2,1)S(1)} collective-permute-done((bf16[512,384]{1,0:T(8,128)(2,1)}, bf16[512,384]{1,0:T(8,128)(2,1)S(1)}, u32[]{:S(2)}, u32[]{:S(2)}) %collective-permute-start.10) | collective-permute-done | bytes 393248 | tf_op jit(solution)/shard_map/ppermute | solution.py:43
  23.7 8.1 %collective-permute-start.20 = (bf16[512,384]{1,0:T(8,128)(2,1)S(1)}, bf16[512,384]{1,0:T(8,128)(2,1)}, u32[]{:S(2)}, u32[]{:S(2)}) collective-permute-start(bf16[512,384]{1,0:T(8,128)(2,1)S(1)} %collective-permute-done.10.refs_13_), channel_id=1, source_target_pairs={{0,1},{1,0},{2,3},{3,2},{4,5},{5,4},{6,7},{7,6},{8,9},{9,8},{10,11... | collective-permute-start | bytes 1179656 | tf_op jit(solution)/shard_map/ppermute | solution.py:43
  53.6 15.2 %all-gather.5.cloned.1.call-done = bf16[2048,256]{1,0:T(8,128)(2,1)} async-done(((bf16[512,256]{1,0:T(8,128)(2,1)}), bf16[2048,256]{1,0:T(8,128)(2,1)}) %all-gather.5.cloned.1.call-update) | async-done | bytes 1048592 | tf_op jit(solution)/shard_map/all_gather | solution.py:184
  122.5 9.6 %pieces_forward.1 = (bf16[128,2048]{1,0:T(8,128)(2,1)S(1)}, bf16[128,1024]{1,0:T(8,128)(2,1)S(1)}, bf16[2048,3072]{1,0:T(8,128)(2,1)}) custom-call(s32[2]{0:T(128)S(1)} %pad_add_fusion.refs_0_, bf16[128,2048]{1,0:T(8,128)(2,1)S(1)} %fusion.2.refs_1_, bf16[512,3072]{1,0:T(8,128)(2,1)} %refs_2_.3, bf16[512,384]{1,0:T(8,128)(2,1)} %copy-done.34, ...), custom_call_target="tpu_custom_call" | custom-call | flops 1610612736 | bytes 25165824 | tf_op jit(solution)/shard_map/pieces_forward/pallas_call | solution.py:154
  152.9 12.8 %attend.1 = (bf16[128,2048]{1,0:T(8,128)(2,1)}, f32[128,2048]{1,0:T(8,128)S(1)}, f32[8,1,512]{2,1,0:T(1,128)S(1)}) custom-call(bf16[128,2048]{1,0:T(8,128)(2,1)S(1)} %get-tuple-element.53.refs_0_, bf16[512,1024]{1,0:T(8,128)(2,1)S(1)} %constant_dynamic-update-slice_fusion.1.refs_1_.refs_2_.refs_3_.refs_4_, ...), custom_call_target="tpu_custom_call" | custom-call | flops 1073741824 | bytes 2097152 | tf_op jit(solution)/shard_map/attend/pallas_call | solution.py:526
  168.7 7.0 %out_forward.1 = (f32[128,2048]{1,0:T(8,128)S(1)}, bf16[128,2048]{1,0:T(8,128)(2,1)S(1)}) custom-call(s32[2]{0:T(128)S(1)} %pad_add_fusion.refs_0_, bf16[128,2048]{1,0:T(8,128)(2,1)} %get-tuple-element.80.refs_1_.refs_9_, bf16[512,2048]{1,0:T(8,128)(2,1)} %refs_2_.5, bf16[8,3,512,256]{3,2,1,0:T(8,128)(2,1)} %bitcast.78, bf16[128,2048]{1,0:T(8,128)(2,1)S(1)} %bitcast.64, ...), custom_call_target="tpu_custom_call" | custom-call | flops 1073741824 | bytes 8388608 | tf_op jit(solution)/shard_map/out_forward/pallas_call | solution.py:251
  176.6 30.9 %collective-permute-done.36.refs_2_.refs_6_ = bf16[128,2048]{1,0:T(8,128)(2,1)} collective-permute-done((bf16[128,2048]{1,0:T(8,128)(2,1)S(1)}, bf16[128,2048]{1,0:T(8,128)(2,1)}, u32[]{:S(2)}, u32[]{:S(2)}) %collective-permute-start.36) | collective-permute-done | bytes 524320 | tf_op jit(solution)/shard_map/ppermute | solution.py:43
  207.4 8.9 %down_back.1.refs_2_ = f32[512,2048]{1,0:T(8,128)} custom-call(bf16[128,2048]{1,0:T(8,128)(2,1)S(1)} %bitcast.69, bf16[128,2048]{1,0:T(8,128)(2,1)} %collective-permute-done.35.refs_1_.refs_5_, bf16[128,2048]{1,0:T(8,128)(2,1)} %collective-permute-done.36.refs_2_.refs_6_, bf16[128,2048]{1,0:T(8,128)(2,1)S(1)} %collective-permute-done.37.refs_3_.refs_7_, ...), custom_call_target="tpu_custom_call" | custom-call | flops 4294967296 | bytes 8388608 | tf_op jit(solution)/shard_map/down_back/pallas_call | solution.py:760
  218.6 14.0 %ffn_middle.2 = (bf16[3,256,2048]{2,1,0:T(8,128)(2,1)}, f32[256,2048]{1,0:T(8,128)S(1)}) custom-call(bf16[128,2048]{1,0:T(8,128)(2,1)S(1)} %get-tuple-element.59.refs_0_, bf16[128,2048]{1,0:T(8,128)(2,1)S(1)} %collective-permute-done.34.refs_1_, f32[512,2048]{1,0:T(8,128)} %down_back.1.refs_2_, bf16[3,2048,2048]{2,1,0:T(8,128)(2,1)} %bitcast.74), custom_call_target="tpu_custom_call" | custom-call | flops 8589934592 | bytes 16777216 | tf_op jit(solution)/shard_map/ffn_middle/pallas_call | solution.py:678
  233.9 14.1 %ffn_middle.3 = (bf16[3,256,2048]{2,1,0:T(8,128)(2,1)}, f32[256,2048]{1,0:T(8,128)S(1)}) custom-call(bf16[128,2048]{1,0:T(8,128)(2,1)S(1)} %collective-permute-done.39.refs_0_.refs_2_, bf16[128,2048]{1,0:T(8,128)(2,1)S(1)} %collective-permute-done.38.refs_1_.refs_3_, f32[512,2048]{1,0:T(8,128)} %down_back.1.refs_2_, bf16[3,2048,2048]{2,1,0:T(8,128)(2,1)} %bitcast.75), custom_call_target="tpu_custom_call" | custom-call | flops 8589934592 | bytes 16777216 | tf_op jit(solution)/shard_map/ffn_middle/pallas_call | solution.py:678
  250.6 19.3 %ffn_products.1 = bf16[3,2048,2048]{2,1,0:T(8,128)(2,1)} custom-call(bf16[128,2048]{1,0:T(8,128)(2,1)S(1)} %get-tuple-element.59.refs_0_, bf16[128,2048]{1,0:T(8,128)(2,1)S(1)} %collective-permute-done.34.refs_1_, bf16[128,2048]{1,0:T(8,128)(2,1)S(1)} %collective-permute-done.39.refs_0_.refs_2_, ...), custom_call_target="tpu_custom_call" | custom-call | flops 12884901888 | bytes 25165824 | tf_op jit(solution)/shard_map/ffn_products/pallas_call | solution.py:733
  275.0 11.3 %collective-permute-done.41 = bf16[128,2048]{1,0:T(8,128)(2,1)S(1)} collective-permute-done((bf16[128,2048]{1,0:T(8,128)(2,1)S(1)}, bf16[128,2048]{1,0:T(8,128)(2,1)S(1)}, u32[]{:S(2)}, u32[]{:S(2)}) %collective-permute-start.41) | collective-permute-done | bytes 524320 | tf_op jit(solution)/shard_map/ppermute | solution.py:43
  289.1 7.3 %collective-permute-done.40 = bf16[128,2048]{1,0:T(8,128)(2,1)S(1)} collective-permute-done((bf16[128,2048]{1,0:T(8,128)(2,1)S(1)}, bf16[128,2048]{1,0:T(8,128)(2,1)S(1)}, u32[]{:S(2)}, u32[]{:S(2)}) %collective-permute-start.40) | collective-permute-done | bytes 524320 | tf_op jit(solution)/shard_map/ppermute | solution.py:43
  296.5 11.4 %collective-permute-done.42 = bf16[128,2048]{1,0:T(8,128)(2,1)S(1)} collective-permute-done((bf16[128,2048]{1,0:T(8,128)(2,1)S(1)}, bf16[128,2048]{1,0:T(8,128)(2,1)S(1)}, u32[]{:S(2)}, u32[]{:S(2)}) %collective-permute-start.42) | collective-permute-done | bytes 524320 | tf_op jit(solution)/shard_map/ppermute | solution.py:43
  316.1 20.3 %attend_back.1 = (bf16[128,2048]{1,0:T(8,128)(2,1)}, bf16[2,512,512]{2,1,0:T(8,128)(2,1)S(1)}, bf16[2,512,512]{2,1,0:T(8,128)(2,1)S(1)}) custom-call(bf16[128,2048]{1,0:T(8,128)(2,1)S(1)} %copy-done.23, bf16[128,2048]{1,0:T(8,128)(2,1)S(1)} %out_back.1.refs_1_, f32[128,2048]{1,0:T(8,128)S(1)} %copy-done.25, bf16[512,1024]{1,0:T(8,128)(2,1)} %copy-done.19, ...), custom_call_target="tpu_custom_call" | custom-call | flops 2684354560 | bytes 4194304 | tf_op jit(solution)/shard_map/attend_back/pallas_call | solution.py:591
  362.8 7.3 %down_forward.1 = f32[512,2048]{1,0:T(8,128)S(1)} custom-call(bf16[3,256,2048]{2,1,0:T(8,128)(2,1)S(1)} %copy-done.5, bf16[3,256,2048]{2,1,0:T(8,128)(2,1)S(1)} %copy-done.7, bf16[3,2048,2048]{2,1,0:T(8,128)(2,1)} %bitcast.76), custom_call_target="tpu_custom_call" | custom-call | flops 4294967296 | bytes 8388608 | tf_op jit(solution)/shard_map/down_forward/pallas_call | solution.py:789
  388.6 26.6 %collective-permute-done.54.refs_7_.refs_3_ = bf16[128,512]{1,0:T(8,128)(2,1)S(1)} collective-permute-done((bf16[128,512]{1,0:T(8,128)(2,1)}, bf16[128,512]{1,0:T(8,128)(2,1)S(1)}, u32[]{:S(2)}, u32[]{:S(2)}) %collective-permute-start.54) | collective-permute-done | bytes 131104 | tf_op jit(solution)/shard_map/ppermute | solution.py:43
  425.4 16.2 %collective-permute-done.66 = f32[1,2048]{1,0:T(1,128)S(1)} collective-permute-done((f32[1,2048]{1,0:T(1,128)S(1)}, f32[1,2048]{1,0:T(1,128)S(1)}, u32[]{:S(2)}, u32[]{:S(2)}) %collective-permute-start.66) | collective-permute-done | bytes 8224 | tf_op jit(solution)/shard_map/ppermute | solution.py:43
  447.9 12.1 %collective-permute-done.61.refs_15_ = bf16[128,2048]{1,0:T(8,128)(2,1)} collective-permute-done((bf16[128,2048]{1,0:T(8,128)(2,1)}, bf16[128,2048]{1,0:T(8,128)(2,1)}, u32[]{:S(2)}, u32[]{:S(2)}) %collective-permute-start.61) | collective-permute-done | bytes 524320 | tf_op jit(solution)/shard_map/ppermute | solution.py:43
  463.2 9.0 %one_back.1 = f32[128,2048]{1,0:T(8,128)} custom-call(bf16[128,2048]{1,0:T(8,128)(2,1)} %get-tuple-element.84.query_ref.refs_13_, bf16[128,1024]{1,0:T(8,128)(2,1)S(1)} %copy-done.8, bf16[2048,3072]{1,0:T(8,128)(2,1)} %get-tuple-element.76.w_ref, bf16[128,2048]{1,0:T(8,128)(2,1)S(1)} %bitcast.65, f32[1,2048]{1,0:T(1,128)S(1)} %bitcast.72, ...), custom_call_target="tpu_custom_call" | custom-call | flops 1610612736 | bytes 12582912 | tf_op jit(solution)/shard_map/one_back/pallas_call | solution.py:320
  473.3 16.9 %collective-permute-done.51.refs_3_ = bf16[128,512]{1,0:T(8,128)(2,1)} collective-permute-done((bf16[128,512]{1,0:T(8,128)(2,1)}, bf16[128,512]{1,0:T(8,128)(2,1)}, u32[]{:S(2)}, u32[]{:S(2)}) %collective-permute-start.51) | collective-permute-done | bytes 131104 | tf_op jit(solution)/shard_map/ppermute | solution.py:43
  490.2 7.5 %share_products.1 = (bf16[4,64,4096]{2,1,0:T(8,128)(2,1)S(1)}, bf16[4,64,4096]{2,1,0:T(8,128)(2,1)}) custom-call(s32[2]{0:T(128)S(1)} %pad_add_fusion.refs_0_, bf16[128,512]{1,0:T(8,128)(2,1)S(1)} %copy.78.refs_1_, bf16[128,512]{1,0:T(8,128)(2,1)S(1)} %collective-permute-done.50.refs_2_, bf16[128,512]{1,0:T(8,128)(2,1)} %collective-permute-done.51.refs_3_, ...), custom_call_target="tpu_custom_call" | custom-call | flops 2147483648 | bytes 4718592 | tf_op jit(solution)/shard_map/share_products/pallas_call | solution.py:867
  519.3 13.1 %collective-permute-done.70 = bf16[64,1152]{1,0:T(8,128)(2,1)S(1)} collective-permute-done((bf16[64,1152]{1,0:T(8,128)(2,1)S(1)}, bf16[64,1152]{1,0:T(8,128)(2,1)S(1)}, u32[]{:S(2)}, u32[]{:S(2)}) %collective-permute-start.70) | collective-permute-done | bytes 147488 | tf_op jit(solution)/shard_map/ppermute | solution.py:43
  533.1 9.4 %collective-permute-done.64 = bf16[64,4096]{1,0:T(8,128)(2,1)S(1)} collective-permute-done((bf16[64,4096]{1,0:T(8,128)(2,1)S(1)}, bf16[64,4096]{1,0:T(8,128)(2,1)S(1)}, u32[]{:S(2)}, u32[]{:S(2)}) %collective-permute-start.64) | collective-permute-done | bytes 524320 | tf_op jit(solution)/shard_map/ppermute | solution.py:43
  (336 shorter events, 227.9 us)
Async XLA Ops:
  7.2 61.6 %all-gather.5.cloned.1.call-start = ((), (), s32[]{:S(2)}) async-start(), calls=%async_computation.3 | async-start | bytes 1310720 | tf_op jit(solution)/shard_map/all_gather | solution.py:184
  40.4 128.3 %all-gather.7.cloned.1.call-start = ((), (), s32[]{:S(2)}) async-start(), calls=%async_computation.4 | async-start | bytes 7077888 | tf_op jit(solution)/shard_map/all_gather | solution.py:191
  71.0 475.4 %reduce-scatter.2.cloned.1.call-start = ((), (), s32[]{:S(2)}) async-start(), calls=%async_computation.2 | async-start | bytes 28311552 | tf_op jit(solution)/shard_map/reduce_scatter | solution.py:1026
  148.4 28.2 %collective-permute-start.37 = (bf16[128,2048]{1,0:T(8,128)(2,1)S(1)}, bf16[128,2048]{1,0:T(8,128)(2,1)S(1)}, u32[]{:S(2)}, u32[]{:S(2)}) collective-permute-start(bf16[128,2048]{1,0:T(8,128)(2,1)S(1)} %bitcast.66), channel_id=1, source_target_pairs={{0,3},{1,2},{2,1},{3,0},{4,7},{5,6},{6,5},{7,4},{8,11},{9,10},{10,... | collective-permute-start | bytes 1572872 | tf_op jit(solution)/shard_map/ppermute | solution.py:43
  149.3 58.1 %collective-permute-start.36 = (bf16[128,2048]{1,0:T(8,128)(2,1)S(1)}, bf16[128,2048]{1,0:T(8,128)(2,1)}, u32[]{:S(2)}, u32[]{:S(2)}) collective-permute-start(bf16[128,2048]{1,0:T(8,128)(2,1)S(1)} %bitcast.67), channel_id=1, source_target_pairs={{0,2},{1,3},{2,0},{3,1},{4,6},{5,7},{6,4},{7,5},{8,10},{9,11},{10,... | collective-permute-start | bytes 1572872 | tf_op jit(solution)/shard_map/ppermute | solution.py:43
  149.6 57.9 %collective-permute-start.35 = (bf16[128,2048]{1,0:T(8,128)(2,1)S(1)}, bf16[128,2048]{1,0:T(8,128)(2,1)}, u32[]{:S(2)}, u32[]{:S(2)}) collective-permute-start(bf16[128,2048]{1,0:T(8,128)(2,1)S(1)} %bitcast.68), channel_id=1, source_target_pairs={{0,1},{1,0},{2,3},{3,2},{4,5},{5,4},{6,7},{7,6},{8,9},{9,8},{10,11... | collective-permute-start | bytes 1572872 | tf_op jit(solution)/shard_map/ppermute | solution.py:43
  175.7 40.6 %collective-permute-start.38 = (bf16[128,2048]{1,0:T(8,128)(2,1)S(1)}, bf16[128,2048]{1,0:T(8,128)(2,1)S(1)}, u32[]{:S(2)}, u32[]{:S(2)}) collective-permute-start(bf16[128,2048]{1,0:T(8,128)(2,1)S(1)} %get-tuple-element.59.refs_0_), channel_id=1, source_target_pairs={{0,3},{1,2},{2,1},{3,0},{4,7},{5,6},{6,5},{7,4},{8,11},{9,10},{10,... | collective-permute-start | bytes 1572872 | tf_op jit(solution)/shard_map/ppermute | solution.py:43
  176.6 42.0 %collective-permute-start.34 = (bf16[128,2048]{1,0:T(8,128)(2,1)S(1)}, bf16[128,2048]{1,0:T(8,128)(2,1)S(1)}, u32[]{:S(2)}, u32[]{:S(2)}) collective-permute-start(bf16[128,2048]{1,0:T(8,128)(2,1)S(1)} %get-tuple-element.59.refs_0_), channel_id=1, source_target_pairs={{0,1},{1,0},{2,3},{3,2},{4,5},{5,4},{6,7},{7,6},{8,9},{9,8},{10,11... | collective-permute-start | bytes 1572872 | tf_op jit(solution)/shard_map/ppermute | solution.py:43
  346.3 40.3 %collective-permute-start.57 = (bf16[128,2048]{1,0:T(8,128)(2,1)}, bf16[128,2048]{1,0:T(8,128)(2,1)}, u32[]{:S(2)}, u32[]{:S(2)}) collective-permute-start(bf16[128,2048]{1,0:T(8,128)(2,1)} %get-tuple-element.80.refs_1_.refs_9_), channel_id=1, source_target_pairs={{0,3},{1,2},{2,1},{3,0},{4,7},{5,6},{6,5},{7,4},{8,11},{9,10},{10,... | collective-permute-start | bytes 1572872 | tf_op jit(solution)/shard_map/ppermute | solution.py:43
  348.8 70.1 %collective-permute-start.56 = (bf16[128,2048]{1,0:T(8,128)(2,1)}, bf16[128,2048]{1,0:T(8,128)(2,1)}, u32[]{:S(2)}, u32[]{:S(2)}) collective-permute-start(bf16[128,2048]{1,0:T(8,128)(2,1)} %get-tuple-element.80.refs_1_.refs_9_), channel_id=1, source_target_pairs={{0,1},{1,0},{2,3},{3,2},{4,5},{5,4},{6,7},{7,6},{8,9},{9,8},{10,11... | collective-permute-start | bytes 1572872 | tf_op jit(solution)/shard_map/ppermute | solution.py:43
  348.8 70.0 %collective-permute-start.60 = (bf16[128,2048]{1,0:T(8,128)(2,1)}, bf16[128,2048]{1,0:T(8,128)(2,1)}, u32[]{:S(2)}, u32[]{:S(2)}) collective-permute-start(bf16[128,2048]{1,0:T(8,128)(2,1)} %get-tuple-element.84.query_ref.refs_13_), channel_id=1, source_target_pairs={{0,3},{1,2},{2,1},{3,0},{4,7},{5,6},{6,5},{7,4},{8,11},{9,10},{10,... | collective-permute-start | bytes 1572872 | tf_op jit(solution)/shard_map/ppermute | solution.py:43
  372.7 42.5 %collective-permute-start.54 = (bf16[128,512]{1,0:T(8,128)(2,1)}, bf16[128,512]{1,0:T(8,128)(2,1)S(1)}, u32[]{:S(2)}, u32[]{:S(2)}) collective-permute-start(bf16[128,512]{1,0:T(8,128)(2,1)} %copy.84), channel_id=1, source_target_pairs={{0,2},{1,3},{2,0},{3,1},{4,6},{5,7},{6,4},{7,5},{8,10},{9,11},{10,... | collective-permute-start | bytes 393224 | tf_op jit(solution)/shard_map/ppermute | solution.py:43
  374.4 42.4 %collective-permute-start.55 = (bf16[128,512]{1,0:T(8,128)(2,1)}, bf16[128,512]{1,0:T(8,128)(2,1)}, u32[]{:S(2)}, u32[]{:S(2)}) collective-permute-start(bf16[128,512]{1,0:T(8,128)(2,1)} %copy.85), channel_id=1, source_target_pairs={{0,3},{1,2},{2,1},{3,0},{4,7},{5,6},{6,5},{7,4},{8,11},{9,10},{10,... | collective-permute-start | bytes 393224 | tf_op jit(solution)/shard_map/ppermute | solution.py:43
  382.1 120.0 %all-to-all-start = ((bf16[4,128,1024]{2,1,0:T(8,128)(2,1)}), bf16[4,128,1024]{2,1,0:T(8,128)(2,1)}, u32[]{:S(2)}, u32[]{:S(2)}) async-start(bf16[4,128,1024]{2,1,0:T(8,128)(2,1)} %broadcast_in_dim.110), calls=%async_computation | async-start | bytes 2097152 | tf_op jit(solution)/shard_map/all_to_all | solution.py:386
  386.5 38.6 %collective-permute-start.58 = (bf16[128,2048]{1,0:T(8,128)(2,1)}, bf16[128,2048]{1,0:T(8,128)(2,1)}, u32[]{:S(2)}, u32[]{:S(2)}) collective-permute-start(bf16[128,2048]{1,0:T(8,128)(2,1)} %collective-permute-done.57.refs_12_), channel_id=1, source_target_pairs={{0,1},{1,0},{2,3},{3,2},{4,5},{5,4},{6,7},{7,6},{8,9},{9,8},{10,11... | collective-permute-start | bytes 1572872 | tf_op jit(solution)/shard_map/ppermute | solution.py:43
  415.2 26.4 %collective-permute-start.59 = (bf16[128,2048]{1,0:T(8,128)(2,1)}, bf16[128,2048]{1,0:T(8,128)(2,1)}, u32[]{:S(2)}, u32[]{:S(2)}) collective-permute-start(bf16[128,2048]{1,0:T(8,128)(2,1)} %get-tuple-element.84.query_ref.refs_13_), channel_id=1, source_target_pairs={{0,1},{1,0},{2,3},{3,2},{4,5},{5,4},{6,7},{7,6},{8,9},{9,8},{10,11... | collective-permute-start | bytes 1572872 | tf_op jit(solution)/shard_map/ppermute | solution.py:43
  418.8 41.2 %collective-permute-start.61 = (bf16[128,2048]{1,0:T(8,128)(2,1)}, bf16[128,2048]{1,0:T(8,128)(2,1)}, u32[]{:S(2)}, u32[]{:S(2)}) collective-permute-start(bf16[128,2048]{1,0:T(8,128)(2,1)} %collective-permute-done.60.refs_16_), channel_id=1, source_target_pairs={{0,1},{1,0},{2,3},{3,2},{4,5},{5,4},{6,7},{7,6},{8,9},{9,8},{10,11... | collective-permute-start | bytes 1572872 | tf_op jit(solution)/shard_map/ppermute | solution.py:43
  418.9 43.8 %collective-permute-start.50 = (bf16[128,512]{1,0:T(8,128)(2,1)}, bf16[128,512]{1,0:T(8,128)(2,1)S(1)}, u32[]{:S(2)}, u32[]{:S(2)}) collective-permute-start(bf16[128,512]{1,0:T(8,128)(2,1)} %copy.79), channel_id=1, source_target_pairs={{0,1},{1,0},{2,3},{3,2},{4,5},{5,4},{6,7},{7,6},{8,9},{9,8},{10,11... | collective-permute-start | bytes 393224 | tf_op jit(solution)/shard_map/ppermute | solution.py:43
  425.2 74.0 %collective-permute-start.43 = (bf16[128,2048]{1,0:T(8,128)(2,1)}, bf16[128,2048]{1,0:T(8,128)(2,1)}, u32[]{:S(2)}, u32[]{:S(2)}) collective-permute-start(bf16[128,2048]{1,0:T(8,128)(2,1)} %slice.232), channel_id=1, source_target_pairs={{0,1},{1,0},{2,3},{3,2},{4,5},{5,4},{6,7},{7,6},{8,9},{9,8},{10,11... | collective-permute-start | bytes 1572872 | tf_op jit(solution)/shard_map/ppermute | solution.py:43
  441.6 57.6 %collective-permute-start.44 = (bf16[128,2048]{1,0:T(8,128)(2,1)}, bf16[128,2048]{1,0:T(8,128)(2,1)}, u32[]{:S(2)}, u32[]{:S(2)}) collective-permute-start(bf16[128,2048]{1,0:T(8,128)(2,1)} %get-tuple-element.122), channel_id=1, source_target_pairs={{0,2},{1,3},{2,0},{3,1},{4,6},{5,7},{6,4},{7,5},{8,10},{9,11},{10,... | collective-permute-start | bytes 1572872 | tf_op jit(solution)/shard_map/ppermute | solution.py:43
  441.6 57.6 %collective-permute-start.45 = (bf16[128,2048]{1,0:T(8,128)(2,1)}, bf16[128,2048]{1,0:T(8,128)(2,1)}, u32[]{:S(2)}, u32[]{:S(2)}) collective-permute-start(bf16[128,2048]{1,0:T(8,128)(2,1)} %get-tuple-element.123), channel_id=1, source_target_pairs={{0,3},{1,2},{2,1},{3,0},{4,7},{5,6},{6,5},{7,4},{8,11},{9,10},{10,... | collective-permute-start | bytes 1572872 | tf_op jit(solution)/shard_map/ppermute | solution.py:43
  460.0 30.2 %collective-permute-start.51 = (bf16[128,512]{1,0:T(8,128)(2,1)}, bf16[128,512]{1,0:T(8,128)(2,1)}, u32[]{:S(2)}, u32[]{:S(2)}) collective-permute-start(bf16[128,512]{1,0:T(8,128)(2,1)} %copy.80), channel_id=1, source_target_pairs={{0,2},{1,3},{2,0},{3,1},{4,6},{5,7},{6,4},{7,5},{8,10},{9,11},{10,... | collective-permute-start | bytes 393224 | tf_op jit(solution)/shard_map/ppermute | solution.py:43
  462.7 27.5 %collective-permute-start.52 = (bf16[128,512]{1,0:T(8,128)(2,1)}, bf16[128,512]{1,0:T(8,128)(2,1)}, u32[]{:S(2)}, u32[]{:S(2)}) collective-permute-start(bf16[128,512]{1,0:T(8,128)(2,1)} %copy.81), channel_id=1, source_target_pairs={{0,3},{1,2},{2,1},{3,0},{4,7},{5,6},{6,5},{7,4},{8,11},{9,10},{10,... | collective-permute-start | bytes 393224 | tf_op jit(solution)/shard_map/ppermute | solution.py:43
  515.3 27.2 %collective-permute-start.64 = (bf16[64,4096]{1,0:T(8,128)(2,1)S(1)}, bf16[64,4096]{1,0:T(8,128)(2,1)S(1)}, u32[]{:S(2)}, u32[]{:S(2)}) collective-permute-start(bf16[64,4096]{1,0:T(8,128)(2,1)S(1)} %get-tuple-element.112), channel_id=1, source_target_pairs={{0,16},{4,20},{8,24},{12,28},{16,0},{20,4},{24,8},{28,12},{1,17},{... | collective-permute-start | bytes 1572872 | tf_op jit(solution)/shard_map/ppermute | solution.py:43
  (102 other events, 1936.8 us)
Sparse Core Ops, SparseCore 0:
  40.5 28.1 all-gather.4
  71.2 57.2 all-gather.6
  270.1 166.8 reduce-scatter.1

commit v6 on v5

--- a/solution.py
+++ b/solution.py
@@ -323,7 +323,7 @@
         out_shape=jax.ShapeDtypeStruct((rows, width), F32),
         in_specs=[
             whole(query_part),
-            whole(pair_part),
+            pl.BlockSpec((rows, pair_part.shape[1]), lambda j: (0, 0)),
             pl.BlockSpec((tile, columns), lambda j: (j, 0)),
             whole(hidden),
             whole(gain),
@@ -340,13 +340,22 @@
     )(query_part, pair_part, in_hbm(weight), hidden, gain, residual_grad)
 
 
-def pass_rows(values):
+def send_rows(values):
     if lax.axis_size("fsdp") != 4:
         return fetch_rows(values)
     third = swap(values, "fsdp", 3)
-    first = swap(values, "fsdp", 1)
-    second = swap(third, "fsdp", 1)
-    return [values, first, second, third]
+    return [values, swap(values, "fsdp", 1), third]
+
+
+def relay_rows(planes):
+    if lax.axis_size("fsdp") != 4:
+        return planes
+    values, first, third = planes
+    return [values, first, swap(third, "fsdp", 1), third]
+
+
+def pass_rows(values):
+    return relay_rows(send_rows(values))
 
 
 def fetch_rows(values):
@@ -365,11 +374,8 @@
         passed = swap(parts[2].astype(BF), "fsdp", 1).astype(F32)
         one = swap(parts[1].astype(BF), "fsdp", 1).astype(F32)
         third = swap((parts[3] + passed).astype(BF), "fsdp", 3).astype(F32)
-        return parts[0] + one + third
-    total = parts[0]
-    for away in range(1, count):
-        total = total + swap(parts[away].astype(BF), "fsdp", away).astype(F32)
-    return total
+        return [parts[0], one, third]
+    return parts[:1] + [swap(parts[i].astype(BF), "fsdp", i) for i in range(1, count)]
 
 
 def by_feature(values):
@@ -377,13 +383,6 @@
     ctx_count, fsdp_count = lax.axis_size("ctx"), lax.axis_size("fsdp")
     blocks = values.reshape(rows, ctx_count, fsdp_count, width // (ctx_count * fsdp_count))
     return blocks.transpose(0, 2, 1, 3).reshape(rows, width)
-
-
-def gather_planes(values):
-    count = lax.axis_size("fsdp")
-    rows, columns = values.shape
-    copies = jnp.broadcast_to(values[None], (count, rows, columns)).reshape(count * rows, columns)
-    return lax.all_to_all(copies, "fsdp", split_axis=0, concat_axis=0, tiled=True)
 
 
 def sum_over_ctx(part_for):
@@ -426,7 +425,7 @@
     got = swap(sent, "ctx", 1)
     sums = (kept.astype(F32) + got.astype(F32)).reshape(2, pairs, count // pairs, width)
     far = [swap(sums[:, pair].astype(BF), "ctx", 2 * pair) for pair in range(1, pairs)]
-    return pair_turn(sums[:, 0], far, cosine, sine), far[0]
+    return pair_turn(sums[:, 0], far, cosine, sine), got
 
 
 def half_mask(shape):
@@ -616,24 +615,31 @@
     )(queries, grads, attended, *arrays, key_anchor, own_anchor, logs, cosine, sine)
 
 
-def pair_turn_kernel(own_ref, *refs):
+def pair_turn_kernel(copies, own_ref, *refs):
     got, (cos_ref, sin_ref, y_ref) = refs[:-3], refs[-3:]
     total = own_ref[...]
     for ref in got:
         total = total + ref[...].astype(F32)
     cosine, sine = cos_ref[...], sin_ref[...]
-    width = total.shape[2]
-    for start in range(0, width, 128):
-        tile = slice(start, start + 128)
-        y_ref[:, tile] = turn(total[0, :, tile], cosine, -sine).astype(BF)
-    y_ref[:, width:] = total[1].astype(BF)
+    _, rows, width = total.shape
+    tiles = [
+        turn(total[0, :, start : start + 128], cosine, -sine).astype(BF)
+        for start in range(0, width, 128)
+    ]
+    values = total[1].astype(BF)
+    for copy in range(copies):
+        at = slice(copy * rows, (copy + 1) * rows)
+        for i, tile in enumerate(tiles):
+            y_ref[at, i * 128 : (i + 1) * 128] = tile
+        y_ref[at, width:] = values
 
 
 def pair_turn(own, got, cosine, sine):
     _, rows, width = own.shape
+    copies = lax.axis_size("fsdp")
     return pl.pallas_call(
-        pair_turn_kernel,
-        out_shape=jax.ShapeDtypeStruct((rows, 2 * width), BF),
+        lambda *refs: pair_turn_kernel(copies, *refs),
+        out_shape=jax.ShapeDtypeStruct((copies * rows, 2 * width), BF),
         name="pair_turn",
     )(own, *got, cosine, sine)
 
@@ -925,16 +931,19 @@
     return lax.dynamic_slice_in_dim(values, index * height, height, 0)
 
 
-def feature_rows(values):
+def feature_parts(values):
     count, plane = lax.axis_size("fsdp"), lax.axis_index("fsdp")
     values = by_feature(values)
     rows, width = values.shape
     width //= count
-    out = []
-    for away in range(count):
-        part = lax.dynamic_slice(values, (0, (plane ^ away) * width), (rows, width))
-        out.append(swap(part, "fsdp", away) if away else part)
-    return out
+    return [
+        lax.dynamic_slice(values, (0, (plane ^ away) * width), (rows, width))
+        for away in range(count)
+    ]
+
+
+def feature_rows(parts):
+    return [swap(part, "fsdp", away) if away else part for away, part in enumerate(parts)]
 
 
 def own_features(terms):
@@ -982,9 +991,10 @@
     scale_one = norm_scale(inputs)
     normed_one = (inputs * scale_one * attn_gain).astype(BF)
 
+    one_parts = feature_parts(normed_one)
     fast = ctx_count == 8 and (qkv_weight.shape[1] // ctx_count) % 128 == 0
     if fast:
-        early = (cosine, sine, own_anchor, key_anchor)
+        early = (cosine, sine, own_anchor, key_anchor, one_parts)
         qkv_pieces, marks = gather_pieces(qkv_weight, early)
         out_blocks = gather_blocks(out_weight, *marks)
         queries, pair, qkv_full = pieces_forward(
@@ -1002,10 +1012,11 @@
         pair = jnp.concatenate(
             [turned[:, queries_width:], projected[:, queries_width + kv_width :]], axis=1
         ).astype(BF)
-    own_one = feature_rows(after(normed_one, marks[1]))
+    own_one = feature_rows(after(one_parts, pair))
     keys_values = gather_keys(pair)
-    rows_out = fetch_rows(after(grad_in, pair))
+    rows_out = send_rows(after(grad_in, pair))
     attn_rows, attended, logs = attend(queries, keys_values, key_anchor, own_anchor)
+    rows_out = relay_rows(after(rows_out, attn_rows))
     residual, normed_two = out_forward(
         attn_rows, out_weight, out_blocks, hidden_in[0], ffn_gain
     )
@@ -1020,8 +1031,8 @@
     for index in range(2):
         blocks = rows_in[index * half : (index + 1) * half]
         middle.append(ffn_middle(blocks, in_hbm(act_grad), index, ffn_parts))
-    parts, partial = [m[0] for m in middle], [m[1] for m in middle]
-    sum_grad = sum_rows(partial, True)
+    parts, partial = [in_hbm(m[0]) for m in middle], [m[1] for m in middle]
+    sum_grad = share_finish(sum_rows(partial, True))
     products = ffn_products(rows_in, rows_out, parts).transpose(1, 0, 2)
     ffn_weight_grad = lax.psum_scatter(products, "ctx", scatter_dimension=0, tiled=True)
     ffn_weight_grad = ffn_weight_grad.astype(F32)
@@ -1034,26 +1045,26 @@
         scaled_two - unit_two * jnp.mean(scaled_two * unit_two, axis=-1, keepdims=True)
     )
     residual_bf = residual_grad.astype(BF)
-    out_sum = sum_rows([after(part, residual_bf) for part in out_partial], False)
-    output = (residual + out_sum).astype(BF)
     (ffn_term,) = own_features([ffn_gain_term])
     attn_grad = out_back(residual_bf, out_weight, out_blocks)
     query_part, kept, sent = attend_back(
         queries, attn_grad, attended, keys_values, key_anchor, own_anchor, logs, cosine, sine
     )
     query_planes = pass_rows(query_part)
-    pair_part, far = sum_pairs(kept, sent, cosine, sine)
-    own_residual = feature_rows(after(residual_bf, far))
-    all_pair = gather_planes(pair_part)
+    pair_copies, near = sum_pairs(kept, sent, cosine, sine)
+    own_residual = feature_rows(feature_parts(after(residual_bf, near)))
+    all_pair = lax.all_to_all(pair_copies, "fsdp", split_axis=0, concat_axis=0, tiled=True)
     input_grad = one_back(
-        query_part, pair_part, qkv_full, hidden_in[0], attn_gain, residual_grad
+        query_part, pair_copies, qkv_full, hidden_in[0], attn_gain, residual_grad
     )
+    out_sum = sum_rows([after(part, input_grad) for part in out_partial], False)
     first_sums = share_start(
         [own_residual, own_one], [after(all_attn, input_grad), after(query_planes, input_grad)], []
     )
     last_sums = share_start([own_one], [all_pair], [ffn_term])
     last_sums = share_finish(last_sums)
     first_sums = share_finish(after(first_sums, last_sums))
+    output = (residual + share_finish(after(out_sum, last_sums))).astype(BF)
 
     pairs_width = 2 * kv_width
     out_weight_grad = first_sums[:, :queries_width]

time: 565 us -> 546 us (0.966)
  waiting for transfers between devices: 251 us -> 204 us
  starting transfers between devices: 84.1 us -> 119 us
  local copies, waits for them, and re-layouts: 47.6 us -> 35.6 us
    ppermute x72, waiting for transfers between devices: 236 us -> 190 us  [swap(): return lax.ppermute(value, axis, [(i, i ^ offset) for i in range(count)])]
    ppermute x72, starting transfers between devices: 79.6 us -> 114 us  [swap(): return lax.ppermute(value, axis, [(i, i ^ offset) for i in range(count)])]
    unnamed x111 -> x120, local copies, waits for them, and re-layouts: 22.8 us -> 11.9 us
  transfers between devices with their start and end apart: 76 -> 76, of which waited for: 35 -> 35; matrix products, arithmetic and copies ran while one was open for 8% -> 8% of each run, Pallas kernels for 19% -> 20%
where the time goes in v6:
time: 546 us; the launch traced here: 539 us
  waiting for transfers between devices  204 us (37%)
  Pallas kernels  146 us (27%)
  starting transfers between devices  119 us (22%)
  local copies, waits for them, and re-layouts  35.6 us (7%)
  other arithmetic  18.7 us (3%)
  between operations  15 us (3%)
    ppermute x72, waiting for transfers between devices, swap(): return lax.ppermute(value, axis, [(i, i ^ offset) for i in range(count)])  190 us
    ppermute x72, starting transfers between devices, swap(): return lax.ppermute(value, axis, [(i, i ^ offset) for i in range(count)])  114 us
    pallas_call x2, Pallas kernels, ffn_middle(): pl.pallas_call(lambda *refs: ffn_kernel(len(blocks), *refs), grid=(hidden...  27.9 us
    pallas_call x1, Pallas kernels, ffn_products(): pl.pallas_call(lambda *refs: products_kernel(count, *refs), grid=(3, widt...  22.2 us
    pallas_call x1, Pallas kernels, attend_back(): pl.pallas_call(lambda *refs: attend_back_kernel(KEY_CHUNK, *refs), grid=(...  20.3 us
    all_gather x1, waiting for transfers between devices, gather_blocks(): planes = lax.all_gather(after(mine, before_fsdp), 'fsdp')  14.1 us
    pallas_call x1, Pallas kernels, attend(): pl.pallas_call(lambda *refs: attend_kernel(KEY_CHUNK, *refs), grid=(KV,),...  13 us
    pallas_call x2, Pallas kernels, out_call(): pl.pallas_call(lambda *refs: out_kernel(back, *refs), out_shape=out_shape...  12.9 us
  transfers between devices with their start and end apart: 76, of which 35 were waited for; matrix products, arithmetic and copies ran while one was open for 8% of the time, Pallas kernels for 20%

profile of v6, /device:TPU:0, one launch (start us, length us, event | category | flops | bytes accessed | tf_op | source)
XLA Modules:
  0.0 539.0 jit_solution(1721523653591669040)
XLA Ops:
  22.9 8.1 %collective-permute-start.20 = (bf16[512,384]{1,0:T(8,128)(2,1)S(1)}, bf16[512,384]{1,0:T(8,128)(2,1)S(1)}, u32[]{:S(2)}, u32[]{:S(2)}) collective-permute-start(bf16[512,384]{1,0:T(8,128)(2,1)S(1)} %collective-permute-done.10.refs_13_), channel_id=1, source_target_pairs={{0,1},{1,0},{2,3},{3,2},{4,5},{5,4},{6,7},{7,6},{8,9},{9,8},{10,11... | collective-permute-start | bytes 1179656 | tf_op jit(solution)/shard_map/ppermute | solution.py:43
  53.7 14.1 %all-gather.5.cloned.1.call-done = bf16[2048,256]{1,0:T(8,128)(2,1)} async-done(((bf16[512,256]{1,0:T(8,128)(2,1)}), bf16[2048,256]{1,0:T(8,128)(2,1)}) %all-gather.5.cloned.1.call-update) | async-done | bytes 1048592 | tf_op jit(solution)/shard_map/all_gather | solution.py:184
  106.0 7.1 %collective-permute-done.6.refs_9_ = bf16[256,384]{1,0:T(8,128)(2,1)S(1)} collective-permute-done((bf16[256,384]{1,0:T(8,128)(2,1)S(1)}, bf16[256,384]{1,0:T(8,128)(2,1)S(1)}, u32[]{:S(2)}, u32[]{:S(2)}) %collective-permute-start.6) | collective-permute-done | bytes 196640 | tf_op jit(solution)/shard_map/ppermute | solution.py:43
  121.3 9.8 %pieces_forward.1 = (bf16[128,2048]{1,0:T(8,128)(2,1)S(1)}, bf16[128,1024]{1,0:T(8,128)(2,1)S(1)}, bf16[2048,3072]{1,0:T(8,128)(2,1)}) custom-call(s32[2]{0:T(128)S(1)} %pad_add_fusion.refs_0_, bf16[128,2048]{1,0:T(8,128)(2,1)S(1)} %fusion.2.refs_1_, bf16[512,3072]{1,0:T(8,128)(2,1)} %refs_2_.3, bf16[512,384]{1,0:T(8,128)(2,1)} %copy-done.35, ...), custom_call_target="tpu_custom_call" | custom-call | flops 1610612736 | bytes 25165824 | tf_op jit(solution)/shard_map/pieces_forward/pallas_call | solution.py:154
  148.7 13.0 %attend.1 = (bf16[128,2048]{1,0:T(8,128)(2,1)}, f32[128,2048]{1,0:T(8,128)S(1)}, f32[8,1,512]{2,1,0:T(1,128)S(1)}) custom-call(bf16[128,2048]{1,0:T(8,128)(2,1)S(1)} %get-tuple-element.63.refs_0_, bf16[512,1024]{1,0:T(8,128)(2,1)S(1)} %constant_dynamic-update-slice_fusion.1.refs_1_.refs_2_.refs_3_.refs_4_, ...), custom_call_target="tpu_custom_call" | custom-call | flops 1073741824 | bytes 2097152 | tf_op jit(solution)/shard_map/attend/pallas_call | solution.py:525
  162.8 10.7 %collective-permute-done.35.refs_1_.refs_5_ = bf16[128,2048]{1,0:T(8,128)(2,1)S(1)} collective-permute-done((bf16[128,2048]{1,0:T(8,128)(2,1)S(1)}, bf16[128,2048]{1,0:T(8,128)(2,1)S(1)}, u32[]{:S(2)}, u32[]{:S(2)}) %collective-permute-start.35) | collective-permute-done | bytes 524320 | tf_op jit(solution)/shard_map/ppermute | solution.py:43
  173.9 7.0 %out_forward.1 = (f32[128,2048]{1,0:T(8,128)S(1)}, bf16[128,2048]{1,0:T(8,128)(2,1)S(1)}) custom-call(s32[2]{0:T(128)S(1)} %pad_add_fusion.refs_0_, bf16[128,2048]{1,0:T(8,128)(2,1)} %get-tuple-element.102.refs_1_.refs_9_, bf16[512,2048]{1,0:T(8,128)(2,1)} %refs_2_.5, bf16[8,3,512,256]{3,2,1,0:T(8,128)(2,1)} %bitcast.80, bf16[128,2048]{1,0:T(8,128)(2,1)S(1)} %bitcast.66, ...), custom_call_target="tpu_custom_call" | custom-call | flops 1073741824 | bytes 8388608 | tf_op jit(solution)/shard_map/out_forward/pallas_call | solution.py:251
  183.4 16.3 %collective-permute-done.37.refs_2_.refs_6_ = bf16[128,2048]{1,0:T(8,128)(2,1)} collective-permute-done((bf16[128,2048]{1,0:T(8,128)(2,1)S(1)}, bf16[128,2048]{1,0:T(8,128)(2,1)}, u32[]{:S(2)}, u32[]{:S(2)}) %collective-permute-start.37) | collective-permute-done | bytes 524320 | tf_op jit(solution)/shard_map/ppermute | solution.py:43
  199.6 8.7 %down_back.1.refs_2_ = f32[512,2048]{1,0:T(8,128)} custom-call(bf16[128,2048]{1,0:T(8,128)(2,1)S(1)} %bitcast.71, bf16[128,2048]{1,0:T(8,128)(2,1)S(1)} %collective-permute-done.35.refs_1_.refs_5_, bf16[128,2048]{1,0:T(8,128)(2,1)} %collective-permute-done.37.refs_2_.refs_6_, bf16[128,2048]{1,0:T(8,128)(2,1)S(1)} %collective-permute-done.36.refs_3_.refs_7_, ...), custom_call_target="tpu_custom_call" | custom-call | flops 4294967296 | bytes 8388608 | tf_op jit(solution)/shard_map/down_back/pallas_call | solution.py:766
  210.8 14.0 %ffn_middle.2 = (bf16[3,256,2048]{2,1,0:T(8,128)(2,1)}, f32[256,2048]{1,0:T(8,128)S(1)}) custom-call(bf16[128,2048]{1,0:T(8,128)(2,1)S(1)} %get-tuple-element.69.refs_0_, bf16[128,2048]{1,0:T(8,128)(2,1)S(1)} %collective-permute-done.34.refs_1_, f32[512,2048]{1,0:T(8,128)} %down_back.1.refs_2_, bf16[3,2048,2048]{2,1,0:T(8,128)(2,1)} %bitcast.76), custom_call_target="tpu_custom_call" | custom-call | flops 8589934592 | bytes 16777216 | tf_op jit(solution)/shard_map/ffn_middle/pallas_call | solution.py:684
  226.1 13.9 %ffn_middle.3 = (bf16[3,256,2048]{2,1,0:T(8,128)(2,1)}, f32[256,2048]{1,0:T(8,128)S(1)}) custom-call(bf16[128,2048]{1,0:T(8,128)(2,1)S(1)} %collective-permute-done.39.refs_0_.refs_2_, bf16[128,2048]{1,0:T(8,128)(2,1)S(1)} %collective-permute-done.38.refs_1_.refs_3_, f32[512,2048]{1,0:T(8,128)} %down_back.1.refs_2_, bf16[3,2048,2048]{2,1,0:T(8,128)(2,1)} %bitcast.77), custom_call_target="tpu_custom_call" | custom-call | flops 8589934592 | bytes 16777216 | tf_op jit(solution)/shard_map/ffn_middle/pallas_call | solution.py:684
  240.0 22.2 %ffn_products.1 = bf16[3,2048,2048]{2,1,0:T(8,128)(2,1)} custom-call(bf16[128,2048]{1,0:T(8,128)(2,1)S(1)} %get-tuple-element.69.refs_0_, bf16[128,2048]{1,0:T(8,128)(2,1)S(1)} %collective-permute-done.34.refs_1_, bf16[128,2048]{1,0:T(8,128)(2,1)S(1)} %collective-permute-done.39.refs_0_.refs_2_, ...), custom_call_target="tpu_custom_call" | custom-call | flops 12884901888 | bytes 25165824 | tf_op jit(solution)/shard_map/ffn_products/pallas_call | solution.py:739
  267.3 11.3 %collective-permute-done.41 = bf16[128,2048]{1,0:T(8,128)(2,1)S(1)} collective-permute-done((bf16[128,2048]{1,0:T(8,128)(2,1)S(1)}, bf16[128,2048]{1,0:T(8,128)(2,1)S(1)}, u32[]{:S(2)}, u32[]{:S(2)}) %collective-permute-start.41) | collective-permute-done | bytes 524320 | tf_op jit(solution)/shard_map/ppermute | solution.py:43
  280.6 17.7 %collective-permute-done.40 = bf16[128,2048]{1,0:T(8,128)(2,1)S(1)} collective-permute-done((bf16[128,2048]{1,0:T(8,128)(2,1)S(1)}, bf16[128,2048]{1,0:T(8,128)(2,1)S(1)}, u32[]{:S(2)}, u32[]{:S(2)}) %collective-permute-start.40) | collective-permute-done | bytes 524320 | tf_op jit(solution)/shard_map/ppermute | solution.py:43
  306.2 20.3 %attend_back.1 = (bf16[128,2048]{1,0:T(8,128)(2,1)}, bf16[2,512,512]{2,1,0:T(8,128)(2,1)S(1)}, bf16[2,512,512]{2,1,0:T(8,128)(2,1)S(1)}) custom-call(bf16[128,2048]{1,0:T(8,128)(2,1)S(1)} %copy-done.19, bf16[128,2048]{1,0:T(8,128)(2,1)S(1)} %out_back.1.refs_1_, f32[128,2048]{1,0:T(8,128)S(1)} %copy-done.25, bf16[512,1024]{1,0:T(8,128)(2,1)} %copy-done.16, ...), custom_call_target="tpu_custom_call" | custom-call | flops 2684354560 | bytes 4194304 | tf_op jit(solution)/shard_map/attend_back/pallas_call | solution.py:590
  333.2 10.4 %collective-permute-done.63.refs_12_ = bf16[128,2048]{1,0:T(8,128)(2,1)} collective-permute-done((bf16[128,2048]{1,0:T(8,128)(2,1)}, bf16[128,2048]{1,0:T(8,128)(2,1)}, u32[]{:S(2)}, u32[]{:S(2)}) %collective-permute-start.63) | collective-permute-done | bytes 524320 | tf_op jit(solution)/shard_map/ppermute | solution.py:43
  343.6 21.4 %collective-permute-start.64 = (bf16[128,2048]{1,0:T(8,128)(2,1)}, bf16[128,2048]{1,0:T(8,128)(2,1)}, u32[]{:S(2)}, u32[]{:S(2)}) collective-permute-start(bf16[128,2048]{1,0:T(8,128)(2,1)} %collective-permute-done.63.refs_12_), channel_id=1, source_target_pairs={{0,1},{1,0},{2,3},{3,2},{4,5},{5,4},{6,7},{7,6},{8,9},{9,8},{10,11... | collective-permute-start | bytes 1572872 | tf_op jit(solution)/shard_map/ppermute | solution.py:43
  365.0 10.8 %collective-permute-start.65 = (bf16[128,2048]{1,0:T(8,128)(2,1)}, bf16[128,2048]{1,0:T(8,128)(2,1)}, u32[]{:S(2)}, u32[]{:S(2)}) collective-permute-start(bf16[128,2048]{1,0:T(8,128)(2,1)} %get-tuple-element.106.query_ref.refs_13_), channel_id=1, source_target_pairs={{0,1},{1,0},{2,3},{3,2},{4,5},{5,4},{6,7},{7,6},{8,9},{9,8},{10,11... | collective-permute-start | bytes 1572872 | tf_op jit(solution)/shard_map/ppermute | solution.py:43
  393.4 22.7 %collective-permute-done.53 = f32[1,2048]{1,0:T(1,128)S(1)} collective-permute-done((f32[1,2048]{1,0:T(1,128)S(1)}, f32[1,2048]{1,0:T(1,128)S(1)}, u32[]{:S(2)}, u32[]{:S(2)}) %collective-permute-start.53) | collective-permute-done | bytes 8224 | tf_op jit(solution)/shard_map/ppermute | solution.py:43
  434.2 9.0 %one_back.1 = f32[128,2048]{1,0:T(8,128)} custom-call(bf16[128,2048]{1,0:T(8,128)(2,1)} %get-tuple-element.106.query_ref.refs_13_, bf16[512,1024]{1,0:T(8,128)(2,1)S(1)} %copy-done.1, bf16[2048,3072]{1,0:T(8,128)(2,1)} %get-tuple-element.87.w_ref, bf16[128,2048]{1,0:T(8,128)(2,1)S(1)} %bitcast.67, f32[1,2048]{1,0:T(1,128)S(1)} %bitcast.73, ...), custom_call_target="tpu_custom_call" | custom-call | flops 1610612736 | bytes 12582912 | tf_op jit(solution)/shard_map/one_back/pallas_call | solution.py:320
  448.5 7.6 %share_products.1 = (bf16[4,64,4096]{2,1,0:T(8,128)(2,1)S(1)}, bf16[4,64,4096]{2,1,0:T(8,128)(2,1)}) custom-call(s32[2]{0:T(128)S(1)} %pad_add_fusion.refs_0_, bf16[128,512]{1,0:T(8,128)(2,1)S(1)} %copy.82.refs_1_, bf16[128,512]{1,0:T(8,128)(2,1)S(1)} %collective-permute-done.59.refs_2_, bf16[128,512]{1,0:T(8,128)(2,1)S(1)} %collective-permute-done.60.refs_3_, ...), custom_call_target="tpu_custom_call" | custom-call | flops 2147483648 | bytes 4718592 | tf_op jit(solution)/shard_map/share_products/pallas_call | solution.py:873
  456.1 8.5 %down_forward.1 = f32[512,2048]{1,0:T(8,128)S(1)} custom-call(bf16[3,256,2048]{2,1,0:T(8,128)(2,1)} %get-tuple-element.78.a_ref.refs_8_, bf16[3,256,2048]{2,1,0:T(8,128)(2,1)} %get-tuple-element.79.b_ref.refs_9_, bf16[3,2048,2048]{2,1,0:T(8,128)(2,1)} %bitcast.78), custom_call_target="tpu_custom_call" | custom-call | flops 4294967296 | bytes 8388608 | tf_op jit(solution)/shard_map/down_forward/pallas_call | solution.py:795
  492.2 10.9 %collective-permute-done.57 = bf16[64,1152]{1,0:T(8,128)(2,1)S(1)} collective-permute-done((bf16[64,1152]{1,0:T(8,128)(2,1)S(1)}, bf16[64,1152]{1,0:T(8,128)(2,1)S(1)}, u32[]{:S(2)}, u32[]{:S(2)}) %collective-permute-start.57) | collective-permute-done | bytes 147488 | tf_op jit(solution)/shard_map/ppermute | solution.py:43
  507.3 12.5 %collective-permute-done.48 = bf16[128,2048]{1,0:T(8,128)(2,1)} collective-permute-done((bf16[128,2048]{1,0:T(8,128)(2,1)}, bf16[128,2048]{1,0:T(8,128)(2,1)}, u32[]{:S(2)}, u32[]{:S(2)}) %collective-permute-start.48) | collective-permute-done | bytes 524320 | tf_op jit(solution)/shard_map/ppermute | solution.py:43
  (352 shorter events, 216.1 us)
Async XLA Ops:
  7.2 60.6 %all-gather.5.cloned.1.call-start = ((), (), s32[]{:S(2)}) async-start(), calls=%async_computation.3 | async-start | bytes 1310720 | tf_op jit(solution)/shard_map/all_gather | solution.py:184
  39.5 134.4 %all-gather.7.cloned.1.call-start = ((), (), s32[]{:S(2)}) async-start(), calls=%async_computation.4 | async-start | bytes 7077888 | tf_op jit(solution)/shard_map/all_gather | solution.py:191
  50.0 20.0 %collective-permute-start.26 = (bf16[256,384]{1,0:T(8,128)(2,1)}, bf16[256,384]{1,0:T(8,128)(2,1)}, u32[]{:S(2)}, u32[]{:S(2)}) collective-permute-start(bf16[256,384]{1,0:T(8,128)(2,1)} %slice.172), channel_id=1, source_target_pairs={{0,8},{4,12},{8,0},{12,4},{16,24},{20,28},{24,16},{28,20},{1,9},{5... | collective-permute-start | bytes 589832 | tf_op jit(solution)/shard_map/ppermute | solution.py:43
  70.0 456.8 %reduce-scatter.2.cloned.1.call-start = ((), (), s32[]{:S(2)}) async-start(), calls=%async_computation.2 | async-start | bytes 28311552 | tf_op jit(solution)/shard_map/reduce_scatter | solution.py:1037
  148.4 25.2 %collective-permute-start.35 = (bf16[128,2048]{1,0:T(8,128)(2,1)S(1)}, bf16[128,2048]{1,0:T(8,128)(2,1)S(1)}, u32[]{:S(2)}, u32[]{:S(2)}) collective-permute-start(bf16[128,2048]{1,0:T(8,128)(2,1)S(1)} %bitcast.70), channel_id=1, source_target_pairs={{0,1},{1,0},{2,3},{3,2},{4,5},{5,4},{6,7},{7,6},{8,9},{9,8},{10,11... | collective-permute-start | bytes 1572872 | tf_op jit(solution)/shard_map/ppermute | solution.py:43
  173.5 26.1 %collective-permute-start.37 = (bf16[128,2048]{1,0:T(8,128)(2,1)S(1)}, bf16[128,2048]{1,0:T(8,128)(2,1)}, u32[]{:S(2)}, u32[]{:S(2)}) collective-permute-start(bf16[128,2048]{1,0:T(8,128)(2,1)S(1)} %collective-permute-done.36.refs_3_.refs_7_), channel_id=1, source_target_pairs={{0,1},{1,0},{2,3},{3,2},{4,5},{5,4},{6,7},{7,6},{8,9},{9,8},{10,11... | collective-permute-start | bytes 1572872 | tf_op jit(solution)/shard_map/ppermute | solution.py:43
  180.9 27.4 %collective-permute-start.38 = (bf16[128,2048]{1,0:T(8,128)(2,1)S(1)}, bf16[128,2048]{1,0:T(8,128)(2,1)S(1)}, u32[]{:S(2)}, u32[]{:S(2)}) collective-permute-start(bf16[128,2048]{1,0:T(8,128)(2,1)S(1)} %get-tuple-element.69.refs_0_), channel_id=1, source_target_pairs={{0,3},{1,2},{2,1},{3,0},{4,7},{5,6},{6,5},{7,4},{8,11},{9,10},{10,... | collective-permute-start | bytes 1572872 | tf_op jit(solution)/shard_map/ppermute | solution.py:43
  182.6 28.2 %collective-permute-start.34 = (bf16[128,2048]{1,0:T(8,128)(2,1)S(1)}, bf16[128,2048]{1,0:T(8,128)(2,1)S(1)}, u32[]{:S(2)}, u32[]{:S(2)}) collective-permute-start(bf16[128,2048]{1,0:T(8,128)(2,1)S(1)} %get-tuple-element.69.refs_0_), channel_id=1, source_target_pairs={{0,1},{1,0},{2,3},{3,2},{4,5},{5,4},{6,7},{7,6},{8,9},{9,8},{10,11... | collective-permute-start | bytes 1572872 | tf_op jit(solution)/shard_map/ppermute | solution.py:43
  265.6 32.7 %collective-permute-start.40 = (bf16[128,2048]{1,0:T(8,128)(2,1)S(1)}, bf16[128,2048]{1,0:T(8,128)(2,1)S(1)}, u32[]{:S(2)}, u32[]{:S(2)}) collective-permute-start(bf16[128,2048]{1,0:T(8,128)(2,1)S(1)} %slice.231), channel_id=1, source_target_pairs={{0,1},{1,0},{2,3},{3,2},{4,5},{5,4},{6,7},{7,6},{8,9},{9,8},{10,11... | collective-permute-start | bytes 1572872 | tf_op jit(solution)/shard_map/ppermute | solution.py:43
  328.2 36.8 %collective-permute-start.66 = (bf16[128,2048]{1,0:T(8,128)(2,1)}, bf16[128,2048]{1,0:T(8,128)(2,1)}, u32[]{:S(2)}, u32[]{:S(2)}) collective-permute-start(bf16[128,2048]{1,0:T(8,128)(2,1)} %get-tuple-element.106.query_ref.refs_13_), channel_id=1, source_target_pairs={{0,3},{1,2},{2,1},{3,0},{4,7},{5,6},{6,5},{7,4},{8,11},{9,10},{10,... | collective-permute-start | bytes 1572872 | tf_op jit(solution)/shard_map/ppermute | solution.py:43
  330.7 45.1 %collective-permute-start.46 = (bf16[2,128,512]{2,1,0:T(8,128)(2,1)S(1)}, bf16[2,128,512]{2,1,0:T(8,128)(2,1)S(1)}, u32[]{:S(2)}, u32[]{:S(2)}) collective-permute-start(bf16[2,128,512]{2,1,0:T(8,128)(2,1)S(1)} %get-tuple-element.141), channel_id=1, source_target_pairs={{0,24},{4,28},{8,16},{12,20},{16,8},{20,12},{24,0},{28,4},{1,25},{... | collective-permute-start | bytes 786440 | tf_op jit(solution)/shard_map/ppermute | solution.py:43
  331.7 44.1 %collective-permute-start.45 = (bf16[2,128,512]{2,1,0:T(8,128)(2,1)S(1)}, bf16[2,128,512]{2,1,0:T(8,128)(2,1)S(1)}, u32[]{:S(2)}, u32[]{:S(2)}) collective-permute-start(bf16[2,128,512]{2,1,0:T(8,128)(2,1)S(1)} %get-tuple-element.142), channel_id=1, source_target_pairs={{0,16},{4,20},{8,24},{12,28},{16,0},{20,4},{24,8},{28,12},{1,17},{... | collective-permute-start | bytes 786440 | tf_op jit(solution)/shard_map/ppermute | solution.py:43
  332.7 93.8 %collective-permute-start.62 = (bf16[128,2048]{1,0:T(8,128)(2,1)}, bf16[128,2048]{1,0:T(8,128)(2,1)}, u32[]{:S(2)}, u32[]{:S(2)}) collective-permute-start(bf16[128,2048]{1,0:T(8,128)(2,1)} %get-tuple-element.102.refs_1_.refs_9_), channel_id=1, source_target_pairs={{0,1},{1,0},{2,3},{3,2},{4,5},{5,4},{6,7},{7,6},{8,9},{9,8},{10,11... | collective-permute-start | bytes 1572872 | tf_op jit(solution)/shard_map/ppermute | solution.py:43
  343.6 85.0 %collective-permute-start.64 = (bf16[128,2048]{1,0:T(8,128)(2,1)}, bf16[128,2048]{1,0:T(8,128)(2,1)}, u32[]{:S(2)}, u32[]{:S(2)}) collective-permute-start(bf16[128,2048]{1,0:T(8,128)(2,1)} %collective-permute-done.63.refs_12_), channel_id=1, source_target_pairs={{0,1},{1,0},{2,3},{3,2},{4,5},{5,4},{6,7},{7,6},{8,9},{9,8},{10,11... | collective-permute-start | bytes 1572872 | tf_op jit(solution)/shard_map/ppermute | solution.py:43
  365.0 64.3 %collective-permute-start.65 = (bf16[128,2048]{1,0:T(8,128)(2,1)}, bf16[128,2048]{1,0:T(8,128)(2,1)}, u32[]{:S(2)}, u32[]{:S(2)}) collective-permute-start(bf16[128,2048]{1,0:T(8,128)(2,1)} %get-tuple-element.106.query_ref.refs_13_), channel_id=1, source_target_pairs={{0,1},{1,0},{2,3},{3,2},{4,5},{5,4},{6,7},{7,6},{8,9},{9,8},{10,11... | collective-permute-start | bytes 1572872 | tf_op jit(solution)/shard_map/ppermute | solution.py:43
  375.8 55.1 %collective-permute-start.67 = (bf16[128,2048]{1,0:T(8,128)(2,1)}, bf16[128,2048]{1,0:T(8,128)(2,1)}, u32[]{:S(2)}, u32[]{:S(2)}) collective-permute-start(bf16[128,2048]{1,0:T(8,128)(2,1)} %collective-permute-done.66.refs_16_), channel_id=1, source_target_pairs={{0,1},{1,0},{2,3},{3,2},{4,5},{5,4},{6,7},{7,6},{8,9},{9,8},{10,11... | collective-permute-start | bytes 1572872 | tf_op jit(solution)/shard_map/ppermute | solution.py:43
  386.9 87.4 %all-to-all-start = ((bf16[4,128,1024]{2,1,0:T(8,128)(2,1)}), bf16[4,128,1024]{2,1,0:T(8,128)(2,1)}, u32[]{:S(2)}, u32[]{:S(2)}) async-start(bf16[4,128,1024]{2,1,0:T(8,128)(2,1)} %bitcast.68), calls=%async_computation | async-start | bytes 2097152 | tf_op jit(solution)/shard_map/all_to_all | solution.py:1056
  391.4 24.8 %collective-permute-start.53 = (f32[1,2048]{1,0:T(1,128)S(1)}, f32[1,2048]{1,0:T(1,128)S(1)}, u32[]{:S(2)}, u32[]{:S(2)}) collective-permute-start(f32[1,2048]{1,0:T(1,128)S(1)} %bitcast.92), channel_id=1, source_target_pairs={{0,1},{1,0},{2,3},{3,2},{4,5},{5,4},{6,7},{7,6},{8,9},{9,8},{10,11... | collective-permute-start | bytes 24584 | tf_op jit(solution)/shard_map/ppermute | solution.py:43
  443.2 23.2 %collective-permute-start.54 = (f32[1,2048]{1,0:T(1,128)S(1)}, f32[1,2048]{1,0:T(1,128)S(1)}, u32[]{:S(2)}, u32[]{:S(2)}) collective-permute-start(f32[1,2048]{1,0:T(1,128)S(1)} %add.410), channel_id=1, source_target_pairs={{0,2},{1,3},{2,0},{3,1},{4,6},{5,7},{6,4},{7,5},{8,10},{9,11},{10,... | collective-permute-start | bytes 24584 | tf_op jit(solution)/shard_map/ppermute | solution.py:43
  456.1 25.5 %collective-permute-start.68 = (bf16[4,64,4096]{2,1,0:T(8,128)(2,1)}, bf16[4,64,4096]{2,1,0:T(8,128)(2,1)}, u32[]{:S(2)}, u32[]{:S(2)}) collective-permute-start(bf16[4,64,4096]{2,1,0:T(8,128)(2,1)} %get-tuple-element.111), channel_id=1, source_target_pairs={{0,4},{4,0},{8,12},{12,8},{16,20},{20,16},{24,28},{28,24},{1,5},{5... | collective-permute-start | bytes 6291464 | tf_op jit(solution)/shard_map/ppermute | solution.py:43
  468.7 37.1 %collective-permute-start.47 = (bf16[128,2048]{1,0:T(8,128)(2,1)}, bf16[128,2048]{1,0:T(8,128)(2,1)}, u32[]{:S(2)}, u32[]{:S(2)}) collective-permute-start(bf16[128,2048]{1,0:T(8,128)(2,1)} %slice.229), channel_id=1, source_target_pairs={{0,1},{1,0},{2,3},{3,2},{4,5},{5,4},{6,7},{7,6},{8,9},{9,8},{10,11... | collective-permute-start | bytes 1572872 | tf_op jit(solution)/shard_map/ppermute | solution.py:43
  472.7 34.6 %collective-permute-start.49 = (bf16[128,2048]{1,0:T(8,128)(2,1)}, bf16[128,2048]{1,0:T(8,128)(2,1)}, u32[]{:S(2)}, u32[]{:S(2)}) collective-permute-start(bf16[128,2048]{1,0:T(8,128)(2,1)} %get-tuple-element.139), channel_id=1, source_target_pairs={{0,3},{1,2},{2,1},{3,0},{4,7},{5,6},{6,5},{7,4},{8,11},{9,10},{10,... | collective-permute-start | bytes 1572872 | tf_op jit(solution)/shard_map/ppermute | solution.py:43
  474.3 45.5 %collective-permute-start.48 = (bf16[128,2048]{1,0:T(8,128)(2,1)}, bf16[128,2048]{1,0:T(8,128)(2,1)}, u32[]{:S(2)}, u32[]{:S(2)}) collective-permute-start(bf16[128,2048]{1,0:T(8,128)(2,1)} %get-tuple-element.140), channel_id=1, source_target_pairs={{0,2},{1,3},{2,0},{3,1},{4,6},{5,7},{6,4},{7,5},{8,10},{9,11},{10,... | collective-permute-start | bytes 1572872 | tf_op jit(solution)/shard_map/ppermute | solution.py:43
  490.8 32.1 %collective-permute-start.71 = (bf16[64,4096]{1,0:T(8,128)(2,1)S(1)}, bf16[64,4096]{1,0:T(8,128)(2,1)S(1)}, u32[]{:S(2)}, u32[]{:S(2)}) collective-permute-start(bf16[64,4096]{1,0:T(8,128)(2,1)S(1)} %get-tuple-element.131), channel_id=1, source_target_pairs={{0,24},{4,28},{8,16},{12,20},{16,8},{20,12},{24,0},{28,4},{1,25},{... | collective-permute-start | bytes 1572872 | tf_op jit(solution)/shard_map/ppermute | solution.py:43
  (110 other events, 1909.8 us)
Sparse Core Ops, SparseCore 0:
  39.6 28.1 all-gather.4
  70.3 57.2 all-gather.6
  262.4 165.4 reduce-scatter.1

commit v7 on v6

--- a/solution.py
+++ b/solution.py
@@ -363,19 +363,14 @@
     return [values] + [swap(values, "fsdp", away) for away in range(1, count)]
 
 
-def sum_rows(halves, forward):
-    count = lax.axis_size("fsdp")
-    half = count // 2
-    rows = halves[0].shape[0] // half
-    parts = [
-        halves[away // half][away % half * rows : (away % half + 1) * rows] for away in range(count)
-    ]
+def sum_rows(parts, forward):
+    count = len(parts)
     if count == 4 and forward:
-        passed = swap(parts[2].astype(BF), "fsdp", 1).astype(F32)
-        one = swap(parts[1].astype(BF), "fsdp", 1).astype(F32)
-        third = swap((parts[3] + passed).astype(BF), "fsdp", 3).astype(F32)
+        passed = swap(parts[2], "fsdp", 1).astype(F32)
+        one = swap(parts[1], "fsdp", 1)
+        third = swap((parts[3].astype(F32) + passed).astype(BF), "fsdp", 3)
         return [parts[0], one, third]
-    return parts[:1] + [swap(parts[i].astype(BF), "fsdp", i) for i in range(1, count)]
+    return parts[:1] + [swap(parts[i], "fsdp", i) for i in range(1, count)]
 
 
 def by_feature(values):
@@ -653,7 +648,8 @@
 
 
 def ffn_kernel(count, *refs):
-    rows_refs, (act_ref, w_ref, out_ref, sum_ref, x_buf) = refs[:count], refs[count:]
+    rows_refs, (act_ref, w_ref, out_ref), refs = refs[:count], refs[count : count + 3], refs[count + 3 :]
+    sum_refs, (x_buf, sum_buf) = refs[:count], refs[count:]
     join_rows(x_buf, rows_refs)
     step = pl.program_id(0)
     gate_w, up_w = w_ref[0], w_ref[1]
@@ -669,35 +665,39 @@
 
     @pl.when(step == 0)
     def _():
-        sum_ref[...] = part
+        sum_buf[...] = part
 
     @pl.when(step > 0)
     def _():
-        sum_ref[...] += part
-
-
-def ffn_middle(blocks, act_grad, half, weights):
+        sum_buf[...] += part
+
+    @pl.when(step == pl.num_programs(0) - 1)
+    def _():
+        rows = sum_refs[0].shape[0]
+        for i, ref in enumerate(sum_refs):
+            ref[...] = sum_buf[i * rows : (i + 1) * rows].astype(ref.dtype)
+
+
+def ffn_middle(blocks, act_grad, half, weights, kinds):
     width = blocks[0].shape[1]
     rows = blocks[0].shape[0] * len(blocks)
     hidden = weights.shape[2]
     tile = FFN_TILE
-    return pl.pallas_call(
+    whole = [pl.BlockSpec(block.shape, lambda j: (0, 0)) for block in blocks]
+    out = pl.pallas_call(
         lambda *refs: ffn_kernel(len(blocks), *refs),
         grid=(hidden // tile,),
         out_shape=(
             pltpu.HBM((3, rows, hidden), BF),
-            jax.ShapeDtypeStruct((rows, width), F32),
-        ),
-        in_specs=[pl.BlockSpec(block.shape, lambda j: (0, 0)) for block in blocks]
+            *[jax.ShapeDtypeStruct(block.shape, kind) for block, kind in zip(blocks, kinds)],
+        ),
+        in_specs=whole
         + [
             pl.BlockSpec((rows, tile), lambda j: (half, j)),
             pl.BlockSpec((2, width, tile), lambda j: (0, 0, j)),
         ],
-        out_specs=(
-            pl.BlockSpec((3, rows, tile), lambda j: (0, 0, j)),
-            pl.BlockSpec((rows, width), lambda j: (0, 0)),
-        ),
-        scratch_shapes=[pltpu.VMEM((rows, width), BF)],
+        out_specs=(pl.BlockSpec((3, rows, tile), lambda j: (0, 0, j)), *whole),
+        scratch_shapes=[pltpu.VMEM((rows, width), BF), pltpu.VMEM((rows, width), F32)],
         compiler_params=pltpu.CompilerParams(vmem_limit_bytes=40 << 20),
         cost_estimate=pl.CostEstimate(
             flops=8 * rows * width * hidden,
@@ -706,6 +706,7 @@
         ),
         name="ffn_middle",
     )(*blocks, act_grad, weights)
+    return out[0], list(out[1:])
 
 
 def products_kernel(count, *refs):
@@ -752,6 +753,98 @@
     )(*rows_in, *rows_out, *parts)
 
 
+def half_products_kernel(count, added, ids_ref, *refs):
+    in_refs, grad_refs = refs[: 2 * count], refs[2 * count : 4 * count]
+    rights, rest = refs[4 * count : 4 * count + 2], refs[4 * count + 2 :]
+    out_ref = rest[-1]
+    half = count // 2
+
+    def emit(lefts):
+        height = lefts[0].shape[1]
+        for j in range(2):
+            part = None
+            for i, right in enumerate(rights):
+                group = lefts[j * count + i * half : j * count + (i + 1) * half]
+                left = jnp.concatenate([ref[...] for ref in group], axis=0)
+                product = tn(left, right[0])
+                part = product if part is None else part + product
+            at = slice(j * height, (j + 1) * height)
+            if added:
+                part = part + rest[0][0, at].astype(F32)
+            out_ref[0, at] = part.astype(BF)
+
+    @pl.when(pl.program_id(0) < 2)
+    def _():
+        emit(in_refs)
+
+    @pl.when(pl.program_id(0) == 2)
+    def _():
+        emit(grad_refs)
+
+
+def half_products(rows_in, rows_out, parts, got):
+    count = len(rows_in)
+    rows, width = rows_in[0].shape
+    hidden = parts[0].shape[2]
+    ctx_count = lax.axis_size("ctx")
+    height = width // ctx_count
+    last = ctx_count // 4 - 1
+
+    def column(i, j, ids_ref):
+        own = ids_ref[0] % 2
+        return 2 * (2 * i + j) + (own if got is not None else 1 - own)
+
+    def left(j):
+        return pl.BlockSpec(
+            (rows, height),
+            lambda k, i, ids_ref: (0, column(jnp.where(k < 2, i, last), j, ids_ref)),
+        )
+
+    def grad(j):
+        return pl.BlockSpec(
+            (rows, height),
+            lambda k, i, ids_ref: (0, column(jnp.where(k == 2, i, 0), j, ids_ref)),
+        )
+
+    right = pl.BlockSpec((1, rows * count // 2, hidden), lambda k, i, ids_ref: (k, 0, 0))
+    out = pl.BlockSpec((1, 2 * height, hidden), lambda k, i, ids_ref: (k, i, 0))
+    extra = [] if got is None else [in_hbm(got)]
+    return pl.pallas_call(
+        lambda *refs: half_products_kernel(count, got is not None, *refs),
+        grid_spec=pltpu.PrefetchScalarGridSpec(
+            num_scalar_prefetch=1,
+            grid=(3, ctx_count // 4),
+            in_specs=[left(0)] * count
+            + [left(1)] * count
+            + [grad(0)] * count
+            + [grad(1)] * count
+            + [right, right]
+            + [out] * len(extra),
+            out_specs=out,
+        ),
+        out_shape=pltpu.HBM((3, width // 2, hidden), BF),
+        compiler_params=pltpu.CompilerParams(vmem_limit_bytes=40 << 20),
+        cost_estimate=pl.CostEstimate(
+            flops=3 * count * rows * width * hidden,
+            bytes_accessed=3 * width * hidden,
+            transcendentals=0,
+        ),
+        name="kept_products" if extra else "sent_products",
+    )(jnp.stack(ids()), *rows_in, *rows_in, *rows_out, *rows_out, *parts, *extra)
+
+
+def ffn_gradient(rows_in, rows_out, parts):
+    count = lax.axis_size("ctx")
+    if count % 4 or (rows_in[0].shape[1] // count) % 128:
+        products = ffn_products(rows_in, rows_out, parts).transpose(1, 0, 2)
+        return lax.psum_scatter(products, "ctx", scatter_dimension=0, tiled=True)
+    sent = half_products(rows_in, rows_out, parts, None)
+    got = swap(sent, "ctx", 1)
+    kept = half_products(rows_in, rows_out, parts, got).transpose(1, 0, 2)
+    groups = [list(range(core, count, 2)) for core in range(2)]
+    return lax.psum_scatter(kept, "ctx", scatter_dimension=0, tiled=True, axis_index_groups=groups)
+
+
 def down_back_kernel(count, *refs):
     rows_refs, (w_ref, y_ref, x_buf) = refs[:count], refs[count:]
     join_rows(x_buf, rows_refs)
@@ -781,23 +874,29 @@
     )(*blocks, weights)
 
 
-def down_kernel(a_ref, b_ref, w_ref, y_ref):
-    rows = a_ref.shape[1]
-    for half, ref in enumerate((a_ref, b_ref)):
-        y_ref[half * rows : (half + 1) * rows] = nt(ref[0], w_ref[0])
-
-
-def down_forward(parts, weights):
+def down_kernel(a_ref, b_ref, w_ref, *y_refs):
+    rows = a_ref.shape[1] * 2 // len(y_refs)
+    totals = [nt(ref[0], w_ref[0]) for ref in (a_ref, b_ref)]
+    half = len(y_refs) // 2
+    for i, y_ref in enumerate(y_refs):
+        start = i % half * rows
+        y_ref[...] = totals[i // half][start : start + rows].astype(y_ref.dtype)
+
+
+def down_forward(parts, weights, count):
     _, rows, hidden = parts[0].shape
     width = weights.shape[1]
     tile = FFN_TILE
+    height = 2 * rows // count
     left = pl.BlockSpec((1, rows, hidden), lambda j: (2, 0, 0))
-    total = pl.pallas_call(
+    return pl.pallas_call(
         down_kernel,
         grid=(width // tile,),
-        out_shape=jax.ShapeDtypeStruct((2 * rows, width), F32),
+        out_shape=tuple(
+            jax.ShapeDtypeStruct((height, width), BF if i else F32) for i in range(count)
+        ),
         in_specs=[left, left, pl.BlockSpec((1, tile, hidden), lambda j: (2, j, 0))],
-        out_specs=pl.BlockSpec((2 * rows, tile), lambda j: (0, j)),
+        out_specs=tuple(pl.BlockSpec((height, tile), lambda j: (0, j)) for _ in range(count)),
         compiler_params=pltpu.CompilerParams(vmem_limit_bytes=24 << 20),
         cost_estimate=pl.CostEstimate(
             flops=4 * rows * width * hidden,
@@ -806,7 +905,6 @@
         ),
         name="down_forward",
     )(*parts, weights)
-    return total[:rows], total[rows:]
 
 
 def share_kernel(count, sizes, ids_ref, *refs):
@@ -1028,15 +1126,16 @@
     all_attn = pass_rows(after(attn_rows, rows_in[2]))
     middle = []
     half = fsdp_count // 2
+    passing = 3 if fsdp_count == 4 else 0
     for index in range(2):
         blocks = rows_in[index * half : (index + 1) * half]
-        middle.append(ffn_middle(blocks, in_hbm(act_grad), index, ffn_parts))
-    parts, partial = [in_hbm(m[0]) for m in middle], [m[1] for m in middle]
+        kinds = [F32 if index * half + i in (0, passing) else BF for i in range(half)]
+        middle.append(ffn_middle(blocks, in_hbm(act_grad), index, ffn_parts, kinds))
+    parts, partial = [in_hbm(m[0]) for m in middle], [block for m in middle for block in m[1]]
     sum_grad = share_finish(sum_rows(partial, True))
-    products = ffn_products(rows_in, rows_out, parts).transpose(1, 0, 2)
-    ffn_weight_grad = lax.psum_scatter(products, "ctx", scatter_dimension=0, tiled=True)
+    ffn_weight_grad = ffn_gradient(rows_in, rows_out, parts)
     ffn_weight_grad = ffn_weight_grad.astype(F32)
-    out_partial = down_forward(parts, ffn_parts)
+    out_partial = list(down_forward(parts, ffn_parts, fsdp_count))
 
     unit_two = residual * scale_two
     ffn_gain_term = jnp.sum(sum_grad * unit_two, axis=0)

time: 546 us -> 593 us (1.086)
  waiting for transfers between devices: 204 us -> 237 us
  Pallas kernels: 146 us -> 155 us
    ppermute x72 -> x73, waiting for transfers between devices: 190 us -> 223 us  [swap(): return lax.ppermute(value, axis, [(i, i ^ offset) for i in range(count)])]
    unnamed x120 -> x138, local copies, waits for them, and re-layouts: 11.9 us -> 24.9 us
    pallas_call x2 -> x3, Pallas kernels: 30.7 us -> 39.1 us  [the longest x2 31.3 us: half_products(): pl.pallas_call(lambda *refs: half_products_kernel(count, got is not None,...]
    slice x8 -> x0, local copies, waits for them, and re-layouts: 7.68 us -> none  [the longest x6 5.99 us: sum_rows(): halves[away // half][away % half * rows:(away % half + 1) * rows]]
    ppermute x72 -> x73, starting transfers between devices: 114 us -> 114 us  [swap(): return lax.ppermute(value, axis, [(i, i ^ offset) for i in range(count)])]
  transfers between devices with their start and end apart: 76 -> 77, of which waited for: 35 -> 37; matrix products, arithmetic and copies ran while one was open for 8% -> 6% of each run, Pallas kernels for 20% -> 19%
where the time goes in v7:
time: 593 us; the launch traced here: 585 us
  waiting for transfers between devices  237 us (40%)
  Pallas kernels  155 us (26%)
  starting transfers between devices  119 us (20%)
  local copies, waits for them, and re-layouts  39.9 us (7%)
  other arithmetic  18.8 us (3%)
  between operations  15 us (3%)
    ppermute x73, waiting for transfers between devices, swap(): return lax.ppermute(value, axis, [(i, i ^ offset) for i in range(count)])  223 us
    ppermute x73, starting transfers between devices, swap(): return lax.ppermute(value, axis, [(i, i ^ offset) for i in range(count)])  114 us
    pallas_call x2, Pallas kernels, half_products(): pl.pallas_call(lambda *refs: half_products_kernel(count, got is not None,...  31.3 us
    pallas_call x2, Pallas kernels, ffn_middle(): pl.pallas_call(lambda *refs: ffn_kernel(len(blocks), *refs), grid=(hidden...  28.1 us
    unnamed x138, local copies, waits for them, and re-layouts  24.9 us
    pallas_call x1, Pallas kernels, attend_back(): pl.pallas_call(lambda *refs: attend_back_kernel(KEY_CHUNK, *refs), grid=(...  20.3 us
    all_gather x1, waiting for transfers between devices, gather_blocks(): planes = lax.all_gather(after(mine, before_fsdp), 'fsdp')  14.1 us
    pallas_call x1, Pallas kernels, attend(): pl.pallas_call(lambda *refs: attend_kernel(KEY_CHUNK, *refs), grid=(KV,),...  13.1 us
  transfers between devices with their start and end apart: 77, of which 37 were waited for; matrix products, arithmetic and copies ran while one was open for 6% of the time, Pallas kernels for 19%

profile of v7, /device:TPU:0, one launch (start us, length us, event | category | flops | bytes accessed | tf_op | source)
XLA Modules:
  0.0 584.7 jit_solution(14416938719368406704)
XLA Ops:
  22.9 8.1 %collective-permute-start.20 = (bf16[512,384]{1,0:T(8,128)(2,1)S(1)}, bf16[512,384]{1,0:T(8,128)(2,1)S(1)}, u32[]{:S(2)}, u32[]{:S(2)}) collective-permute-start(bf16[512,384]{1,0:T(8,128)(2,1)S(1)} %collective-permute-done.10.refs_13_), channel_id=1, source_target_pairs={{0,1},{1,0},{2,3},{3,2},{4,5},{5,4},{6,7},{7,6},{8,9},{9,8},{10,11... | collective-permute-start | bytes 1179656 | tf_op jit(solution)/shard_map/ppermute | solution.py:43
  53.7 14.1 %all-gather.5.cloned.1.call-done = bf16[2048,256]{1,0:T(8,128)(2,1)} async-done(((bf16[512,256]{1,0:T(8,128)(2,1)}), bf16[2048,256]{1,0:T(8,128)(2,1)}) %all-gather.5.cloned.1.call-update) | async-done | bytes 1048592 | tf_op jit(solution)/shard_map/all_gather | solution.py:184
  71.6 9.1 %collective-permute-done.refs_3_ = bf16[512,384]{1,0:T(8,128)(2,1)S(1)} collective-permute-done((bf16[512,384]{1,0:T(8,128)(2,1)}, bf16[512,384]{1,0:T(8,128)(2,1)S(1)}, u32[]{:S(2)}, u32[]{:S(2)}) %collective-permute-start) | collective-permute-done | bytes 393248 | tf_op jit(solution)/shard_map/ppermute | solution.py:43
  84.8 13.3 %collective-permute-done.4.refs_7_ = bf16[512,384]{1,0:T(8,128)(2,1)S(1)} collective-permute-done((bf16[512,384]{1,0:T(8,128)(2,1)S(1)}, bf16[512,384]{1,0:T(8,128)(2,1)S(1)}, u32[]{:S(2)}, u32[]{:S(2)}) %collective-permute-start.4) | collective-permute-done | bytes 393248 | tf_op jit(solution)/shard_map/ppermute | solution.py:43
  99.7 8.8 %collective-permute-done.14.refs_17_ = bf16[512,384]{1,0:T(8,128)(2,1)S(1)} collective-permute-done((bf16[512,384]{1,0:T(8,128)(2,1)}, bf16[512,384]{1,0:T(8,128)(2,1)S(1)}, u32[]{:S(2)}, u32[]{:S(2)}) %collective-permute-start.14) | collective-permute-done | bytes 393248 | tf_op jit(solution)/shard_map/ppermute | solution.py:43
  133.8 9.7 %pieces_forward.1 = (bf16[128,2048]{1,0:T(8,128)(2,1)S(1)}, bf16[128,1024]{1,0:T(8,128)(2,1)S(1)}, bf16[2048,3072]{1,0:T(8,128)(2,1)}) custom-call(s32[2]{0:T(128)S(1)} %pad_add_fusion.refs_0_, bf16[128,2048]{1,0:T(8,128)(2,1)S(1)} %fusion.2.refs_1_, bf16[512,3072]{1,0:T(8,128)(2,1)} %refs_2_.3, bf16[512,384]{1,0:T(8,128)(2,1)} %copy-done.44, ...), custom_call_target="tpu_custom_call" | custom-call | flops 1610612736 | bytes 25165824 | tf_op jit(solution)/shard_map/pieces_forward/pallas_call | solution.py:154
  162.9 13.1 %attend.1 = (bf16[128,2048]{1,0:T(8,128)(2,1)}, f32[128,2048]{1,0:T(8,128)S(1)}, f32[8,1,512]{2,1,0:T(1,128)S(1)}) custom-call(bf16[128,2048]{1,0:T(8,128)(2,1)S(1)} %get-tuple-element.71.refs_0_, bf16[512,1024]{1,0:T(8,128)(2,1)S(1)} %constant_dynamic-update-slice_fusion.1.refs_1_.refs_2_.refs_3_.refs_4_, ...), custom_call_target="tpu_custom_call" | custom-call | flops 1073741824 | bytes 2097152 | tf_op jit(solution)/shard_map/attend/pallas_call | solution.py:520
  177.0 9.4 %collective-permute-done.36.refs_3_.refs_12_.refs_16_ = bf16[128,2048]{1,0:T(8,128)(2,1)S(1)} collective-permute-done((bf16[128,2048]{1,0:T(8,128)(2,1)S(1)}, bf16[128,2048]{1,0:T(8,128)(2,1)S(1)}, u32[]{:S(2)}, u32[]{:S(2)}) %collective-permute-start.36) | collective-permute-done | bytes 524320 | tf_op jit(solution)/shard_map/ppermute | solution.py:43
  202.1 8.6 %down_back.1.refs_2_ = f32[512,2048]{1,0:T(8,128)} custom-call(bf16[128,2048]{1,0:T(8,128)(2,1)S(1)} %bitcast.68, bf16[128,2048]{1,0:T(8,128)(2,1)S(1)} %collective-permute-done.35.refs_1_.refs_10_.refs_14_, bf16[128,2048]{1,0:T(8,128)(2,1)S(1)} %collective-permute-done.37.refs_2_.refs_11_.refs_15_, ...), custom_call_target="tpu_custom_call" | custom-call | flops 4294967296 | bytes 8388608 | tf_op jit(solution)/shard_map/down_back/pallas_call | solution.py:859
  223.0 14.0 %ffn_middle.2 = (bf16[3,256,2048]{2,1,0:T(8,128)(2,1)}, f32[128,2048]{1,0:T(8,128)S(1)}, bf16[128,2048]{1,0:T(8,128)(2,1)S(1)}) custom-call(bf16[128,2048]{1,0:T(8,128)(2,1)S(1)} %get-tuple-element.77.refs_0_.refs_1_.refs_5_, bf16[128,2048]{1,0:T(8,128)(2,1)S(1)} %collective-permute-done.34.refs_1_.refs_2_.refs_6_, f32[512,2048]{1,0:T(8,128)} %down_back.1.refs_2_, ...), custom_call_target="tpu_custom_call" | custom-call | flops 8589934592 | bytes 16777216 | tf_op jit(solution)/shard_map/ffn_middle/pallas_call | solution.py:687
  238.8 14.1 %ffn_middle.3 = (bf16[3,256,2048]{2,1,0:T(8,128)(2,1)}, bf16[128,2048]{1,0:T(8,128)(2,1)S(1)}, f32[128,2048]{1,0:T(8,128)S(1)}) custom-call(bf16[128,2048]{1,0:T(8,128)(2,1)S(1)} %collective-permute-done.39.refs_0_.refs_3_.refs_7_, bf16[128,2048]{1,0:T(8,128)(2,1)S(1)} %collective-permute-done.38.refs_1_.refs_4_.refs_8_, f32[512,2048]{1,0:T(8,128)} %down_back.1.refs_2_, ...), custom_call_target="tpu_custom_call" | custom-call | flops 8589934592 | bytes 16777216 | tf_op jit(solution)/shard_map/ffn_middle/pallas_call | solution.py:687
  253.9 13.9 %sent_products.1 = bf16[3,1024,2048]{2,1,0:T(8,128)(2,1)} custom-call(s32[2]{0:T(128)S(1)} %pad_add_fusion.refs_0_, bf16[128,2048]{1,0:T(8,128)(2,1)S(1)} %get-tuple-element.77.refs_0_.refs_1_.refs_5_, bf16[128,2048]{1,0:T(8,128)(2,1)S(1)} %collective-permute-done.34.refs_1_.refs_2_.refs_6_, ...), custom_call_target="tpu_custom_call" | custom-call | flops 6442450944 | bytes 12582912 | tf_op jit(solution)/shard_map/sent_products/pallas_call | solution.py:812
  267.8 19.4 %collective-permute-done.72.refs_19_ = bf16[3,1024,2048]{2,1,0:T(8,128)(2,1)S(1)} collective-permute-done((bf16[3,1024,2048]{2,1,0:T(8,128)(2,1)}, bf16[3,1024,2048]{2,1,0:T(8,128)(2,1)S(1)}, u32[]{:S(2)}, u32[]{:S(2)}) %collective-permute-start.72) | collective-permute-done | bytes 12582944 | tf_op jit(solution)/shard_map/ppermute | solution.py:43
  291.7 17.3 %kept_products.1 = bf16[3,1024,2048]{2,1,0:T(8,128)(2,1)} custom-call(s32[2]{0:T(128)S(1)} %pad_add_fusion.refs_0_, bf16[128,2048]{1,0:T(8,128)(2,1)S(1)} %get-tuple-element.77.refs_0_.refs_1_.refs_5_, bf16[128,2048]{1,0:T(8,128)(2,1)S(1)} %collective-permute-done.34.refs_1_.refs_2_.refs_6_, ...), custom_call_target="tpu_custom_call" | custom-call | flops 6442450944 | bytes 12582912 | tf_op jit(solution)/shard_map/kept_products/pallas_call | solution.py:812
  311.2 13.0 %collective-permute-done.41 = bf16[128,2048]{1,0:T(8,128)(2,1)S(1)} collective-permute-done((bf16[128,2048]{1,0:T(8,128)(2,1)}, bf16[128,2048]{1,0:T(8,128)(2,1)S(1)}, u32[]{:S(2)}, u32[]{:S(2)}) %collective-permute-start.41) | collective-permute-done | bytes 524320 | tf_op jit(solution)/shard_map/ppermute | solution.py:43
  326.4 8.2 %collective-permute-done.40 = bf16[128,2048]{1,0:T(8,128)(2,1)S(1)} collective-permute-done((bf16[128,2048]{1,0:T(8,128)(2,1)S(1)}, bf16[128,2048]{1,0:T(8,128)(2,1)S(1)}, u32[]{:S(2)}, u32[]{:S(2)}) %collective-permute-start.40) | collective-permute-done | bytes 524320 | tf_op jit(solution)/shard_map/ppermute | solution.py:43
  334.6 13.2 %collective-permute-done.42 = bf16[128,2048]{1,0:T(8,128)(2,1)S(1)} collective-permute-done((bf16[128,2048]{1,0:T(8,128)(2,1)S(1)}, bf16[128,2048]{1,0:T(8,128)(2,1)S(1)}, u32[]{:S(2)}, u32[]{:S(2)}) %collective-permute-start.42) | collective-permute-done | bytes 524320 | tf_op jit(solution)/shard_map/ppermute | solution.py:43
  355.3 20.3 %attend_back.1 = (bf16[128,2048]{1,0:T(8,128)(2,1)}, bf16[2,512,512]{2,1,0:T(8,128)(2,1)S(1)}, bf16[2,512,512]{2,1,0:T(8,128)(2,1)S(1)}) custom-call(bf16[128,2048]{1,0:T(8,128)(2,1)S(1)} %copy-done.21, bf16[128,2048]{1,0:T(8,128)(2,1)S(1)} %out_back.1.refs_1_, f32[128,2048]{1,0:T(8,128)S(1)} %copy-done.33, bf16[512,1024]{1,0:T(8,128)(2,1)} %copy-done.18, ...), custom_call_target="tpu_custom_call" | custom-call | flops 2684354560 | bytes 4194304 | tf_op jit(solution)/shard_map/attend_back/pallas_call | solution.py:585
  407.0 13.3 %collective-permute-start.64 = (bf16[128,2048]{1,0:T(8,128)(2,1)}, bf16[128,2048]{1,0:T(8,128)(2,1)}, u32[]{:S(2)}, u32[]{:S(2)}) collective-permute-start(bf16[128,2048]{1,0:T(8,128)(2,1)} %collective-permute-done.63.refs_12_), channel_id=1, source_target_pairs={{0,1},{1,0},{2,3},{3,2},{4,5},{5,4},{6,7},{7,6},{8,9},{9,8},{10,11... | collective-permute-start | bytes 1572872 | tf_op jit(solution)/shard_map/ppermute | solution.py:43
  420.3 16.6 %collective-permute-start.67 = (bf16[128,2048]{1,0:T(8,128)(2,1)}, bf16[128,2048]{1,0:T(8,128)(2,1)}, u32[]{:S(2)}, u32[]{:S(2)}) collective-permute-start(bf16[128,2048]{1,0:T(8,128)(2,1)} %collective-permute-done.66.refs_16_), channel_id=1, source_target_pairs={{0,1},{1,0},{2,3},{3,2},{4,5},{5,4},{6,7},{7,6},{8,9},{9,8},{10,11... | collective-permute-start | bytes 1572872 | tf_op jit(solution)/shard_map/ppermute | solution.py:43
  445.9 26.2 %collective-permute-done.50.refs_2_.refs_6_ = bf16[128,512]{1,0:T(8,128)(2,1)} collective-permute-done((bf16[128,512]{1,0:T(8,128)(2,1)}, bf16[128,512]{1,0:T(8,128)(2,1)}, u32[]{:S(2)}, u32[]{:S(2)}) %collective-permute-start.50) | collective-permute-done | bytes 131104 | tf_op jit(solution)/shard_map/ppermute | solution.py:43
  480.4 9.0 %one_back.1 = f32[128,2048]{1,0:T(8,128)} custom-call(bf16[128,2048]{1,0:T(8,128)(2,1)} %get-tuple-element.122.query_ref.refs_13_, bf16[512,1024]{1,0:T(8,128)(2,1)S(1)} %copy-done.4, bf16[2048,3072]{1,0:T(8,128)(2,1)} %get-tuple-element.98.w_ref, bf16[128,2048]{1,0:T(8,128)(2,1)S(1)} %bitcast.74, f32[1,2048]{1,0:T(1,128)S(1)} %bitcast.76, ...), custom_call_target="tpu_custom_call" | custom-call | flops 1610612736 | bytes 12582912 | tf_op jit(solution)/shard_map/one_back/pallas_call | solution.py:320
  510.1 7.8 %down_forward.1 = (f32[128,2048]{1,0:T(8,128)S(1)}, bf16[128,2048]{1,0:T(8,128)(2,1)S(1)}, bf16[128,2048]{1,0:T(8,128)(2,1)S(1)}, bf16[128,2048]{1,0:T(8,128)(2,1)S(1)}) custom-call(bf16[3,256,2048]{2,1,0:T(8,128)(2,1)} %get-tuple-element.86.a_ref.refs_17_, bf16[3,256,2048]{2,1,0:T(8,128)(2,1)} %get-tuple-element.87.b_ref.refs_18_, ...), custom_call_target="tpu_custom_call" | custom-call | flops 4294967296 | bytes 8388608 | tf_op jit(solution)/shard_map/down_forward/pallas_call | solution.py:892
  546.8 13.2 %collective-permute-done.48 = bf16[128,2048]{1,0:T(8,128)(2,1)} collective-permute-done((bf16[128,2048]{1,0:T(8,128)(2,1)}, bf16[128,2048]{1,0:T(8,128)(2,1)}, u32[]{:S(2)}, u32[]{:S(2)}) %collective-permute-start.48) | collective-permute-done | bytes 524320 | tf_op jit(solution)/shard_map/ppermute | solution.py:43
  (365 shorter events, 255.8 us)
Async XLA Ops:
  7.2 60.6 %all-gather.5.cloned.1.call-start = ((), (), s32[]{:S(2)}) async-start(), calls=%async_computation.3 | async-start | bytes 1310720 | tf_op jit(solution)/shard_map/all_gather | solution.py:184
  39.5 146.9 %all-gather.7.cloned.1.call-start = ((), (), s32[]{:S(2)}) async-start(), calls=%async_computation.4 | async-start | bytes 7077888 | tf_op jit(solution)/shard_map/all_gather | solution.py:191
  70.0 502.5 %reduce-scatter.2.cloned.1.call-start = ((), (), s32[]{:S(2)}) async-start(), calls=%async_computation.2 | async-start | bytes 15728640 | tf_op jit(solution)/shard_map/reduce_scatter | solution.py:845
  83.7 24.9 %collective-permute-start.14 = (bf16[512,384]{1,0:T(8,128)(2,1)}, bf16[512,384]{1,0:T(8,128)(2,1)S(1)}, u32[]{:S(2)}, u32[]{:S(2)}) collective-permute-start(bf16[512,384]{1,0:T(8,128)(2,1)} %copy-done.42), channel_id=1, source_target_pairs={{0,16},{4,20},{8,24},{12,28},{16,0},{20,4},{24,8},{28,12},{1,17},{... | collective-permute-start | bytes 1179656 | tf_op jit(solution)/shard_map/ppermute | solution.py:43
  84.2 24.7 %collective-permute-start.12 = (bf16[512,384]{1,0:T(8,128)(2,1)}, bf16[512,384]{1,0:T(8,128)(2,1)S(1)}, u32[]{:S(2)}, u32[]{:S(2)}) collective-permute-start(bf16[512,384]{1,0:T(8,128)(2,1)} %copy-done.42), channel_id=1, source_target_pairs={{0,8},{4,12},{8,0},{12,4},{16,24},{20,28},{24,16},{28,20},{1,9},{5... | collective-permute-start | bytes 1179656 | tf_op jit(solution)/shard_map/ppermute | solution.py:43
  84.8 24.3 %collective-permute-start.1 = (bf16[512,384]{1,0:T(8,128)(2,1)S(1)}, bf16[512,384]{1,0:T(8,128)(2,1)S(1)}, u32[]{:S(2)}, u32[]{:S(2)}) collective-permute-start(bf16[512,384]{1,0:T(8,128)(2,1)S(1)} %collective-permute-done.refs_3_), channel_id=1, source_target_pairs={{0,4},{4,0},{8,12},{12,8},{16,20},{20,16},{24,28},{28,24},{1,5},{5... | collective-permute-start | bytes 1179656 | tf_op jit(solution)/shard_map/ppermute | solution.py:43
  160.6 25.8 %collective-permute-start.36 = (bf16[128,2048]{1,0:T(8,128)(2,1)S(1)}, bf16[128,2048]{1,0:T(8,128)(2,1)S(1)}, u32[]{:S(2)}, u32[]{:S(2)}) collective-permute-start(bf16[128,2048]{1,0:T(8,128)(2,1)S(1)} %bitcast.67), channel_id=1, source_target_pairs={{0,3},{1,2},{2,1},{3,0},{4,7},{5,6},{6,5},{7,4},{8,11},{9,10},{10,... | collective-permute-start | bytes 1572872 | tf_op jit(solution)/shard_map/ppermute | solution.py:43
  197.7 25.3 %collective-permute-start.34 = (bf16[128,2048]{1,0:T(8,128)(2,1)S(1)}, bf16[128,2048]{1,0:T(8,128)(2,1)S(1)}, u32[]{:S(2)}, u32[]{:S(2)}) collective-permute-start(bf16[128,2048]{1,0:T(8,128)(2,1)S(1)} %get-tuple-element.77.refs_0_.refs_1_.refs_5_), channel_id=1, source_target_pairs={{0,1},{1,0},{2,3},{3,2},{4,5},{5,4},{6,7},{7,6},{8,9},{9,8},{10,11... | collective-permute-start | bytes 1572872 | tf_op jit(solution)/shard_map/ppermute | solution.py:43
  213.6 25.2 %collective-permute-start.39 = (bf16[128,2048]{1,0:T(8,128)(2,1)S(1)}, bf16[128,2048]{1,0:T(8,128)(2,1)S(1)}, u32[]{:S(2)}, u32[]{:S(2)}) collective-permute-start(bf16[128,2048]{1,0:T(8,128)(2,1)S(1)} %collective-permute-done.38.refs_1_.refs_4_.refs_8_), channel_id=1, source_target_pairs={{0,1},{1,0},{2,3},{3,2},{4,5},{5,4},{6,7},{7,6},{8,9},{9,8},{10,11... | collective-permute-start | bytes 1572872 | tf_op jit(solution)/shard_map/ppermute | solution.py:43
  310.1 24.5 %collective-permute-start.40 = (bf16[128,2048]{1,0:T(8,128)(2,1)S(1)}, bf16[128,2048]{1,0:T(8,128)(2,1)S(1)}, u32[]{:S(2)}, u32[]{:S(2)}) collective-permute-start(bf16[128,2048]{1,0:T(8,128)(2,1)S(1)} %copy-done.26), channel_id=1, source_target_pairs={{0,1},{1,0},{2,3},{3,2},{4,5},{5,4},{6,7},{7,6},{8,9},{9,8},{10,11... | collective-permute-start | bytes 1572872 | tf_op jit(solution)/shard_map/ppermute | solution.py:43
  375.5 31.5 %collective-permute-start.63 = (bf16[128,2048]{1,0:T(8,128)(2,1)}, bf16[128,2048]{1,0:T(8,128)(2,1)}, u32[]{:S(2)}, u32[]{:S(2)}) collective-permute-start(bf16[128,2048]{1,0:T(8,128)(2,1)} %get-tuple-element.118.refs_1_.refs_9_), channel_id=1, source_target_pairs={{0,3},{1,2},{2,1},{3,0},{4,7},{5,6},{6,5},{7,4},{8,11},{9,10},{10,... | collective-permute-start | bytes 1572872 | tf_op jit(solution)/shard_map/ppermute | solution.py:43
  376.1 44.3 %collective-permute-start.66 = (bf16[128,2048]{1,0:T(8,128)(2,1)}, bf16[128,2048]{1,0:T(8,128)(2,1)}, u32[]{:S(2)}, u32[]{:S(2)}) collective-permute-start(bf16[128,2048]{1,0:T(8,128)(2,1)} %get-tuple-element.122.query_ref.refs_13_), channel_id=1, source_target_pairs={{0,3},{1,2},{2,1},{3,0},{4,7},{5,6},{6,5},{7,4},{8,11},{9,10},{10,... | collective-permute-start | bytes 1572872 | tf_op jit(solution)/shard_map/ppermute | solution.py:43
  399.8 126.0 %all-to-all-start = ((bf16[4,128,1024]{2,1,0:T(8,128)(2,1)}), bf16[4,128,1024]{2,1,0:T(8,128)(2,1)}, u32[]{:S(2)}, u32[]{:S(2)}) async-start(bf16[4,128,1024]{2,1,0:T(8,128)(2,1)} %bitcast.75), calls=%async_computation | async-start | bytes 2097152 | tf_op jit(solution)/shard_map/all_to_all | solution.py:1155
  404.9 69.6 %collective-permute-start.62 = (bf16[128,2048]{1,0:T(8,128)(2,1)}, bf16[128,2048]{1,0:T(8,128)(2,1)}, u32[]{:S(2)}, u32[]{:S(2)}) collective-permute-start(bf16[128,2048]{1,0:T(8,128)(2,1)} %get-tuple-element.118.refs_1_.refs_9_), channel_id=1, source_target_pairs={{0,1},{1,0},{2,3},{3,2},{4,5},{5,4},{6,7},{7,6},{8,9},{9,8},{10,11... | collective-permute-start | bytes 1572872 | tf_op jit(solution)/shard_map/ppermute | solution.py:43
  407.0 67.8 %collective-permute-start.64 = (bf16[128,2048]{1,0:T(8,128)(2,1)}, bf16[128,2048]{1,0:T(8,128)(2,1)}, u32[]{:S(2)}, u32[]{:S(2)}) collective-permute-start(bf16[128,2048]{1,0:T(8,128)(2,1)} %collective-permute-done.63.refs_12_), channel_id=1, source_target_pairs={{0,1},{1,0},{2,3},{3,2},{4,5},{5,4},{6,7},{7,6},{8,9},{9,8},{10,11... | collective-permute-start | bytes 1572872 | tf_op jit(solution)/shard_map/ppermute | solution.py:43
  420.3 55.3 %collective-permute-start.65 = (bf16[128,2048]{1,0:T(8,128)(2,1)}, bf16[128,2048]{1,0:T(8,128)(2,1)}, u32[]{:S(2)}, u32[]{:S(2)}) collective-permute-start(bf16[128,2048]{1,0:T(8,128)(2,1)} %get-tuple-element.122.query_ref.refs_13_), channel_id=1, source_target_pairs={{0,1},{1,0},{2,3},{3,2},{4,5},{5,4},{6,7},{7,6},{8,9},{9,8},{10,11... | collective-permute-start | bytes 1572872 | tf_op jit(solution)/shard_map/ppermute | solution.py:43
  420.3 58.6 %collective-permute-start.67 = (bf16[128,2048]{1,0:T(8,128)(2,1)}, bf16[128,2048]{1,0:T(8,128)(2,1)}, u32[]{:S(2)}, u32[]{:S(2)}) collective-permute-start(bf16[128,2048]{1,0:T(8,128)(2,1)} %collective-permute-done.66.refs_16_), channel_id=1, source_target_pairs={{0,1},{1,0},{2,3},{3,2},{4,5},{5,4},{6,7},{7,6},{8,9},{9,8},{10,11... | collective-permute-start | bytes 1572872 | tf_op jit(solution)/shard_map/ppermute | solution.py:43
  437.0 35.1 %collective-permute-start.50 = (bf16[128,512]{1,0:T(8,128)(2,1)}, bf16[128,512]{1,0:T(8,128)(2,1)}, u32[]{:S(2)}, u32[]{:S(2)}) collective-permute-start(bf16[128,512]{1,0:T(8,128)(2,1)} %copy.79), channel_id=1, source_target_pairs={{0,1},{1,0},{2,3},{3,2},{4,5},{5,4},{6,7},{7,6},{8,9},{9,8},{10,11... | collective-permute-start | bytes 393224 | tf_op jit(solution)/shard_map/ppermute | solution.py:43
  502.4 30.5 %collective-permute-start.68 = (bf16[4,64,4096]{2,1,0:T(8,128)(2,1)}, bf16[4,64,4096]{2,1,0:T(8,128)(2,1)}, u32[]{:S(2)}, u32[]{:S(2)}) collective-permute-start(bf16[4,64,4096]{2,1,0:T(8,128)(2,1)} %get-tuple-element.127), channel_id=1, source_target_pairs={{0,4},{4,0},{8,12},{12,8},{16,20},{20,16},{24,28},{28,24},{1,5},{5... | collective-permute-start | bytes 6291464 | tf_op jit(solution)/shard_map/ppermute | solution.py:43
  521.5 23.6 %collective-permute-start.47 = (bf16[128,2048]{1,0:T(8,128)(2,1)}, bf16[128,2048]{1,0:T(8,128)(2,1)}, u32[]{:S(2)}, u32[]{:S(2)}) collective-permute-start(bf16[128,2048]{1,0:T(8,128)(2,1)} %copy-done.24), channel_id=1, source_target_pairs={{0,1},{1,0},{2,3},{3,2},{4,5},{5,4},{6,7},{7,6},{8,9},{9,8},{10,11... | collective-permute-start | bytes 1572872 | tf_op jit(solution)/shard_map/ppermute | solution.py:43
  521.5 38.5 %collective-permute-start.48 = (bf16[128,2048]{1,0:T(8,128)(2,1)}, bf16[128,2048]{1,0:T(8,128)(2,1)}, u32[]{:S(2)}, u32[]{:S(2)}) collective-permute-start(bf16[128,2048]{1,0:T(8,128)(2,1)} %copy-done.23), channel_id=1, source_target_pairs={{0,2},{1,3},{2,0},{3,1},{4,6},{5,7},{6,4},{7,5},{8,10},{9,11},{10,... | collective-permute-start | bytes 1572872 | tf_op jit(solution)/shard_map/ppermute | solution.py:43
  523.6 36.5 %collective-permute-start.49 = (bf16[128,2048]{1,0:T(8,128)(2,1)}, bf16[128,2048]{1,0:T(8,128)(2,1)}, u32[]{:S(2)}, u32[]{:S(2)}) collective-permute-start(bf16[128,2048]{1,0:T(8,128)(2,1)} %copy-done.22), channel_id=1, source_target_pairs={{0,3},{1,2},{2,1},{3,0},{4,7},{5,6},{6,5},{7,4},{8,11},{9,10},{10,... | collective-permute-start | bytes 1572872 | tf_op jit(solution)/shard_map/ppermute | solution.py:43
  545.0 23.6 %collective-permute-start.70 = (bf16[64,4096]{1,0:T(8,128)(2,1)S(1)}, bf16[64,4096]{1,0:T(8,128)(2,1)S(1)}, u32[]{:S(2)}, u32[]{:S(2)}) collective-permute-start(bf16[64,4096]{1,0:T(8,128)(2,1)S(1)} %get-tuple-element.148), channel_id=1, source_target_pairs={{0,16},{4,20},{8,24},{12,28},{16,0},{20,4},{24,8},{28,12},{1,17},{... | collective-permute-start | bytes 1572872 | tf_op jit(solution)/shard_map/ppermute | solution.py:43
  545.1 23.5 %collective-permute-start.71 = (bf16[64,4096]{1,0:T(8,128)(2,1)S(1)}, bf16[64,4096]{1,0:T(8,128)(2,1)S(1)}, u32[]{:S(2)}, u32[]{:S(2)}) collective-permute-start(bf16[64,4096]{1,0:T(8,128)(2,1)S(1)} %get-tuple-element.147), channel_id=1, source_target_pairs={{0,24},{4,28},{8,16},{12,20},{16,8},{20,12},{24,0},{28,4},{1,25},{... | collective-permute-start | bytes 1572872 | tf_op jit(solution)/shard_map/ppermute | solution.py:43
  (119 other events, 2206.3 us)
Sparse Core Ops, SparseCore 0:
  39.6 28.1 all-gather.4
  70.3 62.8 all-gather.6
  309.2 125.1 reduce-scatter.1

commit v8 on v7

--- a/solution.py
+++ b/solution.py
@@ -159,7 +159,7 @@
             pltpu.HBM((width, columns), BF),
         ),
         in_specs=[pl.BlockSpec(memory_space=pltpu.SMEM), vmem, hbm]
-        + [hbm] * len(arrays)
+        + [pl.BlockSpec(memory_space=pl.ANY)] * len(arrays)
         + [vmem, vmem],
         out_specs=(vmem, vmem, hbm),
         scratch_shapes=[
@@ -173,7 +173,7 @@
             flops=2 * rows * width * columns, bytes_accessed=4 * width * columns, transcendentals=0
         ),
         name="pieces_forward",
-    )(jnp.stack([me, plane]), x, in_hbm(own), *[in_hbm(part) for part in arrays], cosine, sine)
+    )(jnp.stack([me, plane]), x, in_hbm(own), *arrays, cosine, sine)
 
 
 def gather_blocks(weight, before_fsdp, before_ctx):
@@ -213,35 +213,45 @@
     own_buf, buf, sems = outs[-3:]
     ctx_count, others, rows, share = buf.shape
     plane = ids_ref[1]
-    copies = [pltpu.make_async_copy(own_ref, own_buf, sems.at[ctx_count])]
+
+    def block_copy(c):
+        return pltpu.make_async_copy(blocks_ref.at[c], buf.at[c], sems.at[c])
+
+    own_copy = pltpu.make_async_copy(own_ref, own_buf, sems.at[ctx_count])
+    own_copy.start()
     for c in range(ctx_count):
-        copies.append(pltpu.make_async_copy(blocks_ref.at[c], buf.at[c], sems.at[c]))
-    for copy in copies:
-        copy.start()
+        block_copy(c).start()
 
     def features(away):
         return pl.ds(pl.multiple_of((plane ^ away) * rows, 128), rows)
 
-    copies[0].wait()
+    def columns(c):
+        return pl.ds(pl.multiple_of(c * share, 128), share)
+
+    own_copy.wait()
     if back:
         y_ref = outs[0]
-        own_part = nn(x_ref[:, features(0)], own_buf[...])
-        for c in range(ctx_count):
-            copies[c + 1].wait()
-            at = slice(c * share, (c + 1) * share)
-            total = own_part[:, at]
+
+        @pl.loop(0, ctx_count)
+        def _(c):
+            block_copy(c).wait()
+            total = nn(x_ref[:, features(0)], own_buf[:, columns(c)])
             for away in range(1, others + 1):
                 total += nn(x_ref[:, features(away)], buf[c, away - 1])
-            y_ref[:, at] = total.astype(BF)
+            y_ref[:, columns(c)] = total.astype(BF)
+
         return
     residual_ref, normed_ref = outs[:2]
     residual_ref[...] = hidden_ref[...].astype(F32)
-    residual_ref[:, features(0)] += nt(x_ref[...], own_buf[...])
-    for c in range(ctx_count):
-        copies[c + 1].wait()
-        x = x_ref[:, c * share : (c + 1) * share]
+
+    @pl.loop(0, ctx_count)
+    def _(c):
+        block_copy(c).wait()
+        x = x_ref[:, columns(c)]
+        residual_ref[:, features(0)] += nt(x, own_buf[:, columns(c)])
         for away in range(1, others + 1):
             residual_ref[:, features(away)] += nt(x, buf[c, away - 1])
+
     residual = residual_ref[...]
     normed_ref[...] = (residual * norm_scale(residual) * gain_ref[...]).astype(BF)
 
@@ -647,8 +657,9 @@
             x_buf[i * rows : (i + 1) * rows] = ref[...]
 
 
-def ffn_kernel(count, *refs):
-    rows_refs, (act_ref, w_ref, out_ref), refs = refs[:count], refs[count : count + 3], refs[count + 3 :]
+def ffn_kernel(count, earlier, *refs):
+    rows_refs, (act_ref, w_ref), refs = refs[:count], refs[count : count + 2], refs[count + 2 :]
+    out_ref, refs = refs[earlier], refs[earlier + 1 :]
     sum_refs, (x_buf, sum_buf) = refs[:count], refs[count:]
     join_rows(x_buf, rows_refs)
     step = pl.program_id(0)
@@ -678,25 +689,27 @@
             ref[...] = sum_buf[i * rows : (i + 1) * rows].astype(ref.dtype)
 
 
-def ffn_middle(blocks, act_grad, half, weights, kinds):
+def ffn_middle(blocks, act_grad, half, weights, kinds, earlier):
     width = blocks[0].shape[1]
     rows = blocks[0].shape[0] * len(blocks)
     hidden = weights.shape[2]
     tile = FFN_TILE
     whole = [pl.BlockSpec(block.shape, lambda j: (0, 0)) for block in blocks]
     out = pl.pallas_call(
-        lambda *refs: ffn_kernel(len(blocks), *refs),
+        lambda *refs: ffn_kernel(len(blocks), len(earlier), *refs),
         grid=(hidden // tile,),
         out_shape=(
-            pltpu.HBM((3, rows, hidden), BF),
+            pltpu.HBM((3, 2 * rows, hidden), BF),
             *[jax.ShapeDtypeStruct(block.shape, kind) for block, kind in zip(blocks, kinds)],
         ),
         in_specs=whole
         + [
             pl.BlockSpec((rows, tile), lambda j: (half, j)),
             pl.BlockSpec((2, width, tile), lambda j: (0, 0, j)),
-        ],
-        out_specs=(pl.BlockSpec((3, rows, tile), lambda j: (0, 0, j)), *whole),
+        ]
+        + [pl.BlockSpec(memory_space=pltpu.HBM)] * len(earlier),
+        out_specs=(pl.BlockSpec((3, rows, tile), lambda j: (0, half, j)), *whole),
+        input_output_aliases={len(blocks) + 2: 0} if earlier else {},
         scratch_shapes=[pltpu.VMEM((rows, width), BF), pltpu.VMEM((rows, width), F32)],
         compiler_params=pltpu.CompilerParams(vmem_limit_bytes=40 << 20),
         cost_estimate=pl.CostEstimate(
@@ -705,87 +718,40 @@
             transcendentals=rows * hidden,
         ),
         name="ffn_middle",
-    )(*blocks, act_grad, weights)
+    )(*blocks, act_grad, weights, *earlier)
     return out[0], list(out[1:])
 
 
-def products_kernel(count, *refs):
-    in_refs, grad_refs = refs[:count], refs[count : 2 * count]
-    right_a, right_b, out_ref = refs[2 * count :]
-    half = count // 2
-
-    def emit(lefts):
-        left_a = jnp.concatenate([ref[...] for ref in lefts[:half]], axis=0)
-        left_b = jnp.concatenate([ref[...] for ref in lefts[half:]], axis=0)
-        out_ref[0] = (tn(left_a, right_a[0]) + tn(left_b, right_b[0])).astype(BF)
+def products_kernel(count, added, ids_ref, *refs):
+    in_refs, grad_refs = refs[: 2 * count], refs[2 * count : 4 * count]
+    right, rest = refs[4 * count], refs[4 * count + 1 :]
+    out_ref, left = rest[-2:]
+
+    def join(blocks):
+        rows, height = blocks[0].shape
+        for j in range(2):
+            for i in range(count):
+                at = (slice(i * rows, (i + 1) * rows), slice(j * height, (j + 1) * height))
+                left[at] = blocks[j * count + i][...]
 
     @pl.when(pl.program_id(0) < 2)
     def _():
-        emit(in_refs)
+        join(in_refs)
 
     @pl.when(pl.program_id(0) == 2)
     def _():
-        emit(grad_refs)
-
-
-def ffn_products(rows_in, rows_out, parts):
-    count = len(rows_in)
-    rows, width = rows_in[0].shape
-    hidden = parts[0].shape[2]
-    tile = FFN_TILE
-    last = width // tile - 1
-    left = pl.BlockSpec((rows, tile), lambda k, i: (0, jnp.where(k < 2, i, last)))
-    grad = pl.BlockSpec((rows, tile), lambda k, i: (0, jnp.where(k == 2, i, 0)))
-    right = pl.BlockSpec((1, rows * count // 2, hidden), lambda k, i: (k, 0, 0))
-    return pl.pallas_call(
-        lambda *refs: products_kernel(count, *refs),
-        grid=(3, width // tile),
-        out_shape=pltpu.HBM((3, width, hidden), BF),
-        in_specs=[left] * count + [grad] * count + [right, right],
-        out_specs=pl.BlockSpec((1, tile, hidden), lambda k, i: (k, i, 0)),
-        compiler_params=pltpu.CompilerParams(vmem_limit_bytes=32 << 20),
-        cost_estimate=pl.CostEstimate(
-            flops=6 * count * rows * width * hidden,
-            bytes_accessed=6 * width * hidden,
-            transcendentals=0,
-        ),
-        name="ffn_products",
-    )(*rows_in, *rows_out, *parts)
-
-
-def half_products_kernel(count, added, ids_ref, *refs):
-    in_refs, grad_refs = refs[: 2 * count], refs[2 * count : 4 * count]
-    rights, rest = refs[4 * count : 4 * count + 2], refs[4 * count + 2 :]
-    out_ref = rest[-1]
-    half = count // 2
-
-    def emit(lefts):
-        height = lefts[0].shape[1]
-        for j in range(2):
-            part = None
-            for i, right in enumerate(rights):
-                group = lefts[j * count + i * half : j * count + (i + 1) * half]
-                left = jnp.concatenate([ref[...] for ref in group], axis=0)
-                product = tn(left, right[0])
-                part = product if part is None else part + product
-            at = slice(j * height, (j + 1) * height)
-            if added:
-                part = part + rest[0][0, at].astype(F32)
-            out_ref[0, at] = part.astype(BF)
-
-    @pl.when(pl.program_id(0) < 2)
-    def _():
-        emit(in_refs)
-
-    @pl.when(pl.program_id(0) == 2)
-    def _():
-        emit(grad_refs)
+        join(grad_refs)
+
+    part = tn(left[...], right[0])
+    if added:
+        part = part + rest[0][0].astype(F32)
+    out_ref[0] = part.astype(BF)
 
 
 def half_products(rows_in, rows_out, parts, got):
     count = len(rows_in)
     rows, width = rows_in[0].shape
-    hidden = parts[0].shape[2]
+    hidden = parts.shape[2]
     ctx_count = lax.axis_size("ctx")
     height = width // ctx_count
     last = ctx_count // 4 - 1
@@ -806,11 +772,11 @@
             lambda k, i, ids_ref: (0, column(jnp.where(k == 2, i, 0), j, ids_ref)),
         )
 
-    right = pl.BlockSpec((1, rows * count // 2, hidden), lambda k, i, ids_ref: (k, 0, 0))
+    right = pl.BlockSpec((1, rows * count, hidden), lambda k, i, ids_ref: (k, 0, 0))
     out = pl.BlockSpec((1, 2 * height, hidden), lambda k, i, ids_ref: (k, i, 0))
-    extra = [] if got is None else [in_hbm(got)]
+    extra = [] if got is None else [got]
     return pl.pallas_call(
-        lambda *refs: half_products_kernel(count, got is not None, *refs),
+        lambda *refs: products_kernel(count, got is not None, *refs),
         grid_spec=pltpu.PrefetchScalarGridSpec(
             num_scalar_prefetch=1,
             grid=(3, ctx_count // 4),
@@ -818,25 +784,28 @@
             + [left(1)] * count
             + [grad(0)] * count
             + [grad(1)] * count
-            + [right, right]
+            + [right]
             + [out] * len(extra),
             out_specs=out,
+            scratch_shapes=[pltpu.VMEM((count * rows, 2 * height), BF)],
         ),
         out_shape=pltpu.HBM((3, width // 2, hidden), BF),
-        compiler_params=pltpu.CompilerParams(vmem_limit_bytes=40 << 20),
+        compiler_params=pltpu.CompilerParams(vmem_limit_bytes=32 << 20),
         cost_estimate=pl.CostEstimate(
             flops=3 * count * rows * width * hidden,
             bytes_accessed=3 * width * hidden,
             transcendentals=0,
         ),
         name="kept_products" if extra else "sent_products",
-    )(jnp.stack(ids()), *rows_in, *rows_in, *rows_out, *rows_out, *parts, *extra)
+    )(jnp.stack(ids()), *rows_in, *rows_in, *rows_out, *rows_out, parts, *extra)
 
 
 def ffn_gradient(rows_in, rows_out, parts):
     count = lax.axis_size("ctx")
     if count % 4 or (rows_in[0].shape[1] // count) % 128:
-        products = ffn_products(rows_in, rows_out, parts).transpose(1, 0, 2)
+        left, grad = (jnp.concatenate(rows, axis=0) for rows in (rows_in, rows_out))
+        products = [tn(left, parts[0]), tn(left, parts[1]), tn(grad, parts[2])]
+        products = jnp.stack(products, axis=1).astype(BF)
         return lax.psum_scatter(products, "ctx", scatter_dimension=0, tiled=True)
     sent = half_products(rows_in, rows_out, parts, None)
     got = swap(sent, "ctx", 1)
@@ -874,37 +843,37 @@
     )(*blocks, weights)
 
 
-def down_kernel(a_ref, b_ref, w_ref, *y_refs):
-    rows = a_ref.shape[1] * 2 // len(y_refs)
-    totals = [nt(ref[0], w_ref[0]) for ref in (a_ref, b_ref)]
-    half = len(y_refs) // 2
+def down_kernel(x_ref, w_ref, *y_refs):
+    rows = x_ref.shape[1] // len(y_refs)
+    total = nt(x_ref[0], w_ref[0])
     for i, y_ref in enumerate(y_refs):
-        start = i % half * rows
-        y_ref[...] = totals[i // half][start : start + rows].astype(y_ref.dtype)
+        y_ref[...] = total[i * rows : (i + 1) * rows].astype(y_ref.dtype)
 
 
 def down_forward(parts, weights, count):
-    _, rows, hidden = parts[0].shape
+    _, rows, hidden = parts.shape
     width = weights.shape[1]
     tile = FFN_TILE
-    height = 2 * rows // count
-    left = pl.BlockSpec((1, rows, hidden), lambda j: (2, 0, 0))
+    height = rows // count
     return pl.pallas_call(
         down_kernel,
         grid=(width // tile,),
         out_shape=tuple(
             jax.ShapeDtypeStruct((height, width), BF if i else F32) for i in range(count)
         ),
-        in_specs=[left, left, pl.BlockSpec((1, tile, hidden), lambda j: (2, j, 0))],
+        in_specs=[
+            pl.BlockSpec((1, rows, hidden), lambda j: (2, 0, 0)),
+            pl.BlockSpec((1, tile, hidden), lambda j: (2, j, 0)),
+        ],
         out_specs=tuple(pl.BlockSpec((height, tile), lambda j: (0, j)) for _ in range(count)),
         compiler_params=pltpu.CompilerParams(vmem_limit_bytes=24 << 20),
         cost_estimate=pl.CostEstimate(
-            flops=4 * rows * width * hidden,
+            flops=2 * rows * width * hidden,
             bytes_accessed=2 * width * hidden,
             transcendentals=0,
         ),
         name="down_forward",
-    )(*parts, weights)
+    )(parts, weights)
 
 
 def share_kernel(count, sizes, ids_ref, *refs):
@@ -1124,14 +1093,15 @@
     act_grad = down_back(rows_out, ffn_parts)
 
     all_attn = pass_rows(after(attn_rows, rows_in[2]))
-    middle = []
+    parts, partial = [], []
     half = fsdp_count // 2
     passing = 3 if fsdp_count == 4 else 0
     for index in range(2):
         blocks = rows_in[index * half : (index + 1) * half]
         kinds = [F32 if index * half + i in (0, passing) else BF for i in range(half)]
-        middle.append(ffn_middle(blocks, in_hbm(act_grad), index, ffn_parts, kinds))
-    parts, partial = [in_hbm(m[0]) for m in middle], [block for m in middle for block in m[1]]
+        out, terms = ffn_middle(blocks, in_hbm(act_grad), index, ffn_parts, kinds, parts)
+        parts, partial = [out], partial + terms
+    parts = parts[0]
     sum_grad = share_finish(sum_rows(partial, True))
     ffn_weight_grad = ffn_gradient(rows_in, rows_out, parts)
     ffn_weight_grad = ffn_weight_grad.astype(F32)
@@ -1144,6 +1114,7 @@
         scaled_two - unit_two * jnp.mean(scaled_two * unit_two, axis=-1, keepdims=True)
     )
     residual_bf = residual_grad.astype(BF)
+    out_sum = sum_rows([after(part, residual_bf) for part in out_partial], False)
     (ffn_term,) = own_features([ffn_gain_term])
     attn_grad = out_back(residual_bf, out_weight, out_blocks)
     query_part, kept, sent = attend_back(
@@ -1156,20 +1127,12 @@
     input_grad = one_back(
         query_part, pair_copies, qkv_full, hidden_in[0], attn_gain, residual_grad
     )
-    out_sum = sum_rows([after(part, input_grad) for part in out_partial], False)
-    first_sums = share_start(
-        [own_residual, own_one], [after(all_attn, input_grad), after(query_planes, input_grad)], []
-    )
-    last_sums = share_start([own_one], [all_pair], [ffn_term])
-    last_sums = share_finish(last_sums)
-    first_sums = share_finish(after(first_sums, last_sums))
-    output = (residual + share_finish(after(out_sum, last_sums))).astype(BF)
-
-    pairs_width = 2 * kv_width
-    out_weight_grad = first_sums[:, :queries_width]
-    qkv_grad = jnp.concatenate(
-        [first_sums[:, queries_width:], last_sums[:, :pairs_width]], axis=1
-    )
+    out_sums = share_start([own_residual], [after(all_attn, input_grad)], [])
+    output = (residual + share_finish(after(out_sum, input_grad))).astype(BF)
+    qkv_sums = share_start([own_one, own_one], [after(query_planes, output), all_pair], [ffn_term])
+    qkv_sums = share_finish(qkv_sums)
+    out_weight_grad = share_finish(after(out_sums, qkv_sums))
+    qkv_grad = qkv_sums[:, : qkv_weight.shape[1]]
     features = own_rows_of(attn_gain, qkv_grad.shape[0])
     gain_grad = jnp.sum(own_rows_of(qkv_full, qkv_grad.shape[0]).astype(F32) * qkv_grad, axis=1)
     return (
@@ -1179,7 +1142,7 @@
         out_weight_grad,
         ffn_weight_grad,
         gain_grad / features,
-        last_sums[:, pairs_width],
+        qkv_sums[:, qkv_weight.shape[1]],
     )
 
 

time: 593 us -> 633 us (1.067); the launches traced: 585 us -> 631 us
  local copies, waits for them, and re-layouts: 39.9 us -> 70.3 us
  waiting for transfers between devices: 237 us -> 257 us
  Pallas kernels: 155 us -> 148 us
    unnamed x138 -> x184, local copies, waits for them, and re-layouts: 24.9 us -> 53.3 us
    ppermute x73, waiting for transfers between devices: 223 us -> 243 us  [swap(): return lax.ppermute(value, axis, [(i, i ^ offset) for i in range(count)])]
  transfers between devices with their start and end apart: 77 -> 77, of which waited for: 37 -> 33; matrix products, arithmetic and copies ran while one was open for 6% -> 6% of each run, Pallas kernels for 19% -> 17%
where the time goes in v8:
time: 633 us; the launch traced here: 631 us
  waiting for transfers between devices  257 us (41%)
  Pallas kernels  148 us (23%)
  starting transfers between devices  120 us (19%)
  local copies, waits for them, and re-layouts  70.3 us (11%)
  other arithmetic  22 us (3%)
  between operations  14.6 us (2%)
    ppermute x73, waiting for transfers between devices, swap(): return lax.ppermute(value, axis, [(i, i ^ offset) for i in range(count)])  243 us
    ppermute x73, starting transfers between devices, swap(): return lax.ppermute(value, axis, [(i, i ^ offset) for i in range(count)])  115 us
    unnamed x184, local copies, waits for them, and re-layouts  53.3 us
    pallas_call x2, Pallas kernels, ffn_middle(): pl.pallas_call(lambda *refs: ffn_kernel(len(blocks), len(earlier), *refs)...  28.1 us
    pallas_call x2, Pallas kernels, half_products(): pl.pallas_call(lambda *refs: products_kernel(count, got is not None, *ref...  26.6 us
    pallas_call x1, Pallas kernels, attend_back(): pl.pallas_call(lambda *refs: attend_back_kernel(KEY_CHUNK, *refs), grid=(...  20.6 us
    all_gather x1, waiting for transfers between devices, gather_blocks(): planes = lax.all_gather(after(mine, before_fsdp), 'fsdp')  14.2 us
  transfers between devices with their start and end apart: 77, of which 33 were waited for; matrix products, arithmetic and copies ran while one was open for 6% of the time, Pallas kernels for 17%

profile of v8, /device:TPU:0, one launch (start us, length us, event | category | flops | bytes accessed | tf_op | source)
XLA Modules:
  0.0 631.1 jit_solution(10916753783458624080)
XLA Ops:
  24.3 8.0 %collective-permute-start.20 = (bf16[512,384]{1,0:T(8,128)(2,1)S(1)}, bf16[512,384]{1,0:T(8,128)(2,1)S(1)}, u32[]{:S(2)}, u32[]{:S(2)}) collective-permute-start(bf16[512,384]{1,0:T(8,128)(2,1)S(1)} %collective-permute-done.10.refs_13_), channel_id=1, source_target_pairs={{0,1},{1,0},{2,3},{3,2},{4,5},{5,4},{6,7},{7,6},{8,9},{9,8},{10,11... | collective-permute-start | bytes 1179656 | tf_op jit(solution)/shard_map/ppermute | solution.py:43
  55.0 14.2 %all-gather.5.cloned.1.call-done = bf16[2048,256]{1,0:T(8,128)(2,1)} async-done(((bf16[512,256]{1,0:T(8,128)(2,1)}), bf16[2048,256]{1,0:T(8,128)(2,1)}) %all-gather.5.cloned.1.call-update) | async-done | bytes 1048592 | tf_op jit(solution)/shard_map/all_gather | solution.py:184
  73.0 8.9 %collective-permute-done.refs_3_ = bf16[512,384]{1,0:T(8,128)(2,1)S(1)} collective-permute-done((bf16[512,384]{1,0:T(8,128)(2,1)S(1)}, bf16[512,384]{1,0:T(8,128)(2,1)S(1)}, u32[]{:S(2)}, u32[]{:S(2)}) %collective-permute-start) | collective-permute-done | bytes 393248 | tf_op jit(solution)/shard_map/ppermute | solution.py:43
  86.0 13.5 %collective-permute-done.4.refs_7_ = bf16[512,384]{1,0:T(8,128)(2,1)S(1)} collective-permute-done((bf16[512,384]{1,0:T(8,128)(2,1)S(1)}, bf16[512,384]{1,0:T(8,128)(2,1)S(1)}, u32[]{:S(2)}, u32[]{:S(2)}) %collective-permute-start.4) | collective-permute-done | bytes 393248 | tf_op jit(solution)/shard_map/ppermute | solution.py:43
  101.1 8.6 %collective-permute-done.14.refs_17_ = bf16[512,384]{1,0:T(8,128)(2,1)S(1)} collective-permute-done((bf16[512,384]{1,0:T(8,128)(2,1)S(1)}, bf16[512,384]{1,0:T(8,128)(2,1)S(1)}, u32[]{:S(2)}, u32[]{:S(2)}) %collective-permute-start.14) | collective-permute-done | bytes 393248 | tf_op jit(solution)/shard_map/ppermute | solution.py:43
  186.3 12.6 %attend.1 = (bf16[128,2048]{1,0:T(8,128)(2,1)}, f32[128,2048]{1,0:T(8,128)S(1)}, f32[8,1,512]{2,1,0:T(1,128)S(1)}) custom-call(bf16[128,2048]{1,0:T(8,128)(2,1)S(1)} %get-tuple-element.71.refs_0_, bf16[512,1024]{1,0:T(8,128)(2,1)S(1)} %constant_dynamic-update-slice_fusion.1.refs_1_.refs_2_.refs_3_.refs_4_, ...), custom_call_target="tpu_custom_call" | custom-call | flops 1073741824 | bytes 2097152 | tf_op jit(solution)/shard_map/attend/pallas_call | solution.py:530
  199.9 9.9 %collective-permute-done.37.refs_3_.refs_12_.refs_16_ = bf16[128,2048]{1,0:T(8,128)(2,1)S(1)} collective-permute-done((bf16[128,2048]{1,0:T(8,128)(2,1)S(1)}, bf16[128,2048]{1,0:T(8,128)(2,1)S(1)}, u32[]{:S(2)}, u32[]{:S(2)}) %collective-permute-start.37) | collective-permute-done | bytes 524320 | tf_op jit(solution)/shard_map/ppermute | solution.py:43
  225.2 8.6 %down_back.1.refs_2_ = f32[512,2048]{1,0:T(8,128)} custom-call(bf16[128,2048]{1,0:T(8,128)(2,1)S(1)} %bitcast.69, bf16[128,2048]{1,0:T(8,128)(2,1)S(1)} %collective-permute-done.36.refs_1_.refs_10_.refs_14_, bf16[128,2048]{1,0:T(8,128)(2,1)S(1)} %collective-permute-done.38.refs_2_.refs_11_.refs_15_, ...), custom_call_target="tpu_custom_call" | custom-call | flops 4294967296 | bytes 8388608 | tf_op jit(solution)/shard_map/down_back/pallas_call | solution.py:828
  246.3 14.0 %ffn_middle.2 = (bf16[3,512,2048]{2,1,0:T(8,128)(2,1)}, f32[128,2048]{1,0:T(8,128)S(1)}, bf16[128,2048]{1,0:T(8,128)(2,1)S(1)}) custom-call(bf16[128,2048]{1,0:T(8,128)(2,1)S(1)} %get-tuple-element.77.refs_0_.refs_1_.refs_5_, bf16[128,2048]{1,0:T(8,128)(2,1)S(1)} %collective-permute-done.39.refs_1_.refs_2_.refs_6_, f32[512,2048]{1,0:T(8,128)} %down_back.1.refs_2_, ...), custom_call_target="tpu_custom_call" | custom-call | flops 8589934592 | bytes 16777216 | tf_op jit(solution)/shard_map/ffn_middle/pallas_call | solution.py:698
  262.2 14.0 %ffn_middle.3 = (bf16[3,512,2048]{2,1,0:T(8,128)(2,1)}, bf16[128,2048]{1,0:T(8,128)(2,1)S(1)}, f32[128,2048]{1,0:T(8,128)S(1)}) custom-call(bf16[128,2048]{1,0:T(8,128)(2,1)S(1)} %collective-permute-done.35.refs_0_.refs_3_.refs_7_, bf16[128,2048]{1,0:T(8,128)(2,1)S(1)} %collective-permute-done.34.refs_1_.refs_4_.refs_8_, ...), custom_call_target="tpu_custom_call", output_to_operand_aliasing={{0}: (4, {})} | custom-call | flops 8589934592 | bytes 16777216 | tf_op jit(solution)/shard_map/ffn_middle/pallas_call | solution.py:698
  279.6 12.2 %sent_products.1 = bf16[3,1024,2048]{2,1,0:T(8,128)(2,1)} custom-call(s32[2]{0:T(128)S(1)} %pad_add_fusion.refs_0_, bf16[128,2048]{1,0:T(8,128)(2,1)S(1)} %get-tuple-element.77.refs_0_.refs_1_.refs_5_, bf16[128,2048]{1,0:T(8,128)(2,1)S(1)} %collective-permute-done.39.refs_1_.refs_2_.refs_6_, ...), custom_call_target="tpu_custom_call" | custom-call | flops 6442450944 | bytes 12582912 | tf_op jit(solution)/shard_map/sent_products/pallas_call | solution.py:778
  291.8 19.4 %collective-permute-done.72.refs_18_ = bf16[3,1024,2048]{2,1,0:T(8,128)(2,1)S(1)} collective-permute-done((bf16[3,1024,2048]{2,1,0:T(8,128)(2,1)}, bf16[3,1024,2048]{2,1,0:T(8,128)(2,1)S(1)}, u32[]{:S(2)}, u32[]{:S(2)}) %collective-permute-start.72) | collective-permute-done | bytes 12582944 | tf_op jit(solution)/shard_map/ppermute | solution.py:43
  315.7 14.4 %kept_products.1 = bf16[3,1024,2048]{2,1,0:T(8,128)(2,1)} custom-call(s32[2]{0:T(128)S(1)} %pad_add_fusion.refs_0_, bf16[128,2048]{1,0:T(8,128)(2,1)S(1)} %get-tuple-element.77.refs_0_.refs_1_.refs_5_, bf16[128,2048]{1,0:T(8,128)(2,1)S(1)} %collective-permute-done.39.refs_1_.refs_2_.refs_6_, ...), custom_call_target="tpu_custom_call" | custom-call | flops 6442450944 | bytes 12582912 | tf_op jit(solution)/shard_map/kept_products/pallas_call | solution.py:778
  332.2 13.0 %collective-permute-done.41 = bf16[128,2048]{1,0:T(8,128)(2,1)S(1)} collective-permute-done((bf16[128,2048]{1,0:T(8,128)(2,1)}, bf16[128,2048]{1,0:T(8,128)(2,1)S(1)}, u32[]{:S(2)}, u32[]{:S(2)}) %collective-permute-start.41) | collective-permute-done | bytes 524320 | tf_op jit(solution)/shard_map/ppermute | solution.py:43
  355.6 13.4 %collective-permute-done.42 = bf16[128,2048]{1,0:T(8,128)(2,1)S(1)} collective-permute-done((bf16[128,2048]{1,0:T(8,128)(2,1)S(1)}, bf16[128,2048]{1,0:T(8,128)(2,1)S(1)}, u32[]{:S(2)}, u32[]{:S(2)}) %collective-permute-start.42) | collective-permute-done | bytes 524320 | tf_op jit(solution)/shard_map/ppermute | solution.py:43
  376.8 20.6 %attend_back.1 = (bf16[128,2048]{1,0:T(8,128)(2,1)}, bf16[2,512,512]{2,1,0:T(8,128)(2,1)S(1)}, bf16[2,512,512]{2,1,0:T(8,128)(2,1)S(1)}) custom-call(bf16[128,2048]{1,0:T(8,128)(2,1)S(1)} %copy-done.61, bf16[128,2048]{1,0:T(8,128)(2,1)S(1)} %out_back.1.refs_1_, f32[128,2048]{1,0:T(8,128)S(1)} %copy-done.74, bf16[512,1024]{1,0:T(8,128)(2,1)} %copy-done.58, ...), custom_call_target="tpu_custom_call" | custom-call | flops 2684354560 | bytes 4194304 | tf_op jit(solution)/shard_map/attend_back/pallas_call | solution.py:595
  427.8 25.9 %collective-permute-done.56 = f32[1,2048]{1,0:T(1,128)S(1)} collective-permute-done((f32[1,2048]{1,0:T(1,128)S(1)}, f32[1,2048]{1,0:T(1,128)S(1)}, u32[]{:S(2)}, u32[]{:S(2)}) %collective-permute-start.56) | collective-permute-done | bytes 8224 | tf_op jit(solution)/shard_map/ppermute | solution.py:43
  459.4 25.7 %collective-permute-done.57 = f32[1,2048]{1,0:T(1,128)S(1)} collective-permute-done((f32[1,2048]{1,0:T(1,128)S(1)}, f32[1,2048]{1,0:T(1,128)S(1)}, u32[]{:S(2)}, u32[]{:S(2)}) %collective-permute-start.57) | collective-permute-done | bytes 8224 | tf_op jit(solution)/shard_map/ppermute | solution.py:43
  497.2 9.1 %one_back.1 = f32[128,2048]{1,0:T(8,128)} custom-call(bf16[128,2048]{1,0:T(8,128)(2,1)} %get-tuple-element.114.query_ref.refs_9_, bf16[512,1024]{1,0:T(8,128)(2,1)S(1)} %copy-done.5, bf16[2048,3072]{1,0:T(8,128)(2,1)} %get-tuple-element.105.w_ref, bf16[128,2048]{1,0:T(8,128)(2,1)S(1)} %bitcast.75, f32[1,2048]{1,0:T(1,128)S(1)} %bitcast.77, ...), custom_call_target="tpu_custom_call" | custom-call | flops 1610612736 | bytes 12582912 | tf_op jit(solution)/shard_map/one_back/pallas_call | solution.py:330
  507.8 12.9 %collective-permute-start.51 = (bf16[128,512]{1,0:T(8,128)(2,1)S(1)}, bf16[128,512]{1,0:T(8,128)(2,1)S(1)}, u32[]{:S(2)}, u32[]{:S(2)}) collective-permute-start(bf16[128,512]{1,0:T(8,128)(2,1)S(1)} %copy-done.79), channel_id=1, source_target_pairs={{0,2},{1,3},{2,0},{3,1},{4,6},{5,7},{6,4},{7,5},{8,10},{9,11},{10,... | collective-permute-start | bytes 393224 | tf_op jit(solution)/shard_map/ppermute | solution.py:43
  521.9 16.2 %collective-permute-start.65 = (bf16[128,2048]{1,0:T(8,128)(2,1)}, bf16[128,2048]{1,0:T(8,128)(2,1)S(1)}, u32[]{:S(2)}, u32[]{:S(2)}) collective-permute-start(bf16[128,2048]{1,0:T(8,128)(2,1)} %get-tuple-element.122.refs_1_.refs_5_), channel_id=1, source_target_pairs={{0,1},{1,0},{2,3},{3,2},{4,5},{5,4},{6,7},{7,6},{8,9},{9,8},{10,11... | collective-permute-start | bytes 1572872 | tf_op jit(solution)/shard_map/ppermute | solution.py:43
  554.8 11.0 %collective-permute-done.67.refs_7_ = bf16[128,2048]{1,0:T(8,128)(2,1)} collective-permute-done((bf16[128,2048]{1,0:T(8,128)(2,1)}, bf16[128,2048]{1,0:T(8,128)(2,1)}, u32[]{:S(2)}, u32[]{:S(2)}) %collective-permute-start.67) | collective-permute-done | bytes 524320 | tf_op jit(solution)/shard_map/ppermute | solution.py:43
  589.7 10.2 %collective-permute-done.61 = bf16[64,3200]{1,0:T(8,128)(2,1)S(1)} collective-permute-done((bf16[64,3200]{1,0:T(8,128)(2,1)S(1)}, bf16[64,3200]{1,0:T(8,128)(2,1)S(1)}, u32[]{:S(2)}, u32[]{:S(2)}) %collective-permute-start.61) | collective-permute-done | bytes 409632 | tf_op jit(solution)/shard_map/ppermute | solution.py:43
  601.3 12.3 %collective-permute-done.60 = bf16[64,3200]{1,0:T(8,128)(2,1)S(1)} collective-permute-done((bf16[64,3200]{1,0:T(8,128)(2,1)S(1)}, bf16[64,3200]{1,0:T(8,128)(2,1)S(1)}, u32[]{:S(2)}, u32[]{:S(2)}) %collective-permute-start.60) | collective-permute-done | bytes 409632 | tf_op jit(solution)/shard_map/ppermute | solution.py:43
  (409 shorter events, 287.7 us)
Async XLA Ops:
  7.2 62.0 %all-gather.5.cloned.1.call-start = ((), (), s32[]{:S(2)}) async-start(), calls=%async_computation.3 | async-start | bytes 1310720 | tf_op jit(solution)/shard_map/all_gather | solution.py:184
  40.9 169.6 %all-gather.7.cloned.1.call-start = ((), (), s32[]{:S(2)}) async-start(), calls=%async_computation.4 | async-start | bytes 7077888 | tf_op jit(solution)/shard_map/all_gather | solution.py:191
  71.4 547.7 %reduce-scatter.2.cloned.1.call-start = ((), (), s32[]{:S(2)}) async-start(), calls=%async_computation.2 | async-start | bytes 15728640 | tf_op jit(solution)/shard_map/reduce_scatter | solution.py:814
  413.0 74.7 %collective-permute-start.43 = (bf16[128,2048]{1,0:T(8,128)(2,1)}, bf16[128,2048]{1,0:T(8,128)(2,1)}, u32[]{:S(2)}, u32[]{:S(2)}) collective-permute-start(bf16[128,2048]{1,0:T(8,128)(2,1)} %get-tuple-element.95), channel_id=1, source_target_pairs={{0,1},{1,0},{2,3},{3,2},{4,5},{5,4},{6,7},{7,6},{8,9},{9,8},{10,11... | collective-permute-start | bytes 1572872 | tf_op jit(solution)/shard_map/ppermute | solution.py:43
  414.4 73.3 %collective-permute-start.54 = (bf16[128,2048]{1,0:T(8,128)(2,1)}, bf16[128,2048]{1,0:T(8,128)(2,1)}, u32[]{:S(2)}, u32[]{:S(2)}) collective-permute-start(bf16[128,2048]{1,0:T(8,128)(2,1)} %get-tuple-element.114.query_ref.refs_9_), channel_id=1, source_target_pairs={{0,3},{1,2},{2,1},{3,0},{4,7},{5,6},{6,5},{7,4},{8,11},{9,10},{10,... | collective-permute-start | bytes 1572872 | tf_op jit(solution)/shard_map/ppermute | solution.py:43
  421.5 123.6 %all-to-all-start = ((bf16[4,128,1024]{2,1,0:T(8,128)(2,1)}), bf16[4,128,1024]{2,1,0:T(8,128)(2,1)}, u32[]{:S(2)}, u32[]{:S(2)}) async-start(bf16[4,128,1024]{2,1,0:T(8,128)(2,1)} %bitcast.76), calls=%async_computation | async-start | bytes 2097152 | tf_op jit(solution)/shard_map/all_to_all | solution.py:1126
  426.0 27.6 %collective-permute-start.56 = (f32[1,2048]{1,0:T(1,128)S(1)}, f32[1,2048]{1,0:T(1,128)S(1)}, u32[]{:S(2)}, u32[]{:S(2)}) collective-permute-start(f32[1,2048]{1,0:T(1,128)S(1)} %bitcast.97), channel_id=1, source_target_pairs={{0,1},{1,0},{2,3},{3,2},{4,5},{5,4},{6,7},{7,6},{8,9},{9,8},{10,11... | collective-permute-start | bytes 24584 | tf_op jit(solution)/shard_map/ppermute | solution.py:43
  453.6 31.5 %collective-permute-start.57 = (f32[1,2048]{1,0:T(1,128)S(1)}, f32[1,2048]{1,0:T(1,128)S(1)}, u32[]{:S(2)}, u32[]{:S(2)}) collective-permute-start(f32[1,2048]{1,0:T(1,128)S(1)} %add.414), channel_id=1, source_target_pairs={{0,2},{1,3},{2,0},{3,1},{4,6},{5,7},{6,4},{7,5},{8,10},{9,11},{10,... | collective-permute-start | bytes 24584 | tf_op jit(solution)/shard_map/ppermute | solution.py:43
  457.5 50.2 %collective-permute-start.44 = (bf16[128,2048]{1,0:T(8,128)(2,1)}, bf16[128,2048]{1,0:T(8,128)(2,1)}, u32[]{:S(2)}, u32[]{:S(2)}) collective-permute-start(bf16[128,2048]{1,0:T(8,128)(2,1)} %copy-done.63), channel_id=1, source_target_pairs={{0,2},{1,3},{2,0},{3,1},{4,6},{5,7},{6,4},{7,5},{8,10},{9,11},{10,... | collective-permute-start | bytes 1572872 | tf_op jit(solution)/shard_map/ppermute | solution.py:43
  457.6 50.2 %collective-permute-start.45 = (bf16[128,2048]{1,0:T(8,128)(2,1)}, bf16[128,2048]{1,0:T(8,128)(2,1)}, u32[]{:S(2)}, u32[]{:S(2)}) collective-permute-start(bf16[128,2048]{1,0:T(8,128)(2,1)} %copy-done.62), channel_id=1, source_target_pairs={{0,3},{1,2},{2,1},{3,0},{4,7},{5,6},{6,5},{7,4},{8,11},{9,10},{10,... | collective-permute-start | bytes 1572872 | tf_op jit(solution)/shard_map/ppermute | solution.py:43
  485.1 35.5 %collective-permute-start.66 = (bf16[128,2048]{1,0:T(8,128)(2,1)}, bf16[128,2048]{1,0:T(8,128)(2,1)}, u32[]{:S(2)}, u32[]{:S(2)}) collective-permute-start(bf16[128,2048]{1,0:T(8,128)(2,1)} %get-tuple-element.122.refs_1_.refs_5_), channel_id=1, source_target_pairs={{0,3},{1,2},{2,1},{3,0},{4,7},{5,6},{6,5},{7,4},{8,11},{9,10},{10,... | collective-permute-start | bytes 1572872 | tf_op jit(solution)/shard_map/ppermute | solution.py:43
  487.7 34.2 %collective-permute-start.53 = (bf16[128,2048]{1,0:T(8,128)(2,1)}, bf16[128,2048]{1,0:T(8,128)(2,1)}, u32[]{:S(2)}, u32[]{:S(2)}) collective-permute-start(bf16[128,2048]{1,0:T(8,128)(2,1)} %get-tuple-element.114.query_ref.refs_9_), channel_id=1, source_target_pairs={{0,1},{1,0},{2,3},{3,2},{4,5},{5,4},{6,7},{7,6},{8,9},{9,8},{10,11... | collective-permute-start | bytes 1572872 | tf_op jit(solution)/shard_map/ppermute | solution.py:43
  487.7 50.4 %collective-permute-start.55 = (bf16[128,2048]{1,0:T(8,128)(2,1)}, bf16[128,2048]{1,0:T(8,128)(2,1)}, u32[]{:S(2)}, u32[]{:S(2)}) collective-permute-start(bf16[128,2048]{1,0:T(8,128)(2,1)} %collective-permute-done.54.refs_12_), channel_id=1, source_target_pairs={{0,1},{1,0},{2,3},{3,2},{4,5},{5,4},{6,7},{7,6},{8,9},{9,8},{10,11... | collective-permute-start | bytes 1572872 | tf_op jit(solution)/shard_map/ppermute | solution.py:43
  507.8 32.9 %collective-permute-start.50 = (bf16[128,512]{1,0:T(8,128)(2,1)S(1)}, bf16[128,512]{1,0:T(8,128)(2,1)S(1)}, u32[]{:S(2)}, u32[]{:S(2)}) collective-permute-start(bf16[128,512]{1,0:T(8,128)(2,1)S(1)} %copy-done.80), channel_id=1, source_target_pairs={{0,1},{1,0},{2,3},{3,2},{4,5},{5,4},{6,7},{7,6},{8,9},{9,8},{10,11... | collective-permute-start | bytes 393224 | tf_op jit(solution)/shard_map/ppermute | solution.py:43
  507.8 34.9 %collective-permute-start.51 = (bf16[128,512]{1,0:T(8,128)(2,1)S(1)}, bf16[128,512]{1,0:T(8,128)(2,1)S(1)}, u32[]{:S(2)}, u32[]{:S(2)}) collective-permute-start(bf16[128,512]{1,0:T(8,128)(2,1)S(1)} %copy-done.79), channel_id=1, source_target_pairs={{0,2},{1,3},{2,0},{3,1},{4,6},{5,7},{6,4},{7,5},{8,10},{9,11},{10,... | collective-permute-start | bytes 393224 | tf_op jit(solution)/shard_map/ppermute | solution.py:43
  521.9 31.9 %collective-permute-start.65 = (bf16[128,2048]{1,0:T(8,128)(2,1)}, bf16[128,2048]{1,0:T(8,128)(2,1)S(1)}, u32[]{:S(2)}, u32[]{:S(2)}) collective-permute-start(bf16[128,2048]{1,0:T(8,128)(2,1)} %get-tuple-element.122.refs_1_.refs_5_), channel_id=1, source_target_pairs={{0,1},{1,0},{2,3},{3,2},{4,5},{5,4},{6,7},{7,6},{8,9},{9,8},{10,11... | collective-permute-start | bytes 1572872 | tf_op jit(solution)/shard_map/ppermute | solution.py:43
  538.1 27.7 %collective-permute-start.67 = (bf16[128,2048]{1,0:T(8,128)(2,1)}, bf16[128,2048]{1,0:T(8,128)(2,1)}, u32[]{:S(2)}, u32[]{:S(2)}) collective-permute-start(bf16[128,2048]{1,0:T(8,128)(2,1)} %collective-permute-done.66.refs_8_), channel_id=1, source_target_pairs={{0,1},{1,0},{2,3},{3,2},{4,5},{5,4},{6,7},{7,6},{8,9},{9,8},{10,11... | collective-permute-start | bytes 1572872 | tf_op jit(solution)/shard_map/ppermute | solution.py:43
  540.7 26.4 %collective-permute-start.62 = (bf16[128,512]{1,0:T(8,128)(2,1)}, bf16[128,512]{1,0:T(8,128)(2,1)S(1)}, u32[]{:S(2)}, u32[]{:S(2)}) collective-permute-start(bf16[128,512]{1,0:T(8,128)(2,1)} %copy.84), channel_id=1, source_target_pairs={{0,1},{1,0},{2,3},{3,2},{4,5},{5,4},{6,7},{7,6},{8,9},{9,8},{10,11... | collective-permute-start | bytes 393224 | tf_op jit(solution)/shard_map/ppermute | solution.py:43
  542.6 26.1 %collective-permute-start.64 = (bf16[128,512]{1,0:T(8,128)(2,1)}, bf16[128,512]{1,0:T(8,128)(2,1)S(1)}, u32[]{:S(2)}, u32[]{:S(2)}) collective-permute-start(bf16[128,512]{1,0:T(8,128)(2,1)} %copy.86), channel_id=1, source_target_pairs={{0,3},{1,2},{2,1},{3,0},{4,7},{5,6},{6,5},{7,4},{8,11},{9,10},{10,... | collective-permute-start | bytes 393224 | tf_op jit(solution)/shard_map/ppermute | solution.py:43
  554.7 28.9 %collective-permute-start.58 = (bf16[4,64,3200]{2,1,0:T(8,128)(2,1)}, bf16[4,64,3200]{2,1,0:T(8,128)(2,1)}, u32[]{:S(2)}, u32[]{:S(2)}) collective-permute-start(bf16[4,64,3200]{2,1,0:T(8,128)(2,1)} %get-tuple-element.119), channel_id=1, source_target_pairs={{0,4},{4,0},{8,12},{12,8},{16,20},{20,16},{24,28},{28,24},{1,5},{5... | collective-permute-start | bytes 4915208 | tf_op jit(solution)/shard_map/ppermute | solution.py:43
  581.8 33.1 %collective-permute-start.69 = (bf16[64,2048]{1,0:T(8,128)(2,1)S(1)}, bf16[64,2048]{1,0:T(8,128)(2,1)S(1)}, u32[]{:S(2)}, u32[]{:S(2)}) collective-permute-start(bf16[64,2048]{1,0:T(8,128)(2,1)S(1)} %get-tuple-element.152), channel_id=1, source_target_pairs={{0,8},{4,12},{8,0},{12,4},{16,24},{20,28},{24,16},{28,20},{1,9},{5... | collective-permute-start | bytes 786440 | tf_op jit(solution)/shard_map/ppermute | solution.py:43
  582.4 32.5 %collective-permute-start.70 = (bf16[64,2048]{1,0:T(8,128)(2,1)S(1)}, bf16[64,2048]{1,0:T(8,128)(2,1)S(1)}, u32[]{:S(2)}, u32[]{:S(2)}) collective-permute-start(bf16[64,2048]{1,0:T(8,128)(2,1)S(1)} %get-tuple-element.151), channel_id=1, source_target_pairs={{0,16},{4,20},{8,24},{12,28},{16,0},{20,4},{24,8},{28,12},{1,17},{... | collective-permute-start | bytes 786440 | tf_op jit(solution)/shard_map/ppermute | solution.py:43
  586.9 26.7 %collective-permute-start.60 = (bf16[64,3200]{1,0:T(8,128)(2,1)S(1)}, bf16[64,3200]{1,0:T(8,128)(2,1)S(1)}, u32[]{:S(2)}, u32[]{:S(2)}) collective-permute-start(bf16[64,3200]{1,0:T(8,128)(2,1)S(1)} %get-tuple-element.149), channel_id=1, source_target_pairs={{0,16},{4,20},{8,24},{12,28},{16,0},{20,4},{24,8},{28,12},{1,17},{... | collective-permute-start | bytes 1228808 | tf_op jit(solution)/shard_map/ppermute | solution.py:43
  587.5 26.1 %collective-permute-start.59 = (bf16[64,3200]{1,0:T(8,128)(2,1)S(1)}, bf16[64,3200]{1,0:T(8,128)(2,1)S(1)}, u32[]{:S(2)}, u32[]{:S(2)}) collective-permute-start(bf16[64,3200]{1,0:T(8,128)(2,1)S(1)} %get-tuple-element.147), channel_id=1, source_target_pairs={{0,8},{4,12},{8,0},{12,4},{16,24},{20,28},{24,16},{28,20},{1,9},{5... | collective-permute-start | bytes 1228808 | tf_op jit(solution)/shard_map/ppermute | solution.py:43
  (141 other events, 2189.4 us)
Sparse Core Ops, SparseCore 0:
  41.0 28.1 all-gather.4
  71.7 62.5 all-gather.6
  330.2 125.6 reduce-scatter.1

commit v9 on v8

--- a/solution.py
+++ b/solution.py
@@ -159,7 +159,7 @@
             pltpu.HBM((width, columns), BF),
         ),
         in_specs=[pl.BlockSpec(memory_space=pltpu.SMEM), vmem, hbm]
-        + [pl.BlockSpec(memory_space=pl.ANY)] * len(arrays)
+        + [hbm] * len(arrays)
         + [vmem, vmem],
         out_specs=(vmem, vmem, hbm),
         scratch_shapes=[
@@ -173,7 +173,7 @@
             flops=2 * rows * width * columns, bytes_accessed=4 * width * columns, transcendentals=0
         ),
         name="pieces_forward",
-    )(jnp.stack([me, plane]), x, in_hbm(own), *arrays, cosine, sine)
+    )(jnp.stack([me, plane]), x, in_hbm(own), *[in_hbm(part) for part in arrays], cosine, sine)
 
 
 def gather_blocks(weight, before_fsdp, before_ctx):
@@ -723,81 +723,62 @@
 
 
 def products_kernel(count, added, ids_ref, *refs):
-    in_refs, grad_refs = refs[: 2 * count], refs[2 * count : 4 * count]
-    right, rest = refs[4 * count], refs[4 * count + 1 :]
+    blocks, right, rest = refs[: 2 * count], refs[2 * count], refs[2 * count + 1 :]
     out_ref, left = rest[-2:]
-
-    def join(blocks):
-        rows, height = blocks[0].shape
-        for j in range(2):
-            for i in range(count):
-                at = (slice(i * rows, (i + 1) * rows), slice(j * height, (j + 1) * height))
-                left[at] = blocks[j * count + i][...]
-
-    @pl.when(pl.program_id(0) < 2)
-    def _():
-        join(in_refs)
-
-    @pl.when(pl.program_id(0) == 2)
-    def _():
-        join(grad_refs)
-
+    rows, height = blocks[0].shape
+    for j in range(2):
+        for i in range(count):
+            at = (slice(i * rows, (i + 1) * rows), slice(j * height, (j + 1) * height))
+            left[at] = blocks[j * count + i][...]
     part = tn(left[...], right[0])
     if added:
         part = part + rest[0][0].astype(F32)
     out_ref[0] = part.astype(BF)
 
 
-def half_products(rows_in, rows_out, parts, got):
-    count = len(rows_in)
-    rows, width = rows_in[0].shape
-    hidden = parts.shape[2]
+def half_products(rows_of, parts, first, size, got, earlier):
+    count = len(rows_of)
+    rows, width = rows_of[0].shape
+    matrices, _, hidden = parts.shape
     ctx_count = lax.axis_size("ctx")
     height = width // ctx_count
-    last = ctx_count // 4 - 1
-
-    def column(i, j, ids_ref):
-        own = ids_ref[0] % 2
-        return 2 * (2 * i + j) + (own if got is not None else 1 - own)
+    kept = got is not None
 
     def left(j):
-        return pl.BlockSpec(
-            (rows, height),
-            lambda k, i, ids_ref: (0, column(jnp.where(k < 2, i, last), j, ids_ref)),
-        )
-
-    def grad(j):
-        return pl.BlockSpec(
-            (rows, height),
-            lambda k, i, ids_ref: (0, column(jnp.where(k == 2, i, 0), j, ids_ref)),
-        )
-
-    right = pl.BlockSpec((1, rows * count, hidden), lambda k, i, ids_ref: (k, 0, 0))
-    out = pl.BlockSpec((1, 2 * height, hidden), lambda k, i, ids_ref: (k, i, 0))
-    extra = [] if got is None else [got]
+        def place(k, i, ids_ref):
+            own = ids_ref[0] % 2
+            return (0, 2 * (2 * i + j) + (own if kept else 1 - own))
+
+        return pl.BlockSpec((rows, height), place)
+
+    def out(start):
+        return pl.BlockSpec((1, 2 * height, hidden), lambda k, i, ids_ref: (start + k, i, 0))
+
+    right = pl.BlockSpec((1, rows * count, hidden), lambda k, i, ids_ref: (first + k, 0, 0))
+    extra = ([got] if kept else []) + earlier
+    operands = 2 * count + 1 + len(extra)
     return pl.pallas_call(
-        lambda *refs: products_kernel(count, got is not None, *refs),
+        lambda *refs: products_kernel(count, kept, *refs),
         grid_spec=pltpu.PrefetchScalarGridSpec(
             num_scalar_prefetch=1,
-            grid=(3, ctx_count // 4),
+            grid=(size, ctx_count // 4),
             in_specs=[left(0)] * count
             + [left(1)] * count
-            + [grad(0)] * count
-            + [grad(1)] * count
             + [right]
-            + [out] * len(extra),
-            out_specs=out,
+            + [out(0)] * kept
+            + [pl.BlockSpec(memory_space=pltpu.HBM)] * len(earlier),
+            out_specs=out(first if kept else 0),
             scratch_shapes=[pltpu.VMEM((count * rows, 2 * height), BF)],
         ),
-        out_shape=pltpu.HBM((3, width // 2, hidden), BF),
-        compiler_params=pltpu.CompilerParams(vmem_limit_bytes=32 << 20),
+        out_shape=pltpu.HBM((matrices if kept else size, width // 2, hidden), BF),
+        input_output_aliases={operands: 0} if earlier else {},
+        compiler_params=pltpu.CompilerParams(vmem_limit_bytes=24 << 20),
         cost_estimate=pl.CostEstimate(
-            flops=3 * count * rows * width * hidden,
-            bytes_accessed=3 * width * hidden,
+            flops=size * count * rows * width * hidden,
+            bytes_accessed=size * width * hidden,
             transcendentals=0,
         ),
-        name="kept_products" if extra else "sent_products",
-    )(jnp.stack(ids()), *rows_in, *rows_in, *rows_out, *rows_out, parts, *extra)
+    )(jnp.stack(ids()), *rows_of, *rows_of, in_hbm(parts), *extra)
 
 
 def ffn_gradient(rows_in, rows_out, parts):
@@ -807,11 +788,22 @@
         products = [tn(left, parts[0]), tn(left, parts[1]), tn(grad, parts[2])]
         products = jnp.stack(products, axis=1).astype(BF)
         return lax.psum_scatter(products, "ctx", scatter_dimension=0, tiled=True)
-    sent = half_products(rows_in, rows_out, parts, None)
-    got = swap(sent, "ctx", 1)
-    kept = half_products(rows_in, rows_out, parts, got).transpose(1, 0, 2)
+    calls = ((rows_out, 2, 1), (rows_in, 0, 2))
+    got = []
+    for rows_of, first, size in calls:
+        sent = half_products(rows_of, parts, first, size, None, [])
+        got.append(swap(sent, "ctx", 1))
+    kept = []
+    for (rows_of, first, size), part in zip(calls, got):
+        kept = [half_products(rows_of, parts, first, size, part, kept)]
     groups = [list(range(core, count, 2)) for core in range(2)]
-    return lax.psum_scatter(kept, "ctx", scatter_dimension=0, tiled=True, axis_index_groups=groups)
+    return lax.psum_scatter(
+        kept[0].transpose(1, 0, 2),
+        "ctx",
+        scatter_dimension=0,
+        tiled=True,
+        axis_index_groups=groups,
+    )
 
 
 def down_back_kernel(count, *refs):
@@ -873,7 +865,7 @@
             transcendentals=0,
         ),
         name="down_forward",
-    )(parts, weights)
+    )(in_hbm(parts), weights)
 
 
 def share_kernel(count, sizes, ids_ref, *refs):

time: 633 us -> 601 us (0.949)
  local copies, waits for them, and re-layouts: 70.3 us -> 34.3 us
  Pallas kernels: 148 us -> 156 us
    unnamed x184 -> x132, local copies, waits for them, and re-layouts: 53.3 us -> 20.3 us
    pallas_call x2 -> x4, Pallas kernels: 26.6 us -> 32.8 us  [half_products(): pl.pallas_call(lambda *refs: products_kernel(count, kept, *refs), grid_sp...]
    ppermute x73 -> x74, waiting for transfers between devices: 243 us -> 239 us  [swap(): return lax.ppermute(value, axis, [(i, i ^ offset) for i in range(count)])]
    ppermute x73 -> x74, starting transfers between devices: 115 us -> 115 us  [swap(): return lax.ppermute(value, axis, [(i, i ^ offset) for i in range(count)])]
  transfers between devices with their start and end apart: 77 -> 78, of which waited for: 33 -> 36; matrix products, arithmetic and copies ran while one was open for 6% -> 6% of each run, Pallas kernels for 17% -> 20%
where the time goes in v9:
time: 601 us; the launch traced here: 599 us
  waiting for transfers between devices  253 us (42%)
  Pallas kernels  156 us (26%)
  starting transfers between devices  119 us (20%)
  local copies, waits for them, and re-layouts  34.3 us (6%)
  other arithmetic  21.6 us (4%)
  between operations  14.7 us (2%)
    ppermute x74, waiting for transfers between devices, swap(): return lax.ppermute(value, axis, [(i, i ^ offset) for i in range(count)])  239 us
    ppermute x74, starting transfers between devices, swap(): return lax.ppermute(value, axis, [(i, i ^ offset) for i in range(count)])  115 us
    pallas_call x4, Pallas kernels, half_products(): pl.pallas_call(lambda *refs: products_kernel(count, kept, *refs), grid_sp...  32.8 us
    pallas_call x2, Pallas kernels, ffn_middle(): pl.pallas_call(lambda *refs: ffn_kernel(len(blocks), len(earlier), *refs)...  28 us
    pallas_call x1, Pallas kernels, attend_back(): pl.pallas_call(lambda *refs: attend_back_kernel(KEY_CHUNK, *refs), grid=(...  20.3 us
    unnamed x132, local copies, waits for them, and re-layouts  20.3 us
    all_gather x1, waiting for transfers between devices, gather_blocks(): planes = lax.all_gather(after(mine, before_fsdp), 'fsdp')  14.1 us
    pallas_call x1, Pallas kernels, attend(): pl.pallas_call(lambda *refs: attend_kernel(KEY_CHUNK, *refs), grid=(KV,),...  12.8 us
  transfers between devices with their start and end apart: 78, of which 36 were waited for; matrix products, arithmetic and copies ran while one was open for 6% of the time, Pallas kernels for 20%

profile of v9, /device:TPU:0, one launch (start us, length us, event | category | flops | bytes accessed | tf_op | source)
XLA Modules:
  0.0 599.0 jit_solution(6318648117392394995)
XLA Ops:
  53.7 14.1 %all-gather.5.cloned.1.call-done = bf16[2048,256]{1,0:T(8,128)(2,1)} async-done(((bf16[512,256]{1,0:T(8,128)(2,1)}), bf16[2048,256]{1,0:T(8,128)(2,1)}) %all-gather.5.cloned.1.call-update) | async-done | bytes 1048592 | tf_op jit(solution)/shard_map/all_gather | solution.py:184
  71.6 8.9 %collective-permute-done.refs_3_ = bf16[512,384]{1,0:T(8,128)(2,1)S(1)} collective-permute-done((bf16[512,384]{1,0:T(8,128)(2,1)S(1)}, bf16[512,384]{1,0:T(8,128)(2,1)S(1)}, u32[]{:S(2)}, u32[]{:S(2)}) %collective-permute-start) | collective-permute-done | bytes 393248 | tf_op jit(solution)/shard_map/ppermute | solution.py:43
  84.5 13.5 %collective-permute-done.4.refs_7_ = bf16[512,384]{1,0:T(8,128)(2,1)S(1)} collective-permute-done((bf16[512,384]{1,0:T(8,128)(2,1)S(1)}, bf16[512,384]{1,0:T(8,128)(2,1)S(1)}, u32[]{:S(2)}, u32[]{:S(2)}) %collective-permute-start.4) | collective-permute-done | bytes 393248 | tf_op jit(solution)/shard_map/ppermute | solution.py:43
  99.7 8.6 %collective-permute-done.14.refs_17_ = bf16[512,384]{1,0:T(8,128)(2,1)S(1)} collective-permute-done((bf16[512,384]{1,0:T(8,128)(2,1)}, bf16[512,384]{1,0:T(8,128)(2,1)S(1)}, u32[]{:S(2)}, u32[]{:S(2)}) %collective-permute-start.14) | collective-permute-done | bytes 393248 | tf_op jit(solution)/shard_map/ppermute | solution.py:43
  133.6 9.7 %pieces_forward.1 = (bf16[128,2048]{1,0:T(8,128)(2,1)S(1)}, bf16[128,1024]{1,0:T(8,128)(2,1)S(1)}, bf16[2048,3072]{1,0:T(8,128)(2,1)}) custom-call(s32[2]{0:T(128)S(1)} %pad_add_fusion.refs_0_, bf16[128,2048]{1,0:T(8,128)(2,1)S(1)} %fusion.2.refs_1_, bf16[512,3072]{1,0:T(8,128)(2,1)} %refs_2_.3, bf16[512,384]{1,0:T(8,128)(2,1)} %copy-done.39, ...), custom_call_target="tpu_custom_call" | custom-call | flops 1610612736 | bytes 25165824 | tf_op jit(solution)/shard_map/pieces_forward/pallas_call | solution.py:154
  162.7 12.8 %attend.1 = (bf16[128,2048]{1,0:T(8,128)(2,1)}, f32[128,2048]{1,0:T(8,128)S(1)}, f32[8,1,512]{2,1,0:T(1,128)S(1)}) custom-call(bf16[128,2048]{1,0:T(8,128)(2,1)S(1)} %get-tuple-element.71.refs_0_, bf16[512,1024]{1,0:T(8,128)(2,1)S(1)} %constant_dynamic-update-slice_fusion.1.refs_1_.refs_2_.refs_3_.refs_4_, ...), custom_call_target="tpu_custom_call" | custom-call | flops 1073741824 | bytes 2097152 | tf_op jit(solution)/shard_map/attend/pallas_call | solution.py:530
  176.4 9.7 %collective-permute-done.37.refs_3_.refs_4_.refs_8_ = bf16[128,2048]{1,0:T(8,128)(2,1)S(1)} collective-permute-done((bf16[128,2048]{1,0:T(8,128)(2,1)S(1)}, bf16[128,2048]{1,0:T(8,128)(2,1)S(1)}, u32[]{:S(2)}, u32[]{:S(2)}) %collective-permute-start.37) | collective-permute-done | bytes 524320 | tf_op jit(solution)/shard_map/ppermute | solution.py:43
  201.8 8.7 %down_back.1.refs_2_ = f32[512,2048]{1,0:T(8,128)} custom-call(bf16[128,2048]{1,0:T(8,128)(2,1)S(1)} %bitcast.67, bf16[128,2048]{1,0:T(8,128)(2,1)S(1)} %collective-permute-done.36.refs_1_.refs_2_.refs_6_, bf16[128,2048]{1,0:T(8,128)(2,1)S(1)} %collective-permute-done.38.refs_2_.refs_3_.refs_7_, ...), custom_call_target="tpu_custom_call" | custom-call | flops 4294967296 | bytes 8388608 | tf_op jit(solution)/shard_map/down_back/pallas_call | solution.py:820
  222.7 14.0 %ffn_middle.2 = (bf16[3,512,2048]{2,1,0:T(8,128)(2,1)}, f32[128,2048]{1,0:T(8,128)S(1)}, bf16[128,2048]{1,0:T(8,128)(2,1)S(1)}) custom-call(bf16[128,2048]{1,0:T(8,128)(2,1)S(1)} %get-tuple-element.77.refs_0_.refs_1_.refs_5_, bf16[128,2048]{1,0:T(8,128)(2,1)S(1)} %collective-permute-done.39.refs_1_.refs_2_.refs_6_, f32[512,2048]{1,0:T(8,128)} %down_back.1.refs_2_, ...), custom_call_target="tpu_custom_call" | custom-call | flops 8589934592 | bytes 16777216 | tf_op jit(solution)/shard_map/ffn_middle/pallas_call | solution.py:698
  238.5 14.0 %ffn_middle.3 = (bf16[3,512,2048]{2,1,0:T(8,128)(2,1)}, bf16[128,2048]{1,0:T(8,128)(2,1)S(1)}, f32[128,2048]{1,0:T(8,128)S(1)}) custom-call(bf16[128,2048]{1,0:T(8,128)(2,1)S(1)} %collective-permute-done.35.refs_0_.refs_3_.refs_7_, bf16[128,2048]{1,0:T(8,128)(2,1)S(1)} %collective-permute-done.34.refs_1_.refs_4_.refs_8_, ...), custom_call_target="tpu_custom_call", output_to_operand_aliasing={{0}: (4, {})} | custom-call | flops 8589934592 | bytes 16777216 | tf_op jit(solution)/shard_map/ffn_middle/pallas_call | solution.py:698
  252.6 9.9 %shard_map.144 = bf16[2,1024,2048]{2,1,0:T(8,128)(2,1)} custom-call(s32[2]{0:T(128)S(1)} %pad_add_fusion.refs_0_, bf16[128,2048]{1,0:T(8,128)(2,1)S(1)} %get-tuple-element.77.refs_0_.refs_1_.refs_5_, bf16[128,2048]{1,0:T(8,128)(2,1)S(1)} %collective-permute-done.39.refs_1_.refs_2_.refs_6_, ...), custom_call_target="tpu_custom_call" | custom-call | flops 4294967296 | bytes 8388608 | tf_op jit(solution)/shard_map/pallas_call | solution.py:760
  269.3 12.5 %collective-permute-done.73.refs_10_ = bf16[1,1024,2048]{2,1,0:T(8,128)(2,1)S(1)} collective-permute-done((bf16[1,1024,2048]{2,1,0:T(8,128)(2,1)}, bf16[1,1024,2048]{2,1,0:T(8,128)(2,1)S(1)}, u32[]{:S(2)}, u32[]{:S(2)}) %collective-permute-start.73) | collective-permute-done | bytes 4194336 | tf_op jit(solution)/shard_map/ppermute | solution.py:43
  288.2 10.2 %shard_map.147 = bf16[3,1024,2048]{2,1,0:T(8,128)(2,1)} custom-call(s32[2]{0:T(128)S(1)} %pad_add_fusion.refs_0_, bf16[128,2048]{1,0:T(8,128)(2,1)S(1)} %get-tuple-element.77.refs_0_.refs_1_.refs_5_, bf16[128,2048]{1,0:T(8,128)(2,1)S(1)} %collective-permute-done.39.refs_1_.refs_2_.refs_6_, ...), custom_call_target="tpu_custom_call", output_to_operand_aliasing={{}: (11, {})} | custom-call | flops 4294967296 | bytes 8388608 | tf_op jit(solution)/shard_map/pallas_call | solution.py:760
  300.5 13.0 %collective-permute-done.41 = bf16[128,2048]{1,0:T(8,128)(2,1)S(1)} collective-permute-done((bf16[128,2048]{1,0:T(8,128)(2,1)}, bf16[128,2048]{1,0:T(8,128)(2,1)S(1)}, u32[]{:S(2)}, u32[]{:S(2)}) %collective-permute-start.41) | collective-permute-done | bytes 524320 | tf_op jit(solution)/shard_map/ppermute | solution.py:43
  323.9 13.2 %collective-permute-done.42 = bf16[128,2048]{1,0:T(8,128)(2,1)S(1)} collective-permute-done((bf16[128,2048]{1,0:T(8,128)(2,1)S(1)}, bf16[128,2048]{1,0:T(8,128)(2,1)S(1)}, u32[]{:S(2)}, u32[]{:S(2)}) %collective-permute-start.42) | collective-permute-done | bytes 524320 | tf_op jit(solution)/shard_map/ppermute | solution.py:43
  344.2 20.3 %attend_back.1 = (bf16[128,2048]{1,0:T(8,128)(2,1)}, bf16[2,512,512]{2,1,0:T(8,128)(2,1)S(1)}, bf16[2,512,512]{2,1,0:T(8,128)(2,1)S(1)}) custom-call(bf16[128,2048]{1,0:T(8,128)(2,1)S(1)} %copy-done.21, bf16[128,2048]{1,0:T(8,128)(2,1)S(1)} %out_back.1.refs_1_, f32[128,2048]{1,0:T(8,128)S(1)} %copy-done.30, bf16[512,1024]{1,0:T(8,128)(2,1)} %copy-done.18, ...), custom_call_target="tpu_custom_call" | custom-call | flops 2684354560 | bytes 4194304 | tf_op jit(solution)/shard_map/attend_back/pallas_call | solution.py:595
  397.8 25.3 %collective-permute-done.56 = f32[1,2048]{1,0:T(1,128)S(1)} collective-permute-done((f32[1,2048]{1,0:T(1,128)S(1)}, f32[1,2048]{1,0:T(1,128)S(1)}, u32[]{:S(2)}, u32[]{:S(2)}) %collective-permute-start.56) | collective-permute-done | bytes 8224 | tf_op jit(solution)/shard_map/ppermute | solution.py:43
  428.9 25.7 %collective-permute-done.57 = f32[1,2048]{1,0:T(1,128)S(1)} collective-permute-done((f32[1,2048]{1,0:T(1,128)S(1)}, f32[1,2048]{1,0:T(1,128)S(1)}, u32[]{:S(2)}, u32[]{:S(2)}) %collective-permute-start.57) | collective-permute-done | bytes 8224 | tf_op jit(solution)/shard_map/ppermute | solution.py:43
  468.2 9.2 %one_back.1 = f32[128,2048]{1,0:T(8,128)} custom-call(bf16[128,2048]{1,0:T(8,128)(2,1)} %get-tuple-element.114.query_ref.refs_9_, bf16[512,1024]{1,0:T(8,128)(2,1)S(1)} %copy-done.4, bf16[2048,3072]{1,0:T(8,128)(2,1)} %get-tuple-element.105.w_ref, bf16[128,2048]{1,0:T(8,128)(2,1)S(1)} %bitcast.73, f32[1,2048]{1,0:T(1,128)S(1)} %bitcast.75, ...), custom_call_target="tpu_custom_call" | custom-call | flops 1610612736 | bytes 12582912 | tf_op jit(solution)/shard_map/one_back/pallas_call | solution.py:330
  477.4 12.4 %collective-permute-start.51 = (bf16[128,512]{1,0:T(8,128)(2,1)S(1)}, bf16[128,512]{1,0:T(8,128)(2,1)S(1)}, u32[]{:S(2)}, u32[]{:S(2)}) collective-permute-start(bf16[128,512]{1,0:T(8,128)(2,1)S(1)} %copy-done.58), channel_id=1, source_target_pairs={{0,2},{1,3},{2,0},{3,1},{4,6},{5,7},{6,4},{7,5},{8,10},{9,11},{10,... | collective-permute-start | bytes 393224 | tf_op jit(solution)/shard_map/ppermute | solution.py:43
  491.4 15.9 %collective-permute-start.65 = (bf16[128,2048]{1,0:T(8,128)(2,1)}, bf16[128,2048]{1,0:T(8,128)(2,1)S(1)}, u32[]{:S(2)}, u32[]{:S(2)}) collective-permute-start(bf16[128,2048]{1,0:T(8,128)(2,1)} %get-tuple-element.122.refs_1_.refs_5_), channel_id=1, source_target_pairs={{0,1},{1,0},{2,3},{3,2},{4,5},{5,4},{6,7},{7,6},{8,9},{9,8},{10,11... | collective-permute-start | bytes 1572872 | tf_op jit(solution)/shard_map/ppermute | solution.py:43
  524.0 10.4 %collective-permute-done.67.refs_7_ = bf16[128,2048]{1,0:T(8,128)(2,1)S(1)} collective-permute-done((bf16[128,2048]{1,0:T(8,128)(2,1)}, bf16[128,2048]{1,0:T(8,128)(2,1)S(1)}, u32[]{:S(2)}, u32[]{:S(2)}) %collective-permute-start.67) | collective-permute-done | bytes 524320 | tf_op jit(solution)/shard_map/ppermute | solution.py:43
  557.1 10.5 %collective-permute-done.61 = bf16[64,3200]{1,0:T(8,128)(2,1)S(1)} collective-permute-done((bf16[64,3200]{1,0:T(8,128)(2,1)S(1)}, bf16[64,3200]{1,0:T(8,128)(2,1)S(1)}, u32[]{:S(2)}, u32[]{:S(2)}) %collective-permute-start.61) | collective-permute-done | bytes 409632 | tf_op jit(solution)/shard_map/ppermute | solution.py:43
  569.1 12.3 %collective-permute-done.60 = bf16[64,3200]{1,0:T(8,128)(2,1)S(1)} collective-permute-done((bf16[64,3200]{1,0:T(8,128)(2,1)S(1)}, bf16[64,3200]{1,0:T(8,128)(2,1)S(1)}, u32[]{:S(2)}, u32[]{:S(2)}) %collective-permute-start.60) | collective-permute-done | bytes 409632 | tf_op jit(solution)/shard_map/ppermute | solution.py:43
  (360 shorter events, 269.3 us)
Async XLA Ops:
  7.2 60.6 %all-gather.5.cloned.1.call-start = ((), (), s32[]{:S(2)}) async-start(), calls=%async_computation.3 | async-start | bytes 1310720 | tf_op jit(solution)/shard_map/all_gather | solution.py:184
  39.5 146.6 %all-gather.7.cloned.1.call-start = ((), (), s32[]{:S(2)}) async-start(), calls=%async_computation.4 | async-start | bytes 7077888 | tf_op jit(solution)/shard_map/all_gather | solution.py:191
  70.0 517.0 %reduce-scatter.2.cloned.1.call-start = ((), (), s32[]{:S(2)}) async-start(), calls=%async_computation.2 | async-start | bytes 15728640 | tf_op jit(solution)/shard_map/reduce_scatter | solution.py:800
  382.3 74.5 %collective-permute-start.43 = (bf16[128,2048]{1,0:T(8,128)(2,1)}, bf16[128,2048]{1,0:T(8,128)(2,1)}, u32[]{:S(2)}, u32[]{:S(2)}) collective-permute-start(bf16[128,2048]{1,0:T(8,128)(2,1)} %get-tuple-element.95), channel_id=1, source_target_pairs={{0,1},{1,0},{2,3},{3,2},{4,5},{5,4},{6,7},{7,6},{8,9},{9,8},{10,11... | collective-permute-start | bytes 1572872 | tf_op jit(solution)/shard_map/ppermute | solution.py:43
  383.8 73.1 %collective-permute-start.54 = (bf16[128,2048]{1,0:T(8,128)(2,1)}, bf16[128,2048]{1,0:T(8,128)(2,1)}, u32[]{:S(2)}, u32[]{:S(2)}) collective-permute-start(bf16[128,2048]{1,0:T(8,128)(2,1)} %get-tuple-element.114.query_ref.refs_9_), channel_id=1, source_target_pairs={{0,3},{1,2},{2,1},{3,0},{4,7},{5,6},{6,5},{7,4},{8,11},{9,10},{10,... | collective-permute-start | bytes 1572872 | tf_op jit(solution)/shard_map/ppermute | solution.py:43
  391.5 122.7 %all-to-all-start = ((bf16[4,128,1024]{2,1,0:T(8,128)(2,1)}), bf16[4,128,1024]{2,1,0:T(8,128)(2,1)}, u32[]{:S(2)}, u32[]{:S(2)}) async-start(bf16[4,128,1024]{2,1,0:T(8,128)(2,1)} %bitcast.74), calls=%async_computation | async-start | bytes 2097152 | tf_op jit(solution)/shard_map/all_to_all | solution.py:1118
  396.1 27.0 %collective-permute-start.56 = (f32[1,2048]{1,0:T(1,128)S(1)}, f32[1,2048]{1,0:T(1,128)S(1)}, u32[]{:S(2)}, u32[]{:S(2)}) collective-permute-start(f32[1,2048]{1,0:T(1,128)S(1)} %bitcast.95), channel_id=1, source_target_pairs={{0,1},{1,0},{2,3},{3,2},{4,5},{5,4},{6,7},{7,6},{8,9},{9,8},{10,11... | collective-permute-start | bytes 24584 | tf_op jit(solution)/shard_map/ppermute | solution.py:43
  423.1 31.5 %collective-permute-start.57 = (f32[1,2048]{1,0:T(1,128)S(1)}, f32[1,2048]{1,0:T(1,128)S(1)}, u32[]{:S(2)}, u32[]{:S(2)}) collective-permute-start(f32[1,2048]{1,0:T(1,128)S(1)} %add.414), channel_id=1, source_target_pairs={{0,2},{1,3},{2,0},{3,1},{4,6},{5,7},{6,4},{7,5},{8,10},{9,11},{10,... | collective-permute-start | bytes 24584 | tf_op jit(solution)/shard_map/ppermute | solution.py:43
  426.9 50.4 %collective-permute-start.44 = (bf16[128,2048]{1,0:T(8,128)(2,1)}, bf16[128,2048]{1,0:T(8,128)(2,1)}, u32[]{:S(2)}, u32[]{:S(2)}) collective-permute-start(bf16[128,2048]{1,0:T(8,128)(2,1)} %copy-done.23), channel_id=1, source_target_pairs={{0,2},{1,3},{2,0},{3,1},{4,6},{5,7},{6,4},{7,5},{8,10},{9,11},{10,... | collective-permute-start | bytes 1572872 | tf_op jit(solution)/shard_map/ppermute | solution.py:43
  427.0 50.4 %collective-permute-start.45 = (bf16[128,2048]{1,0:T(8,128)(2,1)}, bf16[128,2048]{1,0:T(8,128)(2,1)}, u32[]{:S(2)}, u32[]{:S(2)}) collective-permute-start(bf16[128,2048]{1,0:T(8,128)(2,1)} %copy-done.22), channel_id=1, source_target_pairs={{0,3},{1,2},{2,1},{3,0},{4,7},{5,6},{6,5},{7,4},{8,11},{9,10},{10,... | collective-permute-start | bytes 1572872 | tf_op jit(solution)/shard_map/ppermute | solution.py:43
  454.6 35.3 %collective-permute-start.66 = (bf16[128,2048]{1,0:T(8,128)(2,1)}, bf16[128,2048]{1,0:T(8,128)(2,1)}, u32[]{:S(2)}, u32[]{:S(2)}) collective-permute-start(bf16[128,2048]{1,0:T(8,128)(2,1)} %get-tuple-element.122.refs_1_.refs_5_), channel_id=1, source_target_pairs={{0,3},{1,2},{2,1},{3,0},{4,7},{5,6},{6,5},{7,4},{8,11},{9,10},{10,... | collective-permute-start | bytes 1572872 | tf_op jit(solution)/shard_map/ppermute | solution.py:43
  456.9 34.5 %collective-permute-start.53 = (bf16[128,2048]{1,0:T(8,128)(2,1)}, bf16[128,2048]{1,0:T(8,128)(2,1)}, u32[]{:S(2)}, u32[]{:S(2)}) collective-permute-start(bf16[128,2048]{1,0:T(8,128)(2,1)} %get-tuple-element.114.query_ref.refs_9_), channel_id=1, source_target_pairs={{0,1},{1,0},{2,3},{3,2},{4,5},{5,4},{6,7},{7,6},{8,9},{9,8},{10,11... | collective-permute-start | bytes 1572872 | tf_op jit(solution)/shard_map/ppermute | solution.py:43
  456.9 50.4 %collective-permute-start.55 = (bf16[128,2048]{1,0:T(8,128)(2,1)}, bf16[128,2048]{1,0:T(8,128)(2,1)}, u32[]{:S(2)}, u32[]{:S(2)}) collective-permute-start(bf16[128,2048]{1,0:T(8,128)(2,1)} %collective-permute-done.54.refs_12_), channel_id=1, source_target_pairs={{0,1},{1,0},{2,3},{3,2},{4,5},{5,4},{6,7},{7,6},{8,9},{9,8},{10,11... | collective-permute-start | bytes 1572872 | tf_op jit(solution)/shard_map/ppermute | solution.py:43
  477.4 32.5 %collective-permute-start.50 = (bf16[128,512]{1,0:T(8,128)(2,1)S(1)}, bf16[128,512]{1,0:T(8,128)(2,1)S(1)}, u32[]{:S(2)}, u32[]{:S(2)}) collective-permute-start(bf16[128,512]{1,0:T(8,128)(2,1)S(1)} %copy-done.59), channel_id=1, source_target_pairs={{0,1},{1,0},{2,3},{3,2},{4,5},{5,4},{6,7},{7,6},{8,9},{9,8},{10,11... | collective-permute-start | bytes 393224 | tf_op jit(solution)/shard_map/ppermute | solution.py:43
  477.4 34.4 %collective-permute-start.51 = (bf16[128,512]{1,0:T(8,128)(2,1)S(1)}, bf16[128,512]{1,0:T(8,128)(2,1)S(1)}, u32[]{:S(2)}, u32[]{:S(2)}) collective-permute-start(bf16[128,512]{1,0:T(8,128)(2,1)S(1)} %copy-done.58), channel_id=1, source_target_pairs={{0,2},{1,3},{2,0},{3,1},{4,6},{5,7},{6,4},{7,5},{8,10},{9,11},{10,... | collective-permute-start | bytes 393224 | tf_op jit(solution)/shard_map/ppermute | solution.py:43
  491.4 31.7 %collective-permute-start.65 = (bf16[128,2048]{1,0:T(8,128)(2,1)}, bf16[128,2048]{1,0:T(8,128)(2,1)S(1)}, u32[]{:S(2)}, u32[]{:S(2)}) collective-permute-start(bf16[128,2048]{1,0:T(8,128)(2,1)} %get-tuple-element.122.refs_1_.refs_5_), channel_id=1, source_target_pairs={{0,1},{1,0},{2,3},{3,2},{4,5},{5,4},{6,7},{7,6},{8,9},{9,8},{10,11... | collective-permute-start | bytes 1572872 | tf_op jit(solution)/shard_map/ppermute | solution.py:43
  507.2 27.3 %collective-permute-start.67 = (bf16[128,2048]{1,0:T(8,128)(2,1)}, bf16[128,2048]{1,0:T(8,128)(2,1)S(1)}, u32[]{:S(2)}, u32[]{:S(2)}) collective-permute-start(bf16[128,2048]{1,0:T(8,128)(2,1)} %collective-permute-done.66.refs_8_), channel_id=1, source_target_pairs={{0,1},{1,0},{2,3},{3,2},{4,5},{5,4},{6,7},{7,6},{8,9},{9,8},{10,11... | collective-permute-start | bytes 1572872 | tf_op jit(solution)/shard_map/ppermute | solution.py:43
  509.9 26.9 %collective-permute-start.62 = (bf16[128,512]{1,0:T(8,128)(2,1)}, bf16[128,512]{1,0:T(8,128)(2,1)S(1)}, u32[]{:S(2)}, u32[]{:S(2)}) collective-permute-start(bf16[128,512]{1,0:T(8,128)(2,1)} %copy.85), channel_id=1, source_target_pairs={{0,1},{1,0},{2,3},{3,2},{4,5},{5,4},{6,7},{7,6},{8,9},{9,8},{10,11... | collective-permute-start | bytes 393224 | tf_op jit(solution)/shard_map/ppermute | solution.py:43
  512.0 26.9 %collective-permute-start.64 = (bf16[128,512]{1,0:T(8,128)(2,1)}, bf16[128,512]{1,0:T(8,128)(2,1)}, u32[]{:S(2)}, u32[]{:S(2)}) collective-permute-start(bf16[128,512]{1,0:T(8,128)(2,1)} %copy.87), channel_id=1, source_target_pairs={{0,3},{1,2},{2,1},{3,0},{4,7},{5,6},{6,5},{7,4},{8,11},{9,10},{10,... | collective-permute-start | bytes 393224 | tf_op jit(solution)/shard_map/ppermute | solution.py:43
  523.0 28.0 %collective-permute-start.58 = (bf16[4,64,3200]{2,1,0:T(8,128)(2,1)}, bf16[4,64,3200]{2,1,0:T(8,128)(2,1)}, u32[]{:S(2)}, u32[]{:S(2)}) collective-permute-start(bf16[4,64,3200]{2,1,0:T(8,128)(2,1)} %get-tuple-element.119), channel_id=1, source_target_pairs={{0,4},{4,0},{8,12},{12,8},{16,20},{20,16},{24,28},{28,24},{1,5},{5... | collective-permute-start | bytes 4915208 | tf_op jit(solution)/shard_map/ppermute | solution.py:43
  549.4 33.3 %collective-permute-start.69 = (bf16[64,2048]{1,0:T(8,128)(2,1)S(1)}, bf16[64,2048]{1,0:T(8,128)(2,1)S(1)}, u32[]{:S(2)}, u32[]{:S(2)}) collective-permute-start(bf16[64,2048]{1,0:T(8,128)(2,1)S(1)} %get-tuple-element.152), channel_id=1, source_target_pairs={{0,8},{4,12},{8,0},{12,4},{16,24},{20,28},{24,16},{28,20},{1,9},{5... | collective-permute-start | bytes 786440 | tf_op jit(solution)/shard_map/ppermute | solution.py:43
  550.2 32.5 %collective-permute-start.70 = (bf16[64,2048]{1,0:T(8,128)(2,1)S(1)}, bf16[64,2048]{1,0:T(8,128)(2,1)S(1)}, u32[]{:S(2)}, u32[]{:S(2)}) collective-permute-start(bf16[64,2048]{1,0:T(8,128)(2,1)S(1)} %get-tuple-element.151), channel_id=1, source_target_pairs={{0,16},{4,20},{8,24},{12,28},{16,0},{20,4},{24,8},{28,12},{1,17},{... | collective-permute-start | bytes 786440 | tf_op jit(solution)/shard_map/ppermute | solution.py:43
  554.6 26.8 %collective-permute-start.60 = (bf16[64,3200]{1,0:T(8,128)(2,1)S(1)}, bf16[64,3200]{1,0:T(8,128)(2,1)S(1)}, u32[]{:S(2)}, u32[]{:S(2)}) collective-permute-start(bf16[64,3200]{1,0:T(8,128)(2,1)S(1)} %get-tuple-element.149), channel_id=1, source_target_pairs={{0,16},{4,20},{8,24},{12,28},{16,0},{20,4},{24,8},{28,12},{1,17},{... | collective-permute-start | bytes 1228808 | tf_op jit(solution)/shard_map/ppermute | solution.py:43
  555.3 26.1 %collective-permute-start.59 = (bf16[64,3200]{1,0:T(8,128)(2,1)S(1)}, bf16[64,3200]{1,0:T(8,128)(2,1)S(1)}, u32[]{:S(2)}, u32[]{:S(2)}) collective-permute-start(bf16[64,3200]{1,0:T(8,128)(2,1)S(1)} %get-tuple-element.147), channel_id=1, source_target_pairs={{0,8},{4,12},{8,0},{12,4},{16,24},{20,28},{24,16},{28,20},{1,9},{5... | collective-permute-start | bytes 1228808 | tf_op jit(solution)/shard_map/ppermute | solution.py:43
  (116 other events, 2318.3 us)
Sparse Core Ops, SparseCore 0:
  39.6 28.1 all-gather.4
  70.3 62.8 all-gather.6
  298.6 125.7 reduce-scatter.1

commit v10 on v9

--- a/solution.py
+++ b/solution.py
@@ -90,12 +90,18 @@
     for away in (1, 3, 2):
         first = planes[away]
         along_x, along_y = swap(first, "ctx", 2), swap(first, "ctx", 4)
-        top, low = swap(along_y[:half], "ctx", 2), swap(along_x[half:], "ctx", 4)
-        parts = [(0, 0, first), (2, 0, along_x), (4, 0, along_y), (6, 0, top), (6, half, low)]
+        if away == 1:
+            corners = [(6, 0, swap(along_y, "ctx", 2))]
+        elif away == 3:
+            corners = [(6, 0, swap(along_x, "ctx", 4))]
+        else:
+            top, low = swap(along_y[:half], "ctx", 2), swap(along_x[half:], "ctx", 4)
+            corners = [(6, 0, jnp.concatenate([top, low], axis=0))]
+        parts = [(0, 0, first), (2, 0, along_x), (4, 0, along_y)] + corners
         for offset, start, part in parts:
             pieces.append((away, offset, start, part))
             pieces.append((away, offset + 1, start, swap(part, "ctx", 1)))
-    return pieces, (planes[2], (pieces[-4][3], pieces[-2][3]))
+    return pieces, (planes[2], pieces[-2][3])
 
 
 def pieces_kernel(places, rows_in, share, ids_ref, x_ref, own_ref, *refs):
@@ -787,8 +793,8 @@
         left, grad = (jnp.concatenate(rows, axis=0) for rows in (rows_in, rows_out))
         products = [tn(left, parts[0]), tn(left, parts[1]), tn(grad, parts[2])]
         products = jnp.stack(products, axis=1).astype(BF)
-        return lax.psum_scatter(products, "ctx", scatter_dimension=0, tiled=True)
-    calls = ((rows_out, 2, 1), (rows_in, 0, 2))
+        return lax.psum_scatter(products, "ctx", scatter_dimension=0, tiled=True), parts
+    calls = ((rows_out, 2, 1), (rows_in, 0, 1), (rows_in, 1, 1))
     got = []
     for rows_of, first, size in calls:
         sent = half_products(rows_of, parts, first, size, None, [])
@@ -797,13 +803,28 @@
     for (rows_of, first, size), part in zip(calls, got):
         kept = [half_products(rows_of, parts, first, size, part, kept)]
     groups = [list(range(core, count, 2)) for core in range(2)]
-    return lax.psum_scatter(
-        kept[0].transpose(1, 0, 2),
-        "ctx",
-        scatter_dimension=0,
-        tiled=True,
-        axis_index_groups=groups,
-    )
+    kept = kept[0].transpose(1, 0, 2)
+    rows = lax.psum_scatter(kept, "ctx", scatter_dimension=0, tiled=True, axis_index_groups=groups)
+    return rows, after(parts, kept)
+
+
+def widen_kernel(x_ref, y_ref):
+    y_ref[...] = x_ref[...].astype(F32)
+
+
+def widened(values):
+    values = values.transpose(1, 0, 2)
+    matrices, rows, hidden = values.shape
+    block = pl.BlockSpec((1, rows // 2, hidden), lambda k, i: (k, i, 0))
+    return pl.pallas_call(
+        widen_kernel,
+        grid=(matrices, 2),
+        out_shape=jax.ShapeDtypeStruct(values.shape, F32),
+        in_specs=[block],
+        out_specs=block,
+        compiler_params=pltpu.CompilerParams(vmem_limit_bytes=16 << 20),
+        name="widened",
+    )(values).transpose(1, 0, 2)
 
 
 def down_back_kernel(count, *refs):
@@ -1095,8 +1116,8 @@
         parts, partial = [out], partial + terms
     parts = parts[0]
     sum_grad = share_finish(sum_rows(partial, True))
-    ffn_weight_grad = ffn_gradient(rows_in, rows_out, parts)
-    ffn_weight_grad = ffn_weight_grad.astype(F32)
+    ffn_weight_grad, parts = ffn_gradient(rows_in, rows_out, parts)
+    ffn_weight_grad = widened(ffn_weight_grad)
     out_partial = list(down_forward(parts, ffn_parts, fsdp_count))
 
     unit_two = residual * scale_two

time: 601 us -> 594 us (0.988)
  starting transfers between devices: 119 us -> 86.8 us
  waiting for transfers between devices: 253 us -> 265 us
  Pallas kernels: 156 us -> 166 us
    ppermute x74 -> x70, starting transfers between devices: 115 us -> 81.6 us  [swap(): return lax.ppermute(value, axis, [(i, i ^ offset) for i in range(count)])]
    ppermute x74 -> x70, waiting for transfers between devices: 239 us -> 256 us  [swap(): return lax.ppermute(value, axis, [(i, i ^ offset) for i in range(count)])]
    pallas_call x4 -> x6, Pallas kernels: 32.8 us -> 38.3 us  [half_products(): pl.pallas_call(lambda *refs: products_kernel(count, kept, *refs), grid_sp...]
    unnamed x132 -> x121, local copies, waits for them, and re-layouts: 20.3 us -> 23.1 us
  transfers between devices with their start and end apart: 78 -> 74, of which waited for: 36 -> 41; matrix products, arithmetic and copies ran while one was open for 6% -> 6% of each run, Pallas kernels for 20% -> 23%
where the time goes in v10:
time: 594 us; the launch traced here: 587 us
  waiting for transfers between devices  265 us (45%)
  Pallas kernels  166 us (28%)
  starting transfers between devices  86.8 us (15%)
  local copies, waits for them, and re-layouts  37.9 us (6%)
  other arithmetic  16.8 us (3%)
  between operations  14.8 us (2%)
    ppermute x70, waiting for transfers between devices, swap(): return lax.ppermute(value, axis, [(i, i ^ offset) for i in range(count)])  256 us
    ppermute x70, starting transfers between devices, swap(): return lax.ppermute(value, axis, [(i, i ^ offset) for i in range(count)])  81.6 us
    pallas_call x6, Pallas kernels, half_products(): pl.pallas_call(lambda *refs: products_kernel(count, kept, *refs), grid_sp...  38.3 us
    pallas_call x2, Pallas kernels, ffn_middle(): pl.pallas_call(lambda *refs: ffn_kernel(len(blocks), len(earlier), *refs)...  28 us
    unnamed x121, local copies, waits for them, and re-layouts  23.1 us
    pallas_call x1, Pallas kernels, attend_back(): pl.pallas_call(lambda *refs: attend_back_kernel(KEY_CHUNK, *refs), grid=(...  20.3 us
    pallas_call x1, Pallas kernels, attend(): pl.pallas_call(lambda *refs: attend_kernel(KEY_CHUNK, *refs), grid=(KV,),...  13 us
    pallas_call x2, Pallas kernels, out_call(): pl.pallas_call(lambda *refs: out_kernel(back, *refs), out_shape=out_shape...  12.2 us
  transfers between devices with their start and end apart: 74, of which 41 were waited for; matrix products, arithmetic and copies ran while one was open for 6% of the time, Pallas kernels for 23%

profile of v10, /device:TPU:0, one launch (start us, length us, event | category | flops | bytes accessed | tf_op | source)
XLA Modules:
  0.0 587.1 jit_solution(12533672632107749213)
XLA Ops:
  22.9 8.1 %collective-permute-start.16 = (bf16[512,384]{1,0:T(8,128)(2,1)S(1)}, bf16[512,384]{1,0:T(8,128)(2,1)S(1)}, u32[]{:S(2)}, u32[]{:S(2)}) collective-permute-start(bf16[512,384]{1,0:T(8,128)(2,1)S(1)} %collective-permute-done.8.refs_11_), channel_id=1, source_target_pairs={{0,1},{1,0},{2,3},{3,2},{4,5},{5,4},{6,7},{7,6},{8,9},{9,8},{10,11... | collective-permute-start | bytes 1179656 | tf_op jit(solution)/shard_map/ppermute | solution.py:43
  59.0 8.9 %all-gather.5.cloned.1.call-done = bf16[2048,256]{1,0:T(8,128)(2,1)} async-done(((bf16[512,256]{1,0:T(8,128)(2,1)}), bf16[2048,256]{1,0:T(8,128)(2,1)}) %all-gather.5.cloned.1.call-update) | async-done | bytes 1048592 | tf_op jit(solution)/shard_map/all_gather | solution.py:190
  73.0 7.7 %collective-permute-done.refs_3_ = bf16[512,384]{1,0:T(8,128)(2,1)S(1)} collective-permute-done((bf16[512,384]{1,0:T(8,128)(2,1)}, bf16[512,384]{1,0:T(8,128)(2,1)S(1)}, u32[]{:S(2)}, u32[]{:S(2)}) %collective-permute-start) | collective-permute-done | bytes 393248 | tf_op jit(solution)/shard_map/ppermute | solution.py:43
  86.6 11.6 %collective-permute-done.4.refs_7_ = bf16[512,384]{1,0:T(8,128)(2,1)} collective-permute-done((bf16[512,384]{1,0:T(8,128)(2,1)S(1)}, bf16[512,384]{1,0:T(8,128)(2,1)}, u32[]{:S(2)}, u32[]{:S(2)}) %collective-permute-start.4) | collective-permute-done | bytes 393248 | tf_op jit(solution)/shard_map/ppermute | solution.py:43
  98.2 10.4 %collective-permute-done.12.refs_15_ = bf16[512,384]{1,0:T(8,128)(2,1)} collective-permute-done((bf16[512,384]{1,0:T(8,128)(2,1)}, bf16[512,384]{1,0:T(8,128)(2,1)}, u32[]{:S(2)}, u32[]{:S(2)}) %collective-permute-start.12) | collective-permute-done | bytes 393248 | tf_op jit(solution)/shard_map/ppermute | solution.py:43
  111.2 16.8 %collective-permute-done.14.refs_17_ = bf16[512,384]{1,0:T(8,128)(2,1)S(1)} collective-permute-done((bf16[512,384]{1,0:T(8,128)(2,1)S(1)}, bf16[512,384]{1,0:T(8,128)(2,1)S(1)}, u32[]{:S(2)}, u32[]{:S(2)}) %collective-permute-start.14) | collective-permute-done | bytes 393248 | tf_op jit(solution)/shard_map/ppermute | solution.py:43
  134.8 9.6 %pieces_forward.1 = (bf16[128,2048]{1,0:T(8,128)(2,1)S(1)}, bf16[128,1024]{1,0:T(8,128)(2,1)S(1)}, bf16[2048,3072]{1,0:T(8,128)(2,1)}) custom-call(s32[2]{0:T(128)S(1)} %pad_add_fusion.refs_0_, bf16[128,2048]{1,0:T(8,128)(2,1)S(1)} %fusion.2.refs_1_, bf16[512,3072]{1,0:T(8,128)(2,1)} %refs_2_.3, bf16[512,384]{1,0:T(8,128)(2,1)} %copy-done.37, ...), custom_call_target="tpu_custom_call" | custom-call | flops 1610612736 | bytes 25165824 | tf_op jit(solution)/shard_map/pieces_forward/pallas_call | solution.py:160
  163.7 13.0 %attend.1 = (bf16[128,2048]{1,0:T(8,128)(2,1)}, f32[128,2048]{1,0:T(8,128)S(1)}, f32[8,1,512]{2,1,0:T(1,128)S(1)}) custom-call(bf16[128,2048]{1,0:T(8,128)(2,1)S(1)} %get-tuple-element.72.refs_0_, bf16[512,1024]{1,0:T(8,128)(2,1)S(1)} %constant_dynamic-update-slice_fusion.3.refs_1_.refs_2_.refs_3_.refs_4_, ...), custom_call_target="tpu_custom_call" | custom-call | flops 1073741824 | bytes 2097152 | tf_op jit(solution)/shard_map/attend/pallas_call | solution.py:536
  177.7 9.4 %collective-permute-done.32.refs_3_.refs_4_.refs_8_ = bf16[128,2048]{1,0:T(8,128)(2,1)S(1)} collective-permute-done((bf16[128,2048]{1,0:T(8,128)(2,1)S(1)}, bf16[128,2048]{1,0:T(8,128)(2,1)S(1)}, u32[]{:S(2)}, u32[]{:S(2)}) %collective-permute-start.32) | collective-permute-done | bytes 524320 | tf_op jit(solution)/shard_map/ppermute | solution.py:43
  202.8 8.6 %down_back.1.refs_2_ = f32[512,2048]{1,0:T(8,128)} custom-call(bf16[128,2048]{1,0:T(8,128)(2,1)S(1)} %bitcast.69, bf16[128,2048]{1,0:T(8,128)(2,1)S(1)} %collective-permute-done.31.refs_1_.refs_2_.refs_6_, bf16[128,2048]{1,0:T(8,128)(2,1)S(1)} %collective-permute-done.33.refs_2_.refs_3_.refs_7_, ...), custom_call_target="tpu_custom_call" | custom-call | flops 4294967296 | bytes 8388608 | tf_op jit(solution)/shard_map/down_back/pallas_call | solution.py:841
  223.8 14.0 %ffn_middle.2 = (bf16[3,512,2048]{2,1,0:T(8,128)(2,1)}, f32[128,2048]{1,0:T(8,128)S(1)}, bf16[128,2048]{1,0:T(8,128)(2,1)S(1)}) custom-call(bf16[128,2048]{1,0:T(8,128)(2,1)S(1)} %get-tuple-element.78.refs_0_.refs_1_.refs_5_, bf16[128,2048]{1,0:T(8,128)(2,1)S(1)} %collective-permute-done.34.refs_1_.refs_2_.refs_6_, f32[512,2048]{1,0:T(8,128)} %down_back.1.refs_2_, ...), custom_call_target="tpu_custom_call" | custom-call | flops 8589934592 | bytes 16777216 | tf_op jit(solution)/shard_map/ffn_middle/pallas_call | solution.py:704
  239.5 14.0 %ffn_middle.3 = (bf16[3,512,2048]{2,1,0:T(8,128)(2,1)}, bf16[128,2048]{1,0:T(8,128)(2,1)S(1)}, f32[128,2048]{1,0:T(8,128)S(1)}) custom-call(bf16[128,2048]{1,0:T(8,128)(2,1)S(1)} %collective-permute-done.30.refs_0_.refs_3_.refs_7_, bf16[128,2048]{1,0:T(8,128)(2,1)S(1)} %collective-permute-done.29.refs_1_.refs_4_.refs_8_, ...), custom_call_target="tpu_custom_call", output_to_operand_aliasing={{0}: (4, {})} | custom-call | flops 8589934592 | bytes 16777216 | tf_op jit(solution)/shard_map/ffn_middle/pallas_call | solution.py:704
  294.5 13.0 %collective-permute-done.39 = bf16[128,2048]{1,0:T(8,128)(2,1)S(1)} collective-permute-done((bf16[128,2048]{1,0:T(8,128)(2,1)}, bf16[128,2048]{1,0:T(8,128)(2,1)S(1)}, u32[]{:S(2)}, u32[]{:S(2)}) %collective-permute-start.39) | collective-permute-done | bytes 524320 | tf_op jit(solution)/shard_map/ppermute | solution.py:43
  309.9 8.4 %collective-permute-done.38 = bf16[128,2048]{1,0:T(8,128)(2,1)S(1)} collective-permute-done((bf16[128,2048]{1,0:T(8,128)(2,1)S(1)}, bf16[128,2048]{1,0:T(8,128)(2,1)S(1)}, u32[]{:S(2)}, u32[]{:S(2)}) %collective-permute-start.38) | collective-permute-done | bytes 524320 | tf_op jit(solution)/shard_map/ppermute | solution.py:43
  318.3 13.2 %collective-permute-done.40 = bf16[128,2048]{1,0:T(8,128)(2,1)S(1)} collective-permute-done((bf16[128,2048]{1,0:T(8,128)(2,1)S(1)}, bf16[128,2048]{1,0:T(8,128)(2,1)S(1)}, u32[]{:S(2)}, u32[]{:S(2)}) %collective-permute-start.40) | collective-permute-done | bytes 524320 | tf_op jit(solution)/shard_map/ppermute | solution.py:43
  338.7 20.3 %attend_back.1 = (bf16[128,2048]{1,0:T(8,128)(2,1)}, bf16[2,512,512]{2,1,0:T(8,128)(2,1)S(1)}, bf16[2,512,512]{2,1,0:T(8,128)(2,1)S(1)}) custom-call(bf16[128,2048]{1,0:T(8,128)(2,1)S(1)} %copy-done.22, bf16[128,2048]{1,0:T(8,128)(2,1)S(1)} %out_back.1.refs_1_, f32[128,2048]{1,0:T(8,128)S(1)} %copy-done.31, bf16[512,1024]{1,0:T(8,128)(2,1)} %copy-done.19, ...), custom_call_target="tpu_custom_call" | custom-call | flops 2684354560 | bytes 4194304 | tf_op jit(solution)/shard_map/attend_back/pallas_call | solution.py:601
  365.7 8.7 %down_forward.1 = (f32[128,2048]{1,0:T(8,128)S(1)}, bf16[128,2048]{1,0:T(8,128)(2,1)S(1)}, bf16[128,2048]{1,0:T(8,128)(2,1)S(1)}, bf16[128,2048]{1,0:T(8,128)(2,1)}) custom-call(bf16[3,512,2048]{2,1,0:T(8,128)(2,1)} %get-tuple-element.89.refs_9_.x_ref, bf16[3,2048,2048]{2,1,0:T(8,128)(2,1)} %bitcast.83), custom_call_target="tpu_custom_call" | custom-call | flops 4294967296 | bytes 8388608 | tf_op jit(solution)/shard_map/down_forward/pallas_call | solution.py:871
  390.3 15.8 %collective-permute-done.54 = f32[1,2048]{1,0:T(1,128)S(1)} collective-permute-done((f32[1,2048]{1,0:T(1,128)S(1)}, f32[1,2048]{1,0:T(1,128)S(1)}, u32[]{:S(2)}, u32[]{:S(2)}) %collective-permute-start.54) | collective-permute-done | bytes 8224 | tf_op jit(solution)/shard_map/ppermute | solution.py:43
  411.6 31.6 %collective-permute-done.55 = f32[1,2048]{1,0:T(1,128)S(1)} collective-permute-done((f32[1,2048]{1,0:T(1,128)S(1)}, f32[1,2048]{1,0:T(1,128)S(1)}, u32[]{:S(2)}, u32[]{:S(2)}) %collective-permute-start.55) | collective-permute-done | bytes 8224 | tf_op jit(solution)/shard_map/ppermute | solution.py:43
  455.0 9.2 %one_back.1 = f32[128,2048]{1,0:T(8,128)} custom-call(bf16[128,2048]{1,0:T(8,128)(2,1)} %get-tuple-element.116.query_ref.refs_9_, bf16[512,1024]{1,0:T(8,128)(2,1)S(1)} %copy-done.4, bf16[2048,3072]{1,0:T(8,128)(2,1)} %get-tuple-element.107.w_ref, bf16[128,2048]{1,0:T(8,128)(2,1)S(1)} %bitcast.75, f32[1,2048]{1,0:T(1,128)S(1)} %bitcast.78, ...), custom_call_target="tpu_custom_call" | custom-call | flops 1610612736 | bytes 12582912 | tf_op jit(solution)/shard_map/one_back/pallas_call | solution.py:336
  477.8 15.9 %collective-permute-done.53.refs_11_ = bf16[128,2048]{1,0:T(8,128)(2,1)} collective-permute-done((bf16[128,2048]{1,0:T(8,128)(2,1)}, bf16[128,2048]{1,0:T(8,128)(2,1)}, u32[]{:S(2)}, u32[]{:S(2)}) %collective-permute-start.53) | collective-permute-done | bytes 524320 | tf_op jit(solution)/shard_map/ppermute | solution.py:43
  511.4 13.0 %collective-permute-done.65.refs_7_ = bf16[128,2048]{1,0:T(8,128)(2,1)S(1)} collective-permute-done((bf16[128,2048]{1,0:T(8,128)(2,1)}, bf16[128,2048]{1,0:T(8,128)(2,1)S(1)}, u32[]{:S(2)}, u32[]{:S(2)}) %collective-permute-start.65) | collective-permute-done | bytes 524320 | tf_op jit(solution)/shard_map/ppermute | solution.py:43
  545.5 10.2 %collective-permute-done.57 = bf16[64,3200]{1,0:T(8,128)(2,1)S(1)} collective-permute-done((bf16[64,3200]{1,0:T(8,128)(2,1)S(1)}, bf16[64,3200]{1,0:T(8,128)(2,1)S(1)}, u32[]{:S(2)}, u32[]{:S(2)}) %collective-permute-start.57) | collective-permute-done | bytes 409632 | tf_op jit(solution)/shard_map/ppermute | solution.py:43
  556.8 12.6 %collective-permute-done.58 = bf16[64,3200]{1,0:T(8,128)(2,1)S(1)} collective-permute-done((bf16[64,3200]{1,0:T(8,128)(2,1)S(1)}, bf16[64,3200]{1,0:T(8,128)(2,1)S(1)}, u32[]{:S(2)}, u32[]{:S(2)}) %collective-permute-start.58) | collective-permute-done | bytes 409632 | tf_op jit(solution)/shard_map/ppermute | solution.py:43
  (340 shorter events, 268.1 us)
Async XLA Ops:
  7.2 60.7 %all-gather.5.cloned.1.call-start = ((), (), s32[]{:S(2)}) async-start(), calls=%async_computation.3 | async-start | bytes 1310720 | tf_op jit(solution)/shard_map/all_gather | solution.py:190
  39.5 147.7 %all-gather.7.cloned.1.call-start = ((), (), s32[]{:S(2)}) async-start(), calls=%async_computation.4 | async-start | bytes 7077888 | tf_op jit(solution)/shard_map/all_gather | solution.py:197
  70.0 505.0 %reduce-scatter.2.cloned.1.call-start = ((), (), s32[]{:S(2)}) async-start(), calls=%async_computation.2 | async-start | bytes 15728640 | tf_op jit(solution)/shard_map/reduce_scatter | solution.py:807
  82.2 26.4 %collective-permute-start.12 = (bf16[512,384]{1,0:T(8,128)(2,1)}, bf16[512,384]{1,0:T(8,128)(2,1)}, u32[]{:S(2)}, u32[]{:S(2)}) collective-permute-start(bf16[512,384]{1,0:T(8,128)(2,1)} %copy-done.35), channel_id=1, source_target_pairs={{0,16},{4,20},{8,24},{12,28},{16,0},{20,4},{24,8},{28,12},{1,17},{... | collective-permute-start | bytes 1179656 | tf_op jit(solution)/shard_map/ppermute | solution.py:43
  359.1 84.6 %collective-permute-start.52 = (bf16[128,2048]{1,0:T(8,128)(2,1)}, bf16[128,2048]{1,0:T(8,128)(2,1)}, u32[]{:S(2)}, u32[]{:S(2)}) collective-permute-start(bf16[128,2048]{1,0:T(8,128)(2,1)} %get-tuple-element.116.query_ref.refs_9_), channel_id=1, source_target_pairs={{0,3},{1,2},{2,1},{3,0},{4,7},{5,6},{6,5},{7,4},{8,11},{9,10},{10,... | collective-permute-start | bytes 1572872 | tf_op jit(solution)/shard_map/ppermute | solution.py:43
  376.9 66.7 %collective-permute-start.43 = (bf16[128,2048]{1,0:T(8,128)(2,1)}, bf16[128,2048]{1,0:T(8,128)(2,1)}, u32[]{:S(2)}, u32[]{:S(2)}) collective-permute-start(bf16[128,2048]{1,0:T(8,128)(2,1)} %get-tuple-element.101), channel_id=1, source_target_pairs={{0,3},{1,2},{2,1},{3,0},{4,7},{5,6},{6,5},{7,4},{8,11},{9,10},{10,... | collective-permute-start | bytes 1572872 | tf_op jit(solution)/shard_map/ppermute | solution.py:43
  383.1 117.7 %all-to-all-start = ((bf16[4,128,1024]{2,1,0:T(8,128)(2,1)}), bf16[4,128,1024]{2,1,0:T(8,128)(2,1)}, u32[]{:S(2)}, u32[]{:S(2)}) async-start(bf16[4,128,1024]{2,1,0:T(8,128)(2,1)} %bitcast.76), calls=%async_computation | async-start | bytes 2097152 | tf_op jit(solution)/shard_map/all_to_all | solution.py:1139
  406.2 37.1 %collective-permute-start.55 = (f32[1,2048]{1,0:T(1,128)S(1)}, f32[1,2048]{1,0:T(1,128)S(1)}, u32[]{:S(2)}, u32[]{:S(2)}) collective-permute-start(f32[1,2048]{1,0:T(1,128)S(1)} %add.414), channel_id=1, source_target_pairs={{0,2},{1,3},{2,0},{3,1},{4,6},{5,7},{6,4},{7,5},{8,10},{9,11},{10,... | collective-permute-start | bytes 24584 | tf_op jit(solution)/shard_map/ppermute | solution.py:43
  410.2 55.7 %collective-permute-start.42 = (bf16[128,2048]{1,0:T(8,128)(2,1)}, bf16[128,2048]{1,0:T(8,128)(2,1)}, u32[]{:S(2)}, u32[]{:S(2)}) collective-permute-start(bf16[128,2048]{1,0:T(8,128)(2,1)} %copy-done.24), channel_id=1, source_target_pairs={{0,2},{1,3},{2,0},{3,1},{4,6},{5,7},{6,4},{7,5},{8,10},{9,11},{10,... | collective-permute-start | bytes 1572872 | tf_op jit(solution)/shard_map/ppermute | solution.py:43
  410.2 55.7 %collective-permute-start.41 = (bf16[128,2048]{1,0:T(8,128)(2,1)}, bf16[128,2048]{1,0:T(8,128)(2,1)}, u32[]{:S(2)}, u32[]{:S(2)}) collective-permute-start(bf16[128,2048]{1,0:T(8,128)(2,1)} %copy-done.23), channel_id=1, source_target_pairs={{0,1},{1,0},{2,3},{3,2},{4,5},{5,4},{6,7},{7,6},{8,9},{9,8},{10,11... | collective-permute-start | bytes 1572872 | tf_op jit(solution)/shard_map/ppermute | solution.py:43
  443.6 33.5 %collective-permute-start.51 = (bf16[128,2048]{1,0:T(8,128)(2,1)}, bf16[128,2048]{1,0:T(8,128)(2,1)}, u32[]{:S(2)}, u32[]{:S(2)}) collective-permute-start(bf16[128,2048]{1,0:T(8,128)(2,1)} %get-tuple-element.116.query_ref.refs_9_), channel_id=1, source_target_pairs={{0,1},{1,0},{2,3},{3,2},{4,5},{5,4},{6,7},{7,6},{8,9},{9,8},{10,11... | collective-permute-start | bytes 1572872 | tf_op jit(solution)/shard_map/ppermute | solution.py:43
  443.7 50.0 %collective-permute-start.53 = (bf16[128,2048]{1,0:T(8,128)(2,1)}, bf16[128,2048]{1,0:T(8,128)(2,1)}, u32[]{:S(2)}, u32[]{:S(2)}) collective-permute-start(bf16[128,2048]{1,0:T(8,128)(2,1)} %collective-permute-done.52.refs_12_), channel_id=1, source_target_pairs={{0,1},{1,0},{2,3},{3,2},{4,5},{5,4},{6,7},{7,6},{8,9},{9,8},{10,11... | collective-permute-start | bytes 1572872 | tf_op jit(solution)/shard_map/ppermute | solution.py:43
  465.9 30.5 %collective-permute-start.48 = (bf16[128,512]{1,0:T(8,128)(2,1)S(1)}, bf16[128,512]{1,0:T(8,128)(2,1)S(1)}, u32[]{:S(2)}, u32[]{:S(2)}) collective-permute-start(bf16[128,512]{1,0:T(8,128)(2,1)S(1)} %copy-done.54), channel_id=1, source_target_pairs={{0,1},{1,0},{2,3},{3,2},{4,5},{5,4},{6,7},{7,6},{8,9},{9,8},{10,11... | collective-permute-start | bytes 393224 | tf_op jit(solution)/shard_map/ppermute | solution.py:43
  465.9 32.4 %collective-permute-start.49 = (bf16[128,512]{1,0:T(8,128)(2,1)S(1)}, bf16[128,512]{1,0:T(8,128)(2,1)S(1)}, u32[]{:S(2)}, u32[]{:S(2)}) collective-permute-start(bf16[128,512]{1,0:T(8,128)(2,1)S(1)} %copy-done.53), channel_id=1, source_target_pairs={{0,2},{1,3},{2,0},{3,1},{4,6},{5,7},{6,4},{7,5},{8,10},{9,11},{10,... | collective-permute-start | bytes 393224 | tf_op jit(solution)/shard_map/ppermute | solution.py:43
  468.2 30.1 %collective-permute-start.50 = (bf16[128,512]{1,0:T(8,128)(2,1)S(1)}, bf16[128,512]{1,0:T(8,128)(2,1)S(1)}, u32[]{:S(2)}, u32[]{:S(2)}) collective-permute-start(bf16[128,512]{1,0:T(8,128)(2,1)S(1)} %copy-done.52), channel_id=1, source_target_pairs={{0,3},{1,2},{2,1},{3,0},{4,7},{5,6},{6,5},{7,4},{8,11},{9,10},{10,... | collective-permute-start | bytes 393224 | tf_op jit(solution)/shard_map/ppermute | solution.py:43
  477.2 33.2 %collective-permute-start.63 = (bf16[128,2048]{1,0:T(8,128)(2,1)}, bf16[128,2048]{1,0:T(8,128)(2,1)S(1)}, u32[]{:S(2)}, u32[]{:S(2)}) collective-permute-start(bf16[128,2048]{1,0:T(8,128)(2,1)} %get-tuple-element.124.refs_1_.refs_5_), channel_id=1, source_target_pairs={{0,1},{1,0},{2,3},{3,2},{4,5},{5,4},{6,7},{7,6},{8,9},{9,8},{10,11... | collective-permute-start | bytes 1572872 | tf_op jit(solution)/shard_map/ppermute | solution.py:43
  493.7 30.8 %collective-permute-start.65 = (bf16[128,2048]{1,0:T(8,128)(2,1)}, bf16[128,2048]{1,0:T(8,128)(2,1)S(1)}, u32[]{:S(2)}, u32[]{:S(2)}) collective-permute-start(bf16[128,2048]{1,0:T(8,128)(2,1)} %collective-permute-done.64.refs_8_), channel_id=1, source_target_pairs={{0,1},{1,0},{2,3},{3,2},{4,5},{5,4},{6,7},{7,6},{8,9},{9,8},{10,11... | collective-permute-start | bytes 1572872 | tf_op jit(solution)/shard_map/ppermute | solution.py:43
  496.4 30.8 %collective-permute-start.60 = (bf16[128,512]{1,0:T(8,128)(2,1)}, bf16[128,512]{1,0:T(8,128)(2,1)S(1)}, u32[]{:S(2)}, u32[]{:S(2)}) collective-permute-start(bf16[128,512]{1,0:T(8,128)(2,1)} %copy.86), channel_id=1, source_target_pairs={{0,1},{1,0},{2,3},{3,2},{4,5},{5,4},{6,7},{7,6},{8,9},{9,8},{10,11... | collective-permute-start | bytes 393224 | tf_op jit(solution)/shard_map/ppermute | solution.py:43
  498.3 28.9 %collective-permute-start.61 = (bf16[128,512]{1,0:T(8,128)(2,1)}, bf16[128,512]{1,0:T(8,128)(2,1)}, u32[]{:S(2)}, u32[]{:S(2)}) collective-permute-start(bf16[128,512]{1,0:T(8,128)(2,1)} %copy.87), channel_id=1, source_target_pairs={{0,2},{1,3},{2,0},{3,1},{4,6},{5,7},{6,4},{7,5},{8,10},{9,11},{10,... | collective-permute-start | bytes 393224 | tf_op jit(solution)/shard_map/ppermute | solution.py:43
  498.3 28.9 %collective-permute-start.62 = (bf16[128,512]{1,0:T(8,128)(2,1)}, bf16[128,512]{1,0:T(8,128)(2,1)}, u32[]{:S(2)}, u32[]{:S(2)}) collective-permute-start(bf16[128,512]{1,0:T(8,128)(2,1)} %copy.88), channel_id=1, source_target_pairs={{0,3},{1,2},{2,1},{3,0},{4,7},{5,6},{6,5},{7,4},{8,11},{9,10},{10,... | collective-permute-start | bytes 393224 | tf_op jit(solution)/shard_map/ppermute | solution.py:43
  510.4 29.0 %collective-permute-start.56 = (bf16[4,64,3200]{2,1,0:T(8,128)(2,1)}, bf16[4,64,3200]{2,1,0:T(8,128)(2,1)}, u32[]{:S(2)}, u32[]{:S(2)}) collective-permute-start(bf16[4,64,3200]{2,1,0:T(8,128)(2,1)} %get-tuple-element.121), channel_id=1, source_target_pairs={{0,4},{4,0},{8,12},{12,8},{16,20},{20,16},{24,28},{28,24},{1,5},{5... | collective-permute-start | bytes 4915208 | tf_op jit(solution)/shard_map/ppermute | solution.py:43
  537.7 33.0 %collective-permute-start.67 = (bf16[64,2048]{1,0:T(8,128)(2,1)S(1)}, bf16[64,2048]{1,0:T(8,128)(2,1)S(1)}, u32[]{:S(2)}, u32[]{:S(2)}) collective-permute-start(bf16[64,2048]{1,0:T(8,128)(2,1)S(1)} %get-tuple-element.154), channel_id=1, source_target_pairs={{0,8},{4,12},{8,0},{12,4},{16,24},{20,28},{24,16},{28,20},{1,9},{5... | collective-permute-start | bytes 786440 | tf_op jit(solution)/shard_map/ppermute | solution.py:43
  537.9 32.8 %collective-permute-start.68 = (bf16[64,2048]{1,0:T(8,128)(2,1)S(1)}, bf16[64,2048]{1,0:T(8,128)(2,1)S(1)}, u32[]{:S(2)}, u32[]{:S(2)}) collective-permute-start(bf16[64,2048]{1,0:T(8,128)(2,1)S(1)} %get-tuple-element.153), channel_id=1, source_target_pairs={{0,16},{4,20},{8,24},{12,28},{16,0},{20,4},{24,8},{28,12},{1,17},{... | collective-permute-start | bytes 786440 | tf_op jit(solution)/shard_map/ppermute | solution.py:43
  541.6 27.8 %collective-permute-start.58 = (bf16[64,3200]{1,0:T(8,128)(2,1)S(1)}, bf16[64,3200]{1,0:T(8,128)(2,1)S(1)}, u32[]{:S(2)}, u32[]{:S(2)}) collective-permute-start(bf16[64,3200]{1,0:T(8,128)(2,1)S(1)} %get-tuple-element.151), channel_id=1, source_target_pairs={{0,16},{4,20},{8,24},{12,28},{16,0},{20,4},{24,8},{28,12},{1,17},{... | collective-permute-start | bytes 1228808 | tf_op jit(solution)/shard_map/ppermute | solution.py:43
  (106 other events, 2405.0 us)
Sparse Core Ops, SparseCore 0:
  39.6 28.1 all-gather.4
  70.3 62.8 all-gather.6
  292.5 125.1 reduce-scatter.1

commit v11 on v10

--- a/solution.py
+++ b/solution.py
@@ -794,7 +794,7 @@
         products = [tn(left, parts[0]), tn(left, parts[1]), tn(grad, parts[2])]
         products = jnp.stack(products, axis=1).astype(BF)
         return lax.psum_scatter(products, "ctx", scatter_dimension=0, tiled=True), parts
-    calls = ((rows_out, 2, 1), (rows_in, 0, 1), (rows_in, 1, 1))
+    calls = ((rows_out, 2, 1), (rows_in, 0, 2))
     got = []
     for rows_of, first, size in calls:
         sent = half_products(rows_of, parts, first, size, None, [])
@@ -1127,7 +1127,7 @@
         scaled_two - unit_two * jnp.mean(scaled_two * unit_two, axis=-1, keepdims=True)
     )
     residual_bf = residual_grad.astype(BF)
-    out_sum = sum_rows([after(part, residual_bf) for part in out_partial], False)
+    out_sum = sum_rows([after(part, residual_bf) for part in out_partial], True)
     (ffn_term,) = own_features([ffn_gain_term])
     attn_grad = out_back(residual_bf, out_weight, out_blocks)
     query_part, kept, sent = attend_back(
@@ -1144,7 +1144,7 @@
     output = (residual + share_finish(after(out_sum, input_grad))).astype(BF)
     qkv_sums = share_start([own_one, own_one], [after(query_planes, output), all_pair], [ffn_term])
     qkv_sums = share_finish(qkv_sums)
-    out_weight_grad = share_finish(after(out_sums, qkv_sums))
+    out_weight_grad = share_finish(out_sums)
     qkv_grad = qkv_sums[:, : qkv_weight.shape[1]]
     features = own_rows_of(attn_gain, qkv_grad.shape[0])
     gain_grad = jnp.sum(own_rows_of(qkv_full, qkv_grad.shape[0]).astype(F32) * qkv_grad, axis=1)

time: 594 us -> 592 us (level)
  starting transfers between devices: 86.8 us -> 97.8 us
  Pallas kernels: 166 us -> 160 us
    ppermute x70 -> x69, starting transfers between devices: 81.6 us -> 93.2 us  [swap(): return lax.ppermute(value, axis, [(i, i ^ offset) for i in range(count)])]
    pallas_call x6 -> x4, Pallas kernels: 38.3 us -> 32.8 us  [half_products(): pl.pallas_call(lambda *refs: products_kernel(count, kept, *refs), grid_sp...]
    unnamed x121 -> x115, local copies, waits for them, and re-layouts: 23.1 us -> 21.6 us
    ppermute x70 -> x69, waiting for transfers between devices: 256 us -> 257 us  [swap(): return lax.ppermute(value, axis, [(i, i ^ offset) for i in range(count)])]
  transfers between devices with their start and end apart: 74 -> 73, of which waited for: 41 -> 47; matrix products, arithmetic and copies ran while one was open for 6% -> 6% of each run, Pallas kernels for 23% -> 21%
where the time goes in v11:
time: 592 us; the launch traced here: 590 us
  waiting for transfers between devices  266 us (45%)
  Pallas kernels  160 us (27%)
  starting transfers between devices  97.8 us (17%)
  local copies, waits for them, and re-layouts  34.9 us (6%)
  other arithmetic  17.8 us (3%)
  between operations  14.5 us (2%)
    ppermute x69, waiting for transfers between devices, swap(): return lax.ppermute(value, axis, [(i, i ^ offset) for i in range(count)])  257 us
    ppermute x69, starting transfers between devices, swap(): return lax.ppermute(value, axis, [(i, i ^ offset) for i in range(count)])  93.2 us
    pallas_call x4, Pallas kernels, half_products(): pl.pallas_call(lambda *refs: products_kernel(count, kept, *refs), grid_sp...  32.8 us
    pallas_call x2, Pallas kernels, ffn_middle(): pl.pallas_call(lambda *refs: ffn_kernel(len(blocks), len(earlier), *refs)...  28.1 us
    unnamed x115, local copies, waits for them, and re-layouts  21.6 us
    pallas_call x1, Pallas kernels, attend_back(): pl.pallas_call(lambda *refs: attend_back_kernel(KEY_CHUNK, *refs), grid=(...  20.3 us
    pallas_call x1, Pallas kernels, attend(): pl.pallas_call(lambda *refs: attend_kernel(KEY_CHUNK, *refs), grid=(KV,),...  12.8 us
    pallas_call x2, Pallas kernels, out_call(): pl.pallas_call(lambda *refs: out_kernel(back, *refs), out_shape=out_shape...  12.1 us
  transfers between devices with their start and end apart: 73, of which 47 were waited for; matrix products, arithmetic and copies ran while one was open for 6% of the time, Pallas kernels for 21%

profile of v11, /device:TPU:0, one launch (start us, length us, event | category | flops | bytes accessed | tf_op | source)
XLA Modules:
  0.0 590.5 jit_solution(11470084638416003459)
XLA Ops:
  59.0 8.9 %all-gather.5.cloned.1.call-done = bf16[2048,256]{1,0:T(8,128)(2,1)} async-done(((bf16[512,256]{1,0:T(8,128)(2,1)}), bf16[2048,256]{1,0:T(8,128)(2,1)}) %all-gather.5.cloned.1.call-update) | async-done | bytes 1048592 | tf_op jit(solution)/shard_map/all_gather | solution.py:190
  86.7 11.4 %collective-permute-done.4.refs_7_ = bf16[512,384]{1,0:T(8,128)(2,1)} collective-permute-done((bf16[512,384]{1,0:T(8,128)(2,1)S(1)}, bf16[512,384]{1,0:T(8,128)(2,1)}, u32[]{:S(2)}, u32[]{:S(2)}) %collective-permute-start.4) | collective-permute-done | bytes 393248 | tf_op jit(solution)/shard_map/ppermute | solution.py:43
  98.1 10.6 %collective-permute-done.12.refs_15_ = bf16[512,384]{1,0:T(8,128)(2,1)} collective-permute-done((bf16[512,384]{1,0:T(8,128)(2,1)}, bf16[512,384]{1,0:T(8,128)(2,1)}, u32[]{:S(2)}, u32[]{:S(2)}) %collective-permute-start.12) | collective-permute-done | bytes 393248 | tf_op jit(solution)/shard_map/ppermute | solution.py:43
  111.3 17.0 %collective-permute-done.14.refs_17_ = bf16[512,384]{1,0:T(8,128)(2,1)S(1)} collective-permute-done((bf16[512,384]{1,0:T(8,128)(2,1)}, bf16[512,384]{1,0:T(8,128)(2,1)S(1)}, u32[]{:S(2)}, u32[]{:S(2)}) %collective-permute-start.14) | collective-permute-done | bytes 393248 | tf_op jit(solution)/shard_map/ppermute | solution.py:43
  135.2 9.7 %pieces_forward.1 = (bf16[128,2048]{1,0:T(8,128)(2,1)S(1)}, bf16[128,1024]{1,0:T(8,128)(2,1)S(1)}, bf16[2048,3072]{1,0:T(8,128)(2,1)}) custom-call(s32[2]{0:T(128)S(1)} %pad_add_fusion.refs_0_, bf16[128,2048]{1,0:T(8,128)(2,1)S(1)} %fusion.2.refs_1_, bf16[512,3072]{1,0:T(8,128)(2,1)} %refs_2_.3, bf16[512,384]{1,0:T(8,128)(2,1)} %copy-done.37, ...), custom_call_target="tpu_custom_call" | custom-call | flops 1610612736 | bytes 25165824 | tf_op jit(solution)/shard_map/pieces_forward/pallas_call | solution.py:160
  164.1 12.8 %attend.1 = (bf16[128,2048]{1,0:T(8,128)(2,1)}, f32[128,2048]{1,0:T(8,128)S(1)}, f32[8,1,512]{2,1,0:T(1,128)S(1)}) custom-call(bf16[128,2048]{1,0:T(8,128)(2,1)S(1)} %get-tuple-element.66.refs_0_, bf16[512,1024]{1,0:T(8,128)(2,1)S(1)} %constant_dynamic-update-slice_fusion.3.refs_1_.refs_2_.refs_3_.refs_4_, ...), custom_call_target="tpu_custom_call" | custom-call | flops 1073741824 | bytes 2097152 | tf_op jit(solution)/shard_map/attend/pallas_call | solution.py:536
  177.8 9.7 %collective-permute-done.32.refs_3_.refs_4_.refs_8_ = bf16[128,2048]{1,0:T(8,128)(2,1)S(1)} collective-permute-done((bf16[128,2048]{1,0:T(8,128)(2,1)S(1)}, bf16[128,2048]{1,0:T(8,128)(2,1)S(1)}, u32[]{:S(2)}, u32[]{:S(2)}) %collective-permute-start.32) | collective-permute-done | bytes 524320 | tf_op jit(solution)/shard_map/ppermute | solution.py:43
  203.1 8.6 %down_back.1.refs_2_ = f32[512,2048]{1,0:T(8,128)} custom-call(bf16[128,2048]{1,0:T(8,128)(2,1)S(1)} %bitcast.71, bf16[128,2048]{1,0:T(8,128)(2,1)S(1)} %collective-permute-done.31.refs_1_.refs_2_.refs_6_, bf16[128,2048]{1,0:T(8,128)(2,1)S(1)} %collective-permute-done.33.refs_2_.refs_3_.refs_7_, ...), custom_call_target="tpu_custom_call" | custom-call | flops 4294967296 | bytes 8388608 | tf_op jit(solution)/shard_map/down_back/pallas_call | solution.py:841
  224.1 14.0 %ffn_middle.2 = (bf16[3,512,2048]{2,1,0:T(8,128)(2,1)}, f32[128,2048]{1,0:T(8,128)S(1)}, bf16[128,2048]{1,0:T(8,128)(2,1)S(1)}) custom-call(bf16[128,2048]{1,0:T(8,128)(2,1)S(1)} %get-tuple-element.72.refs_0_.refs_1_.refs_5_, bf16[128,2048]{1,0:T(8,128)(2,1)S(1)} %collective-permute-done.34.refs_1_.refs_2_.refs_6_, f32[512,2048]{1,0:T(8,128)} %down_back.1.refs_2_, ...), custom_call_target="tpu_custom_call" | custom-call | flops 8589934592 | bytes 16777216 | tf_op jit(solution)/shard_map/ffn_middle/pallas_call | solution.py:704
  239.9 14.0 %ffn_middle.3 = (bf16[3,512,2048]{2,1,0:T(8,128)(2,1)}, bf16[128,2048]{1,0:T(8,128)(2,1)S(1)}, f32[128,2048]{1,0:T(8,128)S(1)}) custom-call(bf16[128,2048]{1,0:T(8,128)(2,1)S(1)} %collective-permute-done.30.refs_0_.refs_3_.refs_7_, bf16[128,2048]{1,0:T(8,128)(2,1)S(1)} %collective-permute-done.29.refs_1_.refs_4_.refs_8_, ...), custom_call_target="tpu_custom_call", output_to_operand_aliasing={{0}: (4, {})} | custom-call | flops 8589934592 | bytes 16777216 | tf_op jit(solution)/shard_map/ffn_middle/pallas_call | solution.py:704
  253.9 9.9 %shard_map.144 = bf16[2,1024,2048]{2,1,0:T(8,128)(2,1)} custom-call(s32[2]{0:T(128)S(1)} %pad_add_fusion.refs_0_, bf16[128,2048]{1,0:T(8,128)(2,1)S(1)} %get-tuple-element.72.refs_0_.refs_1_.refs_5_, bf16[128,2048]{1,0:T(8,128)(2,1)S(1)} %collective-permute-done.34.refs_1_.refs_2_.refs_6_, ...), custom_call_target="tpu_custom_call" | custom-call | flops 4294967296 | bytes 8388608 | tf_op jit(solution)/shard_map/pallas_call | solution.py:766
  270.7 12.5 %collective-permute-done.36.refs_10_ = bf16[1,1024,2048]{2,1,0:T(8,128)(2,1)S(1)} collective-permute-done((bf16[1,1024,2048]{2,1,0:T(8,128)(2,1)}, bf16[1,1024,2048]{2,1,0:T(8,128)(2,1)S(1)}, u32[]{:S(2)}, u32[]{:S(2)}) %collective-permute-start.36) | collective-permute-done | bytes 4194336 | tf_op jit(solution)/shard_map/ppermute | solution.py:43
  289.6 10.2 %shard_map.147 = bf16[3,1024,2048]{2,1,0:T(8,128)(2,1)} custom-call(s32[2]{0:T(128)S(1)} %pad_add_fusion.refs_0_, bf16[128,2048]{1,0:T(8,128)(2,1)S(1)} %get-tuple-element.72.refs_0_.refs_1_.refs_5_, bf16[128,2048]{1,0:T(8,128)(2,1)S(1)} %collective-permute-done.34.refs_1_.refs_2_.refs_6_, ...), custom_call_target="tpu_custom_call", output_to_operand_aliasing={{}: (11, {})} | custom-call | flops 4294967296 | bytes 8388608 | tf_op jit(solution)/shard_map/pallas_call | solution.py:766
  301.9 13.0 %collective-permute-done.38 = bf16[128,2048]{1,0:T(8,128)(2,1)S(1)} collective-permute-done((bf16[128,2048]{1,0:T(8,128)(2,1)}, bf16[128,2048]{1,0:T(8,128)(2,1)S(1)}, u32[]{:S(2)}, u32[]{:S(2)}) %collective-permute-start.38) | collective-permute-done | bytes 524320 | tf_op jit(solution)/shard_map/ppermute | solution.py:43
  325.3 13.3 %collective-permute-done.39 = bf16[128,2048]{1,0:T(8,128)(2,1)S(1)} collective-permute-done((bf16[128,2048]{1,0:T(8,128)(2,1)S(1)}, bf16[128,2048]{1,0:T(8,128)(2,1)S(1)}, u32[]{:S(2)}, u32[]{:S(2)}) %collective-permute-start.39) | collective-permute-done | bytes 524320 | tf_op jit(solution)/shard_map/ppermute | solution.py:43
  345.7 20.3 %attend_back.1 = (bf16[128,2048]{1,0:T(8,128)(2,1)}, bf16[2,512,512]{2,1,0:T(8,128)(2,1)S(1)}, bf16[2,512,512]{2,1,0:T(8,128)(2,1)S(1)}) custom-call(bf16[128,2048]{1,0:T(8,128)(2,1)S(1)} %copy-done.22, bf16[128,2048]{1,0:T(8,128)(2,1)S(1)} %out_back.1.refs_1_, f32[128,2048]{1,0:T(8,128)S(1)} %copy-done.31, bf16[512,1024]{1,0:T(8,128)(2,1)} %copy-done.19, ...), custom_call_target="tpu_custom_call" | custom-call | flops 2684354560 | bytes 4194304 | tf_op jit(solution)/shard_map/attend_back/pallas_call | solution.py:601
  369.0 8.5 %down_forward.1 = (f32[128,2048]{1,0:T(8,128)S(1)}, bf16[128,2048]{1,0:T(8,128)(2,1)}, bf16[128,2048]{1,0:T(8,128)(2,1)S(1)}, bf16[128,2048]{1,0:T(8,128)(2,1)S(1)}) custom-call(bf16[3,512,2048]{2,1,0:T(8,128)(2,1)} %get-tuple-element.83.refs_9_.x_ref, bf16[3,2048,2048]{2,1,0:T(8,128)(2,1)} %bitcast.85), custom_call_target="tpu_custom_call" | custom-call | flops 4294967296 | bytes 8388608 | tf_op jit(solution)/shard_map/down_forward/pallas_call | solution.py:871
  412.8 12.5 %collective-permute-done.53 = f32[1,2048]{1,0:T(1,128)S(1)} collective-permute-done((f32[1,2048]{1,0:T(1,128)S(1)}, f32[1,2048]{1,0:T(1,128)S(1)}, u32[]{:S(2)}, u32[]{:S(2)}) %collective-permute-start.53) | collective-permute-done | bytes 8224 | tf_op jit(solution)/shard_map/ppermute | solution.py:43
  447.7 9.2 %one_back.1 = f32[128,2048]{1,0:T(8,128)} custom-call(bf16[128,2048]{1,0:T(8,128)(2,1)} %get-tuple-element.109.query_ref.refs_9_, bf16[512,1024]{1,0:T(8,128)(2,1)S(1)} %copy-done.4, bf16[2048,3072]{1,0:T(8,128)(2,1)} %get-tuple-element.101.w_ref, bf16[128,2048]{1,0:T(8,128)(2,1)S(1)} %bitcast.77, f32[1,2048]{1,0:T(1,128)S(1)} %bitcast.80, ...), custom_call_target="tpu_custom_call" | custom-call | flops 1610612736 | bytes 12582912 | tf_op jit(solution)/shard_map/one_back/pallas_call | solution.py:336
  456.8 12.2 %collective-permute-done.40 = bf16[128,2048]{1,0:T(8,128)(2,1)} collective-permute-done((bf16[128,2048]{1,0:T(8,128)(2,1)}, bf16[128,2048]{1,0:T(8,128)(2,1)}, u32[]{:S(2)}, u32[]{:S(2)}) %collective-permute-start.40) | collective-permute-done | bytes 524320 | tf_op jit(solution)/shard_map/ppermute | solution.py:43
  473.4 8.6 %collective-permute-done.50.refs_10_ = bf16[128,2048]{1,0:T(8,128)(2,1)} collective-permute-done((bf16[128,2048]{1,0:T(8,128)(2,1)}, bf16[128,2048]{1,0:T(8,128)(2,1)}, u32[]{:S(2)}, u32[]{:S(2)}) %collective-permute-start.50) | collective-permute-done | bytes 524320 | tf_op jit(solution)/shard_map/ppermute | solution.py:43
  483.0 12.7 %collective-permute-done.52.refs_11_ = bf16[128,2048]{1,0:T(8,128)(2,1)} collective-permute-done((bf16[128,2048]{1,0:T(8,128)(2,1)}, bf16[128,2048]{1,0:T(8,128)(2,1)}, u32[]{:S(2)}, u32[]{:S(2)}) %collective-permute-start.52) | collective-permute-done | bytes 524320 | tf_op jit(solution)/shard_map/ppermute | solution.py:43
  515.6 10.8 %collective-permute-done.64.refs_7_ = bf16[128,2048]{1,0:T(8,128)(2,1)S(1)} collective-permute-done((bf16[128,2048]{1,0:T(8,128)(2,1)}, bf16[128,2048]{1,0:T(8,128)(2,1)S(1)}, u32[]{:S(2)}, u32[]{:S(2)}) %collective-permute-start.64) | collective-permute-done | bytes 524320 | tf_op jit(solution)/shard_map/ppermute | solution.py:43
  563.2 9.0 %collective-permute-done.57 = bf16[64,3200]{1,0:T(8,128)(2,1)S(1)} collective-permute-done((bf16[64,3200]{1,0:T(8,128)(2,1)S(1)}, bf16[64,3200]{1,0:T(8,128)(2,1)S(1)}, u32[]{:S(2)}, u32[]{:S(2)}) %collective-permute-start.57) | collective-permute-done | bytes 409632 | tf_op jit(solution)/shard_map/ppermute | solution.py:43
  (329 shorter events, 296.8 us)
Async XLA Ops:
  7.2 60.6 %all-gather.5.cloned.1.call-start = ((), (), s32[]{:S(2)}) async-start(), calls=%async_computation.3 | async-start | bytes 1310720 | tf_op jit(solution)/shard_map/all_gather | solution.py:190
  39.5 148.1 %all-gather.7.cloned.1.call-start = ((), (), s32[]{:S(2)}) async-start(), calls=%async_computation.4 | async-start | bytes 7077888 | tf_op jit(solution)/shard_map/all_gather | solution.py:197
  70.0 508.5 %reduce-scatter.2.cloned.1.call-start = ((), (), s32[]{:S(2)}) async-start(), calls=%async_computation.2 | async-start | bytes 15728640 | tf_op jit(solution)/shard_map/reduce_scatter | solution.py:807
  82.2 26.5 %collective-permute-start.12 = (bf16[512,384]{1,0:T(8,128)(2,1)}, bf16[512,384]{1,0:T(8,128)(2,1)}, u32[]{:S(2)}, u32[]{:S(2)}) collective-permute-start(bf16[512,384]{1,0:T(8,128)(2,1)} %copy-done.35), channel_id=1, source_target_pairs={{0,16},{4,20},{8,24},{12,28},{16,0},{20,4},{24,8},{28,12},{1,17},{... | collective-permute-start | bytes 1179656 | tf_op jit(solution)/shard_map/ppermute | solution.py:43
  82.8 26.3 %collective-permute-start.2 = (bf16[512,384]{1,0:T(8,128)(2,1)S(1)}, bf16[512,384]{1,0:T(8,128)(2,1)}, u32[]{:S(2)}, u32[]{:S(2)}) collective-permute-start(bf16[512,384]{1,0:T(8,128)(2,1)S(1)} %collective-permute-done.refs_3_), channel_id=1, source_target_pairs={{0,8},{4,12},{8,0},{12,4},{16,24},{20,28},{24,16},{28,20},{1,9},{5... | collective-permute-start | bytes 1179656 | tf_op jit(solution)/shard_map/ppermute | solution.py:43
  84.2 26.5 %collective-permute-start.9 = (bf16[512,384]{1,0:T(8,128)(2,1)}, bf16[512,384]{1,0:T(8,128)(2,1)S(1)}, u32[]{:S(2)}, u32[]{:S(2)}) collective-permute-start(bf16[512,384]{1,0:T(8,128)(2,1)} %copy-done.35), channel_id=1, source_target_pairs={{0,4},{4,0},{8,12},{12,8},{16,20},{20,16},{24,28},{28,24},{1,5},{5... | collective-permute-start | bytes 1179656 | tf_op jit(solution)/shard_map/ppermute | solution.py:43
  161.8 25.8 %collective-permute-start.32 = (bf16[128,2048]{1,0:T(8,128)(2,1)S(1)}, bf16[128,2048]{1,0:T(8,128)(2,1)S(1)}, u32[]{:S(2)}, u32[]{:S(2)}) collective-permute-start(bf16[128,2048]{1,0:T(8,128)(2,1)S(1)} %bitcast.70), channel_id=1, source_target_pairs={{0,3},{1,2},{2,1},{3,0},{4,7},{5,6},{6,5},{7,4},{8,11},{9,10},{10,... | collective-permute-start | bytes 1572872 | tf_op jit(solution)/shard_map/ppermute | solution.py:43
  263.9 25.8 %collective-permute-start.35 = (bf16[2,1024,2048]{2,1,0:T(8,128)(2,1)}, bf16[2,1024,2048]{2,1,0:T(8,128)(2,1)S(1)}, u32[]{:S(2)}, u32[]{:S(2)}) collective-permute-start(bf16[2,1024,2048]{2,1,0:T(8,128)(2,1)} %shard_map.144), channel_id=1, source_target_pairs={{0,4},{4,0},{8,12},{12,8},{16,20},{20,16},{24,28},{28,24},{1,5},{5... | collective-permute-start | bytes 25165832 | tf_op jit(solution)/shard_map/ppermute | solution.py:43
  378.5 52.6 %collective-permute-start.41 = (bf16[128,2048]{1,0:T(8,128)(2,1)S(1)}, bf16[128,2048]{1,0:T(8,128)(2,1)S(1)}, u32[]{:S(2)}, u32[]{:S(2)}) collective-permute-start(bf16[128,2048]{1,0:T(8,128)(2,1)S(1)} %get-tuple-element.95), channel_id=1, source_target_pairs={{0,1},{1,0},{2,3},{3,2},{4,5},{5,4},{6,7},{7,6},{8,9},{9,8},{10,11... | collective-permute-start | bytes 1572872 | tf_op jit(solution)/shard_map/ppermute | solution.py:43
  383.6 54.7 %collective-permute-start.51 = (bf16[128,2048]{1,0:T(8,128)(2,1)}, bf16[128,2048]{1,0:T(8,128)(2,1)}, u32[]{:S(2)}, u32[]{:S(2)}) collective-permute-start(bf16[128,2048]{1,0:T(8,128)(2,1)} %get-tuple-element.109.query_ref.refs_9_), channel_id=1, source_target_pairs={{0,3},{1,2},{2,1},{3,0},{4,7},{5,6},{6,5},{7,4},{8,11},{9,10},{10,... | collective-permute-start | bytes 1572872 | tf_op jit(solution)/shard_map/ppermute | solution.py:43
  406.5 99.1 %all-to-all-start = ((bf16[4,128,1024]{2,1,0:T(8,128)(2,1)}), bf16[4,128,1024]{2,1,0:T(8,128)(2,1)}, u32[]{:S(2)}, u32[]{:S(2)}) async-start(bf16[4,128,1024]{2,1,0:T(8,128)(2,1)} %bitcast.78), calls=%async_computation | async-start | bytes 2097152 | tf_op jit(solution)/shard_map/all_to_all | solution.py:1139
  431.1 37.9 %collective-permute-start.40 = (bf16[128,2048]{1,0:T(8,128)(2,1)}, bf16[128,2048]{1,0:T(8,128)(2,1)}, u32[]{:S(2)}, u32[]{:S(2)}) collective-permute-start(bf16[128,2048]{1,0:T(8,128)(2,1)} %get-tuple-element.91), channel_id=1, source_target_pairs={{0,1},{1,0},{2,3},{3,2},{4,5},{5,4},{6,7},{7,6},{8,9},{9,8},{10,11... | collective-permute-start | bytes 1572872 | tf_op jit(solution)/shard_map/ppermute | solution.py:43
  432.1 36.9 %collective-permute-start.42 = (bf16[128,2048]{1,0:T(8,128)(2,1)}, bf16[128,2048]{1,0:T(8,128)(2,1)}, u32[]{:S(2)}, u32[]{:S(2)}) collective-permute-start(bf16[128,2048]{1,0:T(8,128)(2,1)} %add_convert_fusion.1), channel_id=1, source_target_pairs={{0,3},{1,2},{2,1},{3,0},{4,7},{5,6},{6,5},{7,4},{8,11},{9,10},{10,... | collective-permute-start | bytes 1572872 | tf_op jit(solution)/shard_map/ppermute | solution.py:43
  433.6 37.6 %collective-permute-start.63 = (bf16[128,2048]{1,0:T(8,128)(2,1)}, bf16[128,2048]{1,0:T(8,128)(2,1)}, u32[]{:S(2)}, u32[]{:S(2)}) collective-permute-start(bf16[128,2048]{1,0:T(8,128)(2,1)} %get-tuple-element.117.refs_1_.refs_5_), channel_id=1, source_target_pairs={{0,3},{1,2},{2,1},{3,0},{4,7},{5,6},{6,5},{7,4},{8,11},{9,10},{10,... | collective-permute-start | bytes 1572872 | tf_op jit(solution)/shard_map/ppermute | solution.py:43
  435.9 46.1 %collective-permute-start.50 = (bf16[128,2048]{1,0:T(8,128)(2,1)}, bf16[128,2048]{1,0:T(8,128)(2,1)}, u32[]{:S(2)}, u32[]{:S(2)}) collective-permute-start(bf16[128,2048]{1,0:T(8,128)(2,1)} %get-tuple-element.109.query_ref.refs_9_), channel_id=1, source_target_pairs={{0,1},{1,0},{2,3},{3,2},{4,5},{5,4},{6,7},{7,6},{8,9},{9,8},{10,11... | collective-permute-start | bytes 1572872 | tf_op jit(solution)/shard_map/ppermute | solution.py:43
  438.3 57.4 %collective-permute-start.52 = (bf16[128,2048]{1,0:T(8,128)(2,1)}, bf16[128,2048]{1,0:T(8,128)(2,1)}, u32[]{:S(2)}, u32[]{:S(2)}) collective-permute-start(bf16[128,2048]{1,0:T(8,128)(2,1)} %collective-permute-done.51.refs_12_), channel_id=1, source_target_pairs={{0,1},{1,0},{2,3},{3,2},{4,5},{5,4},{6,7},{7,6},{8,9},{9,8},{10,11... | collective-permute-start | bytes 1572872 | tf_op jit(solution)/shard_map/ppermute | solution.py:43
  469.0 32.2 %collective-permute-start.47 = (bf16[128,512]{1,0:T(8,128)(2,1)S(1)}, bf16[128,512]{1,0:T(8,128)(2,1)S(1)}, u32[]{:S(2)}, u32[]{:S(2)}) collective-permute-start(bf16[128,512]{1,0:T(8,128)(2,1)S(1)} %copy-done.50), channel_id=1, source_target_pairs={{0,1},{1,0},{2,3},{3,2},{4,5},{5,4},{6,7},{7,6},{8,9},{9,8},{10,11... | collective-permute-start | bytes 393224 | tf_op jit(solution)/shard_map/ppermute | solution.py:43
  469.0 32.2 %collective-permute-start.48 = (bf16[128,512]{1,0:T(8,128)(2,1)S(1)}, bf16[128,512]{1,0:T(8,128)(2,1)S(1)}, u32[]{:S(2)}, u32[]{:S(2)}) collective-permute-start(bf16[128,512]{1,0:T(8,128)(2,1)S(1)} %copy-done.49), channel_id=1, source_target_pairs={{0,2},{1,3},{2,0},{3,1},{4,6},{5,7},{6,4},{7,5},{8,10},{9,11},{10,... | collective-permute-start | bytes 393224 | tf_op jit(solution)/shard_map/ppermute | solution.py:43
  471.2 31.7 %collective-permute-start.49 = (bf16[128,512]{1,0:T(8,128)(2,1)S(1)}, bf16[128,512]{1,0:T(8,128)(2,1)S(1)}, u32[]{:S(2)}, u32[]{:S(2)}) collective-permute-start(bf16[128,512]{1,0:T(8,128)(2,1)S(1)} %copy-done.48), channel_id=1, source_target_pairs={{0,3},{1,2},{2,1},{3,0},{4,7},{5,6},{6,5},{7,4},{8,11},{9,10},{10,... | collective-permute-start | bytes 393224 | tf_op jit(solution)/shard_map/ppermute | solution.py:43
  481.9 31.9 %collective-permute-start.62 = (bf16[128,2048]{1,0:T(8,128)(2,1)}, bf16[128,2048]{1,0:T(8,128)(2,1)S(1)}, u32[]{:S(2)}, u32[]{:S(2)}) collective-permute-start(bf16[128,2048]{1,0:T(8,128)(2,1)} %get-tuple-element.117.refs_1_.refs_5_), channel_id=1, source_target_pairs={{0,1},{1,0},{2,3},{3,2},{4,5},{5,4},{6,7},{7,6},{8,9},{9,8},{10,11... | collective-permute-start | bytes 1572872 | tf_op jit(solution)/shard_map/ppermute | solution.py:43
  495.7 30.8 %collective-permute-start.64 = (bf16[128,2048]{1,0:T(8,128)(2,1)}, bf16[128,2048]{1,0:T(8,128)(2,1)S(1)}, u32[]{:S(2)}, u32[]{:S(2)}) collective-permute-start(bf16[128,2048]{1,0:T(8,128)(2,1)} %collective-permute-done.63.refs_8_), channel_id=1, source_target_pairs={{0,1},{1,0},{2,3},{3,2},{4,5},{5,4},{6,7},{7,6},{8,9},{9,8},{10,11... | collective-permute-start | bytes 1572872 | tf_op jit(solution)/shard_map/ppermute | solution.py:43
  501.2 26.6 %collective-permute-start.59 = (bf16[128,512]{1,0:T(8,128)(2,1)}, bf16[128,512]{1,0:T(8,128)(2,1)S(1)}, u32[]{:S(2)}, u32[]{:S(2)}) collective-permute-start(bf16[128,512]{1,0:T(8,128)(2,1)} %copy.85), channel_id=1, source_target_pairs={{0,1},{1,0},{2,3},{3,2},{4,5},{5,4},{6,7},{7,6},{8,9},{9,8},{10,11... | collective-permute-start | bytes 393224 | tf_op jit(solution)/shard_map/ppermute | solution.py:43
  501.2 26.6 %collective-permute-start.60 = (bf16[128,512]{1,0:T(8,128)(2,1)}, bf16[128,512]{1,0:T(8,128)(2,1)S(1)}, u32[]{:S(2)}, u32[]{:S(2)}) collective-permute-start(bf16[128,512]{1,0:T(8,128)(2,1)} %copy.86), channel_id=1, source_target_pairs={{0,2},{1,3},{2,0},{3,1},{4,6},{5,7},{6,4},{7,5},{8,10},{9,11},{10,... | collective-permute-start | bytes 393224 | tf_op jit(solution)/shard_map/ppermute | solution.py:43
  514.6 29.9 %collective-permute-start.55 = (bf16[4,64,3200]{2,1,0:T(8,128)(2,1)}, bf16[4,64,3200]{2,1,0:T(8,128)(2,1)}, u32[]{:S(2)}, u32[]{:S(2)}) collective-permute-start(bf16[4,64,3200]{2,1,0:T(8,128)(2,1)} %get-tuple-element.114), channel_id=1, source_target_pairs={{0,4},{4,0},{8,12},{12,8},{16,20},{20,16},{24,28},{28,24},{1,5},{5... | collective-permute-start | bytes 4915208 | tf_op jit(solution)/shard_map/ppermute | solution.py:43
  (102 other events, 2119.4 us)
Sparse Core Ops, SparseCore 0:
  39.6 28.1 all-gather.4
  70.3 62.9 all-gather.6
  299.9 129.5 reduce-scatter.1

commit v12 on v11

--- a/solution.py
+++ b/solution.py
@@ -1127,7 +1127,6 @@
         scaled_two - unit_two * jnp.mean(scaled_two * unit_two, axis=-1, keepdims=True)
     )
     residual_bf = residual_grad.astype(BF)
-    out_sum = sum_rows([after(part, residual_bf) for part in out_partial], True)
     (ffn_term,) = own_features([ffn_gain_term])
     attn_grad = out_back(residual_bf, out_weight, out_blocks)
     query_part, kept, sent = attend_back(
@@ -1141,9 +1140,12 @@
         query_part, pair_copies, qkv_full, hidden_in[0], attn_gain, residual_grad
     )
     out_sums = share_start([own_residual], [after(all_attn, input_grad)], [])
-    output = (residual + share_finish(after(out_sum, input_grad))).astype(BF)
-    qkv_sums = share_start([own_one, own_one], [after(query_planes, output), all_pair], [ffn_term])
+    out_sum = sum_rows([after(part, input_grad) for part in out_partial], False)
+    qkv_sums = share_start(
+        [own_one, own_one], [after(query_planes, input_grad), all_pair], [ffn_term]
+    )
     qkv_sums = share_finish(qkv_sums)
+    output = (residual + share_finish(after(out_sum, qkv_sums))).astype(BF)
     out_weight_grad = share_finish(out_sums)
     qkv_grad = qkv_sums[:, : qkv_weight.shape[1]]
     features = own_rows_of(attn_gain, qkv_grad.shape[0])

time: 592 us -> 627 us (1.059)
  waiting for transfers between devices: 266 us -> 285 us
  starting transfers between devices: 97.8 us -> 114 us
    ppermute x69, waiting for transfers between devices: 257 us -> 277 us  [swap(): return lax.ppermute(value, axis, [(i, i ^ offset) for i in range(count)])]
    ppermute x69, starting transfers between devices: 93.2 us -> 109 us  [swap(): return lax.ppermute(value, axis, [(i, i ^ offset) for i in range(count)])]
    unnamed x115 -> x125, local copies, waits for them, and re-layouts: 21.6 us -> 23.8 us
  transfers between devices with their start and end apart: 73 -> 73, of which waited for: 47 -> 43; matrix products, arithmetic and copies ran while one was open for 6% -> 5% of each run, Pallas kernels for 21% -> 19%
where the time goes in v12:
time: 627 us; the launch traced here: 625 us
  waiting for transfers between devices  285 us (45%)
  Pallas kernels  158 us (25%)
  starting transfers between devices  114 us (18%)
  local copies, waits for them, and re-layouts  37.1 us (6%)
  other arithmetic  15.9 us (3%)
  between operations  14.6 us (2%)
    ppermute x69, waiting for transfers between devices, swap(): return lax.ppermute(value, axis, [(i, i ^ offset) for i in range(count)])  277 us
    ppermute x69, starting transfers between devices, swap(): return lax.ppermute(value, axis, [(i, i ^ offset) for i in range(count)])  109 us
    pallas_call x4, Pallas kernels, half_products(): pl.pallas_call(lambda *refs: products_kernel(count, kept, *refs), grid_sp...  32.8 us
    pallas_call x2, Pallas kernels, ffn_middle(): pl.pallas_call(lambda *refs: ffn_kernel(len(blocks), len(earlier), *refs)...  28 us
    unnamed x125, local copies, waits for them, and re-layouts  23.8 us
    pallas_call x1, Pallas kernels, attend_back(): pl.pallas_call(lambda *refs: attend_back_kernel(KEY_CHUNK, *refs), grid=(...  19.8 us
  transfers between devices with their start and end apart: 73, of which 43 were waited for; matrix products, arithmetic and copies ran while one was open for 5% of the time, Pallas kernels for 19%

profile of v12, /device:TPU:0, one launch (start us, length us, event | category | flops | bytes accessed | tf_op | source)
XLA Modules:
  0.0 625.0 jit_solution(14664699468880512421)
XLA Ops:
  59.0 8.9 %all-gather.5.cloned.1.call-done = bf16[2048,256]{1,0:T(8,128)(2,1)} async-done(((bf16[512,256]{1,0:T(8,128)(2,1)}), bf16[2048,256]{1,0:T(8,128)(2,1)}) %all-gather.5.cloned.1.call-update) | async-done | bytes 1048592 | tf_op jit(solution)/shard_map/all_gather | solution.py:190
  86.7 11.4 %collective-permute-done.4.refs_7_ = bf16[512,384]{1,0:T(8,128)(2,1)} collective-permute-done((bf16[512,384]{1,0:T(8,128)(2,1)S(1)}, bf16[512,384]{1,0:T(8,128)(2,1)}, u32[]{:S(2)}, u32[]{:S(2)}) %collective-permute-start.4) | collective-permute-done | bytes 393248 | tf_op jit(solution)/shard_map/ppermute | solution.py:43
  98.1 10.6 %collective-permute-done.12.refs_15_ = bf16[512,384]{1,0:T(8,128)(2,1)} collective-permute-done((bf16[512,384]{1,0:T(8,128)(2,1)}, bf16[512,384]{1,0:T(8,128)(2,1)}, u32[]{:S(2)}, u32[]{:S(2)}) %collective-permute-start.12) | collective-permute-done | bytes 393248 | tf_op jit(solution)/shard_map/ppermute | solution.py:43
  111.3 17.0 %collective-permute-done.14.refs_17_ = bf16[512,384]{1,0:T(8,128)(2,1)S(1)} collective-permute-done((bf16[512,384]{1,0:T(8,128)(2,1)}, bf16[512,384]{1,0:T(8,128)(2,1)S(1)}, u32[]{:S(2)}, u32[]{:S(2)}) %collective-permute-start.14) | collective-permute-done | bytes 393248 | tf_op jit(solution)/shard_map/ppermute | solution.py:43
  135.2 9.6 %pieces_forward.1 = (bf16[128,2048]{1,0:T(8,128)(2,1)S(1)}, bf16[128,1024]{1,0:T(8,128)(2,1)S(1)}, bf16[2048,3072]{1,0:T(8,128)(2,1)}) custom-call(s32[2]{0:T(128)S(1)} %pad_add_fusion.refs_0_, bf16[128,2048]{1,0:T(8,128)(2,1)S(1)} %fusion.2.refs_1_, bf16[512,3072]{1,0:T(8,128)(2,1)} %refs_2_.3, bf16[512,384]{1,0:T(8,128)(2,1)} %copy-done.42, ...), custom_call_target="tpu_custom_call" | custom-call | flops 1610612736 | bytes 25165824 | tf_op jit(solution)/shard_map/pieces_forward/pallas_call | solution.py:160
  164.1 12.2 %attend.1 = (bf16[128,2048]{1,0:T(8,128)(2,1)S(1)}, f32[128,2048]{1,0:T(8,128)S(1)}, f32[8,1,512]{2,1,0:T(1,128)S(1)}) custom-call(bf16[128,2048]{1,0:T(8,128)(2,1)S(1)} %get-tuple-element.67.refs_0_, bf16[512,1024]{1,0:T(8,128)(2,1)S(1)} %constant_dynamic-update-slice_fusion.3.refs_1_.refs_2_.refs_3_.refs_4_, ...), custom_call_target="tpu_custom_call" | custom-call | flops 1073741824 | bytes 2097152 | tf_op jit(solution)/shard_map/attend/pallas_call | solution.py:536
  178.1 9.4 %collective-permute-done.32.refs_3_.refs_4_.refs_8_ = bf16[128,2048]{1,0:T(8,128)(2,1)S(1)} collective-permute-done((bf16[128,2048]{1,0:T(8,128)(2,1)S(1)}, bf16[128,2048]{1,0:T(8,128)(2,1)S(1)}, u32[]{:S(2)}, u32[]{:S(2)}) %collective-permute-start.32) | collective-permute-done | bytes 524320 | tf_op jit(solution)/shard_map/ppermute | solution.py:43
  202.6 8.7 %down_back.1.refs_2_ = f32[512,2048]{1,0:T(8,128)} custom-call(bf16[128,2048]{1,0:T(8,128)(2,1)S(1)} %bitcast.72, bf16[128,2048]{1,0:T(8,128)(2,1)S(1)} %collective-permute-done.31.refs_1_.refs_2_.refs_6_, bf16[128,2048]{1,0:T(8,128)(2,1)S(1)} %collective-permute-done.33.refs_2_.refs_3_.refs_7_, ...), custom_call_target="tpu_custom_call" | custom-call | flops 4294967296 | bytes 8388608 | tf_op jit(solution)/shard_map/down_back/pallas_call | solution.py:841
  224.0 14.0 %ffn_middle.2 = (bf16[3,512,2048]{2,1,0:T(8,128)(2,1)}, f32[128,2048]{1,0:T(8,128)S(1)}, bf16[128,2048]{1,0:T(8,128)(2,1)S(1)}) custom-call(bf16[128,2048]{1,0:T(8,128)(2,1)S(1)} %get-tuple-element.73.refs_0_.refs_1_.refs_5_, bf16[128,2048]{1,0:T(8,128)(2,1)S(1)} %collective-permute-done.34.refs_1_.refs_2_.refs_6_, f32[512,2048]{1,0:T(8,128)} %down_back.1.refs_2_, ...), custom_call_target="tpu_custom_call" | custom-call | flops 8589934592 | bytes 16777216 | tf_op jit(solution)/shard_map/ffn_middle/pallas_call | solution.py:704
  239.8 14.0 %ffn_middle.3 = (bf16[3,512,2048]{2,1,0:T(8,128)(2,1)}, bf16[128,2048]{1,0:T(8,128)(2,1)S(1)}, f32[128,2048]{1,0:T(8,128)S(1)}) custom-call(bf16[128,2048]{1,0:T(8,128)(2,1)S(1)} %collective-permute-done.30.refs_0_.refs_3_.refs_7_, bf16[128,2048]{1,0:T(8,128)(2,1)S(1)} %collective-permute-done.29.refs_1_.refs_4_.refs_8_, ...), custom_call_target="tpu_custom_call", output_to_operand_aliasing={{0}: (4, {})} | custom-call | flops 8589934592 | bytes 16777216 | tf_op jit(solution)/shard_map/ffn_middle/pallas_call | solution.py:704
  253.9 9.9 %shard_map.144 = bf16[2,1024,2048]{2,1,0:T(8,128)(2,1)} custom-call(s32[2]{0:T(128)S(1)} %pad_add_fusion.refs_0_, bf16[128,2048]{1,0:T(8,128)(2,1)S(1)} %get-tuple-element.73.refs_0_.refs_1_.refs_5_, bf16[128,2048]{1,0:T(8,128)(2,1)S(1)} %collective-permute-done.34.refs_1_.refs_2_.refs_6_, ...), custom_call_target="tpu_custom_call" | custom-call | flops 4294967296 | bytes 8388608 | tf_op jit(solution)/shard_map/pallas_call | solution.py:766
  270.6 12.5 %collective-permute-done.36.refs_10_ = bf16[1,1024,2048]{2,1,0:T(8,128)(2,1)S(1)} collective-permute-done((bf16[1,1024,2048]{2,1,0:T(8,128)(2,1)}, bf16[1,1024,2048]{2,1,0:T(8,128)(2,1)S(1)}, u32[]{:S(2)}, u32[]{:S(2)}) %collective-permute-start.36) | collective-permute-done | bytes 4194336 | tf_op jit(solution)/shard_map/ppermute | solution.py:43
  289.5 10.2 %shard_map.147 = bf16[3,1024,2048]{2,1,0:T(8,128)(2,1)} custom-call(s32[2]{0:T(128)S(1)} %pad_add_fusion.refs_0_, bf16[128,2048]{1,0:T(8,128)(2,1)S(1)} %get-tuple-element.73.refs_0_.refs_1_.refs_5_, bf16[128,2048]{1,0:T(8,128)(2,1)S(1)} %collective-permute-done.34.refs_1_.refs_2_.refs_6_, ...), custom_call_target="tpu_custom_call", output_to_operand_aliasing={{}: (11, {})} | custom-call | flops 4294967296 | bytes 8388608 | tf_op jit(solution)/shard_map/pallas_call | solution.py:766
  301.9 13.0 %collective-permute-done.38 = bf16[128,2048]{1,0:T(8,128)(2,1)S(1)} collective-permute-done((bf16[128,2048]{1,0:T(8,128)(2,1)}, bf16[128,2048]{1,0:T(8,128)(2,1)S(1)}, u32[]{:S(2)}, u32[]{:S(2)}) %collective-permute-start.38) | collective-permute-done | bytes 524320 | tf_op jit(solution)/shard_map/ppermute | solution.py:43
  316.8 8.4 %collective-permute-done.37 = bf16[128,2048]{1,0:T(8,128)(2,1)S(1)} collective-permute-done((bf16[128,2048]{1,0:T(8,128)(2,1)S(1)}, bf16[128,2048]{1,0:T(8,128)(2,1)S(1)}, u32[]{:S(2)}, u32[]{:S(2)}) %collective-permute-start.37) | collective-permute-done | bytes 524320 | tf_op jit(solution)/shard_map/ppermute | solution.py:43
  325.2 13.0 %collective-permute-done.39 = bf16[128,2048]{1,0:T(8,128)(2,1)S(1)} collective-permute-done((bf16[128,2048]{1,0:T(8,128)(2,1)S(1)}, bf16[128,2048]{1,0:T(8,128)(2,1)S(1)}, u32[]{:S(2)}, u32[]{:S(2)}) %collective-permute-start.39) | collective-permute-done | bytes 524320 | tf_op jit(solution)/shard_map/ppermute | solution.py:43
  345.4 19.8 %attend_back.1 = (bf16[128,2048]{1,0:T(8,128)(2,1)S(1)}, bf16[2,512,512]{2,1,0:T(8,128)(2,1)S(1)}, bf16[2,512,512]{2,1,0:T(8,128)(2,1)S(1)}) custom-call(bf16[128,2048]{1,0:T(8,128)(2,1)S(1)} %copy-done.27, bf16[128,2048]{1,0:T(8,128)(2,1)S(1)} %out_back.1.refs_1_, f32[128,2048]{1,0:T(8,128)S(1)} %copy-done.36, bf16[512,1024]{1,0:T(8,128)(2,1)} %copy-done.24, ...), custom_call_target="tpu_custom_call" | custom-call | flops 2684354560 | bytes 4194304 | tf_op jit(solution)/shard_map/attend_back/pallas_call | solution.py:601
  398.6 29.8 %collective-permute-done.51.refs_12_ = bf16[128,2048]{1,0:T(8,128)(2,1)} collective-permute-done((bf16[128,2048]{1,0:T(8,128)(2,1)}, bf16[128,2048]{1,0:T(8,128)(2,1)}, u32[]{:S(2)}, u32[]{:S(2)}) %collective-permute-start.51) | collective-permute-done | bytes 524320 | tf_op jit(solution)/shard_map/ppermute | solution.py:43
  428.5 27.1 %collective-permute-start.52 = (bf16[128,2048]{1,0:T(8,128)(2,1)}, bf16[128,2048]{1,0:T(8,128)(2,1)}, u32[]{:S(2)}, u32[]{:S(2)}) collective-permute-start(bf16[128,2048]{1,0:T(8,128)(2,1)} %collective-permute-done.51.refs_12_), channel_id=1, source_target_pairs={{0,1},{1,0},{2,3},{3,2},{4,5},{5,4},{6,7},{7,6},{8,9},{9,8},{10,11... | collective-permute-start | bytes 1572872 | tf_op jit(solution)/shard_map/ppermute | solution.py:43
  455.6 10.6 %collective-permute-done.53 = f32[1,2048]{1,0:T(1,128)S(1)} collective-permute-done((f32[1,2048]{1,0:T(1,128)S(1)}, f32[1,2048]{1,0:T(1,128)S(1)}, u32[]{:S(2)}, u32[]{:S(2)}) %collective-permute-start.53) | collective-permute-done | bytes 8224 | tf_op jit(solution)/shard_map/ppermute | solution.py:43
  483.7 8.9 %one_back.1 = f32[128,2048]{1,0:T(8,128)} custom-call(bf16[128,2048]{1,0:T(8,128)(2,1)S(1)} %copy-done.20, bf16[512,1024]{1,0:T(8,128)(2,1)S(1)} %copy-done.4, bf16[2048,3072]{1,0:T(8,128)(2,1)} %get-tuple-element.95.w_ref, bf16[128,2048]{1,0:T(8,128)(2,1)S(1)} %bitcast.78, f32[1,2048]{1,0:T(1,128)S(1)} %bitcast.81, f32[128,2048]{1,0:T(8,128)S(1)} %copy-done.7), custom_call_target="tpu_custom_call" | custom-call | flops 1610612736 | bytes 12582912 | tf_op jit(solution)/shard_map/one_back/pallas_call | solution.py:336
  550.6 8.4 %collective-permute-done.57 = bf16[64,3200]{1,0:T(8,128)(2,1)S(1)} collective-permute-done((bf16[64,3200]{1,0:T(8,128)(2,1)S(1)}, bf16[64,3200]{1,0:T(8,128)(2,1)S(1)}, u32[]{:S(2)}, u32[]{:S(2)}) %collective-permute-start.57) | collective-permute-done | bytes 409632 | tf_op jit(solution)/shard_map/ppermute | solution.py:43
  575.9 9.0 %collective-permute-done.46 = bf16[128,2048]{1,0:T(8,128)(2,1)S(1)} collective-permute-done((bf16[128,2048]{1,0:T(8,128)(2,1)S(1)}, bf16[128,2048]{1,0:T(8,128)(2,1)S(1)}, u32[]{:S(2)}, u32[]{:S(2)}) %collective-permute-start.46) | collective-permute-done | bytes 524320 | tf_op jit(solution)/shard_map/ppermute | solution.py:43
  584.9 27.0 %collective-permute-done.45 = bf16[128,2048]{1,0:T(8,128)(2,1)S(1)} collective-permute-done((bf16[128,2048]{1,0:T(8,128)(2,1)S(1)}, bf16[128,2048]{1,0:T(8,128)(2,1)S(1)}, u32[]{:S(2)}, u32[]{:S(2)}) %collective-permute-start.45) | collective-permute-done | bytes 524320 | tf_op jit(solution)/shard_map/ppermute | solution.py:43
  (338 shorter events, 286.8 us)
Async XLA Ops:
  7.2 60.6 %all-gather.5.cloned.1.call-start = ((), (), s32[]{:S(2)}) async-start(), calls=%async_computation.3 | async-start | bytes 1310720 | tf_op jit(solution)/shard_map/all_gather | solution.py:190
  39.5 148.1 %all-gather.7.cloned.1.call-start = ((), (), s32[]{:S(2)}) async-start(), calls=%async_computation.4 | async-start | bytes 7077888 | tf_op jit(solution)/shard_map/all_gather | solution.py:197
  70.0 543.0 %reduce-scatter.2.cloned.1.call-start = ((), (), s32[]{:S(2)}) async-start(), calls=%async_computation.2 | async-start | bytes 15728640 | tf_op jit(solution)/shard_map/reduce_scatter | solution.py:807
  82.2 26.5 %collective-permute-start.12 = (bf16[512,384]{1,0:T(8,128)(2,1)}, bf16[512,384]{1,0:T(8,128)(2,1)}, u32[]{:S(2)}, u32[]{:S(2)}) collective-permute-start(bf16[512,384]{1,0:T(8,128)(2,1)} %copy-done.40), channel_id=1, source_target_pairs={{0,16},{4,20},{8,24},{12,28},{16,0},{20,4},{24,8},{28,12},{1,17},{... | collective-permute-start | bytes 1179656 | tf_op jit(solution)/shard_map/ppermute | solution.py:43
  82.8 26.3 %collective-permute-start.2 = (bf16[512,384]{1,0:T(8,128)(2,1)S(1)}, bf16[512,384]{1,0:T(8,128)(2,1)}, u32[]{:S(2)}, u32[]{:S(2)}) collective-permute-start(bf16[512,384]{1,0:T(8,128)(2,1)S(1)} %collective-permute-done.refs_3_), channel_id=1, source_target_pairs={{0,8},{4,12},{8,0},{12,4},{16,24},{20,28},{24,16},{28,20},{1,9},{5... | collective-permute-start | bytes 1179656 | tf_op jit(solution)/shard_map/ppermute | solution.py:43
  84.2 26.5 %collective-permute-start.9 = (bf16[512,384]{1,0:T(8,128)(2,1)}, bf16[512,384]{1,0:T(8,128)(2,1)S(1)}, u32[]{:S(2)}, u32[]{:S(2)}) collective-permute-start(bf16[512,384]{1,0:T(8,128)(2,1)} %copy-done.40), channel_id=1, source_target_pairs={{0,4},{4,0},{8,12},{12,8},{16,20},{20,16},{24,28},{28,24},{1,5},{5... | collective-permute-start | bytes 1179656 | tf_op jit(solution)/shard_map/ppermute | solution.py:43
  86.7 24.0 %collective-permute-start.1 = (bf16[512,384]{1,0:T(8,128)(2,1)S(1)}, bf16[512,384]{1,0:T(8,128)(2,1)S(1)}, u32[]{:S(2)}, u32[]{:S(2)}) collective-permute-start(bf16[512,384]{1,0:T(8,128)(2,1)S(1)} %collective-permute-done.refs_3_), channel_id=1, source_target_pairs={{0,4},{4,0},{8,12},{12,8},{16,20},{20,16},{24,28},{28,24},{1,5},{5... | collective-permute-start | bytes 1179656 | tf_op jit(solution)/shard_map/ppermute | solution.py:43
  161.8 25.8 %collective-permute-start.32 = (bf16[128,2048]{1,0:T(8,128)(2,1)S(1)}, bf16[128,2048]{1,0:T(8,128)(2,1)S(1)}, u32[]{:S(2)}, u32[]{:S(2)}) collective-permute-start(bf16[128,2048]{1,0:T(8,128)(2,1)S(1)} %bitcast.71), channel_id=1, source_target_pairs={{0,3},{1,2},{2,1},{3,0},{4,7},{5,6},{6,5},{7,4},{8,11},{9,10},{10,... | collective-permute-start | bytes 1572872 | tf_op jit(solution)/shard_map/ppermute | solution.py:43
  199.4 24.6 %collective-permute-start.34 = (bf16[128,2048]{1,0:T(8,128)(2,1)S(1)}, bf16[128,2048]{1,0:T(8,128)(2,1)S(1)}, u32[]{:S(2)}, u32[]{:S(2)}) collective-permute-start(bf16[128,2048]{1,0:T(8,128)(2,1)S(1)} %get-tuple-element.73.refs_0_.refs_1_.refs_5_), channel_id=1, source_target_pairs={{0,1},{1,0},{2,3},{3,2},{4,5},{5,4},{6,7},{7,6},{8,9},{9,8},{10,11... | collective-permute-start | bytes 1572872 | tf_op jit(solution)/shard_map/ppermute | solution.py:43
  214.8 25.0 %collective-permute-start.30 = (bf16[128,2048]{1,0:T(8,128)(2,1)S(1)}, bf16[128,2048]{1,0:T(8,128)(2,1)S(1)}, u32[]{:S(2)}, u32[]{:S(2)}) collective-permute-start(bf16[128,2048]{1,0:T(8,128)(2,1)S(1)} %collective-permute-done.29.refs_1_.refs_4_.refs_8_), channel_id=1, source_target_pairs={{0,1},{1,0},{2,3},{3,2},{4,5},{5,4},{6,7},{7,6},{8,9},{9,8},{10,11... | collective-permute-start | bytes 1572872 | tf_op jit(solution)/shard_map/ppermute | solution.py:43
  263.8 25.8 %collective-permute-start.35 = (bf16[2,1024,2048]{2,1,0:T(8,128)(2,1)}, bf16[2,1024,2048]{2,1,0:T(8,128)(2,1)S(1)}, u32[]{:S(2)}, u32[]{:S(2)}) collective-permute-start(bf16[2,1024,2048]{2,1,0:T(8,128)(2,1)} %shard_map.144), channel_id=1, source_target_pairs={{0,4},{4,0},{8,12},{12,8},{16,20},{20,16},{24,28},{28,24},{1,5},{5... | collective-permute-start | bytes 25165832 | tf_op jit(solution)/shard_map/ppermute | solution.py:43
  300.8 24.5 %collective-permute-start.37 = (bf16[128,2048]{1,0:T(8,128)(2,1)S(1)}, bf16[128,2048]{1,0:T(8,128)(2,1)S(1)}, u32[]{:S(2)}, u32[]{:S(2)}) collective-permute-start(bf16[128,2048]{1,0:T(8,128)(2,1)S(1)} %copy-done.29), channel_id=1, source_target_pairs={{0,1},{1,0},{2,3},{3,2},{4,5},{5,4},{6,7},{7,6},{8,9},{9,8},{10,11... | collective-permute-start | bytes 1572872 | tf_op jit(solution)/shard_map/ppermute | solution.py:43
  314.9 23.3 %collective-permute-start.39 = (bf16[128,2048]{1,0:T(8,128)(2,1)S(1)}, bf16[128,2048]{1,0:T(8,128)(2,1)S(1)}, u32[]{:S(2)}, u32[]{:S(2)}) collective-permute-start(bf16[128,2048]{1,0:T(8,128)(2,1)S(1)} %add_convert_fusion.1), channel_id=1, source_target_pairs={{0,3},{1,2},{2,1},{3,0},{4,7},{5,6},{6,5},{7,4},{8,11},{9,10},{10,... | collective-permute-start | bytes 1572872 | tf_op jit(solution)/shard_map/ppermute | solution.py:43
  390.2 115.3 %all-to-all-start = ((bf16[4,128,1024]{2,1,0:T(8,128)(2,1)}), bf16[4,128,1024]{2,1,0:T(8,128)(2,1)}, u32[]{:S(2)}, u32[]{:S(2)}) async-start(bf16[4,128,1024]{2,1,0:T(8,128)(2,1)} %bitcast.79), calls=%async_computation | async-start | bytes 2097152 | tf_op jit(solution)/shard_map/all_to_all | solution.py:1138
  394.7 33.7 %collective-permute-start.51 = (bf16[128,2048]{1,0:T(8,128)(2,1)}, bf16[128,2048]{1,0:T(8,128)(2,1)}, u32[]{:S(2)}, u32[]{:S(2)}) collective-permute-start(bf16[128,2048]{1,0:T(8,128)(2,1)} %copy-done.19), channel_id=1, source_target_pairs={{0,3},{1,2},{2,1},{3,0},{4,7},{5,6},{6,5},{7,4},{8,11},{9,10},{10,... | collective-permute-start | bytes 1572872 | tf_op jit(solution)/shard_map/ppermute | solution.py:43
  398.3 69.8 %collective-permute-start.63 = (bf16[128,2048]{1,0:T(8,128)(2,1)}, bf16[128,2048]{1,0:T(8,128)(2,1)}, u32[]{:S(2)}, u32[]{:S(2)}) collective-permute-start(bf16[128,2048]{1,0:T(8,128)(2,1)} %copy-done.14), channel_id=1, source_target_pairs={{0,3},{1,2},{2,1},{3,0},{4,7},{5,6},{6,5},{7,4},{8,11},{9,10},{10,... | collective-permute-start | bytes 1572872 | tf_op jit(solution)/shard_map/ppermute | solution.py:43
  398.6 81.3 %collective-permute-start.50 = (bf16[128,2048]{1,0:T(8,128)(2,1)}, bf16[128,2048]{1,0:T(8,128)(2,1)}, u32[]{:S(2)}, u32[]{:S(2)}) collective-permute-start(bf16[128,2048]{1,0:T(8,128)(2,1)} %copy-done.19), channel_id=1, source_target_pairs={{0,1},{1,0},{2,3},{3,2},{4,5},{5,4},{6,7},{7,6},{8,9},{9,8},{10,11... | collective-permute-start | bytes 1572872 | tf_op jit(solution)/shard_map/ppermute | solution.py:43
  428.5 51.8 %collective-permute-start.52 = (bf16[128,2048]{1,0:T(8,128)(2,1)}, bf16[128,2048]{1,0:T(8,128)(2,1)}, u32[]{:S(2)}, u32[]{:S(2)}) collective-permute-start(bf16[128,2048]{1,0:T(8,128)(2,1)} %collective-permute-done.51.refs_12_), channel_id=1, source_target_pairs={{0,1},{1,0},{2,3},{3,2},{4,5},{5,4},{6,7},{7,6},{8,9},{9,8},{10,11... | collective-permute-start | bytes 1572872 | tf_op jit(solution)/shard_map/ppermute | solution.py:43
  467.5 25.2 %collective-permute-start.47 = (bf16[128,512]{1,0:T(8,128)(2,1)}, bf16[128,512]{1,0:T(8,128)(2,1)}, u32[]{:S(2)}, u32[]{:S(2)}) collective-permute-start(bf16[128,512]{1,0:T(8,128)(2,1)} %copy.81), channel_id=1, source_target_pairs={{0,1},{1,0},{2,3},{3,2},{4,5},{5,4},{6,7},{7,6},{8,9},{9,8},{10,11... | collective-permute-start | bytes 393224 | tf_op jit(solution)/shard_map/ppermute | solution.py:43
  468.2 46.6 %collective-permute-start.62 = (bf16[128,2048]{1,0:T(8,128)(2,1)}, bf16[128,2048]{1,0:T(8,128)(2,1)}, u32[]{:S(2)}, u32[]{:S(2)}) collective-permute-start(bf16[128,2048]{1,0:T(8,128)(2,1)} %copy-done.14), channel_id=1, source_target_pairs={{0,1},{1,0},{2,3},{3,2},{4,5},{5,4},{6,7},{7,6},{8,9},{9,8},{10,11... | collective-permute-start | bytes 1572872 | tf_op jit(solution)/shard_map/ppermute | solution.py:43
  470.9 44.9 %collective-permute-start.64 = (bf16[128,2048]{1,0:T(8,128)(2,1)}, bf16[128,2048]{1,0:T(8,128)(2,1)}, u32[]{:S(2)}, u32[]{:S(2)}) collective-permute-start(bf16[128,2048]{1,0:T(8,128)(2,1)} %collective-permute-done.63.refs_8_), channel_id=1, source_target_pairs={{0,1},{1,0},{2,3},{3,2},{4,5},{5,4},{6,7},{7,6},{8,9},{9,8},{10,11... | collective-permute-start | bytes 1572872 | tf_op jit(solution)/shard_map/ppermute | solution.py:43
  532.7 26.4 %collective-permute-start.57 = (bf16[64,3200]{1,0:T(8,128)(2,1)S(1)}, bf16[64,3200]{1,0:T(8,128)(2,1)S(1)}, u32[]{:S(2)}, u32[]{:S(2)}) collective-permute-start(bf16[64,3200]{1,0:T(8,128)(2,1)S(1)} %get-tuple-element.141), channel_id=1, source_target_pairs={{0,16},{4,20},{8,24},{12,28},{16,0},{20,4},{24,8},{28,12},{1,17},{... | collective-permute-start | bytes 1228808 | tf_op jit(solution)/shard_map/ppermute | solution.py:43
  570.6 41.3 %collective-permute-start.45 = (bf16[128,2048]{1,0:T(8,128)(2,1)S(1)}, bf16[128,2048]{1,0:T(8,128)(2,1)S(1)}, u32[]{:S(2)}, u32[]{:S(2)}) collective-permute-start(bf16[128,2048]{1,0:T(8,128)(2,1)S(1)} %get-tuple-element.100), channel_id=1, source_target_pairs={{0,2},{1,3},{2,0},{3,1},{4,6},{5,7},{6,4},{7,5},{8,10},{9,11},{10,... | collective-permute-start | bytes 1572872 | tf_op jit(solution)/shard_map/ppermute | solution.py:43
  570.6 41.3 %collective-permute-start.44 = (bf16[128,2048]{1,0:T(8,128)(2,1)S(1)}, bf16[128,2048]{1,0:T(8,128)(2,1)S(1)}, u32[]{:S(2)}, u32[]{:S(2)}) collective-permute-start(bf16[128,2048]{1,0:T(8,128)(2,1)S(1)} %get-tuple-element.98), channel_id=1, source_target_pairs={{0,1},{1,0},{2,3},{3,2},{4,5},{5,4},{6,7},{7,6},{8,9},{9,8},{10,11... | collective-permute-start | bytes 1572872 | tf_op jit(solution)/shard_map/ppermute | solution.py:43
  (107 other events, 2114.0 us)
Sparse Core Ops, SparseCore 0:
  39.6 28.1 all-gather.4
  70.3 62.9 all-gather.6
  299.9 125.7 reduce-scatter.1

commit v13 on v12

--- a/solution.py
+++ b/solution.py
@@ -999,6 +999,31 @@
     return parts
 
 
+def finish_kernel(w_ref, gain_ref, *refs):
+    parts, (grad_ref, gain_grad_ref, term_ref) = refs[:-3], refs[-3:]
+    columns = grad_ref.shape[1]
+    total = parts[0][...].astype(F32)
+    for part in parts[1:]:
+        total = total + part[...].astype(F32)
+    grad = total[:, :columns]
+    grad_ref[...] = grad
+    row_sum = jnp.sum(w_ref[...].astype(F32) * grad, axis=1, keepdims=True)
+    gain_grad_ref[...] = row_sum / gain_ref[...]
+    term_ref[...] = total[:, columns:]
+
+
+def finish_last(parts, weight_rows, gain_rows):
+    rows, columns = weight_rows.shape
+    wide = jax.ShapeDtypeStruct((rows, 128), F32)
+    gains = jnp.broadcast_to(gain_rows[:, None], (rows, 128))
+    return pl.pallas_call(
+        finish_kernel,
+        out_shape=(jax.ShapeDtypeStruct((rows, columns), F32), wide, wide),
+        compiler_params=pltpu.CompilerParams(vmem_limit_bytes=16 << 20),
+        name="finish_last",
+    )(weight_rows, gains, *parts)
+
+
 def share_finish(parts):
     total = parts[0].astype(F32)
     for part in parts[1:]:
@@ -1142,22 +1167,22 @@
     out_sums = share_start([own_residual], [after(all_attn, input_grad)], [])
     out_sum = sum_rows([after(part, input_grad) for part in out_partial], False)
     qkv_sums = share_start(
-        [own_one, own_one], [after(query_planes, input_grad), all_pair], [ffn_term]
+        [own_one, own_one], [after(query_planes, (input_grad, ffn_term)), all_pair], [ffn_term]
     )
-    qkv_sums = share_finish(qkv_sums)
-    output = (residual + share_finish(after(out_sum, qkv_sums))).astype(BF)
+    own_rows = qkv_weight.shape[0] // ctx_count
+    qkv_grad, gain_grad, term_grad = finish_last(
+        qkv_sums, own_rows_of(qkv_full, own_rows), own_rows_of(attn_gain, own_rows)
+    )
+    output = (residual + share_finish(after(out_sum, qkv_sums[2:3]))).astype(BF)
     out_weight_grad = share_finish(out_sums)
-    qkv_grad = qkv_sums[:, : qkv_weight.shape[1]]
-    features = own_rows_of(attn_gain, qkv_grad.shape[0])
-    gain_grad = jnp.sum(own_rows_of(qkv_full, qkv_grad.shape[0]).astype(F32) * qkv_grad, axis=1)
     return (
         output[None],
         input_grad[None],
         qkv_grad,
         out_weight_grad,
         ffn_weight_grad,
-        gain_grad / features,
-        qkv_sums[:, qkv_weight.shape[1]],
+        gain_grad[:, 0],
+        term_grad[:, 0],
     )
 
 

time: 627 us -> 601 us (0.959)
  starting transfers between devices: 114 us -> 88.1 us
    ppermute x69, starting transfers between devices: 109 us -> 83.4 us  [swap(): return lax.ppermute(value, axis, [(i, i ^ offset) for i in range(count)])]
  transfers between devices with their start and end apart: 73 -> 73, of which waited for: 43 -> 43; matrix products, arithmetic and copies ran while one was open for 5% -> 5% of each run, Pallas kernels for 19% -> 20%
where the time goes in v13:
time: 601 us; the launch traced here: 599 us
  waiting for transfers between devices  287 us (48%)
  Pallas kernels  160 us (27%)
  starting transfers between devices  88.1 us (15%)
  local copies, waits for them, and re-layouts  36.6 us (6%)
  between operations  14.5 us (2%)
  other arithmetic  12.6 us (2%)
    ppermute x69, waiting for transfers between devices, swap(): return lax.ppermute(value, axis, [(i, i ^ offset) for i in range(count)])  276 us
    ppermute x69, starting transfers between devices, swap(): return lax.ppermute(value, axis, [(i, i ^ offset) for i in range(count)])  83.4 us
    pallas_call x4, Pallas kernels, half_products(): pl.pallas_call(lambda *refs: products_kernel(count, kept, *refs), grid_sp...  32.8 us
    pallas_call x2, Pallas kernels, ffn_middle(): pl.pallas_call(lambda *refs: ffn_kernel(len(blocks), len(earlier), *refs)...  28 us
    unnamed x125, local copies, waits for them, and re-layouts  22.2 us
    pallas_call x1, Pallas kernels, attend_back(): pl.pallas_call(lambda *refs: attend_back_kernel(KEY_CHUNK, *refs), grid=(...  20 us
    pallas_call x1, Pallas kernels, attend(): pl.pallas_call(lambda *refs: attend_kernel(KEY_CHUNK, *refs), grid=(KV,),...  12.8 us
    pallas_call x2, Pallas kernels, out_call(): pl.pallas_call(lambda *refs: out_kernel(back, *refs), out_shape=out_shape...  12.3 us
  transfers between devices with their start and end apart: 73, of which 43 were waited for; matrix products, arithmetic and copies ran while one was open for 5% of the time, Pallas kernels for 20%

profile of v13, /device:TPU:0, one launch (start us, length us, event | category | flops | bytes accessed | tf_op | source)
XLA Modules:
  0.0 599.2 jit_solution(18030670447200646581)
XLA Ops:
  22.9 8.1 %collective-permute-start.16 = (bf16[512,384]{1,0:T(8,128)(2,1)S(1)}, bf16[512,384]{1,0:T(8,128)(2,1)S(1)}, u32[]{:S(2)}, u32[]{:S(2)}) collective-permute-start(bf16[512,384]{1,0:T(8,128)(2,1)S(1)} %collective-permute-done.8.refs_11_), channel_id=1, source_target_pairs={{0,1},{1,0},{2,3},{3,2},{4,5},{5,4},{6,7},{7,6},{8,9},{9,8},{10,11... | collective-permute-start | bytes 1179656 | tf_op jit(solution)/shard_map/ppermute | solution.py:43
  57.1 10.8 %all-gather.5.cloned.1.call-done = bf16[2048,256]{1,0:T(8,128)(2,1)} async-done(((bf16[512,256]{1,0:T(8,128)(2,1)}), bf16[2048,256]{1,0:T(8,128)(2,1)}) %all-gather.5.cloned.1.call-update) | async-done | bytes 1048592 | tf_op jit(solution)/shard_map/all_gather | solution.py:190
  86.7 11.4 %collective-permute-done.4.refs_7_ = bf16[512,384]{1,0:T(8,128)(2,1)} collective-permute-done((bf16[512,384]{1,0:T(8,128)(2,1)S(1)}, bf16[512,384]{1,0:T(8,128)(2,1)}, u32[]{:S(2)}, u32[]{:S(2)}) %collective-permute-start.4) | collective-permute-done | bytes 393248 | tf_op jit(solution)/shard_map/ppermute | solution.py:43
  98.1 10.6 %collective-permute-done.12.refs_15_ = bf16[512,384]{1,0:T(8,128)(2,1)} collective-permute-done((bf16[512,384]{1,0:T(8,128)(2,1)}, bf16[512,384]{1,0:T(8,128)(2,1)}, u32[]{:S(2)}, u32[]{:S(2)}) %collective-permute-start.12) | collective-permute-done | bytes 393248 | tf_op jit(solution)/shard_map/ppermute | solution.py:43
  111.3 17.0 %collective-permute-done.14.refs_17_ = bf16[512,384]{1,0:T(8,128)(2,1)S(1)} collective-permute-done((bf16[512,384]{1,0:T(8,128)(2,1)}, bf16[512,384]{1,0:T(8,128)(2,1)S(1)}, u32[]{:S(2)}, u32[]{:S(2)}) %collective-permute-start.14) | collective-permute-done | bytes 393248 | tf_op jit(solution)/shard_map/ppermute | solution.py:43
  135.2 9.6 %pieces_forward.1 = (bf16[128,2048]{1,0:T(8,128)(2,1)S(1)}, bf16[128,1024]{1,0:T(8,128)(2,1)S(1)}, bf16[2048,3072]{1,0:T(8,128)(2,1)}) custom-call(s32[2]{0:T(128)S(1)} %pad_add_fusion.refs_0_, bf16[128,2048]{1,0:T(8,128)(2,1)S(1)} %fusion.2.refs_1_, bf16[512,3072]{1,0:T(8,128)(2,1)} %refs_2_.3, bf16[512,384]{1,0:T(8,128)(2,1)} %copy-done.41, ...), custom_call_target="tpu_custom_call" | custom-call | flops 1610612736 | bytes 25165824 | tf_op jit(solution)/shard_map/pieces_forward/pallas_call | solution.py:160
  164.1 12.8 %attend.1 = (bf16[128,2048]{1,0:T(8,128)(2,1)}, f32[128,2048]{1,0:T(8,128)S(1)}, f32[8,1,512]{2,1,0:T(1,128)S(1)}) custom-call(bf16[128,2048]{1,0:T(8,128)(2,1)S(1)} %get-tuple-element.70.refs_0_, bf16[512,1024]{1,0:T(8,128)(2,1)S(1)} %constant_dynamic-update-slice_fusion.3.refs_1_.refs_2_.refs_3_.refs_4_, ...), custom_call_target="tpu_custom_call" | custom-call | flops 1073741824 | bytes 2097152 | tf_op jit(solution)/shard_map/attend/pallas_call | solution.py:536
  177.9 9.7 %collective-permute-done.32.refs_3_.refs_4_.refs_8_ = bf16[128,2048]{1,0:T(8,128)(2,1)S(1)} collective-permute-done((bf16[128,2048]{1,0:T(8,128)(2,1)S(1)}, bf16[128,2048]{1,0:T(8,128)(2,1)S(1)}, u32[]{:S(2)}, u32[]{:S(2)}) %collective-permute-start.32) | collective-permute-done | bytes 524320 | tf_op jit(solution)/shard_map/ppermute | solution.py:43
  203.2 8.7 %down_back.1.refs_2_ = f32[512,2048]{1,0:T(8,128)} custom-call(bf16[128,2048]{1,0:T(8,128)(2,1)S(1)} %bitcast.70, bf16[128,2048]{1,0:T(8,128)(2,1)S(1)} %collective-permute-done.31.refs_1_.refs_2_.refs_6_, bf16[128,2048]{1,0:T(8,128)(2,1)S(1)} %collective-permute-done.33.refs_2_.refs_3_.refs_7_, ...), custom_call_target="tpu_custom_call" | custom-call | flops 4294967296 | bytes 8388608 | tf_op jit(solution)/shard_map/down_back/pallas_call | solution.py:841
  224.1 14.0 %ffn_middle.2 = (bf16[3,512,2048]{2,1,0:T(8,128)(2,1)}, f32[128,2048]{1,0:T(8,128)S(1)}, bf16[128,2048]{1,0:T(8,128)(2,1)S(1)}) custom-call(bf16[128,2048]{1,0:T(8,128)(2,1)S(1)} %get-tuple-element.76.refs_0_.refs_1_.refs_5_, bf16[128,2048]{1,0:T(8,128)(2,1)S(1)} %collective-permute-done.34.refs_1_.refs_2_.refs_6_, f32[512,2048]{1,0:T(8,128)} %down_back.1.refs_2_, ...), custom_call_target="tpu_custom_call" | custom-call | flops 8589934592 | bytes 16777216 | tf_op jit(solution)/shard_map/ffn_middle/pallas_call | solution.py:704
  240.0 14.0 %ffn_middle.3 = (bf16[3,512,2048]{2,1,0:T(8,128)(2,1)}, bf16[128,2048]{1,0:T(8,128)(2,1)S(1)}, f32[128,2048]{1,0:T(8,128)S(1)}) custom-call(bf16[128,2048]{1,0:T(8,128)(2,1)S(1)} %collective-permute-done.30.refs_0_.refs_3_.refs_7_, bf16[128,2048]{1,0:T(8,128)(2,1)S(1)} %collective-permute-done.29.refs_1_.refs_4_.refs_8_, ...), custom_call_target="tpu_custom_call", output_to_operand_aliasing={{0}: (4, {})} | custom-call | flops 8589934592 | bytes 16777216 | tf_op jit(solution)/shard_map/ffn_middle/pallas_call | solution.py:704
  254.0 9.9 %shard_map.144 = bf16[2,1024,2048]{2,1,0:T(8,128)(2,1)} custom-call(s32[2]{0:T(128)S(1)} %pad_add_fusion.refs_0_, bf16[128,2048]{1,0:T(8,128)(2,1)S(1)} %get-tuple-element.76.refs_0_.refs_1_.refs_5_, bf16[128,2048]{1,0:T(8,128)(2,1)S(1)} %collective-permute-done.34.refs_1_.refs_2_.refs_6_, ...), custom_call_target="tpu_custom_call" | custom-call | flops 4294967296 | bytes 8388608 | tf_op jit(solution)/shard_map/pallas_call | solution.py:766
  270.7 12.5 %collective-permute-done.36.refs_10_ = bf16[1,1024,2048]{2,1,0:T(8,128)(2,1)S(1)} collective-permute-done((bf16[1,1024,2048]{2,1,0:T(8,128)(2,1)}, bf16[1,1024,2048]{2,1,0:T(8,128)(2,1)S(1)}, u32[]{:S(2)}, u32[]{:S(2)}) %collective-permute-start.36) | collective-permute-done | bytes 4194336 | tf_op jit(solution)/shard_map/ppermute | solution.py:43
  289.7 10.2 %shard_map.147 = bf16[3,1024,2048]{2,1,0:T(8,128)(2,1)} custom-call(s32[2]{0:T(128)S(1)} %pad_add_fusion.refs_0_, bf16[128,2048]{1,0:T(8,128)(2,1)S(1)} %get-tuple-element.76.refs_0_.refs_1_.refs_5_, bf16[128,2048]{1,0:T(8,128)(2,1)S(1)} %collective-permute-done.34.refs_1_.refs_2_.refs_6_, ...), custom_call_target="tpu_custom_call", output_to_operand_aliasing={{}: (11, {})} | custom-call | flops 4294967296 | bytes 8388608 | tf_op jit(solution)/shard_map/pallas_call | solution.py:766
  302.0 13.0 %collective-permute-done.38 = bf16[128,2048]{1,0:T(8,128)(2,1)S(1)} collective-permute-done((bf16[128,2048]{1,0:T(8,128)(2,1)}, bf16[128,2048]{1,0:T(8,128)(2,1)S(1)}, u32[]{:S(2)}, u32[]{:S(2)}) %collective-permute-start.38) | collective-permute-done | bytes 524320 | tf_op jit(solution)/shard_map/ppermute | solution.py:43
  317.3 8.0 %collective-permute-done.37 = bf16[128,2048]{1,0:T(8,128)(2,1)S(1)} collective-permute-done((bf16[128,2048]{1,0:T(8,128)(2,1)S(1)}, bf16[128,2048]{1,0:T(8,128)(2,1)S(1)}, u32[]{:S(2)}, u32[]{:S(2)}) %collective-permute-start.37) | collective-permute-done | bytes 524320 | tf_op jit(solution)/shard_map/ppermute | solution.py:43
  325.3 13.2 %collective-permute-done.39 = bf16[128,2048]{1,0:T(8,128)(2,1)S(1)} collective-permute-done((bf16[128,2048]{1,0:T(8,128)(2,1)S(1)}, bf16[128,2048]{1,0:T(8,128)(2,1)S(1)}, u32[]{:S(2)}, u32[]{:S(2)}) %collective-permute-start.39) | collective-permute-done | bytes 524320 | tf_op jit(solution)/shard_map/ppermute | solution.py:43
  346.5 20.0 %attend_back.1 = (bf16[128,2048]{1,0:T(8,128)(2,1)S(1)}, bf16[2,512,512]{2,1,0:T(8,128)(2,1)S(1)}, bf16[2,512,512]{2,1,0:T(8,128)(2,1)S(1)}) custom-call(bf16[128,2048]{1,0:T(8,128)(2,1)S(1)} %copy-done.24, bf16[128,2048]{1,0:T(8,128)(2,1)S(1)} %out_back.1.refs_1_, f32[128,2048]{1,0:T(8,128)S(1)} %copy-done.35, bf16[512,1024]{1,0:T(8,128)(2,1)} %copy-done.21, ...), custom_call_target="tpu_custom_call" | custom-call | flops 2684354560 | bytes 4194304 | tf_op jit(solution)/shard_map/attend_back/pallas_call | solution.py:601
  411.1 16.0 %collective-permute-done.62.refs_6_ = bf16[128,2048]{1,0:T(8,128)(2,1)} collective-permute-done((bf16[128,2048]{1,0:T(8,128)(2,1)}, bf16[128,2048]{1,0:T(8,128)(2,1)}, u32[]{:S(2)}, u32[]{:S(2)}) %collective-permute-start.62) | collective-permute-done | bytes 524320 | tf_op jit(solution)/shard_map/ppermute | solution.py:43
  430.7 8.9 %one_back.1 = f32[128,2048]{1,0:T(8,128)} custom-call(bf16[128,2048]{1,0:T(8,128)(2,1)S(1)} %copy-done.17, bf16[512,1024]{1,0:T(8,128)(2,1)S(1)} %copy-done.4, bf16[2048,3072]{1,0:T(8,128)(2,1)} %get-tuple-element.98.w_ref, bf16[128,2048]{1,0:T(8,128)(2,1)S(1)} %bitcast.76, f32[1,2048]{1,0:T(1,128)S(1)} %bitcast.79, f32[128,2048]{1,0:T(8,128)S(1)} %copy-done.7), custom_call_target="tpu_custom_call" | custom-call | flops 1610612736 | bytes 12582912 | tf_op jit(solution)/shard_map/one_back/pallas_call | solution.py:336
  439.6 12.8 %collective-permute-done.64.refs_7_ = bf16[128,2048]{1,0:T(8,128)(2,1)} collective-permute-done((bf16[128,2048]{1,0:T(8,128)(2,1)}, bf16[128,2048]{1,0:T(8,128)(2,1)}, u32[]{:S(2)}, u32[]{:S(2)}) %collective-permute-start.64) | collective-permute-done | bytes 524320 | tf_op jit(solution)/shard_map/ppermute | solution.py:43
  468.3 12.7 %collective-permute-done.53 = f32[1,2048]{1,0:T(1,128)S(1)} collective-permute-done((f32[1,2048]{1,0:T(1,128)S(1)}, f32[1,2048]{1,0:T(1,128)S(1)}, u32[]{:S(2)}, u32[]{:S(2)}) %collective-permute-start.53) | collective-permute-done | bytes 8224 | tf_op jit(solution)/shard_map/ppermute | solution.py:43
  530.3 7.9 %down_forward.1 = (f32[128,2048]{1,0:T(8,128)S(1)}, bf16[128,2048]{1,0:T(8,128)(2,1)S(1)}, bf16[128,2048]{1,0:T(8,128)(2,1)S(1)}, bf16[128,2048]{1,0:T(8,128)(2,1)S(1)}) custom-call(bf16[3,512,2048]{2,1,0:T(8,128)(2,1)} %get-tuple-element.87.refs_9_.x_ref, bf16[3,2048,2048]{2,1,0:T(8,128)(2,1)} %bitcast.84), custom_call_target="tpu_custom_call" | custom-call | flops 4294967296 | bytes 8388608 | tf_op jit(solution)/shard_map/down_forward/pallas_call | solution.py:871
  555.0 31.2 %collective-permute-done.45 = bf16[128,2048]{1,0:T(8,128)(2,1)S(1)} collective-permute-done((bf16[128,2048]{1,0:T(8,128)(2,1)S(1)}, bf16[128,2048]{1,0:T(8,128)(2,1)S(1)}, u32[]{:S(2)}, u32[]{:S(2)}) %collective-permute-start.45) | collective-permute-done | bytes 524320 | tf_op jit(solution)/shard_map/ppermute | solution.py:43
  (342 shorter events, 281.7 us)
Async XLA Ops:
  7.2 60.6 %all-gather.5.cloned.1.call-start = ((), (), s32[]{:S(2)}) async-start(), calls=%async_computation.3 | async-start | bytes 1310720 | tf_op jit(solution)/shard_map/all_gather | solution.py:190
  39.5 148.1 %all-gather.7.cloned.1.call-start = ((), (), s32[]{:S(2)}) async-start(), calls=%async_computation.4 | async-start | bytes 7077888 | tf_op jit(solution)/shard_map/all_gather | solution.py:197
  70.0 517.3 %reduce-scatter.2.cloned.1.call-start = ((), (), s32[]{:S(2)}) async-start(), calls=%async_computation.2 | async-start | bytes 15728640 | tf_op jit(solution)/shard_map/reduce_scatter | solution.py:807
  82.2 26.5 %collective-permute-start.12 = (bf16[512,384]{1,0:T(8,128)(2,1)}, bf16[512,384]{1,0:T(8,128)(2,1)}, u32[]{:S(2)}, u32[]{:S(2)}) collective-permute-start(bf16[512,384]{1,0:T(8,128)(2,1)} %copy-done.39), channel_id=1, source_target_pairs={{0,16},{4,20},{8,24},{12,28},{16,0},{20,4},{24,8},{28,12},{1,17},{... | collective-permute-start | bytes 1179656 | tf_op jit(solution)/shard_map/ppermute | solution.py:43
  82.8 26.3 %collective-permute-start.2 = (bf16[512,384]{1,0:T(8,128)(2,1)S(1)}, bf16[512,384]{1,0:T(8,128)(2,1)}, u32[]{:S(2)}, u32[]{:S(2)}) collective-permute-start(bf16[512,384]{1,0:T(8,128)(2,1)S(1)} %collective-permute-done.refs_3_), channel_id=1, source_target_pairs={{0,8},{4,12},{8,0},{12,4},{16,24},{20,28},{24,16},{28,20},{1,9},{5... | collective-permute-start | bytes 1179656 | tf_op jit(solution)/shard_map/ppermute | solution.py:43
  84.2 26.5 %collective-permute-start.9 = (bf16[512,384]{1,0:T(8,128)(2,1)}, bf16[512,384]{1,0:T(8,128)(2,1)S(1)}, u32[]{:S(2)}, u32[]{:S(2)}) collective-permute-start(bf16[512,384]{1,0:T(8,128)(2,1)} %copy-done.39), channel_id=1, source_target_pairs={{0,4},{4,0},{8,12},{12,8},{16,20},{20,16},{24,28},{28,24},{1,5},{5... | collective-permute-start | bytes 1179656 | tf_op jit(solution)/shard_map/ppermute | solution.py:43
  86.7 24.0 %collective-permute-start.1 = (bf16[512,384]{1,0:T(8,128)(2,1)S(1)}, bf16[512,384]{1,0:T(8,128)(2,1)S(1)}, u32[]{:S(2)}, u32[]{:S(2)}) collective-permute-start(bf16[512,384]{1,0:T(8,128)(2,1)S(1)} %collective-permute-done.refs_3_), channel_id=1, source_target_pairs={{0,4},{4,0},{8,12},{12,8},{16,20},{20,16},{24,28},{28,24},{1,5},{5... | collective-permute-start | bytes 1179656 | tf_op jit(solution)/shard_map/ppermute | solution.py:43
  161.8 25.8 %collective-permute-start.32 = (bf16[128,2048]{1,0:T(8,128)(2,1)S(1)}, bf16[128,2048]{1,0:T(8,128)(2,1)S(1)}, u32[]{:S(2)}, u32[]{:S(2)}) collective-permute-start(bf16[128,2048]{1,0:T(8,128)(2,1)S(1)} %bitcast.69), channel_id=1, source_target_pairs={{0,3},{1,2},{2,1},{3,0},{4,7},{5,6},{6,5},{7,4},{8,11},{9,10},{10,... | collective-permute-start | bytes 1572872 | tf_op jit(solution)/shard_map/ppermute | solution.py:43
  198.9 25.3 %collective-permute-start.34 = (bf16[128,2048]{1,0:T(8,128)(2,1)S(1)}, bf16[128,2048]{1,0:T(8,128)(2,1)S(1)}, u32[]{:S(2)}, u32[]{:S(2)}) collective-permute-start(bf16[128,2048]{1,0:T(8,128)(2,1)S(1)} %get-tuple-element.76.refs_0_.refs_1_.refs_5_), channel_id=1, source_target_pairs={{0,1},{1,0},{2,3},{3,2},{4,5},{5,4},{6,7},{7,6},{8,9},{9,8},{10,11... | collective-permute-start | bytes 1572872 | tf_op jit(solution)/shard_map/ppermute | solution.py:43
  214.8 25.1 %collective-permute-start.30 = (bf16[128,2048]{1,0:T(8,128)(2,1)S(1)}, bf16[128,2048]{1,0:T(8,128)(2,1)S(1)}, u32[]{:S(2)}, u32[]{:S(2)}) collective-permute-start(bf16[128,2048]{1,0:T(8,128)(2,1)S(1)} %collective-permute-done.29.refs_1_.refs_4_.refs_8_), channel_id=1, source_target_pairs={{0,1},{1,0},{2,3},{3,2},{4,5},{5,4},{6,7},{7,6},{8,9},{9,8},{10,11... | collective-permute-start | bytes 1572872 | tf_op jit(solution)/shard_map/ppermute | solution.py:43
  263.9 25.8 %collective-permute-start.35 = (bf16[2,1024,2048]{2,1,0:T(8,128)(2,1)}, bf16[2,1024,2048]{2,1,0:T(8,128)(2,1)S(1)}, u32[]{:S(2)}, u32[]{:S(2)}) collective-permute-start(bf16[2,1024,2048]{2,1,0:T(8,128)(2,1)} %shard_map.144), channel_id=1, source_target_pairs={{0,4},{4,0},{8,12},{12,8},{16,20},{20,16},{24,28},{28,24},{1,5},{5... | collective-permute-start | bytes 25165832 | tf_op jit(solution)/shard_map/ppermute | solution.py:43
  300.9 24.5 %collective-permute-start.37 = (bf16[128,2048]{1,0:T(8,128)(2,1)S(1)}, bf16[128,2048]{1,0:T(8,128)(2,1)S(1)}, u32[]{:S(2)}, u32[]{:S(2)}) collective-permute-start(bf16[128,2048]{1,0:T(8,128)(2,1)S(1)} %copy-done.30), channel_id=1, source_target_pairs={{0,1},{1,0},{2,3},{3,2},{4,5},{5,4},{6,7},{7,6},{8,9},{9,8},{10,11... | collective-permute-start | bytes 1572872 | tf_op jit(solution)/shard_map/ppermute | solution.py:43
  373.2 24.0 %collective-permute-start.63 = (bf16[128,2048]{1,0:T(8,128)(2,1)}, bf16[128,2048]{1,0:T(8,128)(2,1)}, u32[]{:S(2)}, u32[]{:S(2)}) collective-permute-start(bf16[128,2048]{1,0:T(8,128)(2,1)} %get-tuple-element.123.refs_1_.refs_5_), channel_id=1, source_target_pairs={{0,3},{1,2},{2,1},{3,0},{4,7},{5,6},{6,5},{7,4},{8,11},{9,10},{10,... | collective-permute-start | bytes 1572872 | tf_op jit(solution)/shard_map/ppermute | solution.py:43
  390.6 107.3 %all-to-all-start = ((bf16[4,128,1024]{2,1,0:T(8,128)(2,1)}), bf16[4,128,1024]{2,1,0:T(8,128)(2,1)}, u32[]{:S(2)}, u32[]{:S(2)}) async-start(bf16[4,128,1024]{2,1,0:T(8,128)(2,1)} %bitcast.77), calls=%async_computation | async-start | bytes 2097152 | tf_op jit(solution)/shard_map/all_to_all | solution.py:1163
  395.2 32.0 %collective-permute-start.62 = (bf16[128,2048]{1,0:T(8,128)(2,1)}, bf16[128,2048]{1,0:T(8,128)(2,1)}, u32[]{:S(2)}, u32[]{:S(2)}) collective-permute-start(bf16[128,2048]{1,0:T(8,128)(2,1)} %get-tuple-element.123.refs_1_.refs_5_), channel_id=1, source_target_pairs={{0,1},{1,0},{2,3},{3,2},{4,5},{5,4},{6,7},{7,6},{8,9},{9,8},{10,11... | collective-permute-start | bytes 1572872 | tf_op jit(solution)/shard_map/ppermute | solution.py:43
  397.2 55.2 %collective-permute-start.64 = (bf16[128,2048]{1,0:T(8,128)(2,1)}, bf16[128,2048]{1,0:T(8,128)(2,1)}, u32[]{:S(2)}, u32[]{:S(2)}) collective-permute-start(bf16[128,2048]{1,0:T(8,128)(2,1)} %collective-permute-done.63.refs_8_), channel_id=1, source_target_pairs={{0,1},{1,0},{2,3},{3,2},{4,5},{5,4},{6,7},{7,6},{8,9},{9,8},{10,11... | collective-permute-start | bytes 1572872 | tf_op jit(solution)/shard_map/ppermute | solution.py:43
  399.6 66.6 %collective-permute-start.51 = (bf16[128,2048]{1,0:T(8,128)(2,1)}, bf16[128,2048]{1,0:T(8,128)(2,1)}, u32[]{:S(2)}, u32[]{:S(2)}) collective-permute-start(bf16[128,2048]{1,0:T(8,128)(2,1)} %copy-done.16), channel_id=1, source_target_pairs={{0,3},{1,2},{2,1},{3,0},{4,7},{5,6},{6,5},{7,4},{8,11},{9,10},{10,... | collective-permute-start | bytes 1572872 | tf_op jit(solution)/shard_map/ppermute | solution.py:43
  404.7 51.2 %collective-permute-start.59 = (bf16[128,512]{1,0:T(8,128)(2,1)}, bf16[128,512]{1,0:T(8,128)(2,1)S(1)}, u32[]{:S(2)}, u32[]{:S(2)}) collective-permute-start(bf16[128,512]{1,0:T(8,128)(2,1)} %copy.85), channel_id=1, source_target_pairs={{0,1},{1,0},{2,3},{3,2},{4,5},{5,4},{6,7},{7,6},{8,9},{9,8},{10,11... | collective-permute-start | bytes 393224 | tf_op jit(solution)/shard_map/ppermute | solution.py:43
  406.4 49.5 %collective-permute-start.60 = (bf16[128,512]{1,0:T(8,128)(2,1)}, bf16[128,512]{1,0:T(8,128)(2,1)}, u32[]{:S(2)}, u32[]{:S(2)}) collective-permute-start(bf16[128,512]{1,0:T(8,128)(2,1)} %copy.86), channel_id=1, source_target_pairs={{0,2},{1,3},{2,0},{3,1},{4,6},{5,7},{6,4},{7,5},{8,10},{9,11},{10,... | collective-permute-start | bytes 393224 | tf_op jit(solution)/shard_map/ppermute | solution.py:43
  427.1 32.6 %collective-permute-start.61 = (bf16[128,512]{1,0:T(8,128)(2,1)}, bf16[128,512]{1,0:T(8,128)(2,1)S(1)}, u32[]{:S(2)}, u32[]{:S(2)}) collective-permute-start(bf16[128,512]{1,0:T(8,128)(2,1)} %copy.87), channel_id=1, source_target_pairs={{0,3},{1,2},{2,1},{3,0},{4,7},{5,6},{6,5},{7,4},{8,11},{9,10},{10,... | collective-permute-start | bytes 393224 | tf_op jit(solution)/shard_map/ppermute | solution.py:43
  452.4 34.0 %collective-permute-start.50 = (bf16[128,2048]{1,0:T(8,128)(2,1)S(1)}, bf16[128,2048]{1,0:T(8,128)(2,1)S(1)}, u32[]{:S(2)}, u32[]{:S(2)}) collective-permute-start(bf16[128,2048]{1,0:T(8,128)(2,1)S(1)} %copy-done.17), channel_id=1, source_target_pairs={{0,1},{1,0},{2,3},{3,2},{4,5},{5,4},{6,7},{7,6},{8,9},{9,8},{10,11... | collective-permute-start | bytes 1572872 | tf_op jit(solution)/shard_map/ppermute | solution.py:43
  466.2 40.8 %collective-permute-start.65 = (bf16[4,64,2048]{2,1,0:T(8,128)(2,1)}, bf16[4,64,2048]{2,1,0:T(8,128)(2,1)}, u32[]{:S(2)}, u32[]{:S(2)}) collective-permute-start(bf16[4,64,2048]{2,1,0:T(8,128)(2,1)} %get-tuple-element.128), channel_id=1, source_target_pairs={{0,4},{4,0},{8,12},{12,8},{16,20},{20,16},{24,28},{28,24},{1,5},{5... | collective-permute-start | bytes 3145736 | tf_op jit(solution)/shard_map/ppermute | solution.py:43
  539.1 47.0 %collective-permute-start.45 = (bf16[128,2048]{1,0:T(8,128)(2,1)S(1)}, bf16[128,2048]{1,0:T(8,128)(2,1)S(1)}, u32[]{:S(2)}, u32[]{:S(2)}) collective-permute-start(bf16[128,2048]{1,0:T(8,128)(2,1)S(1)} %get-tuple-element.103), channel_id=1, source_target_pairs={{0,2},{1,3},{2,0},{3,1},{4,6},{5,7},{6,4},{7,5},{8,10},{9,11},{10,... | collective-permute-start | bytes 1572872 | tf_op jit(solution)/shard_map/ppermute | solution.py:43
  542.2 43.9 %collective-permute-start.44 = (bf16[128,2048]{1,0:T(8,128)(2,1)S(1)}, bf16[128,2048]{1,0:T(8,128)(2,1)S(1)}, u32[]{:S(2)}, u32[]{:S(2)}) collective-permute-start(bf16[128,2048]{1,0:T(8,128)(2,1)S(1)} %get-tuple-element.101), channel_id=1, source_target_pairs={{0,1},{1,0},{2,3},{3,2},{4,5},{5,4},{6,7},{7,6},{8,9},{9,8},{10,11... | collective-permute-start | bytes 1572872 | tf_op jit(solution)/shard_map/ppermute | solution.py:43
  (107 other events, 2096.0 us)
Sparse Core Ops, SparseCore 0:
  39.6 28.1 all-gather.4
  70.3 62.9 all-gather.6
  300.0 125.7 reduce-scatter.1

commit v14 on v13

--- a/solution.py
+++ b/solution.py
@@ -19,6 +19,7 @@
 
 
 BF = jnp.bfloat16
+CTX, FSDP = "ctx", "fsdp"
 F32 = jnp.float32
 
 
@@ -74,33 +75,33 @@
 
 
 def ids():
-    return lax.axis_index("ctx"), lax.axis_index("fsdp")
+    return lax.axis_index(CTX), lax.axis_index(FSDP)
 
 
 def gather_pieces(weight, early):
     rows, columns = weight.shape
-    share = columns // lax.axis_size("ctx")
+    share = columns // lax.axis_size(CTX)
     half = rows // 2
-    mine = lax.dynamic_slice(weight, (0, lax.axis_index("ctx") * share), (rows, share))
+    mine = lax.dynamic_slice(weight, (0, lax.axis_index(CTX) * share), (rows, share))
     planes = {}
-    planes[3] = swap(mine, "fsdp", 3)
-    planes[1] = swap(mine, "fsdp", 1)
-    planes[2] = swap(after(planes[3], early), "fsdp", 1)
+    planes[3] = swap(mine, FSDP, 3)
+    planes[1] = swap(mine, FSDP, 1)
+    planes[2] = swap(after(planes[3], early), FSDP, 1)
     pieces = []
     for away in (1, 3, 2):
         first = planes[away]
-        along_x, along_y = swap(first, "ctx", 2), swap(first, "ctx", 4)
+        along_x, along_y = swap(first, CTX, 2), swap(first, CTX, 4)
         if away == 1:
-            corners = [(6, 0, swap(along_y, "ctx", 2))]
+            corners = [(6, 0, swap(along_y, CTX, 2))]
         elif away == 3:
-            corners = [(6, 0, swap(along_x, "ctx", 4))]
+            corners = [(6, 0, swap(along_x, CTX, 4))]
         else:
-            top, low = swap(along_y[:half], "ctx", 2), swap(along_x[half:], "ctx", 4)
+            top, low = swap(along_y[:half], CTX, 2), swap(along_x[half:], CTX, 4)
             corners = [(6, 0, jnp.concatenate([top, low], axis=0))]
         parts = [(0, 0, first), (2, 0, along_x), (4, 0, along_y)] + corners
         for offset, start, part in parts:
             pieces.append((away, offset, start, part))
-            pieces.append((away, offset + 1, start, swap(part, "ctx", 1)))
+            pieces.append((away, offset + 1, start, swap(part, CTX, 1)))
     return pieces, (planes[2], pieces[-2][3])
 
 
@@ -153,7 +154,7 @@
     me, plane = ids()
     rows_in, columns = own.shape
     rows, width = x.shape
-    share = columns // lax.axis_size("ctx")
+    share = columns // lax.axis_size(CTX)
     places = tuple((away, offset, start, part.shape[0]) for away, offset, start, part in pieces)
     arrays = [part for _, _, _, part in pieces]
     hbm, vmem = pl.BlockSpec(memory_space=pltpu.HBM), pl.BlockSpec(memory_space=pltpu.VMEM)
@@ -178,28 +179,28 @@
         cost_estimate=pl.CostEstimate(
             flops=2 * rows * width * columns, bytes_accessed=4 * width * columns, transcendentals=0
         ),
-        name="pieces_forward",
+        name="pieces",
     )(jnp.stack([me, plane]), x, in_hbm(own), *[in_hbm(part) for part in arrays], cosine, sine)
 
 
 def gather_blocks(weight, before_fsdp, before_ctx):
     rows, columns = weight.shape
     me, plane = ids()
-    share = columns // lax.axis_size("ctx")
+    share = columns // lax.axis_size(CTX)
     mine = lax.dynamic_slice(weight, (0, me * share), (rows, share))
-    planes = lax.all_gather(after(mine, before_fsdp), "fsdp")
+    planes = lax.all_gather(after(mine, before_fsdp), FSDP)
     others = jnp.stack(
         [
             lax.dynamic_index_in_dim(planes, plane ^ away, 0, keepdims=False)
             for away in range(1, planes.shape[0])
         ]
     )
-    return lax.all_gather(after(others, before_ctx), "ctx")
+    return lax.all_gather(after(others, before_ctx), CTX)
 
 
 def whole_of(own, blocks):
     ctx_count, others, rows, share = blocks.shape
-    plane = lax.axis_index("fsdp")
+    plane = lax.axis_index(FSDP)
     columns = ctx_count * share
     full = jnp.zeros(((others + 1) * rows, columns), own.dtype)
     full = lax.dynamic_update_slice(full, own, (plane * rows, 0))
@@ -280,7 +281,7 @@
             bytes_accessed=2 * own.size * (blocks.shape[1] + 1),
             transcendentals=0,
         ),
-        name="out_back" if back else "out_forward",
+        name="out_b" if back else "out_f",
     )(jnp.stack(ids()), x, in_hbm(own), in_hbm(blocks), *extra)
 
 
@@ -352,22 +353,22 @@
             bytes_accessed=2 * width * columns,
             transcendentals=0,
         ),
-        name="one_back",
+        name="one_b",
     )(query_part, pair_part, in_hbm(weight), hidden, gain, residual_grad)
 
 
 def send_rows(values):
-    if lax.axis_size("fsdp") != 4:
+    if lax.axis_size(FSDP) != 4:
         return fetch_rows(values)
-    third = swap(values, "fsdp", 3)
-    return [values, swap(values, "fsdp", 1), third]
+    third = swap(values, FSDP, 3)
+    return [values, swap(values, FSDP, 1), third]
 
 
 def relay_rows(planes):
-    if lax.axis_size("fsdp") != 4:
+    if lax.axis_size(FSDP) != 4:
         return planes
     values, first, third = planes
-    return [values, first, swap(third, "fsdp", 1), third]
+    return [values, first, swap(third, FSDP, 1), third]
 
 
 def pass_rows(values):
@@ -375,41 +376,41 @@
 
 
 def fetch_rows(values):
-    count = lax.axis_size("fsdp")
-    return [values] + [swap(values, "fsdp", away) for away in range(1, count)]
+    count = lax.axis_size(FSDP)
+    return [values] + [swap(values, FSDP, away) for away in range(1, count)]
 
 
 def sum_rows(parts, forward):
     count = len(parts)
     if count == 4 and forward:
-        passed = swap(parts[2], "fsdp", 1).astype(F32)
-        one = swap(parts[1], "fsdp", 1)
-        third = swap((parts[3].astype(F32) + passed).astype(BF), "fsdp", 3)
+        passed = swap(parts[2], FSDP, 1).astype(F32)
+        one = swap(parts[1], FSDP, 1)
+        third = swap((parts[3].astype(F32) + passed).astype(BF), FSDP, 3)
         return [parts[0], one, third]
-    return parts[:1] + [swap(parts[i], "fsdp", i) for i in range(1, count)]
+    return parts[:1] + [swap(parts[i], FSDP, i) for i in range(1, count)]
 
 
 def by_feature(values):
     rows, width = values.shape
-    ctx_count, fsdp_count = lax.axis_size("ctx"), lax.axis_size("fsdp")
+    ctx_count, fsdp_count = lax.axis_size(CTX), lax.axis_size(FSDP)
     blocks = values.reshape(rows, ctx_count, fsdp_count, width // (ctx_count * fsdp_count))
     return blocks.transpose(0, 2, 1, 3).reshape(rows, width)
 
 
 def sum_over_ctx(part_for):
-    pairs = lax.axis_size("ctx") // 2
+    pairs = lax.axis_size(CTX) // 2
     sent = jnp.stack([part_for(2 * pair + 1).astype(BF) for pair in range(pairs)])
-    got = swap(sent, "ctx", 1)
+    got = swap(sent, CTX, 1)
     sums = [part_for(2 * pair).astype(F32) + got[pair].astype(F32) for pair in range(pairs)]
     total = sums[0]
     for pair in range(1, pairs):
-        total = total + swap(sums[pair].astype(BF), "ctx", 2 * pair).astype(F32)
+        total = total + swap(sums[pair].astype(BF), CTX, 2 * pair).astype(F32)
     return total
 
 
 def ctx_rows_sum(values):
-    height = values.shape[0] // lax.axis_size("ctx")
-    me = lax.axis_index("ctx")
+    height = values.shape[0] // lax.axis_size(CTX)
+    me = lax.axis_index(CTX)
 
     def part(offset):
         return lax.dynamic_slice(
@@ -420,22 +421,22 @@
 
 
 def key_offsets():
-    count = lax.axis_size("ctx")
+    count = lax.axis_size(CTX)
     return list(range(0, count, 2)) + list(range(1, count, 2))
 
 
 def gather_keys(piece):
-    same = [piece] + [swap(piece, "ctx", far) for far in range(2, lax.axis_size("ctx"), 2)]
+    same = [piece] + [swap(piece, CTX, far) for far in range(2, lax.axis_size(CTX), 2)]
     mine = jnp.concatenate(same, axis=0)
-    return mine, swap(mine, "ctx", 1)
+    return mine, swap(mine, CTX, 1)
 
 
 def sum_pairs(kept, sent, cosine, sine):
     _, count, width = kept.shape
-    pairs = lax.axis_size("ctx") // 2
-    got = swap(sent, "ctx", 1)
+    pairs = lax.axis_size(CTX) // 2
+    got = swap(sent, CTX, 1)
     sums = (kept.astype(F32) + got.astype(F32)).reshape(2, pairs, count // pairs, width)
-    far = [swap(sums[:, pair].astype(BF), "ctx", 2 * pair) for pair in range(1, pairs)]
+    far = [swap(sums[:, pair].astype(BF), CTX, 2 * pair) for pair in range(1, pairs)]
     return pair_turn(sums[:, 0], far, cosine, sine), got
 
 
@@ -622,7 +623,7 @@
             bytes_accessed=8 * count * KV * HD,
             transcendentals=rows * H * count,
         ),
-        name="attend_back",
+        name="att_b",
     )(queries, grads, attended, *arrays, key_anchor, own_anchor, logs, cosine, sine)
 
 
@@ -647,11 +648,11 @@
 
 def pair_turn(own, got, cosine, sine):
     _, rows, width = own.shape
-    copies = lax.axis_size("fsdp")
+    copies = lax.axis_size(FSDP)
     return pl.pallas_call(
         lambda *refs: pair_turn_kernel(copies, *refs),
         out_shape=jax.ShapeDtypeStruct((copies * rows, 2 * width), BF),
-        name="pair_turn",
+        name="turned",
     )(own, *got, cosine, sine)
 
 
@@ -723,7 +724,7 @@
             bytes_accessed=4 * width * hidden,
             transcendentals=rows * hidden,
         ),
-        name="ffn_middle",
+        name="ffn",
     )(*blocks, act_grad, weights, *earlier)
     return out[0], list(out[1:])
 
@@ -746,7 +747,7 @@
     count = len(rows_of)
     rows, width = rows_of[0].shape
     matrices, _, hidden = parts.shape
-    ctx_count = lax.axis_size("ctx")
+    ctx_count = lax.axis_size(CTX)
     height = width // ctx_count
     kept = got is not None
 
@@ -788,23 +789,23 @@
 
 
 def ffn_gradient(rows_in, rows_out, parts):
-    count = lax.axis_size("ctx")
+    count = lax.axis_size(CTX)
     if count % 4 or (rows_in[0].shape[1] // count) % 128:
         left, grad = (jnp.concatenate(rows, axis=0) for rows in (rows_in, rows_out))
         products = [tn(left, parts[0]), tn(left, parts[1]), tn(grad, parts[2])]
         products = jnp.stack(products, axis=1).astype(BF)
-        return lax.psum_scatter(products, "ctx", scatter_dimension=0, tiled=True), parts
+        return lax.psum_scatter(products, CTX, scatter_dimension=0, tiled=True), parts
     calls = ((rows_out, 2, 1), (rows_in, 0, 2))
     got = []
     for rows_of, first, size in calls:
         sent = half_products(rows_of, parts, first, size, None, [])
-        got.append(swap(sent, "ctx", 1))
+        got.append(swap(sent, CTX, 1))
     kept = []
     for (rows_of, first, size), part in zip(calls, got):
         kept = [half_products(rows_of, parts, first, size, part, kept)]
     groups = [list(range(core, count, 2)) for core in range(2)]
     kept = kept[0].transpose(1, 0, 2)
-    rows = lax.psum_scatter(kept, "ctx", scatter_dimension=0, tiled=True, axis_index_groups=groups)
+    rows = lax.psum_scatter(kept, CTX, scatter_dimension=0, tiled=True, axis_index_groups=groups)
     return rows, after(parts, kept)
 
 
@@ -812,7 +813,9 @@
     y_ref[...] = x_ref[...].astype(F32)
 
 
-def widened(values):
+def widened(values, fast):
+    if not fast:
+        return values.astype(F32)
     values = values.transpose(1, 0, 2)
     matrices, rows, hidden = values.shape
     block = pl.BlockSpec((1, rows // 2, hidden), lambda k, i: (k, i, 0))
@@ -823,8 +826,8 @@
         in_specs=[block],
         out_specs=block,
         compiler_params=pltpu.CompilerParams(vmem_limit_bytes=16 << 20),
-        name="widened",
-    )(values).transpose(1, 0, 2)
+        name="wide",
+    )(in_hbm(values)).transpose(1, 0, 2)
 
 
 def down_back_kernel(count, *refs):
@@ -852,7 +855,7 @@
             bytes_accessed=2 * width * hidden,
             transcendentals=0,
         ),
-        name="down_back",
+        name="act",
     )(*blocks, weights)
 
 
@@ -885,7 +888,7 @@
             bytes_accessed=2 * width * hidden,
             transcendentals=0,
         ),
-        name="down_forward",
+        name="down",
     )(in_hbm(parts), weights)
 
 
@@ -931,7 +934,7 @@
 
 
 def share_products(lefts, rights, terms):
-    ctx_count = lax.axis_size("ctx")
+    ctx_count = lax.axis_size(CTX)
     pairs = ctx_count // 2
     count = len(lefts[0])
     rows, width = lefts[0][0].shape
@@ -968,14 +971,14 @@
             bytes_accessed=2 * (count * rows + columns) * width,
             transcendentals=0,
         ),
-        name="share_terms" if terms else "share_products",
+        name="share_t" if terms else "share",
     )(jnp.stack(ids()), *flat_lefts, *flat_rights, *[term[None] for term in terms])
 
 
 def in_fsdp_order(value):
     if not isinstance(value, list):
         return value
-    plane = lax.axis_index("fsdp")
+    plane = lax.axis_index(FSDP)
     stacked = jnp.stack(value)
     parts = [
         lax.dynamic_index_in_dim(stacked, plane ^ away, 0, keepdims=False)
@@ -985,17 +988,17 @@
 
 
 def share_start(lefts, rights, terms):
-    pairs = lax.axis_size("ctx") // 2
+    pairs = lax.axis_size(CTX) // 2
     if (lefts[0][0].shape[1] // pairs) % 128:
         values = [tn(in_fsdp_order(a), in_fsdp_order(b)) for a, b in zip(lefts, rights)]
         values += [jnp.broadcast_to(term[:, None], (term.shape[0], 128)) for term in terms]
         return [ctx_rows_sum(jnp.concatenate(values, axis=1))]
     kept, sent = share_products(lefts, rights, terms)
-    got = swap(sent, "ctx", 1)
+    got = swap(sent, CTX, 1)
     parts = [kept[0], got[0]]
     for pair in range(1, pairs):
         part = (kept[pair].astype(F32) + got[pair].astype(F32)).astype(BF)
-        parts.append(swap(part, "ctx", 2 * pair))
+        parts.append(swap(part, CTX, 2 * pair))
     return parts
 
 
@@ -1020,7 +1023,7 @@
         finish_kernel,
         out_shape=(jax.ShapeDtypeStruct((rows, columns), F32), wide, wide),
         compiler_params=pltpu.CompilerParams(vmem_limit_bytes=16 << 20),
-        name="finish_last",
+        name="finish",
     )(weight_rows, gains, *parts)
 
 
@@ -1032,12 +1035,12 @@
 
 
 def own_rows_of(values, height):
-    index = lax.axis_index("ctx") * lax.axis_size("fsdp") + lax.axis_index("fsdp")
+    index = lax.axis_index(CTX) * lax.axis_size(FSDP) + lax.axis_index(FSDP)
     return lax.dynamic_slice_in_dim(values, index * height, height, 0)
 
 
 def feature_parts(values):
-    count, plane = lax.axis_size("fsdp"), lax.axis_index("fsdp")
+    count, plane = lax.axis_size(FSDP), lax.axis_index(FSDP)
     values = by_feature(values)
     rows, width = values.shape
     width //= count
@@ -1048,18 +1051,18 @@
 
 
 def feature_rows(parts):
-    return [swap(part, "fsdp", away) if away else part for away, part in enumerate(parts)]
+    return [swap(part, FSDP, away) if away else part for away, part in enumerate(parts)]
 
 
 def own_features(terms):
-    ctx_count, fsdp_count = lax.axis_size("ctx"), lax.axis_size("fsdp")
+    ctx_count, fsdp_count = lax.axis_size(CTX), lax.axis_size(FSDP)
     total = jnp.stack(terms)
     away = 1
     while away < fsdp_count:
-        total = total + swap(total, "fsdp", away)
+        total = total + swap(total, FSDP, away)
         away *= 2
     blocks = total.reshape(len(terms), ctx_count, fsdp_count, -1)
-    own = lax.dynamic_index_in_dim(blocks, lax.axis_index("fsdp"), 2, keepdims=False)
+    own = lax.dynamic_index_in_dim(blocks, lax.axis_index(FSDP), 2, keepdims=False)
     own = own.reshape(len(terms), -1)
     return [own[i] for i in range(len(terms))]
 
@@ -1075,7 +1078,7 @@
     out_weight,
     ffn_weight,
 ):
-    ctx_count, fsdp_count = lax.axis_size("ctx"), lax.axis_size("fsdp")
+    ctx_count, fsdp_count = lax.axis_size(CTX), lax.axis_size(FSDP)
     me, _ = ids()
     rows = hidden_in.shape[1]
     queries_width, kv_width = H * HD, KV * HD
@@ -1142,7 +1145,7 @@
     parts = parts[0]
     sum_grad = share_finish(sum_rows(partial, True))
     ffn_weight_grad, parts = ffn_gradient(rows_in, rows_out, parts)
-    ffn_weight_grad = widened(ffn_weight_grad)
+    ffn_weight_grad = widened(ffn_weight_grad, fast)
     out_partial = list(down_forward(parts, ffn_parts, fsdp_count))
 
     unit_two = residual * scale_two
@@ -1160,7 +1163,7 @@
     query_planes = pass_rows(query_part)
     pair_copies, near = sum_pairs(kept, sent, cosine, sine)
     own_residual = feature_rows(feature_parts(after(residual_bf, near)))
-    all_pair = lax.all_to_all(pair_copies, "fsdp", split_axis=0, concat_axis=0, tiled=True)
+    all_pair = lax.all_to_all(pair_copies, FSDP, split_axis=0, concat_axis=0, tiled=True)
     input_grad = one_back(
         query_part, pair_copies, qkv_full, hidden_in[0], attn_gain, residual_grad
     )
@@ -1196,24 +1199,24 @@
         layer,
         mesh=mesh,
         in_specs=(
-            P("fsdp", "ctx", None),
-            P("fsdp", "ctx", None),
-            P("fsdp", "ctx"),
+            P(FSDP, CTX, None),
+            P(FSDP, CTX, None),
+            P(FSDP, CTX),
             P(),
             P(),
             P(),
-            P("fsdp", None),
-            P("fsdp", None),
-            P(None, None, "fsdp"),
+            P(FSDP, None),
+            P(FSDP, None),
+            P(None, None, FSDP),
         ),
         out_specs=(
-            P("fsdp", "ctx", None),
-            P("fsdp", "ctx", None),
-            P(("ctx", "fsdp"), None),
-            P(("ctx", "fsdp"), None),
-            P("ctx", None, "fsdp"),
-            P(("ctx", "fsdp")),
-            P(("ctx", "fsdp")),
+            P(FSDP, CTX, None),
+            P(FSDP, CTX, None),
+            P((CTX, FSDP), None),
+            P((CTX, FSDP), None),
+            P(CTX, None, FSDP),
+            P((CTX, FSDP)),
+            P((CTX, FSDP)),
         ),
         check_vma=False,
     )

time: 601 us -> 601 us (level)
    unnamed x125 -> x123, local copies, waits for them, and re-layouts: 22.2 us -> 20.2 us
where the time goes in v14:
time: 601 us; the launch traced here: 599 us
  waiting for transfers between devices  287 us (48%)
  Pallas kernels  163 us (27%)
  starting transfers between devices  88.1 us (15%)
  local copies, waits for them, and re-layouts  34.6 us (6%)
  between operations  14.5 us (2%)
  other arithmetic  12.6 us (2%)
    ppermute x69, waiting for transfers between devices, swap(): return lax.ppermute(value, axis, [(i, i ^ offset) for i in range(count)])  276 us
    ppermute x69, starting transfers between devices, swap(): return lax.ppermute(value, axis, [(i, i ^ offset) for i in range(count)])  83.4 us
    pallas_call x4, Pallas kernels, half_products(): pl.pallas_call(lambda *refs: products_kernel(count, kept, *refs), grid_sp...  32.8 us
    pallas_call x2, Pallas kernels, ffn_middle(): pl.pallas_call(lambda *refs: ffn_kernel(len(blocks), len(earlier), *refs)...  28.1 us
    unnamed x123, local copies, waits for them, and re-layouts  20.2 us
    pallas_call x1, Pallas kernels, attend_back(): pl.pallas_call(lambda *refs: attend_back_kernel(KEY_CHUNK, *refs), grid=(...  20 us
    pallas_call x1, Pallas kernels, attend(): pl.pallas_call(lambda *refs: attend_kernel(KEY_CHUNK, *refs), grid=(KV,),...  12.8 us
    pallas_call x2, Pallas kernels, out_call(): pl.pallas_call(lambda *refs: out_kernel(back, *refs), out_shape=out_shape...  12.3 us
  transfers between devices with their start and end apart: 73, of which 43 were waited for; matrix products, arithmetic and copies ran while one was open for 5% of the time, Pallas kernels for 20%

profile of v14, /device:TPU:0, one launch (start us, length us, event | category | flops | bytes accessed | tf_op | source)
XLA Modules:
  0.0 599.4 jit_solution(3004077962735698706)
XLA Ops:
  22.9 8.1 %collective-permute-start.16 = (bf16[512,384]{1,0:T(8,128)(2,1)S(1)}, bf16[512,384]{1,0:T(8,128)(2,1)S(1)}, u32[]{:S(2)}, u32[]{:S(2)}) collective-permute-start(bf16[512,384]{1,0:T(8,128)(2,1)S(1)} %collective-permute-done.8.refs_11_), channel_id=1, source_target_pairs={{0,1},{1,0},{2,3},{3,2},{4,5},{5,4},{6,7},{7,6},{8,9},{9,8},{10,11... | collective-permute-start | bytes 1179656 | tf_op jit(solution)/shard_map/ppermute | solution.py:44
  57.1 10.8 %all-gather.5.cloned.1.call-done = bf16[2048,256]{1,0:T(8,128)(2,1)} async-done(((bf16[512,256]{1,0:T(8,128)(2,1)}), bf16[2048,256]{1,0:T(8,128)(2,1)}) %all-gather.5.cloned.1.call-update) | async-done | bytes 1048592 | tf_op jit(solution)/shard_map/all_gather | solution.py:191
  86.7 11.4 %collective-permute-done.4.refs_7_ = bf16[512,384]{1,0:T(8,128)(2,1)} collective-permute-done((bf16[512,384]{1,0:T(8,128)(2,1)S(1)}, bf16[512,384]{1,0:T(8,128)(2,1)}, u32[]{:S(2)}, u32[]{:S(2)}) %collective-permute-start.4) | collective-permute-done | bytes 393248 | tf_op jit(solution)/shard_map/ppermute | solution.py:44
  98.1 10.6 %collective-permute-done.12.refs_15_ = bf16[512,384]{1,0:T(8,128)(2,1)} collective-permute-done((bf16[512,384]{1,0:T(8,128)(2,1)}, bf16[512,384]{1,0:T(8,128)(2,1)}, u32[]{:S(2)}, u32[]{:S(2)}) %collective-permute-start.12) | collective-permute-done | bytes 393248 | tf_op jit(solution)/shard_map/ppermute | solution.py:44
  111.3 17.0 %collective-permute-done.14.refs_17_ = bf16[512,384]{1,0:T(8,128)(2,1)S(1)} collective-permute-done((bf16[512,384]{1,0:T(8,128)(2,1)}, bf16[512,384]{1,0:T(8,128)(2,1)S(1)}, u32[]{:S(2)}, u32[]{:S(2)}) %collective-permute-start.14) | collective-permute-done | bytes 393248 | tf_op jit(solution)/shard_map/ppermute | solution.py:44
  135.2 9.6 %pieces.1 = (bf16[128,2048]{1,0:T(8,128)(2,1)S(1)}, bf16[128,1024]{1,0:T(8,128)(2,1)S(1)}, bf16[2048,3072]{1,0:T(8,128)(2,1)}) custom-call(s32[2]{0:T(128)S(1)} %pad_add_fusion.refs_0_, bf16[128,2048]{1,0:T(8,128)(2,1)S(1)} %fusion.2.refs_1_, bf16[512,3072]{1,0:T(8,128)(2,1)} %refs_2_.3, bf16[512,384]{1,0:T(8,128)(2,1)} %copy-done.40, ...), custom_call_target="tpu_custom_call" | custom-call | flops 1610612736 | bytes 25165824 | tf_op jit(solution)/shard_map/pieces/pallas_call | solution.py:161
  164.1 12.8 %attend.1 = (bf16[128,2048]{1,0:T(8,128)(2,1)}, f32[128,2048]{1,0:T(8,128)S(1)}, f32[8,1,512]{2,1,0:T(1,128)S(1)}) custom-call(bf16[128,2048]{1,0:T(8,128)(2,1)S(1)} %get-tuple-element.70.refs_0_, bf16[512,1024]{1,0:T(8,128)(2,1)S(1)} %constant_dynamic-update-slice_fusion.3.refs_1_.refs_2_.refs_3_.refs_4_, ...), custom_call_target="tpu_custom_call" | custom-call | flops 1073741824 | bytes 2097152 | tf_op jit(solution)/shard_map/attend/pallas_call | solution.py:537
  177.9 9.7 %collective-permute-done.32.refs_3_.refs_4_.refs_8_ = bf16[128,2048]{1,0:T(8,128)(2,1)S(1)} collective-permute-done((bf16[128,2048]{1,0:T(8,128)(2,1)S(1)}, bf16[128,2048]{1,0:T(8,128)(2,1)S(1)}, u32[]{:S(2)}, u32[]{:S(2)}) %collective-permute-start.32) | collective-permute-done | bytes 524320 | tf_op jit(solution)/shard_map/ppermute | solution.py:44
  203.2 8.6 %act.1.refs_2_ = f32[512,2048]{1,0:T(8,128)} custom-call(bf16[128,2048]{1,0:T(8,128)(2,1)S(1)} %bitcast.70, bf16[128,2048]{1,0:T(8,128)(2,1)S(1)} %collective-permute-done.31.refs_1_.refs_2_.refs_6_, bf16[128,2048]{1,0:T(8,128)(2,1)S(1)} %collective-permute-done.33.refs_2_.refs_3_.refs_7_, ...), custom_call_target="tpu_custom_call" | custom-call | flops 4294967296 | bytes 8388608 | tf_op jit(solution)/shard_map/act/pallas_call | solution.py:844
  224.1 14.0 %ffn.2 = (bf16[3,512,2048]{2,1,0:T(8,128)(2,1)}, f32[128,2048]{1,0:T(8,128)S(1)}, bf16[128,2048]{1,0:T(8,128)(2,1)S(1)}) custom-call(bf16[128,2048]{1,0:T(8,128)(2,1)S(1)} %get-tuple-element.76.refs_0_.refs_1_.refs_5_, bf16[128,2048]{1,0:T(8,128)(2,1)S(1)} %collective-permute-done.34.refs_1_.refs_2_.refs_6_, f32[512,2048]{1,0:T(8,128)} %act.1.refs_2_, ...), custom_call_target="tpu_custom_call" | custom-call | flops 8589934592 | bytes 16777216 | tf_op jit(solution)/shard_map/ffn/pallas_call | solution.py:705
  239.9 14.0 %ffn.3 = (bf16[3,512,2048]{2,1,0:T(8,128)(2,1)}, bf16[128,2048]{1,0:T(8,128)(2,1)S(1)}, f32[128,2048]{1,0:T(8,128)S(1)}) custom-call(bf16[128,2048]{1,0:T(8,128)(2,1)S(1)} %collective-permute-done.30.refs_0_.refs_3_.refs_7_, bf16[128,2048]{1,0:T(8,128)(2,1)S(1)} %collective-permute-done.29.refs_1_.refs_4_.refs_8_, ...), custom_call_target="tpu_custom_call", output_to_operand_aliasing={{0}: (4, {})} | custom-call | flops 8589934592 | bytes 16777216 | tf_op jit(solution)/shard_map/ffn/pallas_call | solution.py:705
  254.0 9.9 %shard_map.144 = bf16[2,1024,2048]{2,1,0:T(8,128)(2,1)} custom-call(s32[2]{0:T(128)S(1)} %pad_add_fusion.refs_0_, bf16[128,2048]{1,0:T(8,128)(2,1)S(1)} %get-tuple-element.76.refs_0_.refs_1_.refs_5_, bf16[128,2048]{1,0:T(8,128)(2,1)S(1)} %collective-permute-done.34.refs_1_.refs_2_.refs_6_, ...), custom_call_target="tpu_custom_call" | custom-call | flops 4294967296 | bytes 8388608 | tf_op jit(solution)/shard_map/pallas_call | solution.py:767
  270.7 12.5 %collective-permute-done.36.refs_10_ = bf16[1,1024,2048]{2,1,0:T(8,128)(2,1)S(1)} collective-permute-done((bf16[1,1024,2048]{2,1,0:T(8,128)(2,1)}, bf16[1,1024,2048]{2,1,0:T(8,128)(2,1)S(1)}, u32[]{:S(2)}, u32[]{:S(2)}) %collective-permute-start.36) | collective-permute-done | bytes 4194336 | tf_op jit(solution)/shard_map/ppermute | solution.py:44
  289.6 10.2 %shard_map.147 = bf16[3,1024,2048]{2,1,0:T(8,128)(2,1)} custom-call(s32[2]{0:T(128)S(1)} %pad_add_fusion.refs_0_, bf16[128,2048]{1,0:T(8,128)(2,1)S(1)} %get-tuple-element.76.refs_0_.refs_1_.refs_5_, bf16[128,2048]{1,0:T(8,128)(2,1)S(1)} %collective-permute-done.34.refs_1_.refs_2_.refs_6_, ...), custom_call_target="tpu_custom_call", output_to_operand_aliasing={{}: (11, {})} | custom-call | flops 4294967296 | bytes 8388608 | tf_op jit(solution)/shard_map/pallas_call | solution.py:767
  301.9 13.0 %collective-permute-done.38 = bf16[128,2048]{1,0:T(8,128)(2,1)S(1)} collective-permute-done((bf16[128,2048]{1,0:T(8,128)(2,1)}, bf16[128,2048]{1,0:T(8,128)(2,1)S(1)}, u32[]{:S(2)}, u32[]{:S(2)}) %collective-permute-start.38) | collective-permute-done | bytes 524320 | tf_op jit(solution)/shard_map/ppermute | solution.py:44
  317.2 8.1 %collective-permute-done.37 = bf16[128,2048]{1,0:T(8,128)(2,1)S(1)} collective-permute-done((bf16[128,2048]{1,0:T(8,128)(2,1)S(1)}, bf16[128,2048]{1,0:T(8,128)(2,1)S(1)}, u32[]{:S(2)}, u32[]{:S(2)}) %collective-permute-start.37) | collective-permute-done | bytes 524320 | tf_op jit(solution)/shard_map/ppermute | solution.py:44
  325.3 13.2 %collective-permute-done.39 = bf16[128,2048]{1,0:T(8,128)(2,1)S(1)} collective-permute-done((bf16[128,2048]{1,0:T(8,128)(2,1)S(1)}, bf16[128,2048]{1,0:T(8,128)(2,1)S(1)}, u32[]{:S(2)}, u32[]{:S(2)}) %collective-permute-start.39) | collective-permute-done | bytes 524320 | tf_op jit(solution)/shard_map/ppermute | solution.py:44
  346.4 20.0 %att_b.1 = (bf16[128,2048]{1,0:T(8,128)(2,1)S(1)}, bf16[2,512,512]{2,1,0:T(8,128)(2,1)S(1)}, bf16[2,512,512]{2,1,0:T(8,128)(2,1)S(1)}) custom-call(bf16[128,2048]{1,0:T(8,128)(2,1)S(1)} %copy-done.23, bf16[128,2048]{1,0:T(8,128)(2,1)S(1)} %out_b.1.refs_1_, f32[128,2048]{1,0:T(8,128)S(1)} %copy-done.34, bf16[512,1024]{1,0:T(8,128)(2,1)} %copy-done.20, ...), custom_call_target="tpu_custom_call" | custom-call | flops 2684354560 | bytes 4194304 | tf_op jit(solution)/shard_map/att_b/pallas_call | solution.py:602
  411.0 16.1 %collective-permute-done.62.refs_6_ = bf16[128,2048]{1,0:T(8,128)(2,1)} collective-permute-done((bf16[128,2048]{1,0:T(8,128)(2,1)}, bf16[128,2048]{1,0:T(8,128)(2,1)}, u32[]{:S(2)}, u32[]{:S(2)}) %collective-permute-start.62) | collective-permute-done | bytes 524320 | tf_op jit(solution)/shard_map/ppermute | solution.py:44
  430.7 8.9 %one_b.1 = f32[128,2048]{1,0:T(8,128)} custom-call(bf16[128,2048]{1,0:T(8,128)(2,1)S(1)} %copy-done.16, bf16[512,1024]{1,0:T(8,128)(2,1)S(1)} %copy-done.4, bf16[2048,3072]{1,0:T(8,128)(2,1)} %get-tuple-element.98.w_ref, bf16[128,2048]{1,0:T(8,128)(2,1)S(1)} %bitcast.76, f32[1,2048]{1,0:T(1,128)S(1)} %bitcast.78, f32[128,2048]{1,0:T(8,128)S(1)} %copy-done.7), custom_call_target="tpu_custom_call" | custom-call | flops 1610612736 | bytes 12582912 | tf_op jit(solution)/shard_map/one_b/pallas_call | solution.py:337
  439.6 12.8 %collective-permute-done.64.refs_7_ = bf16[128,2048]{1,0:T(8,128)(2,1)} collective-permute-done((bf16[128,2048]{1,0:T(8,128)(2,1)}, bf16[128,2048]{1,0:T(8,128)(2,1)}, u32[]{:S(2)}, u32[]{:S(2)}) %collective-permute-start.64) | collective-permute-done | bytes 524320 | tf_op jit(solution)/shard_map/ppermute | solution.py:44
  468.2 12.7 %collective-permute-done.53 = f32[1,2048]{1,0:T(1,128)S(1)} collective-permute-done((f32[1,2048]{1,0:T(1,128)S(1)}, f32[1,2048]{1,0:T(1,128)S(1)}, u32[]{:S(2)}, u32[]{:S(2)}) %collective-permute-start.53) | collective-permute-done | bytes 8224 | tf_op jit(solution)/shard_map/ppermute | solution.py:44
  530.2 7.9 %down.1 = (f32[128,2048]{1,0:T(8,128)S(1)}, bf16[128,2048]{1,0:T(8,128)(2,1)S(1)}, bf16[128,2048]{1,0:T(8,128)(2,1)S(1)}, bf16[128,2048]{1,0:T(8,128)(2,1)S(1)}) custom-call(bf16[3,512,2048]{2,1,0:T(8,128)(2,1)} %get-tuple-element.87.refs_9_.x_ref, bf16[3,2048,2048]{2,1,0:T(8,128)(2,1)} %bitcast.83), custom_call_target="tpu_custom_call" | custom-call | flops 4294967296 | bytes 8388608 | tf_op jit(solution)/shard_map/down/pallas_call | solution.py:874
  554.9 31.2 %collective-permute-done.45 = bf16[128,2048]{1,0:T(8,128)(2,1)S(1)} collective-permute-done((bf16[128,2048]{1,0:T(8,128)(2,1)S(1)}, bf16[128,2048]{1,0:T(8,128)(2,1)S(1)}, u32[]{:S(2)}, u32[]{:S(2)}) %collective-permute-start.45) | collective-permute-done | bytes 524320 | tf_op jit(solution)/shard_map/ppermute | solution.py:44
  (340 shorter events, 281.9 us)
Async XLA Ops:
  7.2 60.6 %all-gather.5.cloned.1.call-start = ((), (), s32[]{:S(2)}) async-start(), calls=%async_computation.3 | async-start | bytes 1310720 | tf_op jit(solution)/shard_map/all_gather | solution.py:191
  39.5 148.1 %all-gather.7.cloned.1.call-start = ((), (), s32[]{:S(2)}) async-start(), calls=%async_computation.4 | async-start | bytes 7077888 | tf_op jit(solution)/shard_map/all_gather | solution.py:198
  70.0 517.1 %reduce-scatter.2.cloned.1.call-start = ((), (), s32[]{:S(2)}) async-start(), calls=%async_computation.2 | async-start | bytes 15728640 | tf_op jit(solution)/shard_map/reduce_scatter | solution.py:808
  82.2 26.5 %collective-permute-start.12 = (bf16[512,384]{1,0:T(8,128)(2,1)}, bf16[512,384]{1,0:T(8,128)(2,1)}, u32[]{:S(2)}, u32[]{:S(2)}) collective-permute-start(bf16[512,384]{1,0:T(8,128)(2,1)} %copy-done.38), channel_id=1, source_target_pairs={{0,16},{4,20},{8,24},{12,28},{16,0},{20,4},{24,8},{28,12},{1,17},{... | collective-permute-start | bytes 1179656 | tf_op jit(solution)/shard_map/ppermute | solution.py:44
  82.8 26.3 %collective-permute-start.2 = (bf16[512,384]{1,0:T(8,128)(2,1)S(1)}, bf16[512,384]{1,0:T(8,128)(2,1)}, u32[]{:S(2)}, u32[]{:S(2)}) collective-permute-start(bf16[512,384]{1,0:T(8,128)(2,1)S(1)} %collective-permute-done.refs_3_), channel_id=1, source_target_pairs={{0,8},{4,12},{8,0},{12,4},{16,24},{20,28},{24,16},{28,20},{1,9},{5... | collective-permute-start | bytes 1179656 | tf_op jit(solution)/shard_map/ppermute | solution.py:44
  84.2 26.5 %collective-permute-start.9 = (bf16[512,384]{1,0:T(8,128)(2,1)}, bf16[512,384]{1,0:T(8,128)(2,1)S(1)}, u32[]{:S(2)}, u32[]{:S(2)}) collective-permute-start(bf16[512,384]{1,0:T(8,128)(2,1)} %copy-done.38), channel_id=1, source_target_pairs={{0,4},{4,0},{8,12},{12,8},{16,20},{20,16},{24,28},{28,24},{1,5},{5... | collective-permute-start | bytes 1179656 | tf_op jit(solution)/shard_map/ppermute | solution.py:44
  86.7 24.0 %collective-permute-start.1 = (bf16[512,384]{1,0:T(8,128)(2,1)S(1)}, bf16[512,384]{1,0:T(8,128)(2,1)S(1)}, u32[]{:S(2)}, u32[]{:S(2)}) collective-permute-start(bf16[512,384]{1,0:T(8,128)(2,1)S(1)} %collective-permute-done.refs_3_), channel_id=1, source_target_pairs={{0,4},{4,0},{8,12},{12,8},{16,20},{20,16},{24,28},{28,24},{1,5},{5... | collective-permute-start | bytes 1179656 | tf_op jit(solution)/shard_map/ppermute | solution.py:44
  161.8 25.8 %collective-permute-start.32 = (bf16[128,2048]{1,0:T(8,128)(2,1)S(1)}, bf16[128,2048]{1,0:T(8,128)(2,1)S(1)}, u32[]{:S(2)}, u32[]{:S(2)}) collective-permute-start(bf16[128,2048]{1,0:T(8,128)(2,1)S(1)} %bitcast.69), channel_id=1, source_target_pairs={{0,3},{1,2},{2,1},{3,0},{4,7},{5,6},{6,5},{7,4},{8,11},{9,10},{10,... | collective-permute-start | bytes 1572872 | tf_op jit(solution)/shard_map/ppermute | solution.py:44
  198.8 25.3 %collective-permute-start.34 = (bf16[128,2048]{1,0:T(8,128)(2,1)S(1)}, bf16[128,2048]{1,0:T(8,128)(2,1)S(1)}, u32[]{:S(2)}, u32[]{:S(2)}) collective-permute-start(bf16[128,2048]{1,0:T(8,128)(2,1)S(1)} %get-tuple-element.76.refs_0_.refs_1_.refs_5_), channel_id=1, source_target_pairs={{0,1},{1,0},{2,3},{3,2},{4,5},{5,4},{6,7},{7,6},{8,9},{9,8},{10,11... | collective-permute-start | bytes 1572872 | tf_op jit(solution)/shard_map/ppermute | solution.py:44
  214.8 25.1 %collective-permute-start.30 = (bf16[128,2048]{1,0:T(8,128)(2,1)S(1)}, bf16[128,2048]{1,0:T(8,128)(2,1)S(1)}, u32[]{:S(2)}, u32[]{:S(2)}) collective-permute-start(bf16[128,2048]{1,0:T(8,128)(2,1)S(1)} %collective-permute-done.29.refs_1_.refs_4_.refs_8_), channel_id=1, source_target_pairs={{0,1},{1,0},{2,3},{3,2},{4,5},{5,4},{6,7},{7,6},{8,9},{9,8},{10,11... | collective-permute-start | bytes 1572872 | tf_op jit(solution)/shard_map/ppermute | solution.py:44
  263.9 25.8 %collective-permute-start.35 = (bf16[2,1024,2048]{2,1,0:T(8,128)(2,1)}, bf16[2,1024,2048]{2,1,0:T(8,128)(2,1)S(1)}, u32[]{:S(2)}, u32[]{:S(2)}) collective-permute-start(bf16[2,1024,2048]{2,1,0:T(8,128)(2,1)} %shard_map.144), channel_id=1, source_target_pairs={{0,4},{4,0},{8,12},{12,8},{16,20},{20,16},{24,28},{28,24},{1,5},{5... | collective-permute-start | bytes 25165832 | tf_op jit(solution)/shard_map/ppermute | solution.py:44
  300.8 24.5 %collective-permute-start.37 = (bf16[128,2048]{1,0:T(8,128)(2,1)S(1)}, bf16[128,2048]{1,0:T(8,128)(2,1)S(1)}, u32[]{:S(2)}, u32[]{:S(2)}) collective-permute-start(bf16[128,2048]{1,0:T(8,128)(2,1)S(1)} %copy-done.29), channel_id=1, source_target_pairs={{0,1},{1,0},{2,3},{3,2},{4,5},{5,4},{6,7},{7,6},{8,9},{9,8},{10,11... | collective-permute-start | bytes 1572872 | tf_op jit(solution)/shard_map/ppermute | solution.py:44
  373.1 24.0 %collective-permute-start.63 = (bf16[128,2048]{1,0:T(8,128)(2,1)}, bf16[128,2048]{1,0:T(8,128)(2,1)}, u32[]{:S(2)}, u32[]{:S(2)}) collective-permute-start(bf16[128,2048]{1,0:T(8,128)(2,1)} %get-tuple-element.123.refs_1_.refs_5_), channel_id=1, source_target_pairs={{0,3},{1,2},{2,1},{3,0},{4,7},{5,6},{6,5},{7,4},{8,11},{9,10},{10,... | collective-permute-start | bytes 1572872 | tf_op jit(solution)/shard_map/ppermute | solution.py:44
  390.5 107.2 %all-to-all-start = ((bf16[4,128,1024]{2,1,0:T(8,128)(2,1)}), bf16[4,128,1024]{2,1,0:T(8,128)(2,1)}, u32[]{:S(2)}, u32[]{:S(2)}) async-start(bf16[4,128,1024]{2,1,0:T(8,128)(2,1)} %bitcast.77), calls=%async_computation | async-start | bytes 2097152 | tf_op jit(solution)/shard_map/all_to_all | solution.py:1166
  395.1 32.0 %collective-permute-start.62 = (bf16[128,2048]{1,0:T(8,128)(2,1)}, bf16[128,2048]{1,0:T(8,128)(2,1)}, u32[]{:S(2)}, u32[]{:S(2)}) collective-permute-start(bf16[128,2048]{1,0:T(8,128)(2,1)} %get-tuple-element.123.refs_1_.refs_5_), channel_id=1, source_target_pairs={{0,1},{1,0},{2,3},{3,2},{4,5},{5,4},{6,7},{7,6},{8,9},{9,8},{10,11... | collective-permute-start | bytes 1572872 | tf_op jit(solution)/shard_map/ppermute | solution.py:44
  397.1 55.2 %collective-permute-start.64 = (bf16[128,2048]{1,0:T(8,128)(2,1)}, bf16[128,2048]{1,0:T(8,128)(2,1)}, u32[]{:S(2)}, u32[]{:S(2)}) collective-permute-start(bf16[128,2048]{1,0:T(8,128)(2,1)} %collective-permute-done.63.refs_8_), channel_id=1, source_target_pairs={{0,1},{1,0},{2,3},{3,2},{4,5},{5,4},{6,7},{7,6},{8,9},{9,8},{10,11... | collective-permute-start | bytes 1572872 | tf_op jit(solution)/shard_map/ppermute | solution.py:44
  399.5 66.6 %collective-permute-start.51 = (bf16[128,2048]{1,0:T(8,128)(2,1)}, bf16[128,2048]{1,0:T(8,128)(2,1)}, u32[]{:S(2)}, u32[]{:S(2)}) collective-permute-start(bf16[128,2048]{1,0:T(8,128)(2,1)} %copy-done.15), channel_id=1, source_target_pairs={{0,3},{1,2},{2,1},{3,0},{4,7},{5,6},{6,5},{7,4},{8,11},{9,10},{10,... | collective-permute-start | bytes 1572872 | tf_op jit(solution)/shard_map/ppermute | solution.py:44
  404.6 51.2 %collective-permute-start.59 = (bf16[128,512]{1,0:T(8,128)(2,1)}, bf16[128,512]{1,0:T(8,128)(2,1)S(1)}, u32[]{:S(2)}, u32[]{:S(2)}) collective-permute-start(bf16[128,512]{1,0:T(8,128)(2,1)} %copy.85), channel_id=1, source_target_pairs={{0,1},{1,0},{2,3},{3,2},{4,5},{5,4},{6,7},{7,6},{8,9},{9,8},{10,11... | collective-permute-start | bytes 393224 | tf_op jit(solution)/shard_map/ppermute | solution.py:44
  406.3 49.5 %collective-permute-start.60 = (bf16[128,512]{1,0:T(8,128)(2,1)}, bf16[128,512]{1,0:T(8,128)(2,1)}, u32[]{:S(2)}, u32[]{:S(2)}) collective-permute-start(bf16[128,512]{1,0:T(8,128)(2,1)} %copy.86), channel_id=1, source_target_pairs={{0,2},{1,3},{2,0},{3,1},{4,6},{5,7},{6,4},{7,5},{8,10},{9,11},{10,... | collective-permute-start | bytes 393224 | tf_op jit(solution)/shard_map/ppermute | solution.py:44
  427.1 32.6 %collective-permute-start.61 = (bf16[128,512]{1,0:T(8,128)(2,1)}, bf16[128,512]{1,0:T(8,128)(2,1)S(1)}, u32[]{:S(2)}, u32[]{:S(2)}) collective-permute-start(bf16[128,512]{1,0:T(8,128)(2,1)} %copy.87), channel_id=1, source_target_pairs={{0,3},{1,2},{2,1},{3,0},{4,7},{5,6},{6,5},{7,4},{8,11},{9,10},{10,... | collective-permute-start | bytes 393224 | tf_op jit(solution)/shard_map/ppermute | solution.py:44
  452.3 34.0 %collective-permute-start.50 = (bf16[128,2048]{1,0:T(8,128)(2,1)S(1)}, bf16[128,2048]{1,0:T(8,128)(2,1)S(1)}, u32[]{:S(2)}, u32[]{:S(2)}) collective-permute-start(bf16[128,2048]{1,0:T(8,128)(2,1)S(1)} %copy-done.16), channel_id=1, source_target_pairs={{0,1},{1,0},{2,3},{3,2},{4,5},{5,4},{6,7},{7,6},{8,9},{9,8},{10,11... | collective-permute-start | bytes 1572872 | tf_op jit(solution)/shard_map/ppermute | solution.py:44
  466.1 40.8 %collective-permute-start.65 = (bf16[4,64,2048]{2,1,0:T(8,128)(2,1)}, bf16[4,64,2048]{2,1,0:T(8,128)(2,1)}, u32[]{:S(2)}, u32[]{:S(2)}) collective-permute-start(bf16[4,64,2048]{2,1,0:T(8,128)(2,1)} %get-tuple-element.128), channel_id=1, source_target_pairs={{0,4},{4,0},{8,12},{12,8},{16,20},{20,16},{24,28},{28,24},{1,5},{5... | collective-permute-start | bytes 3145736 | tf_op jit(solution)/shard_map/ppermute | solution.py:44
  539.1 46.9 %collective-permute-start.45 = (bf16[128,2048]{1,0:T(8,128)(2,1)S(1)}, bf16[128,2048]{1,0:T(8,128)(2,1)S(1)}, u32[]{:S(2)}, u32[]{:S(2)}) collective-permute-start(bf16[128,2048]{1,0:T(8,128)(2,1)S(1)} %get-tuple-element.103), channel_id=1, source_target_pairs={{0,2},{1,3},{2,0},{3,1},{4,6},{5,7},{6,4},{7,5},{8,10},{9,11},{10,... | collective-permute-start | bytes 1572872 | tf_op jit(solution)/shard_map/ppermute | solution.py:44
  542.1 43.9 %collective-permute-start.44 = (bf16[128,2048]{1,0:T(8,128)(2,1)S(1)}, bf16[128,2048]{1,0:T(8,128)(2,1)S(1)}, u32[]{:S(2)}, u32[]{:S(2)}) collective-permute-start(bf16[128,2048]{1,0:T(8,128)(2,1)S(1)} %get-tuple-element.101), channel_id=1, source_target_pairs={{0,1},{1,0},{2,3},{3,2},{4,5},{5,4},{6,7},{7,6},{8,9},{9,8},{10,11... | collective-permute-start | bytes 1572872 | tf_op jit(solution)/shard_map/ppermute | solution.py:44
  (106 other events, 2093.6 us)
Sparse Core Ops, SparseCore 0:
  39.6 28.1 all-gather.4
  70.3 62.8 all-gather.6
  299.9 125.6 reduce-scatter.1

commit v15 on v14

--- a/solution.py
+++ b/solution.py
@@ -818,10 +818,10 @@
         return values.astype(F32)
     values = values.transpose(1, 0, 2)
     matrices, rows, hidden = values.shape
-    block = pl.BlockSpec((1, rows // 2, hidden), lambda k, i: (k, i, 0))
+    block = pl.BlockSpec((1, rows // 4, hidden), lambda k, i: (k, i, 0))
     return pl.pallas_call(
         widen_kernel,
-        grid=(matrices, 2),
+        grid=(matrices, 4),
         out_shape=jax.ShapeDtypeStruct(values.shape, F32),
         in_specs=[block],
         out_specs=block,
@@ -1176,8 +1176,8 @@
     qkv_grad, gain_grad, term_grad = finish_last(
         qkv_sums, own_rows_of(qkv_full, own_rows), own_rows_of(attn_gain, own_rows)
     )
-    output = (residual + share_finish(after(out_sum, qkv_sums[2:3]))).astype(BF)
     out_weight_grad = share_finish(out_sums)
+    output = (residual + share_finish(after(out_sum, out_weight_grad))).astype(BF)
     return (
         output[None],
         input_grad[None],

time: 601 us -> 604 us (level)
  no operation moved by 1% of the time
where the time goes in v15:
time: 604 us; the launch traced here: 602 us
  waiting for transfers between devices  287 us (48%)
  Pallas kernels  165 us (27%)
  starting transfers between devices  88.1 us (15%)
  local copies, waits for them, and re-layouts  34.6 us (6%)
  between operations  14.5 us (2%)
  other arithmetic  12.6 us (2%)
    ppermute x69, waiting for transfers between devices, swap(): return lax.ppermute(value, axis, [(i, i ^ offset) for i in range(count)])  276 us
    ppermute x69, starting transfers between devices, swap(): return lax.ppermute(value, axis, [(i, i ^ offset) for i in range(count)])  83.4 us
    pallas_call x4, Pallas kernels, half_products(): pl.pallas_call(lambda *refs: products_kernel(count, kept, *refs), grid_sp...  32.8 us
    pallas_call x2, Pallas kernels, ffn_middle(): pl.pallas_call(lambda *refs: ffn_kernel(len(blocks), len(earlier), *refs)...  28.1 us
    unnamed x123, local copies, waits for them, and re-layouts  20.2 us
    pallas_call x1, Pallas kernels, attend_back(): pl.pallas_call(lambda *refs: attend_back_kernel(KEY_CHUNK, *refs), grid=(...  20 us
    pallas_call x1, Pallas kernels, attend(): pl.pallas_call(lambda *refs: attend_kernel(KEY_CHUNK, *refs), grid=(KV,),...  12.8 us
    pallas_call x2, Pallas kernels, out_call(): pl.pallas_call(lambda *refs: out_kernel(back, *refs), out_shape=out_shape...  12.3 us
  transfers between devices with their start and end apart: 73, of which 43 were waited for; matrix products, arithmetic and copies ran while one was open for 5% of the time, Pallas kernels for 20%

profile of v15, /device:TPU:0, one launch (start us, length us, event | category | flops | bytes accessed | tf_op | source)
XLA Modules:
  0.0 602.1 jit_solution(12904528818830836674)
XLA Ops:
  22.9 8.1 %collective-permute-start.16 = (bf16[512,384]{1,0:T(8,128)(2,1)S(1)}, bf16[512,384]{1,0:T(8,128)(2,1)S(1)}, u32[]{:S(2)}, u32[]{:S(2)}) collective-permute-start(bf16[512,384]{1,0:T(8,128)(2,1)S(1)} %collective-permute-done.8.refs_11_), channel_id=1, source_target_pairs={{0,1},{1,0},{2,3},{3,2},{4,5},{5,4},{6,7},{7,6},{8,9},{9,8},{10,11... | collective-permute-start | bytes 1179656 | tf_op jit(solution)/shard_map/ppermute | solution.py:44
  57.1 10.8 %all-gather.5.cloned.1.call-done = bf16[2048,256]{1,0:T(8,128)(2,1)} async-done(((bf16[512,256]{1,0:T(8,128)(2,1)}), bf16[2048,256]{1,0:T(8,128)(2,1)}) %all-gather.5.cloned.1.call-update) | async-done | bytes 1048592 | tf_op jit(solution)/shard_map/all_gather | solution.py:191
  86.7 11.4 %collective-permute-done.4.refs_7_ = bf16[512,384]{1,0:T(8,128)(2,1)} collective-permute-done((bf16[512,384]{1,0:T(8,128)(2,1)S(1)}, bf16[512,384]{1,0:T(8,128)(2,1)}, u32[]{:S(2)}, u32[]{:S(2)}) %collective-permute-start.4) | collective-permute-done | bytes 393248 | tf_op jit(solution)/shard_map/ppermute | solution.py:44
  98.1 10.6 %collective-permute-done.12.refs_15_ = bf16[512,384]{1,0:T(8,128)(2,1)} collective-permute-done((bf16[512,384]{1,0:T(8,128)(2,1)}, bf16[512,384]{1,0:T(8,128)(2,1)}, u32[]{:S(2)}, u32[]{:S(2)}) %collective-permute-start.12) | collective-permute-done | bytes 393248 | tf_op jit(solution)/shard_map/ppermute | solution.py:44
  111.3 17.0 %collective-permute-done.14.refs_17_ = bf16[512,384]{1,0:T(8,128)(2,1)S(1)} collective-permute-done((bf16[512,384]{1,0:T(8,128)(2,1)}, bf16[512,384]{1,0:T(8,128)(2,1)S(1)}, u32[]{:S(2)}, u32[]{:S(2)}) %collective-permute-start.14) | collective-permute-done | bytes 393248 | tf_op jit(solution)/shard_map/ppermute | solution.py:44
  135.2 9.6 %pieces.1 = (bf16[128,2048]{1,0:T(8,128)(2,1)S(1)}, bf16[128,1024]{1,0:T(8,128)(2,1)S(1)}, bf16[2048,3072]{1,0:T(8,128)(2,1)}) custom-call(s32[2]{0:T(128)S(1)} %pad_add_fusion.refs_0_, bf16[128,2048]{1,0:T(8,128)(2,1)S(1)} %fusion.2.refs_1_, bf16[512,3072]{1,0:T(8,128)(2,1)} %refs_2_.3, bf16[512,384]{1,0:T(8,128)(2,1)} %copy-done.40, ...), custom_call_target="tpu_custom_call" | custom-call | flops 1610612736 | bytes 25165824 | tf_op jit(solution)/shard_map/pieces/pallas_call | solution.py:161
  164.1 12.8 %attend.1 = (bf16[128,2048]{1,0:T(8,128)(2,1)}, f32[128,2048]{1,0:T(8,128)S(1)}, f32[8,1,512]{2,1,0:T(1,128)S(1)}) custom-call(bf16[128,2048]{1,0:T(8,128)(2,1)S(1)} %get-tuple-element.70.refs_0_, bf16[512,1024]{1,0:T(8,128)(2,1)S(1)} %constant_dynamic-update-slice_fusion.3.refs_1_.refs_2_.refs_3_.refs_4_, ...), custom_call_target="tpu_custom_call" | custom-call | flops 1073741824 | bytes 2097152 | tf_op jit(solution)/shard_map/attend/pallas_call | solution.py:537
  177.9 9.7 %collective-permute-done.32.refs_3_.refs_4_.refs_8_ = bf16[128,2048]{1,0:T(8,128)(2,1)S(1)} collective-permute-done((bf16[128,2048]{1,0:T(8,128)(2,1)S(1)}, bf16[128,2048]{1,0:T(8,128)(2,1)S(1)}, u32[]{:S(2)}, u32[]{:S(2)}) %collective-permute-start.32) | collective-permute-done | bytes 524320 | tf_op jit(solution)/shard_map/ppermute | solution.py:44
  203.2 8.6 %act.1.refs_2_ = f32[512,2048]{1,0:T(8,128)} custom-call(bf16[128,2048]{1,0:T(8,128)(2,1)S(1)} %bitcast.70, bf16[128,2048]{1,0:T(8,128)(2,1)S(1)} %collective-permute-done.31.refs_1_.refs_2_.refs_6_, bf16[128,2048]{1,0:T(8,128)(2,1)S(1)} %collective-permute-done.33.refs_2_.refs_3_.refs_7_, ...), custom_call_target="tpu_custom_call" | custom-call | flops 4294967296 | bytes 8388608 | tf_op jit(solution)/shard_map/act/pallas_call | solution.py:844
  224.1 14.0 %ffn.2 = (bf16[3,512,2048]{2,1,0:T(8,128)(2,1)}, f32[128,2048]{1,0:T(8,128)S(1)}, bf16[128,2048]{1,0:T(8,128)(2,1)S(1)}) custom-call(bf16[128,2048]{1,0:T(8,128)(2,1)S(1)} %get-tuple-element.76.refs_0_.refs_1_.refs_5_, bf16[128,2048]{1,0:T(8,128)(2,1)S(1)} %collective-permute-done.34.refs_1_.refs_2_.refs_6_, f32[512,2048]{1,0:T(8,128)} %act.1.refs_2_, ...), custom_call_target="tpu_custom_call" | custom-call | flops 8589934592 | bytes 16777216 | tf_op jit(solution)/shard_map/ffn/pallas_call | solution.py:705
  239.9 14.0 %ffn.3 = (bf16[3,512,2048]{2,1,0:T(8,128)(2,1)}, bf16[128,2048]{1,0:T(8,128)(2,1)S(1)}, f32[128,2048]{1,0:T(8,128)S(1)}) custom-call(bf16[128,2048]{1,0:T(8,128)(2,1)S(1)} %collective-permute-done.30.refs_0_.refs_3_.refs_7_, bf16[128,2048]{1,0:T(8,128)(2,1)S(1)} %collective-permute-done.29.refs_1_.refs_4_.refs_8_, ...), custom_call_target="tpu_custom_call", output_to_operand_aliasing={{0}: (4, {})} | custom-call | flops 8589934592 | bytes 16777216 | tf_op jit(solution)/shard_map/ffn/pallas_call | solution.py:705
  254.0 9.9 %shard_map.144 = bf16[2,1024,2048]{2,1,0:T(8,128)(2,1)} custom-call(s32[2]{0:T(128)S(1)} %pad_add_fusion.refs_0_, bf16[128,2048]{1,0:T(8,128)(2,1)S(1)} %get-tuple-element.76.refs_0_.refs_1_.refs_5_, bf16[128,2048]{1,0:T(8,128)(2,1)S(1)} %collective-permute-done.34.refs_1_.refs_2_.refs_6_, ...), custom_call_target="tpu_custom_call" | custom-call | flops 4294967296 | bytes 8388608 | tf_op jit(solution)/shard_map/pallas_call | solution.py:767
  270.7 12.5 %collective-permute-done.36.refs_10_ = bf16[1,1024,2048]{2,1,0:T(8,128)(2,1)S(1)} collective-permute-done((bf16[1,1024,2048]{2,1,0:T(8,128)(2,1)}, bf16[1,1024,2048]{2,1,0:T(8,128)(2,1)S(1)}, u32[]{:S(2)}, u32[]{:S(2)}) %collective-permute-start.36) | collective-permute-done | bytes 4194336 | tf_op jit(solution)/shard_map/ppermute | solution.py:44
  289.6 10.2 %shard_map.147 = bf16[3,1024,2048]{2,1,0:T(8,128)(2,1)} custom-call(s32[2]{0:T(128)S(1)} %pad_add_fusion.refs_0_, bf16[128,2048]{1,0:T(8,128)(2,1)S(1)} %get-tuple-element.76.refs_0_.refs_1_.refs_5_, bf16[128,2048]{1,0:T(8,128)(2,1)S(1)} %collective-permute-done.34.refs_1_.refs_2_.refs_6_, ...), custom_call_target="tpu_custom_call", output_to_operand_aliasing={{}: (11, {})} | custom-call | flops 4294967296 | bytes 8388608 | tf_op jit(solution)/shard_map/pallas_call | solution.py:767
  301.9 13.0 %collective-permute-done.38 = bf16[128,2048]{1,0:T(8,128)(2,1)S(1)} collective-permute-done((bf16[128,2048]{1,0:T(8,128)(2,1)}, bf16[128,2048]{1,0:T(8,128)(2,1)S(1)}, u32[]{:S(2)}, u32[]{:S(2)}) %collective-permute-start.38) | collective-permute-done | bytes 524320 | tf_op jit(solution)/shard_map/ppermute | solution.py:44
  317.2 8.1 %collective-permute-done.37 = bf16[128,2048]{1,0:T(8,128)(2,1)S(1)} collective-permute-done((bf16[128,2048]{1,0:T(8,128)(2,1)S(1)}, bf16[128,2048]{1,0:T(8,128)(2,1)S(1)}, u32[]{:S(2)}, u32[]{:S(2)}) %collective-permute-start.37) | collective-permute-done | bytes 524320 | tf_op jit(solution)/shard_map/ppermute | solution.py:44
  325.3 13.2 %collective-permute-done.39 = bf16[128,2048]{1,0:T(8,128)(2,1)S(1)} collective-permute-done((bf16[128,2048]{1,0:T(8,128)(2,1)S(1)}, bf16[128,2048]{1,0:T(8,128)(2,1)S(1)}, u32[]{:S(2)}, u32[]{:S(2)}) %collective-permute-start.39) | collective-permute-done | bytes 524320 | tf_op jit(solution)/shard_map/ppermute | solution.py:44
  346.4 20.0 %att_b.1 = (bf16[128,2048]{1,0:T(8,128)(2,1)S(1)}, bf16[2,512,512]{2,1,0:T(8,128)(2,1)S(1)}, bf16[2,512,512]{2,1,0:T(8,128)(2,1)S(1)}) custom-call(bf16[128,2048]{1,0:T(8,128)(2,1)S(1)} %copy-done.23, bf16[128,2048]{1,0:T(8,128)(2,1)S(1)} %out_b.1.refs_1_, f32[128,2048]{1,0:T(8,128)S(1)} %copy-done.34, bf16[512,1024]{1,0:T(8,128)(2,1)} %copy-done.20, ...), custom_call_target="tpu_custom_call" | custom-call | flops 2684354560 | bytes 4194304 | tf_op jit(solution)/shard_map/att_b/pallas_call | solution.py:602
  411.0 16.1 %collective-permute-done.50.refs_6_ = bf16[128,2048]{1,0:T(8,128)(2,1)} collective-permute-done((bf16[128,2048]{1,0:T(8,128)(2,1)}, bf16[128,2048]{1,0:T(8,128)(2,1)}, u32[]{:S(2)}, u32[]{:S(2)}) %collective-permute-start.50) | collective-permute-done | bytes 524320 | tf_op jit(solution)/shard_map/ppermute | solution.py:44
  430.7 8.9 %one_b.1 = f32[128,2048]{1,0:T(8,128)} custom-call(bf16[128,2048]{1,0:T(8,128)(2,1)S(1)} %copy-done.16, bf16[512,1024]{1,0:T(8,128)(2,1)S(1)} %copy-done.4, bf16[2048,3072]{1,0:T(8,128)(2,1)} %get-tuple-element.98.w_ref, bf16[128,2048]{1,0:T(8,128)(2,1)S(1)} %bitcast.76, f32[1,2048]{1,0:T(1,128)S(1)} %bitcast.78, f32[128,2048]{1,0:T(8,128)S(1)} %copy-done.7), custom_call_target="tpu_custom_call" | custom-call | flops 1610612736 | bytes 12582912 | tf_op jit(solution)/shard_map/one_b/pallas_call | solution.py:337
  439.6 12.8 %collective-permute-done.52.refs_7_ = bf16[128,2048]{1,0:T(8,128)(2,1)} collective-permute-done((bf16[128,2048]{1,0:T(8,128)(2,1)}, bf16[128,2048]{1,0:T(8,128)(2,1)}, u32[]{:S(2)}, u32[]{:S(2)}) %collective-permute-start.52) | collective-permute-done | bytes 524320 | tf_op jit(solution)/shard_map/ppermute | solution.py:44
  468.2 12.7 %collective-permute-done.63 = f32[1,2048]{1,0:T(1,128)S(1)} collective-permute-done((f32[1,2048]{1,0:T(1,128)S(1)}, f32[1,2048]{1,0:T(1,128)S(1)}, u32[]{:S(2)}, u32[]{:S(2)}) %collective-permute-start.63) | collective-permute-done | bytes 8224 | tf_op jit(solution)/shard_map/ppermute | solution.py:44
  554.9 31.2 %collective-permute-done.45 = bf16[128,2048]{1,0:T(8,128)(2,1)S(1)} collective-permute-done((bf16[128,2048]{1,0:T(8,128)(2,1)S(1)}, bf16[128,2048]{1,0:T(8,128)(2,1)S(1)}, u32[]{:S(2)}, u32[]{:S(2)}) %collective-permute-start.45) | collective-permute-done | bytes 524320 | tf_op jit(solution)/shard_map/ppermute | solution.py:44
  587.2 8.4 %wide.1 = f32[3,256,2048]{2,1,0:T(8,128)} custom-call(bf16[3,256,2048]{2,1,0:T(8,128)(2,1)} %bitcast.90), custom_call_target="tpu_custom_call" | custom-call | tf_op jit(solution)/shard_map/wide/pallas_call | solution.py:822
  (340 shorter events, 284.1 us)
Async XLA Ops:
  7.2 60.6 %all-gather.5.cloned.1.call-start = ((), (), s32[]{:S(2)}) async-start(), calls=%async_computation.3 | async-start | bytes 1310720 | tf_op jit(solution)/shard_map/all_gather | solution.py:191
  39.5 148.1 %all-gather.7.cloned.1.call-start = ((), (), s32[]{:S(2)}) async-start(), calls=%async_computation.4 | async-start | bytes 7077888 | tf_op jit(solution)/shard_map/all_gather | solution.py:198
  70.0 517.1 %reduce-scatter.2.cloned.1.call-start = ((), (), s32[]{:S(2)}) async-start(), calls=%async_computation.2 | async-start | bytes 15728640 | tf_op jit(solution)/shard_map/reduce_scatter | solution.py:808
  82.2 26.5 %collective-permute-start.12 = (bf16[512,384]{1,0:T(8,128)(2,1)}, bf16[512,384]{1,0:T(8,128)(2,1)}, u32[]{:S(2)}, u32[]{:S(2)}) collective-permute-start(bf16[512,384]{1,0:T(8,128)(2,1)} %copy-done.38), channel_id=1, source_target_pairs={{0,16},{4,20},{8,24},{12,28},{16,0},{20,4},{24,8},{28,12},{1,17},{... | collective-permute-start | bytes 1179656 | tf_op jit(solution)/shard_map/ppermute | solution.py:44
  82.8 26.3 %collective-permute-start.2 = (bf16[512,384]{1,0:T(8,128)(2,1)S(1)}, bf16[512,384]{1,0:T(8,128)(2,1)}, u32[]{:S(2)}, u32[]{:S(2)}) collective-permute-start(bf16[512,384]{1,0:T(8,128)(2,1)S(1)} %collective-permute-done.refs_3_), channel_id=1, source_target_pairs={{0,8},{4,12},{8,0},{12,4},{16,24},{20,28},{24,16},{28,20},{1,9},{5... | collective-permute-start | bytes 1179656 | tf_op jit(solution)/shard_map/ppermute | solution.py:44
  84.2 26.5 %collective-permute-start.9 = (bf16[512,384]{1,0:T(8,128)(2,1)}, bf16[512,384]{1,0:T(8,128)(2,1)S(1)}, u32[]{:S(2)}, u32[]{:S(2)}) collective-permute-start(bf16[512,384]{1,0:T(8,128)(2,1)} %copy-done.38), channel_id=1, source_target_pairs={{0,4},{4,0},{8,12},{12,8},{16,20},{20,16},{24,28},{28,24},{1,5},{5... | collective-permute-start | bytes 1179656 | tf_op jit(solution)/shard_map/ppermute | solution.py:44
  86.7 24.0 %collective-permute-start.1 = (bf16[512,384]{1,0:T(8,128)(2,1)S(1)}, bf16[512,384]{1,0:T(8,128)(2,1)S(1)}, u32[]{:S(2)}, u32[]{:S(2)}) collective-permute-start(bf16[512,384]{1,0:T(8,128)(2,1)S(1)} %collective-permute-done.refs_3_), channel_id=1, source_target_pairs={{0,4},{4,0},{8,12},{12,8},{16,20},{20,16},{24,28},{28,24},{1,5},{5... | collective-permute-start | bytes 1179656 | tf_op jit(solution)/shard_map/ppermute | solution.py:44
  161.8 25.8 %collective-permute-start.32 = (bf16[128,2048]{1,0:T(8,128)(2,1)S(1)}, bf16[128,2048]{1,0:T(8,128)(2,1)S(1)}, u32[]{:S(2)}, u32[]{:S(2)}) collective-permute-start(bf16[128,2048]{1,0:T(8,128)(2,1)S(1)} %bitcast.69), channel_id=1, source_target_pairs={{0,3},{1,2},{2,1},{3,0},{4,7},{5,6},{6,5},{7,4},{8,11},{9,10},{10,... | collective-permute-start | bytes 1572872 | tf_op jit(solution)/shard_map/ppermute | solution.py:44
  198.8 25.3 %collective-permute-start.34 = (bf16[128,2048]{1,0:T(8,128)(2,1)S(1)}, bf16[128,2048]{1,0:T(8,128)(2,1)S(1)}, u32[]{:S(2)}, u32[]{:S(2)}) collective-permute-start(bf16[128,2048]{1,0:T(8,128)(2,1)S(1)} %get-tuple-element.76.refs_0_.refs_1_.refs_5_), channel_id=1, source_target_pairs={{0,1},{1,0},{2,3},{3,2},{4,5},{5,4},{6,7},{7,6},{8,9},{9,8},{10,11... | collective-permute-start | bytes 1572872 | tf_op jit(solution)/shard_map/ppermute | solution.py:44
  214.8 25.1 %collective-permute-start.30 = (bf16[128,2048]{1,0:T(8,128)(2,1)S(1)}, bf16[128,2048]{1,0:T(8,128)(2,1)S(1)}, u32[]{:S(2)}, u32[]{:S(2)}) collective-permute-start(bf16[128,2048]{1,0:T(8,128)(2,1)S(1)} %collective-permute-done.29.refs_1_.refs_4_.refs_8_), channel_id=1, source_target_pairs={{0,1},{1,0},{2,3},{3,2},{4,5},{5,4},{6,7},{7,6},{8,9},{9,8},{10,11... | collective-permute-start | bytes 1572872 | tf_op jit(solution)/shard_map/ppermute | solution.py:44
  263.9 25.8 %collective-permute-start.35 = (bf16[2,1024,2048]{2,1,0:T(8,128)(2,1)}, bf16[2,1024,2048]{2,1,0:T(8,128)(2,1)S(1)}, u32[]{:S(2)}, u32[]{:S(2)}) collective-permute-start(bf16[2,1024,2048]{2,1,0:T(8,128)(2,1)} %shard_map.144), channel_id=1, source_target_pairs={{0,4},{4,0},{8,12},{12,8},{16,20},{20,16},{24,28},{28,24},{1,5},{5... | collective-permute-start | bytes 25165832 | tf_op jit(solution)/shard_map/ppermute | solution.py:44
  300.8 24.5 %collective-permute-start.37 = (bf16[128,2048]{1,0:T(8,128)(2,1)S(1)}, bf16[128,2048]{1,0:T(8,128)(2,1)S(1)}, u32[]{:S(2)}, u32[]{:S(2)}) collective-permute-start(bf16[128,2048]{1,0:T(8,128)(2,1)S(1)} %copy-done.29), channel_id=1, source_target_pairs={{0,1},{1,0},{2,3},{3,2},{4,5},{5,4},{6,7},{7,6},{8,9},{9,8},{10,11... | collective-permute-start | bytes 1572872 | tf_op jit(solution)/shard_map/ppermute | solution.py:44
  373.1 24.0 %collective-permute-start.51 = (bf16[128,2048]{1,0:T(8,128)(2,1)}, bf16[128,2048]{1,0:T(8,128)(2,1)}, u32[]{:S(2)}, u32[]{:S(2)}) collective-permute-start(bf16[128,2048]{1,0:T(8,128)(2,1)} %get-tuple-element.108.refs_1_.refs_5_), channel_id=1, source_target_pairs={{0,3},{1,2},{2,1},{3,0},{4,7},{5,6},{6,5},{7,4},{8,11},{9,10},{10,... | collective-permute-start | bytes 1572872 | tf_op jit(solution)/shard_map/ppermute | solution.py:44
  390.5 107.2 %all-to-all-start = ((bf16[4,128,1024]{2,1,0:T(8,128)(2,1)}), bf16[4,128,1024]{2,1,0:T(8,128)(2,1)}, u32[]{:S(2)}, u32[]{:S(2)}) async-start(bf16[4,128,1024]{2,1,0:T(8,128)(2,1)} %bitcast.77), calls=%async_computation | async-start | bytes 2097152 | tf_op jit(solution)/shard_map/all_to_all | solution.py:1166
  395.1 32.0 %collective-permute-start.50 = (bf16[128,2048]{1,0:T(8,128)(2,1)}, bf16[128,2048]{1,0:T(8,128)(2,1)}, u32[]{:S(2)}, u32[]{:S(2)}) collective-permute-start(bf16[128,2048]{1,0:T(8,128)(2,1)} %get-tuple-element.108.refs_1_.refs_5_), channel_id=1, source_target_pairs={{0,1},{1,0},{2,3},{3,2},{4,5},{5,4},{6,7},{7,6},{8,9},{9,8},{10,11... | collective-permute-start | bytes 1572872 | tf_op jit(solution)/shard_map/ppermute | solution.py:44
  397.1 55.2 %collective-permute-start.52 = (bf16[128,2048]{1,0:T(8,128)(2,1)}, bf16[128,2048]{1,0:T(8,128)(2,1)}, u32[]{:S(2)}, u32[]{:S(2)}) collective-permute-start(bf16[128,2048]{1,0:T(8,128)(2,1)} %collective-permute-done.51.refs_8_), channel_id=1, source_target_pairs={{0,1},{1,0},{2,3},{3,2},{4,5},{5,4},{6,7},{7,6},{8,9},{9,8},{10,11... | collective-permute-start | bytes 1572872 | tf_op jit(solution)/shard_map/ppermute | solution.py:44
  399.5 66.6 %collective-permute-start.61 = (bf16[128,2048]{1,0:T(8,128)(2,1)}, bf16[128,2048]{1,0:T(8,128)(2,1)}, u32[]{:S(2)}, u32[]{:S(2)}) collective-permute-start(bf16[128,2048]{1,0:T(8,128)(2,1)} %copy-done.15), channel_id=1, source_target_pairs={{0,3},{1,2},{2,1},{3,0},{4,7},{5,6},{6,5},{7,4},{8,11},{9,10},{10,... | collective-permute-start | bytes 1572872 | tf_op jit(solution)/shard_map/ppermute | solution.py:44
  404.6 51.2 %collective-permute-start.47 = (bf16[128,512]{1,0:T(8,128)(2,1)}, bf16[128,512]{1,0:T(8,128)(2,1)S(1)}, u32[]{:S(2)}, u32[]{:S(2)}) collective-permute-start(bf16[128,512]{1,0:T(8,128)(2,1)} %copy.85), channel_id=1, source_target_pairs={{0,1},{1,0},{2,3},{3,2},{4,5},{5,4},{6,7},{7,6},{8,9},{9,8},{10,11... | collective-permute-start | bytes 393224 | tf_op jit(solution)/shard_map/ppermute | solution.py:44
  406.3 49.5 %collective-permute-start.48 = (bf16[128,512]{1,0:T(8,128)(2,1)}, bf16[128,512]{1,0:T(8,128)(2,1)}, u32[]{:S(2)}, u32[]{:S(2)}) collective-permute-start(bf16[128,512]{1,0:T(8,128)(2,1)} %copy.86), channel_id=1, source_target_pairs={{0,2},{1,3},{2,0},{3,1},{4,6},{5,7},{6,4},{7,5},{8,10},{9,11},{10,... | collective-permute-start | bytes 393224 | tf_op jit(solution)/shard_map/ppermute | solution.py:44
  427.1 32.6 %collective-permute-start.49 = (bf16[128,512]{1,0:T(8,128)(2,1)}, bf16[128,512]{1,0:T(8,128)(2,1)S(1)}, u32[]{:S(2)}, u32[]{:S(2)}) collective-permute-start(bf16[128,512]{1,0:T(8,128)(2,1)} %copy.87), channel_id=1, source_target_pairs={{0,3},{1,2},{2,1},{3,0},{4,7},{5,6},{6,5},{7,4},{8,11},{9,10},{10,... | collective-permute-start | bytes 393224 | tf_op jit(solution)/shard_map/ppermute | solution.py:44
  452.3 34.0 %collective-permute-start.60 = (bf16[128,2048]{1,0:T(8,128)(2,1)S(1)}, bf16[128,2048]{1,0:T(8,128)(2,1)S(1)}, u32[]{:S(2)}, u32[]{:S(2)}) collective-permute-start(bf16[128,2048]{1,0:T(8,128)(2,1)S(1)} %copy-done.16), channel_id=1, source_target_pairs={{0,1},{1,0},{2,3},{3,2},{4,5},{5,4},{6,7},{7,6},{8,9},{9,8},{10,11... | collective-permute-start | bytes 1572872 | tf_op jit(solution)/shard_map/ppermute | solution.py:44
  466.1 40.8 %collective-permute-start.53 = (bf16[4,64,2048]{2,1,0:T(8,128)(2,1)}, bf16[4,64,2048]{2,1,0:T(8,128)(2,1)}, u32[]{:S(2)}, u32[]{:S(2)}) collective-permute-start(bf16[4,64,2048]{2,1,0:T(8,128)(2,1)} %get-tuple-element.113), channel_id=1, source_target_pairs={{0,4},{4,0},{8,12},{12,8},{16,20},{20,16},{24,28},{28,24},{1,5},{5... | collective-permute-start | bytes 3145736 | tf_op jit(solution)/shard_map/ppermute | solution.py:44
  539.1 46.9 %collective-permute-start.45 = (bf16[128,2048]{1,0:T(8,128)(2,1)S(1)}, bf16[128,2048]{1,0:T(8,128)(2,1)S(1)}, u32[]{:S(2)}, u32[]{:S(2)}) collective-permute-start(bf16[128,2048]{1,0:T(8,128)(2,1)S(1)} %get-tuple-element.103), channel_id=1, source_target_pairs={{0,2},{1,3},{2,0},{3,1},{4,6},{5,7},{6,4},{7,5},{8,10},{9,11},{10,... | collective-permute-start | bytes 1572872 | tf_op jit(solution)/shard_map/ppermute | solution.py:44
  542.1 43.9 %collective-permute-start.44 = (bf16[128,2048]{1,0:T(8,128)(2,1)S(1)}, bf16[128,2048]{1,0:T(8,128)(2,1)S(1)}, u32[]{:S(2)}, u32[]{:S(2)}) collective-permute-start(bf16[128,2048]{1,0:T(8,128)(2,1)S(1)} %get-tuple-element.101), channel_id=1, source_target_pairs={{0,1},{1,0},{2,3},{3,2},{4,5},{5,4},{6,7},{7,6},{8,9},{9,8},{10,11... | collective-permute-start | bytes 1572872 | tf_op jit(solution)/shard_map/ppermute | solution.py:44
  (106 other events, 2093.6 us)
Sparse Core Ops, SparseCore 0:
  39.6 28.1 all-gather.4
  70.3 62.8 all-gather.6
  299.9 125.6 reduce-scatter.1
